TPU v7x, 512 devices: a whole 4x4x16 slice. The times are simulated.
512 devices in a mesh: fine: 128 (over y, z, core), tele: 4 (over x).
Axes of the slice: x: 4, y: 4, z: 16, core: 2. Of those that a mesh axis runs over, the one named last changes fastest.
Arguments:
- right_side: float32 [8192, 320], P(('fine', 'tele')), may hold values from -6 to 6
- fine_inverse: bfloat16 [8192, 320, 320], P(('fine', 'tele')), may hold values from -0.08 to 0.45
- fine_links: int32 [8192, 6], P(('fine', 'tele')), may hold values from -1 to 8191, as said below
- fine_faces: int32 [8192, 6], P(('fine', 'tele')), may hold values from 0 to 23
- coarse_inverse: bfloat16 [1024, 320, 320], P(('fine', 'tele')), may hold values from -0.04 to 0.21
- coarse_links: int32 [1024, 6], P(('fine', 'tele')), may hold values from -1 to 1023, as said below
- coarse_faces: int32 [1024, 6], P(('fine', 'tele')), may hold values from 0 to 23
- face_operators: bfloat16 [24, 80, 80], replicated, may hold values from -1.25 to 1.25
- agglomerate: int32 [8192], P(('fine', 'tele')), may hold values from 0 to 1023, as said below
Outputs:
- solution: float32 [8192, 320], P(('fine', 'tele'))
Inputs may be any that keep to these rules, and one draw needn't show every extreme that they name: `fine_links`: any entry other than -1 is an element held by the same device as the element, or by the device just before or after it in the order of fine+tele, cyclically. `coarse_links`: coarse elements form blocks of 8 consecutive ones; any entry other than -1 lies in the element's own block or in the block just before or after it, cyclically. `agglomerate`: fine element i maps into block i // 64 of 8 consecutive coarse elements; every coarse element collects exactly 8 fine elements.
All inputs are finite; a program needn't handle non-finite values.
Results may differ from a plain program's by a relative error of at most 0.02.
Values may be sent and summed in bfloat16 or wider, within the bound.
No kernel may reach another device: no remote copies, remote signals or barrier semaphores. Data moves between devices by JAX's collectives and lax.ppermute only.
A program may use at most 64 MiB of HBM per device.

v0:
```python
import jax
import jax.numpy as jnp
from jax import lax
from jax.sharding import PartitionSpec as P

FIELDS = 5
NODES = 4
SWEEPS = 3
CYCLES = 2


OPPOSITE = (1, 0, 3, 2, 5, 4)


def passed_along(block, axis, distance):
    devices = range(lax.axis_size(axis))
    route = [((i - distance) % len(devices), i) for i in devices]
    return lax.ppermute(block, axis, route)


def face_table():
    face_size = NODES * NODES
    column = jnp.arange(6 * FIELDS * face_size, dtype=jnp.int32)
    face_index = column // (FIELDS * face_size)
    within = column % (FIELDS * face_size)
    field_index = within // face_size
    first = within // NODES % NODES
    second = within % NODES
    far_node = NODES - 1
    side = jnp.where(face_index % 2 == 0, 0, far_node)
    node_a = jnp.where(face_index < 2, side, first)
    node_b = jnp.where(face_index < 2, first, jnp.where(face_index < 4, side, second))
    node_c = jnp.where(face_index < 4, second, side)
    target = ((field_index * NODES + node_a) * NODES + node_b) * NODES + node_c
    dof_index = jnp.arange(FIELDS * NODES * NODES * NODES, dtype=jnp.int32)
    return (dof_index[:, None] == target[None, :]).astype(jnp.float32)


def take_traces(field_state, table):
    row_count = field_state.shape[0]
    picked = jnp.dot(
        field_state, table, precision=lax.Precision.HIGHEST, preferred_element_type=jnp.float32
    )
    return picked.astype(jnp.bfloat16).reshape(row_count, 6, -1)


def lift_faces(coupled, table):
    return lax.dot_general(
        coupled,
        table,
        (((1,), (1,)), ((), ())),
        precision=lax.Precision.HIGHEST,
        preferred_element_type=jnp.float32,
    )


def neighbour_rows(preceding, own_traces, following, links, position, row_count, devices):
    trace_pool = jnp.concatenate([preceding, own_traces, following], axis=0).reshape(
        -1, own_traces.shape[2]
    )
    clamped = jnp.maximum(links, 0)
    relative = (clamped // row_count - position + 1) % devices
    opposite = jnp.array(OPPOSITE, jnp.int32)
    row_index = (relative * row_count + clamped % row_count) * 6 + opposite[None, :]
    face_rows = jnp.take(trace_pool, row_index.reshape(-1), axis=0).reshape(links.shape[0], 6, -1)
    return jnp.where((links >= 0)[:, :, None], face_rows, jnp.zeros_like(face_rows))


def face_apply(face_operators, face_rows, faces, table):
    flat_rows = face_rows.reshape(-1, face_rows.shape[2])
    face_kinds = faces.reshape(-1)
    products = jnp.einsum(
        "rk,qjk->rqj", flat_rows, face_operators, preferred_element_type=jnp.float32
    )
    picked = face_kinds[:, None] == jnp.arange(face_operators.shape[0], dtype=jnp.int32)[None, :]
    result = jnp.sum(jnp.where(picked[:, :, None], products, 0.0), axis=1)
    return lift_faces(result.reshape(face_rows.shape[0], -1), table)


def fine_coupling(field_state, face_operators, links, faces, position, devices, table):
    own_traces = take_traces(field_state, table)
    preceding = passed_along(own_traces, ("fine", "tele"), 1)
    following = passed_along(own_traces, ("fine", "tele"), -1)
    face_rows = neighbour_rows(
        preceding, own_traces, following, links, position, field_state.shape[0], devices
    )
    return face_apply(face_operators, face_rows, faces, table)


def coarse_coupling(column_traces, face_operators, links, faces, position, devices, table):
    preceding = passed_along(column_traces, "fine", 1)
    following = passed_along(column_traces, "fine", -1)
    face_rows = neighbour_rows(
        preceding, column_traces, following, links, position, column_traces.shape[0], devices
    )
    return face_apply(face_operators, face_rows, faces, table)


def apply_inverse(inverse, lowered):
    return jnp.einsum("nij,nj->ni", inverse, lowered, preferred_element_type=jnp.float32)


def shards(
    right_side,
    fine_inverse,
    fine_links,
    fine_faces,
    coarse_inverse,
    coarse_links,
    coarse_faces,
    face_operators,
    agglomerate,
):
    table = face_table()
    tele_size = lax.axis_size("tele")
    fine_position = lax.axis_index("fine") * tele_size + lax.axis_index("tele")
    fine_devices = lax.axis_size("fine") * tele_size
    column_position = lax.axis_index("fine")
    columns = lax.axis_size("fine")
    column_rows = coarse_inverse.shape[0] * tele_size
    local_target = agglomerate % column_rows
    member = (local_target[:, None] == jnp.arange(column_rows, dtype=jnp.int32)[None, :]).astype(
        jnp.float32
    )
    block_inverse = lax.all_gather(coarse_inverse, "tele", axis=0, tiled=True)
    index_lists = lax.all_gather(
        jnp.concatenate([coarse_links, coarse_faces], axis=1), "tele", axis=0, tiled=True
    )
    block_links = index_lists[:, :6]
    block_faces = index_lists[:, 6:]
    solution = jnp.zeros(right_side.shape, jnp.float32)
    for cycle_index in range(CYCLES):
        for sweep_index in range(SWEEPS):
            if cycle_index == 0 and sweep_index == 0:
                coupled = jnp.zeros(right_side.shape, jnp.float32)
            else:
                coupled = fine_coupling(
                    solution,
                    face_operators,
                    fine_links,
                    fine_faces,
                    fine_position,
                    fine_devices,
                    table,
                )
            lowered = (right_side - coupled).astype(jnp.bfloat16)
            solution = apply_inverse(fine_inverse, lowered)
        residual = lowered.astype(jnp.float32) - fine_coupling(
            solution, face_operators, fine_links, fine_faces, fine_position, fine_devices, table
        )
        partial_sum = jnp.dot(
            member.T, residual, precision=lax.Precision.HIGHEST, preferred_element_type=jnp.float32
        )
        restricted = lax.psum(partial_sum, "tele")
        coarse_state = apply_inverse(block_inverse, restricted.astype(jnp.bfloat16))
        for sweep_index in range(SWEEPS - 1):
            coupled_coarse = coarse_coupling(
                take_traces(coarse_state, table),
                face_operators,
                block_links,
                block_faces,
                column_position,
                columns,
                table,
            )
            coarse_state = apply_inverse(
                block_inverse, (restricted - coupled_coarse).astype(jnp.bfloat16)
            )
        solution = solution + jnp.take(coarse_state, local_target, axis=0)
    return solution


def solution(mesh):
    return jax.shard_map(
        shards,
        mesh=mesh,
        in_specs=(
            P(("fine", "tele"), None),
            P(("fine", "tele"), None, None),
            P(("fine", "tele"), None),
            P(("fine", "tele"), None),
            P(("fine", "tele"), None, None),
            P(("fine", "tele"), None),
            P(("fine", "tele"), None),
            P(),
            P(("fine", "tele")),
        ),
        out_specs=P(("fine", "tele"), None),
        check_vma=False,
    )
```

profile of v0, /device:TPU:1, one launch (start us, length us, event | category | flops | bytes accessed | tf_op | source)
XLA Modules:
  0.0 239.6 jit_solution(18185007734287332940)
XLA Ops:
  7.5 3.3 %fusion.76 = f32[16,1,320]{2,1,0:T(1,128)S(1)} fusion(bf16[16,320,320]{2,1,0:T(8,128)(2,1)} %param.27, bf16[16,320,1]{1,0,2:T(8,128)(2,1)S(1)} %convert_bitcast_fusion), kind=kOutput, calls=%fused_computation.136 | convolution fusion | flops 3276800 | bytes 3307520 | tf_op jit(solution)/shard_map/nij,nj->ni/dot_general | solution.py:100
  11.3 5.8 %collective-permute-start.1 = (bf16[16,6,80]{2,1,0:T(8,128)(2,1)S(1)}, bf16[16,6,80]{2,1,0:T(8,128)(2,1)S(1)}, u32[]{:S(2)}, u32[]{:S(2)}) collective-permute-start(bf16[16,6,80]{2,1,0:T(8,128)(2,1)S(1)} %reshape.333), channel_id=1, source_target_pairs={{1,0},{2,1},{3,2},{4,3},{5,4},{6,5},{7,6},{8,7},{9,8},{10,9},{11,1... | collective-permute-start | bytes 46088 | tf_op jit(solution)/shard_map/ppermute | solution.py:18
  19.1 8.5 %all-gather = s32[4,2,12]{2,1,0:T(2,128)S(1)} all-gather(s32[1,2,12]{2,1,0:T(2,128)S(1)} %add_bitcast_fusion), channel_id=1, replica_groups=mesh['fine'=128,'tele'=4] {'tele'}, dimensions={0}, use_global_device_ids=true | all-gather | bytes 480 | tf_op jit(solution)/shard_map/all_gather | solution.py:126
  30.3 3.3 %fusion.73 = f32[16,1,320]{2,1,0:T(1,128)S(1)} fusion(bf16[16,320,320]{2,1,0:T(8,128)(2,1)} %param.27, bf16[16,320,1]{1,0,2:T(8,128)(2,1)S(1)} %fusion.18), kind=kOutput, calls=%fused_computation.133 | convolution fusion | flops 3276800 | bytes 3307520 | tf_op jit(solution)/shard_map/nij,nj->ni/dot_general | solution.py:100
  34.1 13.4 %collective-permute-start.3 = (bf16[16,6,80]{2,1,0:T(8,128)(2,1)S(1)}, bf16[16,6,80]{2,1,0:T(8,128)(2,1)S(1)}, u32[]{:S(2)}, u32[]{:S(2)}) collective-permute-start(bf16[16,6,80]{2,1,0:T(8,128)(2,1)S(1)} %reshape.337), channel_id=1, source_target_pairs={{1,0},{2,1},{3,2},{4,3},{5,4},{6,5},{7,6},{8,7},{9,8},{10,9},{11,1... | collective-permute-start | bytes 46088 | tf_op jit(solution)/shard_map/ppermute | solution.py:18
  49.4 5.6 %collective-permute-done.2 = bf16[16,6,80]{2,1,0:T(8,128)(2,1)S(1)} collective-permute-done((bf16[16,6,80]{2,1,0:T(8,128)(2,1)S(1)}, bf16[16,6,80]{2,1,0:T(8,128)(2,1)S(1)}, u32[]{:S(2)}, u32[]{:S(2)}) %collective-permute-start.2) | collective-permute-done | bytes 15392 | tf_op jit(solution)/shard_map/ppermute | solution.py:18
  56.7 3.3 %fusion.70 = f32[16,1,320]{2,1,0:T(1,128)S(1)} fusion(bf16[16,320,320]{2,1,0:T(8,128)(2,1)} %param.27, bf16[16,320,1]{1,0,2:T(8,128)(2,1)S(1)} %bitcast.138), kind=kOutput, calls=%fused_computation.130 | convolution fusion | flops 3276800 | bytes 3307520 | tf_op jit(solution)/shard_map/nij,nj->ni/dot_general | solution.py:100
  62.4 3.4 %collective-permute-start.4 = (bf16[16,6,80]{2,1,0:T(8,128)(2,1)S(1)}, bf16[16,6,80]{2,1,0:T(8,128)(2,1)S(1)}, u32[]{:S(2)}, u32[]{:S(2)}) collective-permute-start(bf16[16,6,80]{2,1,0:T(8,128)(2,1)S(1)} %reshape.341), channel_id=1, source_target_pairs={{511,0},{0,1},{1,2},{2,3},{3,4},{4,5},{5,6},{6,7},{7,8},{8,9},{9,1... | collective-permute-start | bytes 46088 | tf_op jit(solution)/shard_map/ppermute | solution.py:18
  65.7 3.1 %collective-permute-done.4 = bf16[16,6,80]{2,1,0:T(8,128)(2,1)S(1)} collective-permute-done((bf16[16,6,80]{2,1,0:T(8,128)(2,1)S(1)}, bf16[16,6,80]{2,1,0:T(8,128)(2,1)S(1)}, u32[]{:S(2)}, u32[]{:S(2)}) %collective-permute-start.4) | collective-permute-done | bytes 15392 | tf_op jit(solution)/shard_map/ppermute | solution.py:18
  70.8 11.1 %psum.14 = f32[8,320]{1,0:T(8,128)S(1)} all-reduce(f32[8,320]{1,0:T(8,128)S(1)} %fusion.145), channel_id=1, replica_groups=mesh['fine'=128,'tele'=4] {'tele'}, use_global_device_ids=true, to_apply=%region_3.5 | all-reduce | flops 2560 | bytes 20480 | tf_op jit(solution)/shard_map/psum | solution.py:154
  84.6 16.0 %collective-permute-start.7 = (bf16[8,6,80]{2,1,0:T(8,128)(2,1)S(1)}, bf16[8,6,80]{2,1,0:T(8,128)(2,1)S(1)}, u32[]{:S(2)}, u32[]{:S(2)}) collective-permute-start(bf16[8,6,80]{2,1,0:T(8,128)(2,1)S(1)} %reshape.345), channel_id=1, source_target_pairs={{4,0},{8,4},{12,8},{16,12},{20,16},{24,20},{28,24},{32,28},{36,32}... | collective-permute-start | bytes 23048 | tf_op jit(solution)/shard_map/ppermute | solution.py:18
  107.9 7.2 %collective-permute-start.9 = (bf16[8,6,80]{2,1,0:T(8,128)(2,1)S(1)}, bf16[8,6,80]{2,1,0:T(8,128)(2,1)S(1)}, u32[]{:S(2)}, u32[]{:S(2)}) collective-permute-start(bf16[8,6,80]{2,1,0:T(8,128)(2,1)S(1)} %reshape.349), channel_id=1, source_target_pairs={{4,0},{8,4},{12,8},{16,12},{20,16},{24,20},{28,24},{32,28},{36,32}... | collective-permute-start | bytes 23048 | tf_op jit(solution)/shard_map/ppermute | solution.py:18
  121.6 8.1 %collective-permute-start.11 = (bf16[16,6,80]{2,1,0:T(8,128)(2,1)S(1)}, bf16[16,6,80]{2,1,0:T(8,128)(2,1)S(1)}, u32[]{:S(2)}, u32[]{:S(2)}) collective-permute-start(bf16[16,6,80]{2,1,0:T(8,128)(2,1)S(1)} %reshape.353), channel_id=1, source_target_pairs={{1,0},{2,1},{3,2},{4,3},{5,4},{6,5},{7,6},{8,7},{9,8},{10,9},{11,1... | collective-permute-start | bytes 46088 | tf_op jit(solution)/shard_map/ppermute | solution.py:18
  131.6 4.5 %collective-permute-done.10 = bf16[16,6,80]{2,1,0:T(8,128)(2,1)S(1)} collective-permute-done((bf16[16,6,80]{2,1,0:T(8,128)(2,1)S(1)}, bf16[16,6,80]{2,1,0:T(8,128)(2,1)S(1)}, u32[]{:S(2)}, u32[]{:S(2)}) %collective-permute-start.10) | collective-permute-done | bytes 15392 | tf_op jit(solution)/shard_map/ppermute | solution.py:18
  137.8 3.3 %fusion.68 = f32[16,1,320]{2,1,0:T(1,128)S(1)} fusion(bf16[16,320,320]{2,1,0:T(8,128)(2,1)} %param.27, bf16[16,320,1]{1,0,2:T(8,128)(2,1)S(1)} %fusion.17), kind=kOutput, calls=%fused_computation.128 | convolution fusion | flops 3276800 | bytes 3307520 | tf_op jit(solution)/shard_map/nij,nj->ni/dot_general | solution.py:100
  143.5 3.5 %collective-permute-start.12 = (bf16[16,6,80]{2,1,0:T(8,128)(2,1)S(1)}, bf16[16,6,80]{2,1,0:T(8,128)(2,1)S(1)}, u32[]{:S(2)}, u32[]{:S(2)}) collective-permute-start(bf16[16,6,80]{2,1,0:T(8,128)(2,1)S(1)} %reshape.357), channel_id=1, source_target_pairs={{511,0},{0,1},{1,2},{2,3},{3,4},{4,5},{5,6},{6,7},{7,8},{8,9},{9,1... | collective-permute-start | bytes 46088 | tf_op jit(solution)/shard_map/ppermute | solution.py:18
  151.7 3.3 %fusion.65 = f32[16,1,320]{2,1,0:T(1,128)S(1)} fusion(bf16[16,320,320]{2,1,0:T(8,128)(2,1)} %param.27, bf16[16,320,1]{1,0,2:T(8,128)(2,1)S(1)} %fusion.16), kind=kOutput, calls=%fused_computation.125 | convolution fusion | flops 3276800 | bytes 3307520 | tf_op jit(solution)/shard_map/nij,nj->ni/dot_general | solution.py:100
  160.7 5.2 %collective-permute-done.14 = bf16[16,6,80]{2,1,0:T(8,128)(2,1)S(1)} collective-permute-done((bf16[16,6,80]{2,1,0:T(8,128)(2,1)S(1)}, bf16[16,6,80]{2,1,0:T(8,128)(2,1)S(1)}, u32[]{:S(2)}, u32[]{:S(2)}) %collective-permute-start.14) | collective-permute-done | bytes 15392 | tf_op jit(solution)/shard_map/ppermute | solution.py:18
  167.6 3.3 %fusion.62 = f32[16,1,320]{2,1,0:T(1,128)S(1)} fusion(bf16[16,320,320]{2,1,0:T(8,128)(2,1)} %param.27, bf16[16,320,1]{1,0,2:T(8,128)(2,1)S(1)} %bitcast.137), kind=kOutput, calls=%fused_computation.122 | convolution fusion | flops 3276800 | bytes 3307520 | tf_op jit(solution)/shard_map/nij,nj->ni/dot_general | solution.py:100
  171.4 4.2 %collective-permute-start.17 = (bf16[16,6,80]{2,1,0:T(8,128)(2,1)S(1)}, bf16[16,6,80]{2,1,0:T(8,128)(2,1)S(1)}, u32[]{:S(2)}, u32[]{:S(2)}) collective-permute-start(bf16[16,6,80]{2,1,0:T(8,128)(2,1)S(1)} %reshape.365), channel_id=1, source_target_pairs={{1,0},{2,1},{3,2},{4,3},{5,4},{6,5},{7,6},{8,7},{9,8},{10,9},{11,1... | collective-permute-start | bytes 46088 | tf_op jit(solution)/shard_map/ppermute | solution.py:18
  177.5 6.4 %collective-permute-done.16 = bf16[16,6,80]{2,1,0:T(8,128)(2,1)S(1)} collective-permute-done((bf16[16,6,80]{2,1,0:T(8,128)(2,1)S(1)}, bf16[16,6,80]{2,1,0:T(8,128)(2,1)S(1)}, u32[]{:S(2)}, u32[]{:S(2)}) %collective-permute-start.16) | collective-permute-done | bytes 15392 | tf_op jit(solution)/shard_map/ppermute | solution.py:18
  185.9 11.1 %psum.15 = f32[8,320]{1,0:T(8,128)S(1)} all-reduce(f32[8,320]{1,0:T(8,128)S(1)} %fusion.144), channel_id=1, replica_groups=mesh['fine'=128,'tele'=4] {'tele'}, use_global_device_ids=true, to_apply=%region_10.14 | all-reduce | flops 2560 | bytes 20480 | tf_op jit(solution)/shard_map/psum | solution.py:154
  198.1 14.9 %collective-permute-start.19 = (bf16[8,6,80]{2,1,0:T(8,128)(2,1)S(1)}, bf16[8,6,80]{2,1,0:T(8,128)(2,1)S(1)}, u32[]{:S(2)}, u32[]{:S(2)}) collective-permute-start(bf16[8,6,80]{2,1,0:T(8,128)(2,1)S(1)} %reshape.369), channel_id=1, source_target_pairs={{4,0},{8,4},{12,8},{16,12},{20,16},{24,20},{28,24},{32,28},{36,32}... | collective-permute-start | bytes 23048 | tf_op jit(solution)/shard_map/ppermute | solution.py:18
  218.8 7.2 %collective-permute-start.21 = (bf16[8,6,80]{2,1,0:T(8,128)(2,1)S(1)}, bf16[8,6,80]{2,1,0:T(8,128)(2,1)S(1)}, u32[]{:S(2)}, u32[]{:S(2)}) collective-permute-start(bf16[8,6,80]{2,1,0:T(8,128)(2,1)S(1)} %reshape.373), channel_id=1, source_target_pairs={{4,0},{8,4},{12,8},{16,12},{20,16},{24,20},{28,24},{32,28},{36,32}... | collective-permute-start | bytes 23048 | tf_op jit(solution)/shard_map/ppermute | solution.py:18
  (187 shorter events, 66.4 us)
Async XLA Ops:
  6.6 75.3 %all-gather.3.cloned.1.call-start = ((), (), s32[]{:S(2)}) async-start(), calls=%async_computation | async-start | bytes 2457600 | tf_op jit(solution)/shard_map/all_gather | solution.py:125
  11.3 17.4 %collective-permute-start.1 = (bf16[16,6,80]{2,1,0:T(8,128)(2,1)S(1)}, bf16[16,6,80]{2,1,0:T(8,128)(2,1)S(1)}, u32[]{:S(2)}, u32[]{:S(2)}) collective-permute-start(bf16[16,6,80]{2,1,0:T(8,128)(2,1)S(1)} %reshape.333), channel_id=1, source_target_pairs={{1,0},{2,1},{3,2},{4,3},{5,4},{6,5},{7,6},{8,7},{9,8},{10,9},{11,1... | collective-permute-start | bytes 46088 | tf_op jit(solution)/shard_map/ppermute | solution.py:18
  17.0 11.6 %collective-permute-start = (bf16[16,6,80]{2,1,0:T(8,128)(2,1)S(1)}, bf16[16,6,80]{2,1,0:T(8,128)(2,1)S(1)}, u32[]{:S(2)}, u32[]{:S(2)}) collective-permute-start(bf16[16,6,80]{2,1,0:T(8,128)(2,1)S(1)} %reshape.333), channel_id=1, source_target_pairs={{511,0},{0,1},{1,2},{2,3},{3,4},{4,5},{5,6},{6,7},{7,8},{8,9},{9,1... | collective-permute-start | bytes 46088 | tf_op jit(solution)/shard_map/ppermute | solution.py:18
  34.1 15.3 %collective-permute-start.3 = (bf16[16,6,80]{2,1,0:T(8,128)(2,1)S(1)}, bf16[16,6,80]{2,1,0:T(8,128)(2,1)S(1)}, u32[]{:S(2)}, u32[]{:S(2)}) collective-permute-start(bf16[16,6,80]{2,1,0:T(8,128)(2,1)S(1)} %reshape.337), channel_id=1, source_target_pairs={{1,0},{2,1},{3,2},{4,3},{5,4},{6,5},{7,6},{8,7},{9,8},{10,9},{11,1... | collective-permute-start | bytes 46088 | tf_op jit(solution)/shard_map/ppermute | solution.py:18
  47.4 7.5 %collective-permute-start.2 = (bf16[16,6,80]{2,1,0:T(8,128)(2,1)S(1)}, bf16[16,6,80]{2,1,0:T(8,128)(2,1)S(1)}, u32[]{:S(2)}, u32[]{:S(2)}) collective-permute-start(bf16[16,6,80]{2,1,0:T(8,128)(2,1)S(1)} %reshape.337), channel_id=1, source_target_pairs={{511,0},{0,1},{1,2},{2,3},{3,4},{4,5},{5,6},{6,7},{7,8},{8,9},{9,1... | collective-permute-start | bytes 46088 | tf_op jit(solution)/shard_map/ppermute | solution.py:18
  60.4 5.3 %collective-permute-start.5 = (bf16[16,6,80]{2,1,0:T(8,128)(2,1)S(1)}, bf16[16,6,80]{2,1,0:T(8,128)(2,1)S(1)}, u32[]{:S(2)}, u32[]{:S(2)}) collective-permute-start(bf16[16,6,80]{2,1,0:T(8,128)(2,1)S(1)} %reshape.341), channel_id=1, source_target_pairs={{1,0},{2,1},{3,2},{4,3},{5,4},{6,5},{7,6},{8,7},{9,8},{10,9},{11,1... | collective-permute-start | bytes 46088 | tf_op jit(solution)/shard_map/ppermute | solution.py:18
  62.4 6.4 %collective-permute-start.4 = (bf16[16,6,80]{2,1,0:T(8,128)(2,1)S(1)}, bf16[16,6,80]{2,1,0:T(8,128)(2,1)S(1)}, u32[]{:S(2)}, u32[]{:S(2)}) collective-permute-start(bf16[16,6,80]{2,1,0:T(8,128)(2,1)S(1)} %reshape.341), channel_id=1, source_target_pairs={{511,0},{0,1},{1,2},{2,3},{3,4},{4,5},{5,6},{6,7},{7,8},{8,9},{9,1... | collective-permute-start | bytes 46088 | tf_op jit(solution)/shard_map/ppermute | solution.py:18
  81.9 38.0 %copy-start.1 = (bf16[8,320,320]{2,1,0:T(8,128)(2,1)S(1)}, bf16[8,320,320]{2,1,0:T(8,128)(2,1)}, u32[]{:S(2)}) copy-start(bf16[8,320,320]{2,1,0:T(8,128)(2,1)} %all-gather.3.cloned.1.call-done) | copy-start | bytes 4915204
  84.6 18.0 %collective-permute-start.7 = (bf16[8,6,80]{2,1,0:T(8,128)(2,1)S(1)}, bf16[8,6,80]{2,1,0:T(8,128)(2,1)S(1)}, u32[]{:S(2)}, u32[]{:S(2)}) collective-permute-start(bf16[8,6,80]{2,1,0:T(8,128)(2,1)S(1)} %reshape.345), channel_id=1, source_target_pairs={{4,0},{8,4},{12,8},{16,12},{20,16},{24,20},{28,24},{32,28},{36,32}... | collective-permute-start | bytes 23048 | tf_op jit(solution)/shard_map/ppermute | solution.py:18
  100.6 3.1 %collective-permute-start.6 = (bf16[8,6,80]{2,1,0:T(8,128)(2,1)S(1)}, bf16[8,6,80]{2,1,0:T(8,128)(2,1)S(1)}, u32[]{:S(2)}, u32[]{:S(2)}) collective-permute-start(bf16[8,6,80]{2,1,0:T(8,128)(2,1)S(1)} %reshape.345), channel_id=1, source_target_pairs={{508,0},{0,4},{4,8},{8,12},{12,16},{16,20},{20,24},{24,28},{28,32}... | collective-permute-start | bytes 23048 | tf_op jit(solution)/shard_map/ppermute | solution.py:18
  107.9 9.2 %collective-permute-start.9 = (bf16[8,6,80]{2,1,0:T(8,128)(2,1)S(1)}, bf16[8,6,80]{2,1,0:T(8,128)(2,1)S(1)}, u32[]{:S(2)}, u32[]{:S(2)}) collective-permute-start(bf16[8,6,80]{2,1,0:T(8,128)(2,1)S(1)} %reshape.349), channel_id=1, source_target_pairs={{4,0},{8,4},{12,8},{16,12},{20,16},{24,20},{28,24},{32,28},{36,32}... | collective-permute-start | bytes 23048 | tf_op jit(solution)/shard_map/ppermute | solution.py:18
  115.2 3.1 %collective-permute-start.8 = (bf16[8,6,80]{2,1,0:T(8,128)(2,1)S(1)}, bf16[8,6,80]{2,1,0:T(8,128)(2,1)S(1)}, u32[]{:S(2)}, u32[]{:S(2)}) collective-permute-start(bf16[8,6,80]{2,1,0:T(8,128)(2,1)S(1)} %reshape.349), channel_id=1, source_target_pairs={{508,0},{0,4},{4,8},{8,12},{12,16},{16,20},{20,24},{24,28},{28,32}... | collective-permute-start | bytes 23048 | tf_op jit(solution)/shard_map/ppermute | solution.py:18
  121.6 10.0 %collective-permute-start.11 = (bf16[16,6,80]{2,1,0:T(8,128)(2,1)S(1)}, bf16[16,6,80]{2,1,0:T(8,128)(2,1)S(1)}, u32[]{:S(2)}, u32[]{:S(2)}) collective-permute-start(bf16[16,6,80]{2,1,0:T(8,128)(2,1)S(1)} %reshape.353), channel_id=1, source_target_pairs={{1,0},{2,1},{3,2},{4,3},{5,4},{6,5},{7,6},{8,7},{9,8},{10,9},{11,1... | collective-permute-start | bytes 46088 | tf_op jit(solution)/shard_map/ppermute | solution.py:18
  129.7 6.4 %collective-permute-start.10 = (bf16[16,6,80]{2,1,0:T(8,128)(2,1)S(1)}, bf16[16,6,80]{2,1,0:T(8,128)(2,1)S(1)}, u32[]{:S(2)}, u32[]{:S(2)}) collective-permute-start(bf16[16,6,80]{2,1,0:T(8,128)(2,1)S(1)} %reshape.353), channel_id=1, source_target_pairs={{511,0},{0,1},{1,2},{2,3},{3,4},{4,5},{5,6},{6,7},{7,8},{8,9},{9,1... | collective-permute-start | bytes 46088 | tf_op jit(solution)/shard_map/ppermute | solution.py:18
  141.6 5.5 %collective-permute-start.13 = (bf16[16,6,80]{2,1,0:T(8,128)(2,1)S(1)}, bf16[16,6,80]{2,1,0:T(8,128)(2,1)S(1)}, u32[]{:S(2)}, u32[]{:S(2)}) collective-permute-start(bf16[16,6,80]{2,1,0:T(8,128)(2,1)S(1)} %reshape.357), channel_id=1, source_target_pairs={{1,0},{2,1},{3,2},{4,3},{5,4},{6,5},{7,6},{8,7},{9,8},{10,9},{11,1... | collective-permute-start | bytes 46088 | tf_op jit(solution)/shard_map/ppermute | solution.py:18
  143.5 6.4 %collective-permute-start.12 = (bf16[16,6,80]{2,1,0:T(8,128)(2,1)S(1)}, bf16[16,6,80]{2,1,0:T(8,128)(2,1)S(1)}, u32[]{:S(2)}, u32[]{:S(2)}) collective-permute-start(bf16[16,6,80]{2,1,0:T(8,128)(2,1)S(1)} %reshape.357), channel_id=1, source_target_pairs={{511,0},{0,1},{1,2},{2,3},{3,4},{4,5},{5,6},{6,7},{7,8},{8,9},{9,1... | collective-permute-start | bytes 46088 | tf_op jit(solution)/shard_map/ppermute | solution.py:18
  155.4 5.3 %collective-permute-start.15 = (bf16[16,6,80]{2,1,0:T(8,128)(2,1)S(1)}, bf16[16,6,80]{2,1,0:T(8,128)(2,1)S(1)}, u32[]{:S(2)}, u32[]{:S(2)}) collective-permute-start(bf16[16,6,80]{2,1,0:T(8,128)(2,1)S(1)} %reshape.361), channel_id=1, source_target_pairs={{1,0},{2,1},{3,2},{4,3},{5,4},{6,5},{7,6},{8,7},{9,8},{10,9},{11,1... | collective-permute-start | bytes 46088 | tf_op jit(solution)/shard_map/ppermute | solution.py:18
  158.0 7.9 %collective-permute-start.14 = (bf16[16,6,80]{2,1,0:T(8,128)(2,1)S(1)}, bf16[16,6,80]{2,1,0:T(8,128)(2,1)S(1)}, u32[]{:S(2)}, u32[]{:S(2)}) collective-permute-start(bf16[16,6,80]{2,1,0:T(8,128)(2,1)S(1)} %reshape.361), channel_id=1, source_target_pairs={{511,0},{0,1},{1,2},{2,3},{3,4},{4,5},{5,6},{6,7},{7,8},{8,9},{9,1... | collective-permute-start | bytes 46088 | tf_op jit(solution)/shard_map/ppermute | solution.py:18
  171.4 6.2 %collective-permute-start.17 = (bf16[16,6,80]{2,1,0:T(8,128)(2,1)S(1)}, bf16[16,6,80]{2,1,0:T(8,128)(2,1)S(1)}, u32[]{:S(2)}, u32[]{:S(2)}) collective-permute-start(bf16[16,6,80]{2,1,0:T(8,128)(2,1)S(1)} %reshape.365), channel_id=1, source_target_pairs={{1,0},{2,1},{3,2},{4,3},{5,4},{6,5},{7,6},{8,7},{9,8},{10,9},{11,1... | collective-permute-start | bytes 46088 | tf_op jit(solution)/shard_map/ppermute | solution.py:18
  175.6 8.4 %collective-permute-start.16 = (bf16[16,6,80]{2,1,0:T(8,128)(2,1)S(1)}, bf16[16,6,80]{2,1,0:T(8,128)(2,1)S(1)}, u32[]{:S(2)}, u32[]{:S(2)}) collective-permute-start(bf16[16,6,80]{2,1,0:T(8,128)(2,1)S(1)} %reshape.365), channel_id=1, source_target_pairs={{511,0},{0,1},{1,2},{2,3},{3,4},{4,5},{5,6},{6,7},{7,8},{8,9},{9,1... | collective-permute-start | bytes 46088 | tf_op jit(solution)/shard_map/ppermute | solution.py:18
  198.1 16.8 %collective-permute-start.19 = (bf16[8,6,80]{2,1,0:T(8,128)(2,1)S(1)}, bf16[8,6,80]{2,1,0:T(8,128)(2,1)S(1)}, u32[]{:S(2)}, u32[]{:S(2)}) collective-permute-start(bf16[8,6,80]{2,1,0:T(8,128)(2,1)S(1)} %reshape.369), channel_id=1, source_target_pairs={{4,0},{8,4},{12,8},{16,12},{20,16},{24,20},{28,24},{32,28},{36,32}... | collective-permute-start | bytes 23048 | tf_op jit(solution)/shard_map/ppermute | solution.py:18
  213.0 3.1 %collective-permute-start.18 = (bf16[8,6,80]{2,1,0:T(8,128)(2,1)S(1)}, bf16[8,6,80]{2,1,0:T(8,128)(2,1)S(1)}, u32[]{:S(2)}, u32[]{:S(2)}) collective-permute-start(bf16[8,6,80]{2,1,0:T(8,128)(2,1)S(1)} %reshape.369), channel_id=1, source_target_pairs={{508,0},{0,4},{4,8},{8,12},{12,16},{16,20},{20,24},{24,28},{28,32}... | collective-permute-start | bytes 23048 | tf_op jit(solution)/shard_map/ppermute | solution.py:18
  218.8 9.2 %collective-permute-start.21 = (bf16[8,6,80]{2,1,0:T(8,128)(2,1)S(1)}, bf16[8,6,80]{2,1,0:T(8,128)(2,1)S(1)}, u32[]{:S(2)}, u32[]{:S(2)}) collective-permute-start(bf16[8,6,80]{2,1,0:T(8,128)(2,1)S(1)} %reshape.373), channel_id=1, source_target_pairs={{4,0},{8,4},{12,8},{16,12},{20,16},{24,20},{28,24},{32,28},{36,32}... | collective-permute-start | bytes 23048 | tf_op jit(solution)/shard_map/ppermute | solution.py:18
  226.0 3.1 %collective-permute-start.20 = (bf16[8,6,80]{2,1,0:T(8,128)(2,1)S(1)}, bf16[8,6,80]{2,1,0:T(8,128)(2,1)S(1)}, u32[]{:S(2)}, u32[]{:S(2)}) collective-permute-start(bf16[8,6,80]{2,1,0:T(8,128)(2,1)S(1)} %reshape.373), channel_id=1, source_target_pairs={{508,0},{0,4},{4,8},{8,12},{12,16},{16,20},{20,24},{24,28},{28,32}... | collective-permute-start | bytes 23048 | tf_op jit(solution)/shard_map/ppermute | solution.py:18
  (8 other events, 147.8 us)
Sparse Core Ops, SparseCore 0:
  19.1 42.5 all-gather.2
where the time goes:
time: 244 us; the launch traced here: 240 us
  starting transfers between devices  108 us (44%)
  matrix products  40 us (16%)
  waiting for transfers between devices  32.1 us (13%)
  blocking collectives  30.7 us (13%)
  between operations  14.2 us (6%)
  local copies, waits for them, and re-layouts  12.1 us (5%)
    ppermute x22, starting transfers between devices, passed_along(): return lax.ppermute(block, axis, route)  108 us
    ppermute x22, waiting for transfers between devices, passed_along(): return lax.ppermute(block, axis, route)  32.1 us
    dot_general x12, matrix products, apply_inverse(): jnp.einsum('nij,nj->ni', inverse, lowered, preferred_element_type=jnp.flo...  27.2 us
    psum x2, blocking collectives, shards(): restricted = lax.psum(partial_sum, 'tele')  22.2 us
    all_gather x1, blocking collectives, shards(): lax.all_gather(jnp.concatenate([coarse_links, coarse_faces], axis=1), 'te...  8.52 us
    gather x11, local copies, waits for them, and re-layouts, neighbour_rows(): jnp.take(trace_pool, row_index.reshape(-1), axis=0)  7.2 us
  transfers between devices with their start and end apart: 23, of which 10 were waited for; matrix products, arithmetic and copies ran while one was open for 6% of the time, Pallas kernels for 0%

commit v1 on v0

v1 whole, which is shorter than its diff:
```python
import functools

import jax
import jax.numpy as jnp
import numpy as np
from jax import lax
from jax.experimental import pallas as pl
from jax.experimental.pallas import tpu as pltpu
from jax.sharding import PartitionSpec as P

FIELDS = 5
NODES = 4
SWEEPS = 3
CYCLES = 2
LANES = 128
OPPOSITE = (1, 0, 3, 2, 5, 4)


def passed_along(block, axis, distance):
    devices = range(lax.axis_size(axis))
    route = [((i - distance) % len(devices), i) for i in devices]
    return lax.ppermute(block, axis, route)


def face_tables():
    cube = np.arange(FIELDS * NODES**3).reshape(FIELDS, NODES, NODES, NODES)
    far = NODES - 1
    faces = (cube[:, 0], cube[:, far], cube[:, :, 0], cube[:, :, far], cube[..., 0], cube[..., far])
    table = np.zeros((cube.size, 6 * LANES), np.float32)
    for k, face in enumerate(faces):
        nodes = face.reshape(-1)
        table[nodes, k * LANES + np.arange(nodes.size)] = 1.0
    return table


def halves(value):
    high = value.astype(jnp.bfloat16)
    low = (value - high.astype(jnp.float32)).astype(jnp.bfloat16)
    return high, low


def exact_dot(left, right):
    high, low = halves(right)
    return jnp.dot(left, high, preferred_element_type=jnp.float32) + jnp.dot(
        left, low, preferred_element_type=jnp.float32
    )


def coupling(states, rows, kinds, operators, pick, lift):
    count = states[0].shape[0]
    pool = jnp.concatenate([state.astype(jnp.float32) for state in states], axis=0).astype(jnp.bfloat16)
    traces = jnp.dot(pool, pick, preferred_element_type=jnp.float32).astype(jnp.bfloat16)
    chosen = rows == lax.broadcasted_iota(jnp.int32, (6 * count, pool.shape[0]), 1)
    chosen = jnp.where(chosen, 1.0, 0.0)
    face_rows = jnp.concatenate(
        [
            jnp.dot(
                chosen[k * count : (k + 1) * count].astype(jnp.bfloat16),
                traces[:, OPPOSITE[k] * LANES : (OPPOSITE[k] + 1) * LANES],
                preferred_element_type=jnp.float32,
            )
            for k in range(6)
        ],
        axis=0,
    )
    types = operators.shape[0] // LANES
    kinds = jnp.broadcast_to(kinds, face_rows.shape)
    spread = jnp.concatenate(
        [jnp.where(kinds == q, face_rows, 0.0).astype(jnp.bfloat16) for q in range(types)], axis=1
    )
    coupled = jnp.dot(spread, operators, preferred_element_type=jnp.float32)
    side_by_side = jnp.concatenate([coupled[k * count : (k + 1) * count] for k in range(6)], axis=1)
    high, low = halves(side_by_side)
    return jnp.dot(high, lift, preferred_element_type=jnp.float32) + jnp.dot(
        low, lift, preferred_element_type=jnp.float32
    )


def apply_inverse(inverse_ref, vector):
    count = vector.shape[0]
    row = lax.broadcasted_iota(jnp.int32, vector.shape, 0)
    result = jnp.zeros(vector.shape, jnp.float32)
    for e in range(count):
        product = lax.dot_general(
            vector, inverse_ref[e], (((1,), (1,)), ((), ())), preferred_element_type=jnp.float32
        )
        result = jnp.where(row == e, product, result)
    return result


def first_kernel(right_ref, inverse_ref, state_ref):
    lowered = right_ref[...].astype(jnp.bfloat16)
    state_ref[...] = apply_inverse(inverse_ref, lowered).astype(jnp.bfloat16)


def sweep_kernel(
    prev_ref, own_ref, next_ref, index_ref, operators_ref, pick_ref, lift_ref, right_ref, inverse_ref, *outs
):
    states = [prev_ref[...], own_ref[...], next_ref[...]]
    index = index_ref[...]
    coupled = coupling(
        states, index[:, 0:1], index[:, 1:2], operators_ref[...], pick_ref[...], lift_ref[...]
    )
    lowered = (right_ref[...] - coupled).astype(jnp.bfloat16)
    result = apply_inverse(inverse_ref, lowered)
    outs[0][...] = result.astype(jnp.bfloat16)
    if len(outs) > 1:
        outs[1][...] = result
        outs[2][...] = lowered


def restrict_kernel(
    prev_ref, own_ref, next_ref, index_ref, operators_ref, pick_ref, lift_ref, lowered_ref, target_ref, out_ref
):
    states = [prev_ref[...], own_ref[...], next_ref[...]]
    index = index_ref[...]
    coupled = coupling(
        states, index[:, 0:1], index[:, 1:2], operators_ref[...], pick_ref[...], lift_ref[...]
    )
    residual = lowered_ref[...].astype(jnp.float32) - coupled
    rows = out_ref.shape[1]
    member = target_ref[...] == lax.broadcasted_iota(jnp.int32, (rows, residual.shape[0]), 0)
    partial = exact_dot(jnp.where(member, 1.0, 0.0).astype(jnp.bfloat16), residual)
    for t in range(out_ref.shape[0]):
        out_ref[t] = partial


def coarse_first_kernel(parts_ref, inverse_ref, restricted_ref, state_ref):
    restricted = parts_ref[0]
    for t in range(1, parts_ref.shape[0]):
        restricted = restricted + parts_ref[t]
    restricted_ref[...] = restricted
    state_ref[...] = apply_inverse(inverse_ref, restricted.astype(jnp.bfloat16)).astype(jnp.bfloat16)


def correct_kernel(
    prev_ref,
    own_ref,
    next_ref,
    index_ref,
    operators_ref,
    pick_ref,
    lift_ref,
    right_ref,
    inverse_ref,
    target_ref,
    solution_ref,
    out_ref,
):
    states = [prev_ref[...], own_ref[...], next_ref[...]]
    index = index_ref[...]
    coupled = coupling(
        states, index[:, 0:1], index[:, 1:2], operators_ref[...], pick_ref[...], lift_ref[...]
    )
    coarse = apply_inverse(inverse_ref, (right_ref[...] - coupled).astype(jnp.bfloat16))
    rows, fine = coarse.shape[0], solution_ref.shape[0]
    member = target_ref[...] == lax.broadcasted_iota(jnp.int32, (fine, rows), 1)
    added = exact_dot(jnp.where(member, 1.0, 0.0).astype(jnp.bfloat16), coarse)
    out_ref[...] = (solution_ref[...] + added).astype(out_ref.dtype)


def run(kernel, outs, *operands, flops=1 << 28):
    single = not isinstance(outs, list)
    shapes = [outs] if single else outs
    vmem = pl.BlockSpec(memory_space=pltpu.VMEM)
    moved = sum(o.size * o.dtype.itemsize for o in operands)
    result = pl.pallas_call(
        kernel,
        out_shape=[jax.ShapeDtypeStruct(s, d) for s, d in shapes],
        in_specs=[vmem] * len(operands),
        out_specs=[vmem] * len(shapes),
        compiler_params=pltpu.CompilerParams(vmem_limit_bytes=20 << 20),
        cost_estimate=pl.CostEstimate(flops=flops, bytes_accessed=moved, transcendentals=0),
    )(*operands)
    return result[0] if single else result


def face_index(links, faces, position, devices):
    count = links.shape[0]
    clamped = jnp.maximum(links, 0)
    relative = (clamped // count - position + 1) % devices
    rows = jnp.where(links >= 0, relative * count + clamped % count, -1)
    return jnp.stack([rows.T.reshape(-1), faces.T.reshape(-1)], axis=1)


def shards(
    right_side,
    fine_inverse,
    fine_links,
    fine_faces,
    coarse_inverse,
    coarse_links,
    coarse_faces,
    face_operators,
    agglomerate,
):
    f32, bf16 = jnp.float32, jnp.bfloat16
    fine_rows, dofs = right_side.shape
    tele_size = lax.axis_size("tele")
    tele = lax.axis_index("tele")
    column = lax.axis_index("fine")
    columns = lax.axis_size("fine")
    coarse_rows = coarse_inverse.shape[0] * tele_size

    state = run(first_kernel, ((fine_rows, dofs), bf16), right_side, fine_inverse)

    table = face_tables()
    pick = jnp.asarray(table, bf16)
    lift = jnp.asarray(table.T.copy(), bf16)
    types, face_dofs, _ = face_operators.shape
    pad = LANES - face_dofs
    operators = jnp.pad(face_operators.transpose(0, 2, 1), ((0, 0), (0, pad), (0, pad)))
    operators = operators.reshape(types * LANES, LANES)
    fine_index = face_index(fine_links, fine_faces, column * tele_size + tele, columns * tele_size)
    block_inverse = lax.all_gather(coarse_inverse, "tele", axis=0, tiled=True)
    lists = lax.all_gather(
        jnp.concatenate([coarse_links, coarse_faces], axis=1), "tele", axis=0, tiled=True
    )
    coarse_index = face_index(lists[:, :6], lists[:, 6:], column, columns)
    target = agglomerate % coarse_rows
    target_row, target_column = target[None, :], target[:, None]
    shared = (operators, pick, lift)

    def fine_halo(block):
        axes = ("fine", "tele")
        return passed_along(block, axes, 1), block, passed_along(block, axes, -1)

    def coarse_halo(block):
        return passed_along(block, "fine", 1), block, passed_along(block, "fine", -1)

    for cycle in range(CYCLES):
        for sweep in range(SWEEPS):
            if cycle == 0 and sweep == 0:
                continue
            outs = [((fine_rows, dofs), bf16)]
            if sweep == SWEEPS - 1:
                outs += [((fine_rows, dofs), f32), ((fine_rows, dofs), bf16)]
            result = run(
                sweep_kernel, outs, *fine_halo(state), fine_index, *shared, right_side, fine_inverse
            )
            state = result[0]
        solution, lowered = result[1], result[2]
        parts = run(
            restrict_kernel,
            ((tele_size, coarse_rows, dofs), f32),
            *fine_halo(state),
            fine_index,
            *shared,
            lowered,
            target_row,
        )
        parts = lax.all_to_all(parts, "tele", 0, 0, tiled=True)
        restricted, coarse = run(
            coarse_first_kernel,
            [((coarse_rows, dofs), f32), ((coarse_rows, dofs), bf16)],
            parts,
            block_inverse,
        )
        for sweep in range(SWEEPS - 2):
            coarse = run(
                sweep_kernel,
                [((coarse_rows, dofs), bf16)],
                *coarse_halo(coarse),
                coarse_index,
                *shared,
                restricted,
                block_inverse,
            )[0]
        last = cycle == CYCLES - 1
        state = run(
            correct_kernel,
            ((fine_rows, dofs), f32 if last else bf16),
            *coarse_halo(coarse),
            coarse_index,
            *shared,
            restricted,
            block_inverse,
            target_column,
            solution,
        )
    return state


def solution(mesh):
    both = P(("fine", "tele"))
    return jax.shard_map(
        shards,
        mesh=mesh,
        in_specs=(both, both, both, both, both, both, both, P(), both),
        out_specs=both,
        check_vma=False,
    )
```

time: 244 us -> 205 us (0.84)
  the two profiles are of different devices: /device:TPU:1 before, /device:TPU:2 now
where the time goes in v1:
time: 205 us; the launch traced here: 204 us
  starting transfers between devices  110 us (54%)
  blocking collectives  27.8 us (14%)
  Pallas kernels  22.2 us (11%)
  waiting for transfers between devices  17.6 us (9%)
  between operations  13.8 us (7%)
  local copies, waits for them, and re-layouts  12.4 us (6%)
    ppermute x22, starting transfers between devices, passed_along(): return lax.ppermute(block, axis, route)  107 us
    pallas_call x14, Pallas kernels, run(): pl.pallas_call(kernel, out_shape=[jax.ShapeDtypeStruct(s, d) for s, d in...  22.2 us
    all_gather x1, blocking collectives, shards(): lax.all_gather(jnp.concatenate([coarse_links, coarse_faces], axis=1), 'te...  14.2 us
    all_to_all x1, blocking collectives, shards(): parts = lax.all_to_all(parts, 'tele', 0, 0, tiled=True)  13.6 us
    ppermute x22, waiting for transfers between devices, passed_along(): return lax.ppermute(block, axis, route)  13.2 us
    unnamed x39, local copies, waits for them, and re-layouts  11.4 us
  transfers between devices with their start and end apart: 24, of which 11 were waited for; matrix products, arithmetic and copies ran while one was open for 1% of the time, Pallas kernels for 3%

profile of v1, /device:TPU:2, one launch (start us, length us, event | category | flops | bytes accessed | tf_op | source)
XLA Modules:
  0.0 204.1 jit_solution(1910324914011337202)
XLA Ops:
  7.3 2.1 %copy-done = bf16[16,320,320]{2,1,0:T(8,128)(2,1)S(1)} copy-done((bf16[16,320,320]{2,1,0:T(8,128)(2,1)S(1)}, bf16[16,320,320]{2,1,0:T(8,128)(2,1)}, u32[]{:S(2)}) %copy-start) | copy-done | bytes 3276824
  11.2 3.5 %collective-permute-start = (bf16[16,320]{1,0:T(8,128)(2,1)S(1)}, bf16[16,320]{1,0:T(8,128)(2,1)S(1)}, u32[]{:S(2)}, u32[]{:S(2)}) collective-permute-start(bf16[16,320]{1,0:T(8,128)(2,1)S(1)} %shard_map.109.own_ref), channel_id=1, source_target_pairs={{511,0},{0,1},{1,2},{2,3},{3,4},{4,5},{5,6},{6,7},{7,8},{8,9},{9,1... | collective-permute-start | bytes 30728 | tf_op jit(solution)/shard_map/ppermute | solution.py:22
  14.7 6.3 %collective-permute-start.1 = (bf16[16,320]{1,0:T(8,128)(2,1)S(1)}, bf16[16,320]{1,0:T(8,128)(2,1)S(1)}, u32[]{:S(2)}, u32[]{:S(2)}) collective-permute-start(bf16[16,320]{1,0:T(8,128)(2,1)S(1)} %shard_map.109.own_ref), channel_id=1, source_target_pairs={{1,0},{2,1},{3,2},{4,3},{5,4},{6,5},{7,6},{8,7},{9,8},{10,9},{11,1... | collective-permute-start | bytes 30728 | tf_op jit(solution)/shard_map/ppermute | solution.py:22
  22.5 2.1 %copy-done.1 = bf16[16,320,320]{2,1,0:T(8,128)(2,1)S(1)} copy-done((bf16[16,320,320]{2,1,0:T(8,128)(2,1)S(1)}, bf16[16,320,320]{2,1,0:T(8,128)(2,1)}, u32[]{:S(2)}) %copy-start.1) | copy-done | bytes 3276824
  26.7 2.1 %collective-permute-start.2 = (bf16[16,320]{1,0:T(8,128)(2,1)S(1)}, bf16[16,320]{1,0:T(8,128)(2,1)S(1)}, u32[]{:S(2)}, u32[]{:S(2)}) collective-permute-start(bf16[16,320]{1,0:T(8,128)(2,1)S(1)} %shard_map.110.own_ref), channel_id=1, source_target_pairs={{511,0},{0,1},{1,2},{2,3},{3,4},{4,5},{5,6},{6,7},{7,8},{8,9},{9,1... | collective-permute-start | bytes 30728 | tf_op jit(solution)/shard_map/ppermute | solution.py:22
  28.8 10.3 %collective-permute-start.3 = (bf16[16,320]{1,0:T(8,128)(2,1)S(1)}, bf16[16,320]{1,0:T(8,128)(2,1)S(1)}, u32[]{:S(2)}, u32[]{:S(2)}) collective-permute-start(bf16[16,320]{1,0:T(8,128)(2,1)S(1)} %shard_map.110.own_ref), channel_id=1, source_target_pairs={{1,0},{2,1},{3,2},{4,3},{5,4},{6,5},{7,6},{8,7},{9,8},{10,9},{11,1... | collective-permute-start | bytes 30728 | tf_op jit(solution)/shard_map/ppermute | solution.py:22
  40.5 2.0 %shard_map.111 = (bf16[16,320]{1,0:T(8,128)(2,1)S(1)}, f32[16,320]{1,0:T(8,128)S(1)}, bf16[16,320]{1,0:T(8,128)(2,1)S(1)}) custom-call(bf16[16,320]{1,0:T(8,128)(2,1)S(1)} %collective-permute-done.2.prev_ref, bf16[16,320]{1,0:T(8,128)(2,1)S(1)} %shard_map.110.own_ref, bf16[16,320]{1,0:T(8,128)(2,1)S(1)} %collective-permute-done.3.next_ref, ...), custom_call_target="tpu_custom_call" | custom-call | flops 268435456 | bytes 5098240 | tf_op jit(solution)/shard_map/pallas_call | solution.py:167
  44.6 9.0 %collective-permute-start.5 = (bf16[16,320]{1,0:T(8,128)(2,1)S(1)}, bf16[16,320]{1,0:T(8,128)(2,1)S(1)}, u32[]{:S(2)}, u32[]{:S(2)}) collective-permute-start(bf16[16,320]{1,0:T(8,128)(2,1)S(1)} %get-tuple-element.15.own_ref), channel_id=1, source_target_pairs={{1,0},{2,1},{3,2},{4,3},{5,4},{6,5},{7,6},{8,7},{9,8},{10,9},{11,1... | collective-permute-start | bytes 30728 | tf_op jit(solution)/shard_map/ppermute | solution.py:22
  53.7 14.2 %all-gather = s32[4,2,12]{2,1,0:T(2,128)S(1)} all-gather(s32[1,2,12]{2,1,0:T(2,128)S(1)} %add_bitcast_fusion), channel_id=1, replica_groups=mesh['fine'=128,'tele'=4] {'tele'}, dimensions={0}, use_global_device_ids=true | all-gather | bytes 480 | tf_op jit(solution)/shard_map/all_gather | solution.py:216
  69.6 3.3 %all-to-all-start = ((f32[4,8,320]{2,1,0:T(8,128)}), f32[4,8,320]{2,1,0:T(8,128)S(1)}, u32[]{:S(2)}, u32[]{:S(2)}) async-start(f32[4,8,320]{2,1,0:T(8,128)} %shard_map.112), calls=%async_computation | async-start | bytes 98304 | tf_op jit(solution)/shard_map/all_to_all | solution.py:252
  73.3 3.7 %all-to-all-done.parts_ref = f32[4,8,320]{2,1,0:T(8,128)S(1)} async-done(((f32[4,8,320]{2,1,0:T(8,128)}), f32[4,8,320]{2,1,0:T(8,128)S(1)}, u32[]{:S(2)}, u32[]{:S(2)}) %all-to-all-start) | async-done | bytes 40992 | tf_op jit(solution)/shard_map/all_to_all | solution.py:252
  81.1 7.0 %collective-permute-start.7 = (bf16[8,320]{1,0:T(8,128)(2,1)S(1)}, bf16[8,320]{1,0:T(8,128)(2,1)S(1)}, u32[]{:S(2)}, u32[]{:S(2)}) collective-permute-start(bf16[8,320]{1,0:T(8,128)(2,1)S(1)} %get-tuple-element.17.own_ref), channel_id=1, source_target_pairs={{4,0},{8,4},{12,8},{16,12},{20,16},{24,20},{28,24},{32,28},{36,32}... | collective-permute-start | bytes 15368 | tf_op jit(solution)/shard_map/ppermute | solution.py:22
  95.4 7.0 %collective-permute-start.9 = (bf16[8,320]{1,0:T(8,128)(2,1)S(1)}, bf16[8,320]{1,0:T(8,128)(2,1)S(1)}, u32[]{:S(2)}, u32[]{:S(2)}) collective-permute-start(bf16[8,320]{1,0:T(8,128)(2,1)S(1)} %shard_map.114.own_ref), channel_id=1, source_target_pairs={{4,0},{8,4},{12,8},{16,12},{20,16},{24,20},{28,24},{32,28},{36,32}... | collective-permute-start | bytes 15368 | tf_op jit(solution)/shard_map/ppermute | solution.py:22
  106.4 2.4 %collective-permute-start.10 = (bf16[16,320]{1,0:T(8,128)(2,1)S(1)}, bf16[16,320]{1,0:T(8,128)(2,1)S(1)}, u32[]{:S(2)}, u32[]{:S(2)}) collective-permute-start(bf16[16,320]{1,0:T(8,128)(2,1)S(1)} %shard_map.115.own_ref), channel_id=1, source_target_pairs={{511,0},{0,1},{1,2},{2,3},{3,4},{4,5},{5,6},{6,7},{7,8},{8,9},{9,1... | collective-permute-start | bytes 30728 | tf_op jit(solution)/shard_map/ppermute | solution.py:22
  108.8 3.5 %collective-permute-start.11 = (bf16[16,320]{1,0:T(8,128)(2,1)S(1)}, bf16[16,320]{1,0:T(8,128)(2,1)S(1)}, u32[]{:S(2)}, u32[]{:S(2)}) collective-permute-start(bf16[16,320]{1,0:T(8,128)(2,1)S(1)} %shard_map.115.own_ref), channel_id=1, source_target_pairs={{1,0},{2,1},{3,2},{4,3},{5,4},{6,5},{7,6},{8,7},{9,8},{10,9},{11,1... | collective-permute-start | bytes 30728 | tf_op jit(solution)/shard_map/ppermute | solution.py:22
  112.3 2.1 %collective-permute-done.11.next_ref = bf16[16,320]{1,0:T(8,128)(2,1)S(1)} collective-permute-done((bf16[16,320]{1,0:T(8,128)(2,1)S(1)}, bf16[16,320]{1,0:T(8,128)(2,1)S(1)}, u32[]{:S(2)}, u32[]{:S(2)}) %collective-permute-start.11) | collective-permute-done | bytes 10272 | tf_op jit(solution)/shard_map/ppermute | solution.py:22
  117.4 3.6 %collective-permute-start.12 = (bf16[16,320]{1,0:T(8,128)(2,1)S(1)}, bf16[16,320]{1,0:T(8,128)(2,1)S(1)}, u32[]{:S(2)}, u32[]{:S(2)}) collective-permute-start(bf16[16,320]{1,0:T(8,128)(2,1)S(1)} %shard_map.116.own_ref), channel_id=1, source_target_pairs={{511,0},{0,1},{1,2},{2,3},{3,4},{4,5},{5,6},{6,7},{7,8},{8,9},{9,1... | collective-permute-start | bytes 30728 | tf_op jit(solution)/shard_map/ppermute | solution.py:22
  121.0 6.3 %collective-permute-start.13 = (bf16[16,320]{1,0:T(8,128)(2,1)S(1)}, bf16[16,320]{1,0:T(8,128)(2,1)S(1)}, u32[]{:S(2)}, u32[]{:S(2)}) collective-permute-start(bf16[16,320]{1,0:T(8,128)(2,1)S(1)} %shard_map.116.own_ref), channel_id=1, source_target_pairs={{1,0},{2,1},{3,2},{4,3},{5,4},{6,5},{7,6},{8,7},{9,8},{10,9},{11,1... | collective-permute-start | bytes 30728 | tf_op jit(solution)/shard_map/ppermute | solution.py:22
  132.7 9.1 %collective-permute-start.15 = (bf16[16,320]{1,0:T(8,128)(2,1)S(1)}, bf16[16,320]{1,0:T(8,128)(2,1)S(1)}, u32[]{:S(2)}, u32[]{:S(2)}) collective-permute-start(bf16[16,320]{1,0:T(8,128)(2,1)S(1)} %shard_map.117.own_ref), channel_id=1, source_target_pairs={{1,0},{2,1},{3,2},{4,3},{5,4},{6,5},{7,6},{8,7},{9,8},{10,9},{11,1... | collective-permute-start | bytes 30728 | tf_op jit(solution)/shard_map/ppermute | solution.py:22
  147.3 9.1 %collective-permute-start.17 = (bf16[16,320]{1,0:T(8,128)(2,1)S(1)}, bf16[16,320]{1,0:T(8,128)(2,1)S(1)}, u32[]{:S(2)}, u32[]{:S(2)}) collective-permute-start(bf16[16,320]{1,0:T(8,128)(2,1)S(1)} %get-tuple-element.20.own_ref), channel_id=1, source_target_pairs={{1,0},{2,1},{3,2},{4,3},{5,4},{6,5},{7,6},{8,7},{9,8},{10,9},{11,1... | collective-permute-start | bytes 30728 | tf_op jit(solution)/shard_map/ppermute | solution.py:22
  158.8 13.6 %all_to_all.10.parts_ref = f32[4,8,320]{2,1,0:T(8,128)S(1)} all-to-all(f32[4,8,320]{2,1,0:T(8,128)S(1)} %shard_map.119), channel_id=1, replica_groups=mesh['fine'=128,'tele'=4] {'tele'}, dimensions={0} | all-to-all | bytes 81920 | tf_op jit(solution)/shard_map/all_to_all | solution.py:252
  175.0 7.0 %collective-permute-start.19 = (bf16[8,320]{1,0:T(8,128)(2,1)S(1)}, bf16[8,320]{1,0:T(8,128)(2,1)S(1)}, u32[]{:S(2)}, u32[]{:S(2)}) collective-permute-start(bf16[8,320]{1,0:T(8,128)(2,1)S(1)} %get-tuple-element.22.own_ref), channel_id=1, source_target_pairs={{4,0},{8,4},{12,8},{16,12},{20,16},{24,20},{28,24},{32,28},{36,32}... | collective-permute-start | bytes 15368 | tf_op jit(solution)/shard_map/ppermute | solution.py:22
  186.7 7.0 %collective-permute-start.21 = (bf16[8,320]{1,0:T(8,128)(2,1)S(1)}, bf16[8,320]{1,0:T(8,128)(2,1)S(1)}, u32[]{:S(2)}, u32[]{:S(2)}) collective-permute-start(bf16[8,320]{1,0:T(8,128)(2,1)S(1)} %shard_map.121.own_ref), channel_id=1, source_target_pairs={{4,0},{8,4},{12,8},{16,12},{20,16},{24,20},{28,24},{32,28},{36,32}... | collective-permute-start | bytes 15368 | tf_op jit(solution)/shard_map/ppermute | solution.py:22
  195.0 2.3 %shard_map.122 = f32[16,320]{1,0:T(8,128)} custom-call(bf16[8,320]{1,0:T(8,128)(2,1)S(1)} %collective-permute-done.20.prev_ref, bf16[8,320]{1,0:T(8,128)(2,1)S(1)} %shard_map.121.own_ref, bf16[8,320]{1,0:T(8,128)(2,1)S(1)} %collective-permute-done.21.next_ref, s32[48,2]{1,0:T(8,128)S(1)} %copy.27.index_ref, bf16[3072,128]{1,0:T(8,128)(2,1)S(1)} %bitcast.26, ...), custom_call_target="tpu_custom_call" | custom-call | flops 268435456 | bytes 3454400 | tf_op jit(solution)/shard_map/pallas_call | solution.py:167
  (97 shorter events, 51.9 us)
Async XLA Ops:
  6.5 70.5 %all-gather.3.cloned.1.call-start = ((), (), s32[]{:S(2)}) async-start(), calls=%async_computation.2 | async-start | bytes 2457600 | tf_op jit(solution)/shard_map/all_gather | solution.py:215
  11.2 10.6 %collective-permute-start = (bf16[16,320]{1,0:T(8,128)(2,1)S(1)}, bf16[16,320]{1,0:T(8,128)(2,1)S(1)}, u32[]{:S(2)}, u32[]{:S(2)}) collective-permute-start(bf16[16,320]{1,0:T(8,128)(2,1)S(1)} %shard_map.109.own_ref), channel_id=1, source_target_pairs={{511,0},{0,1},{1,2},{2,3},{3,4},{4,5},{5,6},{6,7},{7,8},{8,9},{9,1... | collective-permute-start | bytes 30728 | tf_op jit(solution)/shard_map/ppermute | solution.py:22
  14.7 7.7 %collective-permute-start.1 = (bf16[16,320]{1,0:T(8,128)(2,1)S(1)}, bf16[16,320]{1,0:T(8,128)(2,1)S(1)}, u32[]{:S(2)}, u32[]{:S(2)}) collective-permute-start(bf16[16,320]{1,0:T(8,128)(2,1)S(1)} %shard_map.109.own_ref), channel_id=1, source_target_pairs={{1,0},{2,1},{3,2},{4,3},{5,4},{6,5},{7,6},{8,7},{9,8},{10,9},{11,1... | collective-permute-start | bytes 30728 | tf_op jit(solution)/shard_map/ppermute | solution.py:22
  26.7 12.5 %collective-permute-start.2 = (bf16[16,320]{1,0:T(8,128)(2,1)S(1)}, bf16[16,320]{1,0:T(8,128)(2,1)S(1)}, u32[]{:S(2)}, u32[]{:S(2)}) collective-permute-start(bf16[16,320]{1,0:T(8,128)(2,1)S(1)} %shard_map.110.own_ref), channel_id=1, source_target_pairs={{511,0},{0,1},{1,2},{2,3},{3,4},{4,5},{5,6},{6,7},{7,8},{8,9},{9,1... | collective-permute-start | bytes 30728 | tf_op jit(solution)/shard_map/ppermute | solution.py:22
  28.8 11.7 %collective-permute-start.3 = (bf16[16,320]{1,0:T(8,128)(2,1)S(1)}, bf16[16,320]{1,0:T(8,128)(2,1)S(1)}, u32[]{:S(2)}, u32[]{:S(2)}) collective-permute-start(bf16[16,320]{1,0:T(8,128)(2,1)S(1)} %shard_map.110.own_ref), channel_id=1, source_target_pairs={{1,0},{2,1},{3,2},{4,3},{5,4},{6,5},{7,6},{8,7},{9,8},{10,9},{11,1... | collective-permute-start | bytes 30728 | tf_op jit(solution)/shard_map/ppermute | solution.py:22
  42.6 25.4 %collective-permute-start.4 = (bf16[16,320]{1,0:T(8,128)(2,1)S(1)}, bf16[16,320]{1,0:T(8,128)(2,1)S(1)}, u32[]{:S(2)}, u32[]{:S(2)}) collective-permute-start(bf16[16,320]{1,0:T(8,128)(2,1)S(1)} %get-tuple-element.15.own_ref), channel_id=1, source_target_pairs={{511,0},{0,1},{1,2},{2,3},{3,4},{4,5},{5,6},{6,7},{7,8},{8,9},{9,1... | collective-permute-start | bytes 30728 | tf_op jit(solution)/shard_map/ppermute | solution.py:22
  44.6 23.3 %collective-permute-start.5 = (bf16[16,320]{1,0:T(8,128)(2,1)S(1)}, bf16[16,320]{1,0:T(8,128)(2,1)S(1)}, u32[]{:S(2)}, u32[]{:S(2)}) collective-permute-start(bf16[16,320]{1,0:T(8,128)(2,1)S(1)} %get-tuple-element.15.own_ref), channel_id=1, source_target_pairs={{1,0},{2,1},{3,2},{4,3},{5,4},{6,5},{7,6},{8,7},{9,8},{10,9},{11,1... | collective-permute-start | bytes 30728 | tf_op jit(solution)/shard_map/ppermute | solution.py:22
  69.6 7.4 %all-to-all-start = ((f32[4,8,320]{2,1,0:T(8,128)}), f32[4,8,320]{2,1,0:T(8,128)S(1)}, u32[]{:S(2)}, u32[]{:S(2)}) async-start(f32[4,8,320]{2,1,0:T(8,128)} %shard_map.112), calls=%async_computation | async-start | bytes 98304 | tf_op jit(solution)/shard_map/all_to_all | solution.py:252
  79.2 9.0 %collective-permute-start.6 = (bf16[8,320]{1,0:T(8,128)(2,1)S(1)}, bf16[8,320]{1,0:T(8,128)(2,1)S(1)}, u32[]{:S(2)}, u32[]{:S(2)}) collective-permute-start(bf16[8,320]{1,0:T(8,128)(2,1)S(1)} %get-tuple-element.17.own_ref), channel_id=1, source_target_pairs={{508,0},{0,4},{4,8},{8,12},{12,16},{16,20},{20,24},{24,28},{28,32}... | collective-permute-start | bytes 15368 | tf_op jit(solution)/shard_map/ppermute | solution.py:22
  81.1 8.3 %collective-permute-start.7 = (bf16[8,320]{1,0:T(8,128)(2,1)S(1)}, bf16[8,320]{1,0:T(8,128)(2,1)S(1)}, u32[]{:S(2)}, u32[]{:S(2)}) collective-permute-start(bf16[8,320]{1,0:T(8,128)(2,1)S(1)} %get-tuple-element.17.own_ref), channel_id=1, source_target_pairs={{4,0},{8,4},{12,8},{16,12},{20,16},{24,20},{28,24},{32,28},{36,32}... | collective-permute-start | bytes 15368 | tf_op jit(solution)/shard_map/ppermute | solution.py:22
  93.5 9.0 %collective-permute-start.8 = (bf16[8,320]{1,0:T(8,128)(2,1)S(1)}, bf16[8,320]{1,0:T(8,128)(2,1)S(1)}, u32[]{:S(2)}, u32[]{:S(2)}) collective-permute-start(bf16[8,320]{1,0:T(8,128)(2,1)S(1)} %shard_map.114.own_ref), channel_id=1, source_target_pairs={{508,0},{0,4},{4,8},{8,12},{12,16},{16,20},{20,24},{24,28},{28,32}... | collective-permute-start | bytes 15368 | tf_op jit(solution)/shard_map/ppermute | solution.py:22
  95.4 8.3 %collective-permute-start.9 = (bf16[8,320]{1,0:T(8,128)(2,1)S(1)}, bf16[8,320]{1,0:T(8,128)(2,1)S(1)}, u32[]{:S(2)}, u32[]{:S(2)}) collective-permute-start(bf16[8,320]{1,0:T(8,128)(2,1)S(1)} %shard_map.114.own_ref), channel_id=1, source_target_pairs={{4,0},{8,4},{12,8},{16,12},{20,16},{24,20},{28,24},{32,28},{36,32}... | collective-permute-start | bytes 15368 | tf_op jit(solution)/shard_map/ppermute | solution.py:22
  106.4 5.9 %collective-permute-start.10 = (bf16[16,320]{1,0:T(8,128)(2,1)S(1)}, bf16[16,320]{1,0:T(8,128)(2,1)S(1)}, u32[]{:S(2)}, u32[]{:S(2)}) collective-permute-start(bf16[16,320]{1,0:T(8,128)(2,1)S(1)} %shard_map.115.own_ref), channel_id=1, source_target_pairs={{511,0},{0,1},{1,2},{2,3},{3,4},{4,5},{5,6},{6,7},{7,8},{8,9},{9,1... | collective-permute-start | bytes 30728 | tf_op jit(solution)/shard_map/ppermute | solution.py:22
  108.8 5.6 %collective-permute-start.11 = (bf16[16,320]{1,0:T(8,128)(2,1)S(1)}, bf16[16,320]{1,0:T(8,128)(2,1)S(1)}, u32[]{:S(2)}, u32[]{:S(2)}) collective-permute-start(bf16[16,320]{1,0:T(8,128)(2,1)S(1)} %shard_map.115.own_ref), channel_id=1, source_target_pairs={{1,0},{2,1},{3,2},{4,3},{5,4},{6,5},{7,6},{8,7},{9,8},{10,9},{11,1... | collective-permute-start | bytes 30728 | tf_op jit(solution)/shard_map/ppermute | solution.py:22
  117.4 9.9 %collective-permute-start.12 = (bf16[16,320]{1,0:T(8,128)(2,1)S(1)}, bf16[16,320]{1,0:T(8,128)(2,1)S(1)}, u32[]{:S(2)}, u32[]{:S(2)}) collective-permute-start(bf16[16,320]{1,0:T(8,128)(2,1)S(1)} %shard_map.116.own_ref), channel_id=1, source_target_pairs={{511,0},{0,1},{1,2},{2,3},{3,4},{4,5},{5,6},{6,7},{7,8},{8,9},{9,1... | collective-permute-start | bytes 30728 | tf_op jit(solution)/shard_map/ppermute | solution.py:22
  121.0 7.6 %collective-permute-start.13 = (bf16[16,320]{1,0:T(8,128)(2,1)S(1)}, bf16[16,320]{1,0:T(8,128)(2,1)S(1)}, u32[]{:S(2)}, u32[]{:S(2)}) collective-permute-start(bf16[16,320]{1,0:T(8,128)(2,1)S(1)} %shard_map.116.own_ref), channel_id=1, source_target_pairs={{1,0},{2,1},{3,2},{4,3},{5,4},{6,5},{7,6},{8,7},{9,8},{10,9},{11,1... | collective-permute-start | bytes 30728 | tf_op jit(solution)/shard_map/ppermute | solution.py:22
  130.7 11.1 %collective-permute-start.14 = (bf16[16,320]{1,0:T(8,128)(2,1)S(1)}, bf16[16,320]{1,0:T(8,128)(2,1)S(1)}, u32[]{:S(2)}, u32[]{:S(2)}) collective-permute-start(bf16[16,320]{1,0:T(8,128)(2,1)S(1)} %shard_map.117.own_ref), channel_id=1, source_target_pairs={{511,0},{0,1},{1,2},{2,3},{3,4},{4,5},{5,6},{6,7},{7,8},{8,9},{9,1... | collective-permute-start | bytes 30728 | tf_op jit(solution)/shard_map/ppermute | solution.py:22
  132.7 10.5 %collective-permute-start.15 = (bf16[16,320]{1,0:T(8,128)(2,1)S(1)}, bf16[16,320]{1,0:T(8,128)(2,1)S(1)}, u32[]{:S(2)}, u32[]{:S(2)}) collective-permute-start(bf16[16,320]{1,0:T(8,128)(2,1)S(1)} %shard_map.117.own_ref), channel_id=1, source_target_pairs={{1,0},{2,1},{3,2},{4,3},{5,4},{6,5},{7,6},{8,7},{9,8},{10,9},{11,1... | collective-permute-start | bytes 30728 | tf_op jit(solution)/shard_map/ppermute | solution.py:22
  145.2 11.1 %collective-permute-start.16 = (bf16[16,320]{1,0:T(8,128)(2,1)S(1)}, bf16[16,320]{1,0:T(8,128)(2,1)S(1)}, u32[]{:S(2)}, u32[]{:S(2)}) collective-permute-start(bf16[16,320]{1,0:T(8,128)(2,1)S(1)} %get-tuple-element.20.own_ref), channel_id=1, source_target_pairs={{511,0},{0,1},{1,2},{2,3},{3,4},{4,5},{5,6},{6,7},{7,8},{8,9},{9,1... | collective-permute-start | bytes 30728 | tf_op jit(solution)/shard_map/ppermute | solution.py:22
  147.3 10.5 %collective-permute-start.17 = (bf16[16,320]{1,0:T(8,128)(2,1)S(1)}, bf16[16,320]{1,0:T(8,128)(2,1)S(1)}, u32[]{:S(2)}, u32[]{:S(2)}) collective-permute-start(bf16[16,320]{1,0:T(8,128)(2,1)S(1)} %get-tuple-element.20.own_ref), channel_id=1, source_target_pairs={{1,0},{2,1},{3,2},{4,3},{5,4},{6,5},{7,6},{8,7},{9,8},{10,9},{11,1... | collective-permute-start | bytes 30728 | tf_op jit(solution)/shard_map/ppermute | solution.py:22
  173.0 8.9 %collective-permute-start.18 = (bf16[8,320]{1,0:T(8,128)(2,1)S(1)}, bf16[8,320]{1,0:T(8,128)(2,1)S(1)}, u32[]{:S(2)}, u32[]{:S(2)}) collective-permute-start(bf16[8,320]{1,0:T(8,128)(2,1)S(1)} %get-tuple-element.22.own_ref), channel_id=1, source_target_pairs={{508,0},{0,4},{4,8},{8,12},{12,16},{16,20},{20,24},{24,28},{28,32}... | collective-permute-start | bytes 15368 | tf_op jit(solution)/shard_map/ppermute | solution.py:22
  175.0 8.3 %collective-permute-start.19 = (bf16[8,320]{1,0:T(8,128)(2,1)S(1)}, bf16[8,320]{1,0:T(8,128)(2,1)S(1)}, u32[]{:S(2)}, u32[]{:S(2)}) collective-permute-start(bf16[8,320]{1,0:T(8,128)(2,1)S(1)} %get-tuple-element.22.own_ref), channel_id=1, source_target_pairs={{4,0},{8,4},{12,8},{16,12},{20,16},{24,20},{28,24},{32,28},{36,32}... | collective-permute-start | bytes 15368 | tf_op jit(solution)/shard_map/ppermute | solution.py:22
  184.7 8.9 %collective-permute-start.20 = (bf16[8,320]{1,0:T(8,128)(2,1)S(1)}, bf16[8,320]{1,0:T(8,128)(2,1)S(1)}, u32[]{:S(2)}, u32[]{:S(2)}) collective-permute-start(bf16[8,320]{1,0:T(8,128)(2,1)S(1)} %shard_map.121.own_ref), channel_id=1, source_target_pairs={{508,0},{0,4},{4,8},{8,12},{12,16},{16,20},{20,24},{24,28},{28,32}... | collective-permute-start | bytes 15368 | tf_op jit(solution)/shard_map/ppermute | solution.py:22
  186.7 8.3 %collective-permute-start.21 = (bf16[8,320]{1,0:T(8,128)(2,1)S(1)}, bf16[8,320]{1,0:T(8,128)(2,1)S(1)}, u32[]{:S(2)}, u32[]{:S(2)}) collective-permute-start(bf16[8,320]{1,0:T(8,128)(2,1)S(1)} %shard_map.121.own_ref), channel_id=1, source_target_pairs={{4,0},{8,4},{12,8},{16,12},{20,16},{24,20},{28,24},{32,28},{36,32}... | collective-permute-start | bytes 15368 | tf_op jit(solution)/shard_map/ppermute | solution.py:22
  (19 other events, 197.4 us)
Sparse Core Ops, SparseCore 0:
  9.5 41.2 all-gather.2

commit v2 on v1

v2 whole, which is shorter than its diff:
```python
import jax
import jax.numpy as jnp
import numpy as np
from jax import lax
from jax.experimental import pallas as pl
from jax.experimental.pallas import tpu as pltpu
from jax.sharding import PartitionSpec as P

FIELDS = 5
NODES = 4
SWEEPS = 3
CYCLES = 2
LANES = 128
OPPOSITE = (1, 0, 3, 2, 5, 4)


def swapped(block, axis):
    count = lax.axis_size(axis)
    outer = lax.ppermute(block, axis, [(i, (i - 1 if i % 2 == 0 else i + 1) % count) for i in range(count)])
    inner = lax.ppermute(block, axis, [(i, i ^ 1) for i in range(count)])
    return inner, outer


def face_table():
    cube = np.arange(FIELDS * NODES**3).reshape(FIELDS, NODES, NODES, NODES)
    far = NODES - 1
    faces = (cube[:, 0], cube[:, far], cube[:, :, 0], cube[:, :, far], cube[..., 0], cube[..., far])
    table = np.zeros((6 * LANES, cube.size), np.float32)
    for k, face in enumerate(faces):
        nodes = face.reshape(-1)
        table[k * LANES + np.arange(nodes.size), nodes] = 1.0
    return table


def halves(value):
    high = value.astype(jnp.bfloat16)
    low = (value - high.astype(jnp.float32)).astype(jnp.bfloat16)
    return high, low


def exact_dot(left, right):
    high, low = halves(right)
    return jnp.dot(left, high, preferred_element_type=jnp.float32) + jnp.dot(
        left, low, preferred_element_type=jnp.float32
    )


def coupling(states, index, operators, lift):
    count = states[0].shape[0]
    pool = jnp.concatenate([state.astype(jnp.float32) for state in states], axis=0).astype(jnp.bfloat16)
    traces = lax.dot_general(pool, lift, (((1,), (1,)), ((), ())), preferred_element_type=jnp.float32)
    traces = traces.astype(jnp.bfloat16)
    column = lax.broadcasted_iota(jnp.int32, (count, pool.shape[0]), 1)
    face_rows, kinds = [], []
    for k in range(6):
        chosen = jnp.where(index[:, k : k + 1] == column, 1.0, 0.0).astype(jnp.bfloat16)
        across = traces[:, OPPOSITE[k] * LANES : (OPPOSITE[k] + 1) * LANES]
        face_rows.append(jnp.dot(chosen, across, preferred_element_type=jnp.float32))
        kinds.append(jnp.broadcast_to(index[:, 6 + k : 7 + k], (count, LANES)))
    face_rows = jnp.concatenate(face_rows, axis=0)
    kinds = jnp.concatenate(kinds, axis=0)
    types = operators.shape[0] // LANES
    spread = jnp.concatenate(
        [jnp.where(kinds == q, face_rows, 0.0).astype(jnp.bfloat16) for q in range(types)], axis=1
    )
    coupled = jnp.dot(spread, operators, preferred_element_type=jnp.float32)
    side_by_side = jnp.concatenate([coupled[k * count : (k + 1) * count] for k in range(6)], axis=1)
    high, low = halves(side_by_side)
    return jnp.dot(high, lift, preferred_element_type=jnp.float32) + jnp.dot(
        low, lift, preferred_element_type=jnp.float32
    )


def apply_inverse(inverse_ref, vector):
    count, dofs = vector.shape
    row = lax.broadcasted_iota(jnp.int32, vector.shape, 0)
    result = jnp.zeros(vector.shape, jnp.float32)
    for e in range(count):
        product = lax.dot_general(
            vector, inverse_ref[e][:, :dofs], (((1,), (1,)), ((), ())), preferred_element_type=jnp.float32
        )
        result = jnp.where(row == e, product, result)
    return result


def first_kernel(right_ref, inverse_ref, state_ref):
    lowered = right_ref[...].astype(jnp.bfloat16)
    state_ref[...] = apply_inverse(inverse_ref, lowered).astype(jnp.bfloat16)


def sweep_kernel(
    prev_ref, own_ref, next_ref, index_ref, operators_ref, lift_ref, right_ref, inverse_ref, *outs
):
    states = [prev_ref[...], own_ref[...], next_ref[...]]
    coupled = coupling(states, index_ref[...], operators_ref[...], lift_ref[...])
    lowered = (right_ref[...] - coupled).astype(jnp.bfloat16)
    result = apply_inverse(inverse_ref, lowered)
    outs[0][...] = result.astype(jnp.bfloat16)
    if len(outs) > 1:
        outs[1][...] = result
        outs[2][...] = lowered


def restrict_kernel(
    prev_ref, own_ref, next_ref, index_ref, operators_ref, lift_ref, lowered_ref, target_ref, *rest
):
    out_ref = rest[-1] if len(rest) == 1 else rest[1]
    states = [prev_ref[...], own_ref[...], next_ref[...]]
    coupled = coupling(states, index_ref[...], operators_ref[...], lift_ref[...])
    residual = lowered_ref[...].astype(jnp.float32) - coupled
    rows = out_ref.shape[1]
    member = target_ref[...] == lax.broadcasted_iota(jnp.int32, (rows, residual.shape[0]), 0)
    partial = exact_dot(jnp.where(member, 1.0, 0.0).astype(jnp.bfloat16), residual)
    for t in range(out_ref.shape[0]):
        out_ref[t] = partial
    if len(rest) > 1:
        packed_ref, _, list_ref = rest
        dofs = residual.shape[1]
        for c in range(rows):
            list_ref[c : c + 1] = packed_ref[c, 0:1, dofs:].astype(jnp.int32)


def coarse_first_kernel(parts_ref, inverse_ref, restricted_ref, state_ref):
    restricted = parts_ref[0]
    for t in range(1, parts_ref.shape[0]):
        restricted = restricted + parts_ref[t]
    restricted_ref[...] = restricted
    state_ref[...] = apply_inverse(inverse_ref, restricted.astype(jnp.bfloat16)).astype(jnp.bfloat16)


def correct_kernel(
    prev_ref,
    own_ref,
    next_ref,
    index_ref,
    operators_ref,
    lift_ref,
    right_ref,
    inverse_ref,
    target_ref,
    solution_ref,
    out_ref,
):
    states = [prev_ref[...], own_ref[...], next_ref[...]]
    coupled = coupling(states, index_ref[...], operators_ref[...], lift_ref[...])
    coarse = apply_inverse(inverse_ref, (right_ref[...] - coupled).astype(jnp.bfloat16))
    rows, fine = coarse.shape[0], solution_ref.shape[0]
    member = target_ref[...] == lax.broadcasted_iota(jnp.int32, (rows, fine), 0)
    added = exact_dot(jnp.where(member, 1.0, 0.0).T.astype(jnp.bfloat16), coarse)
    out_ref[...] = (solution_ref[...] + added).astype(out_ref.dtype)


def run(kernel, outs, *operands, held=(), keep=()):
    count = len(operands)

    def body(*refs):
        kernel(*refs[:count], *refs[count + len(keep) :])

    single = not isinstance(outs, list)
    shapes = [outs] if single else outs
    vmem = pl.BlockSpec(memory_space=pltpu.VMEM)
    moved = sum(o.size * o.dtype.itemsize for o in operands)
    operands = [
        pltpu.with_memory_space_constraint(o, pltpu.VMEM) if i in held else o for i, o in enumerate(operands)
    ]
    operands += [pltpu.with_memory_space_constraint(o, pltpu.VMEM) for o in keep]
    result = pl.pallas_call(
        body,
        out_shape=[jax.ShapeDtypeStruct(s, d) for s, d in shapes],
        in_specs=[vmem] * len(operands),
        out_specs=[vmem] * len(shapes),
        compiler_params=pltpu.CompilerParams(vmem_limit_bytes=20 << 20),
        cost_estimate=pl.CostEstimate(flops=1 << 28, bytes_accessed=moved, transcendentals=0),
    )(*operands)
    return result[0] if single else result


def local_rows(links, count, position):
    owner, within = links // count, links % count
    place = jnp.where(owner == position, 1, jnp.where(owner == position ^ 1, 0, 2))
    return jnp.where(links >= 0, place * count + within, -1)


def shards(
    right_side,
    fine_inverse,
    fine_links,
    fine_faces,
    coarse_inverse,
    coarse_links,
    coarse_faces,
    face_operators,
    agglomerate,
):
    f32, bf16 = jnp.float32, jnp.bfloat16
    fine_rows, dofs = right_side.shape
    tele_size = lax.axis_size("tele")
    tele = lax.axis_index("tele")
    column = lax.axis_index("fine")
    coarse_own = coarse_inverse.shape[0]
    coarse_rows = coarse_own * tele_size

    lift = jnp.asarray(face_table(), bf16)
    types, face_dofs, _ = face_operators.shape
    pad = LANES - face_dofs
    operators = jnp.pad(face_operators.transpose(0, 2, 1), ((0, 0), (0, pad), (0, pad)))
    operators = operators.reshape(types * LANES, LANES)
    fine_index = jnp.concatenate([local_rows(fine_links, fine_rows, column * tele_size + tele), fine_faces], axis=1)
    target = agglomerate % coarse_rows
    target = target[None, :]

    lists = jnp.concatenate([local_rows(coarse_links, coarse_rows, column), coarse_faces], axis=1).astype(bf16)
    lists = jnp.pad(lists[:, None, :], ((0, 0), (0, dofs - 1), (0, -dofs % LANES - lists.shape[1])))
    packed = jnp.concatenate([coarse_inverse, lists], axis=2)
    packed = jnp.broadcast_to(packed[None], (tele_size,) + packed.shape)
    right_side, operators, fine_index, target, packed = lax.optimization_barrier(
        (right_side, operators, fine_index, target, packed)
    )
    packed = lax.all_to_all(packed, "tele", 0, 0, tiled=True)
    block_inverse = packed.reshape((coarse_rows,) + packed.shape[2:])
    shared = (operators, lift)
    inverse = fine_inverse
    state = run(first_kernel, ((fine_rows, dofs), bf16), right_side, inverse, held=(1,))

    def halo(block, axis):
        inner, outer = swapped(block, axis)
        return inner, block, outer

    both = ("fine", "tele")
    for cycle in range(CYCLES):
        keep = (inverse,) if cycle < CYCLES - 1 else ()
        for sweep in range(SWEEPS):
            if cycle == 0 and sweep == 0:
                continue
            outs = [((fine_rows, dofs), bf16)]
            if sweep == SWEEPS - 1:
                outs += [((fine_rows, dofs), f32), ((fine_rows, dofs), bf16)]
            result = run(
                sweep_kernel, outs, *halo(state, both), fine_index, *shared, right_side, inverse, held=(5, 7)
            )
            state = result[0]
        solution, lowered = result[1], result[2]
        operands = (*halo(state, both), fine_index, *shared, lowered, target)
        part_shape = ((tele_size, coarse_rows, dofs), f32)
        if cycle == 0:
            lists_shape = ((coarse_rows, block_inverse.shape[2] - dofs), jnp.int32)
            parts, coarse_index = run(
                restrict_kernel, [part_shape, lists_shape], *operands, block_inverse, held=(5, 8), keep=keep
            )
        else:
            parts = run(restrict_kernel, part_shape, *operands, held=(5,), keep=keep)
        parts = lax.all_to_all(parts, "tele", 0, 0, tiled=True)
        restricted, coarse = run(
            coarse_first_kernel,
            [((coarse_rows, dofs), f32), ((coarse_rows, dofs), bf16)],
            parts,
            block_inverse,
            held=(1,),
            keep=keep,
        )
        for sweep in range(SWEEPS - 2):
            coarse = run(
                sweep_kernel,
                [((coarse_rows, dofs), bf16)],
                *halo(coarse, "fine"),
                coarse_index,
                *shared,
                restricted,
                block_inverse,
                held=(5, 7),
                keep=keep,
            )[0]
        last = cycle == CYCLES - 1
        state = run(
            correct_kernel,
            ((fine_rows, dofs), f32 if last else bf16),
            *halo(coarse, "fine"),
            coarse_index,
            *shared,
            restricted,
            block_inverse,
            target,
            solution,
            held=(5, 7),
            keep=keep,
        )
    return state


def solution(mesh):
    both = P(("fine", "tele"))
    return jax.shard_map(
        shards,
        mesh=mesh,
        in_specs=(both, both, both, both, both, both, both, P(), both),
        out_specs=both,
        check_vma=False,
    )
```

time: 205 us -> 181 us (0.88)
  the two profiles are of different devices: /device:TPU:2 before, /device:TPU:1 now
where the time goes in v2:
time: 181 us; the launch traced here: 180 us
  starting transfers between devices  103 us (57%)
  waiting for transfers between devices  28.5 us (16%)
  Pallas kernels  23.1 us (13%)
  blocking collectives  13.8 us (8%)
  local copies, waits for them, and re-layouts  8.71 us (5%)
  other arithmetic  2.66 us (1%)
    ppermute x11, starting transfers between devices, swapped(): inner = lax.ppermute(block, axis, [(i, i ^ 1) for i in range(count)])  49.7 us
    ppermute x11, starting transfers between devices, swapped(): lax.ppermute(block, axis, [(i, (i - 1 if i % 2 == 0 else i + 1) % count)...  48.5 us
    pallas_call x14, Pallas kernels, run(): pl.pallas_call(body, out_shape=[jax.ShapeDtypeStruct(s, d) for s, d in sh...  23.1 us
    ppermute x11, waiting for transfers between devices, swapped(): inner = lax.ppermute(block, axis, [(i, i ^ 1) for i in range(count)])  15.6 us
    all_to_all x2, blocking collectives, shards(): parts = lax.all_to_all(parts, 'tele', 0, 0, tiled=True)  13.8 us
    ppermute x11, waiting for transfers between devices, swapped(): lax.ppermute(block, axis, [(i, (i - 1 if i % 2 == 0 else i + 1) % count)...  12.9 us
    unnamed x14, local copies, waits for them, and re-layouts  7.04 us
    all_to_all x1, starting transfers between devices, shards(): packed = lax.all_to_all(packed, 'tele', 0, 0, tiled=True)  4.97 us
  transfers between devices with their start and end apart: 23, of which 13 were waited for; matrix products, arithmetic and copies ran while one was open for 0% of the time, Pallas kernels for 3%

profile of v2, /device:TPU:1, one launch (start us, length us, event | category | flops | bytes accessed | tf_op | source)
XLA Modules:
  0.0 180.3 jit_solution(17524920544794468553)
XLA Ops:
  7.2 5.0 %all-to-all-start = ((bf16[4,2,320,384]{3,2,1,0:T(8,128)(2,1)}), bf16[4,2,320,384]{3,2,1,0:T(8,128)(2,1)S(1)}, u32[]{:S(2)}, u32[]{:S(2)}) async-start(bf16[4,2,320,384]{3,2,1,0:T(8,128)(2,1)} %broadcast_in_dim.33), calls=%async_computation | async-start | bytes 3932160 | tf_op jit(solution)/shard_map/all_to_all | solution.py:219
  15.4 10.4 %collective-permute-start.1 = (bf16[16,320]{1,0:T(8,128)(2,1)S(1)}, bf16[16,320]{1,0:T(8,128)(2,1)S(1)}, u32[]{:S(2)}, u32[]{:S(2)}) collective-permute-start(bf16[16,320]{1,0:T(8,128)(2,1)S(1)} %shard_map.100.refs_1_), channel_id=1, source_target_pairs={{0,511},{1,2},{2,1},{3,4},{4,3},{5,6},{6,5},{7,8},{8,7},{9,10},{10... | collective-permute-start | bytes 30728 | tf_op jit(solution)/shard_map/ppermute | solution.py:19
  27.7 10.0 %collective-permute-done.1.refs_2_ = bf16[16,320]{1,0:T(8,128)(2,1)S(1)} collective-permute-done((bf16[16,320]{1,0:T(8,128)(2,1)S(1)}, bf16[16,320]{1,0:T(8,128)(2,1)S(1)}, u32[]{:S(2)}, u32[]{:S(2)}) %collective-permute-start.1) | collective-permute-done | bytes 10272 | tf_op jit(solution)/shard_map/ppermute | solution.py:19
  37.8 2.2 %shard_map.101.refs_1_ = bf16[16,320]{1,0:T(8,128)(2,1)S(1)} custom-call(bf16[16,320]{1,0:T(8,128)(2,1)S(1)} %collective-permute-done.refs_0_, bf16[16,320]{1,0:T(8,128)(2,1)S(1)} %shard_map.100.refs_1_, bf16[16,320]{1,0:T(8,128)(2,1)S(1)} %collective-permute-done.1.refs_2_, s32[16,12]{1,0:T(8,128)S(1)} %pad_add_fusion.refs_3_, ...), custom_call_target="tpu_custom_call" | custom-call | flops 268435456 | bytes 4606720 | tf_op jit(solution)/shard_map/pallas_call | solution.py:167
  39.9 2.7 %collective-permute-start.3 = (bf16[16,320]{1,0:T(8,128)(2,1)S(1)}, bf16[16,320]{1,0:T(8,128)(2,1)S(1)}, u32[]{:S(2)}, u32[]{:S(2)}) collective-permute-start(bf16[16,320]{1,0:T(8,128)(2,1)S(1)} %shard_map.101.refs_1_), channel_id=1, source_target_pairs={{0,511},{1,2},{2,1},{3,4},{4,3},{5,6},{6,5},{7,8},{8,7},{9,10},{10... | collective-permute-start | bytes 30728 | tf_op jit(solution)/shard_map/ppermute | solution.py:19
  49.2 5.4 %collective-permute-start.5 = (bf16[16,320]{1,0:T(8,128)(2,1)S(1)}, bf16[16,320]{1,0:T(8,128)(2,1)S(1)}, u32[]{:S(2)}, u32[]{:S(2)}) collective-permute-start(bf16[16,320]{1,0:T(8,128)(2,1)S(1)} %get-tuple-element.25.refs_1_), channel_id=1, source_target_pairs={{0,511},{1,2},{2,1},{3,4},{4,3},{5,6},{6,5},{7,8},{8,7},{9,10},{10... | collective-permute-start | bytes 30728 | tf_op jit(solution)/shard_map/ppermute | solution.py:19
  56.6 2.5 %collective-permute-done.4.refs_0_ = bf16[16,320]{1,0:T(8,128)(2,1)S(1)} collective-permute-done((bf16[16,320]{1,0:T(8,128)(2,1)S(1)}, bf16[16,320]{1,0:T(8,128)(2,1)S(1)}, u32[]{:S(2)}, u32[]{:S(2)}) %collective-permute-start.4) | collective-permute-done | bytes 10272 | tf_op jit(solution)/shard_map/ppermute | solution.py:20
  62.4 7.0 %all_to_all.15.refs_0_ = f32[4,8,320]{2,1,0:T(8,128)S(1)} all-to-all(f32[4,8,320]{2,1,0:T(8,128)S(1)} %get-tuple-element.29), channel_id=1, replica_groups=mesh['fine'=128,'tele'=4] {'tele'}, dimensions={0} | all-to-all | bytes 81920 | tf_op jit(solution)/shard_map/all_to_all | solution.py:252
  70.1 4.9 %collective-permute-start.7 = (bf16[8,320]{1,0:T(8,128)(2,1)S(1)}, bf16[8,320]{1,0:T(8,128)(2,1)S(1)}, u32[]{:S(2)}, u32[]{:S(2)}) collective-permute-start(bf16[8,320]{1,0:T(8,128)(2,1)S(1)} %get-tuple-element.30.refs_1_), channel_id=1, source_target_pairs={{0,508},{4,8},{8,4},{12,16},{16,12},{20,24},{24,20},{28,32},{32,28... | collective-permute-start | bytes 15368 | tf_op jit(solution)/shard_map/ppermute | solution.py:19
  75.0 12.5 %collective-permute-start.6 = (bf16[8,320]{1,0:T(8,128)(2,1)S(1)}, bf16[8,320]{1,0:T(8,128)(2,1)S(1)}, u32[]{:S(2)}, u32[]{:S(2)}) collective-permute-start(bf16[8,320]{1,0:T(8,128)(2,1)S(1)} %get-tuple-element.30.refs_1_), channel_id=1, source_target_pairs={{0,4},{4,0},{8,12},{12,8},{16,20},{20,16},{24,28},{28,24},{32,36},... | collective-permute-start | bytes 15368 | tf_op jit(solution)/shard_map/ppermute | solution.py:20
  92.0 6.4 %collective-permute-start.8 = (bf16[8,320]{1,0:T(8,128)(2,1)S(1)}, bf16[8,320]{1,0:T(8,128)(2,1)S(1)}, u32[]{:S(2)}, u32[]{:S(2)}) collective-permute-start(bf16[8,320]{1,0:T(8,128)(2,1)S(1)} %shard_map.105.refs_1_), channel_id=1, source_target_pairs={{0,4},{4,0},{8,12},{12,8},{16,20},{20,16},{24,28},{28,24},{32,36},... | collective-permute-start | bytes 15368 | tf_op jit(solution)/shard_map/ppermute | solution.py:20
  100.9 4.6 %collective-permute-start.11 = (bf16[16,320]{1,0:T(8,128)(2,1)S(1)}, bf16[16,320]{1,0:T(8,128)(2,1)S(1)}, u32[]{:S(2)}, u32[]{:S(2)}) collective-permute-start(bf16[16,320]{1,0:T(8,128)(2,1)S(1)} %shard_map.106.refs_1_), channel_id=1, source_target_pairs={{0,511},{1,2},{2,1},{3,4},{4,3},{5,6},{6,5},{7,8},{8,7},{9,10},{10... | collective-permute-start | bytes 30728 | tf_op jit(solution)/shard_map/ppermute | solution.py:19
  107.5 2.8 %collective-permute-done.10.refs_0_ = bf16[16,320]{1,0:T(8,128)(2,1)S(1)} collective-permute-done((bf16[16,320]{1,0:T(8,128)(2,1)S(1)}, bf16[16,320]{1,0:T(8,128)(2,1)S(1)}, u32[]{:S(2)}, u32[]{:S(2)}) %collective-permute-start.10) | collective-permute-done | bytes 10272 | tf_op jit(solution)/shard_map/ppermute | solution.py:20
  110.3 2.2 %shard_map.107.refs_1_ = bf16[16,320]{1,0:T(8,128)(2,1)S(1)} custom-call(bf16[16,320]{1,0:T(8,128)(2,1)S(1)} %collective-permute-done.10.refs_0_, bf16[16,320]{1,0:T(8,128)(2,1)S(1)} %shard_map.106.refs_1_, bf16[16,320]{1,0:T(8,128)(2,1)S(1)} %collective-permute-done.11.refs_2_, s32[16,12]{1,0:T(8,128)S(1)} %pad_add_fusion.refs_3_, ...), custom_call_target="tpu_custom_call" | custom-call | flops 268435456 | bytes 4606720 | tf_op jit(solution)/shard_map/pallas_call | solution.py:167
  112.4 3.2 %collective-permute-start.13 = (bf16[16,320]{1,0:T(8,128)(2,1)S(1)}, bf16[16,320]{1,0:T(8,128)(2,1)S(1)}, u32[]{:S(2)}, u32[]{:S(2)}) collective-permute-start(bf16[16,320]{1,0:T(8,128)(2,1)S(1)} %shard_map.107.refs_1_), channel_id=1, source_target_pairs={{0,511},{1,2},{2,1},{3,4},{4,3},{5,6},{6,5},{7,8},{8,7},{9,10},{10... | collective-permute-start | bytes 30728 | tf_op jit(solution)/shard_map/ppermute | solution.py:19
  122.2 4.9 %collective-permute-start.15 = (bf16[16,320]{1,0:T(8,128)(2,1)S(1)}, bf16[16,320]{1,0:T(8,128)(2,1)S(1)}, u32[]{:S(2)}, u32[]{:S(2)}) collective-permute-start(bf16[16,320]{1,0:T(8,128)(2,1)S(1)} %shard_map.108.refs_1_), channel_id=1, source_target_pairs={{0,511},{1,2},{2,1},{3,4},{4,3},{5,6},{6,5},{7,8},{8,7},{9,10},{10... | collective-permute-start | bytes 30728 | tf_op jit(solution)/shard_map/ppermute | solution.py:19
  129.1 2.5 %collective-permute-done.14.refs_0_ = bf16[16,320]{1,0:T(8,128)(2,1)S(1)} collective-permute-done((bf16[16,320]{1,0:T(8,128)(2,1)S(1)}, bf16[16,320]{1,0:T(8,128)(2,1)S(1)}, u32[]{:S(2)}, u32[]{:S(2)}) %collective-permute-start.14) | collective-permute-done | bytes 10272 | tf_op jit(solution)/shard_map/ppermute | solution.py:20
  131.6 2.2 %shard_map.109 = (bf16[16,320]{1,0:T(8,128)(2,1)S(1)}, f32[16,320]{1,0:T(8,128)S(1)}, bf16[16,320]{1,0:T(8,128)(2,1)S(1)}) custom-call(bf16[16,320]{1,0:T(8,128)(2,1)S(1)} %collective-permute-done.14.refs_0_, bf16[16,320]{1,0:T(8,128)(2,1)S(1)} %shard_map.108.refs_1_, bf16[16,320]{1,0:T(8,128)(2,1)S(1)} %collective-permute-done.15.refs_2_, ...), custom_call_target="tpu_custom_call" | custom-call | flops 268435456 | bytes 4606720 | tf_op jit(solution)/shard_map/pallas_call | solution.py:167
  133.8 6.5 %collective-permute-start.17 = (bf16[16,320]{1,0:T(8,128)(2,1)S(1)}, bf16[16,320]{1,0:T(8,128)(2,1)S(1)}, u32[]{:S(2)}, u32[]{:S(2)}) collective-permute-start(bf16[16,320]{1,0:T(8,128)(2,1)S(1)} %get-tuple-element.34.refs_1_), channel_id=1, source_target_pairs={{0,511},{1,2},{2,1},{3,4},{4,3},{5,6},{6,5},{7,8},{8,7},{9,10},{10... | collective-permute-start | bytes 30728 | tf_op jit(solution)/shard_map/ppermute | solution.py:19
  142.3 2.5 %collective-permute-done.16.refs_0_ = bf16[16,320]{1,0:T(8,128)(2,1)S(1)} collective-permute-done((bf16[16,320]{1,0:T(8,128)(2,1)S(1)}, bf16[16,320]{1,0:T(8,128)(2,1)S(1)}, u32[]{:S(2)}, u32[]{:S(2)}) %collective-permute-start.16) | collective-permute-done | bytes 10272 | tf_op jit(solution)/shard_map/ppermute | solution.py:20
  145.9 6.8 %all_to_all.16.refs_0_ = f32[4,8,320]{2,1,0:T(8,128)S(1)} all-to-all(f32[4,8,320]{2,1,0:T(8,128)S(1)} %shard_map.110), channel_id=1, replica_groups=mesh['fine'=128,'tele'=4] {'tele'}, dimensions={0} | all-to-all | bytes 81920 | tf_op jit(solution)/shard_map/all_to_all | solution.py:252
  155.3 11.0 %collective-permute-start.18 = (bf16[8,320]{1,0:T(8,128)(2,1)S(1)}, bf16[8,320]{1,0:T(8,128)(2,1)S(1)}, u32[]{:S(2)}, u32[]{:S(2)}) collective-permute-start(bf16[8,320]{1,0:T(8,128)(2,1)S(1)} %get-tuple-element.36.refs_1_), channel_id=1, source_target_pairs={{0,4},{4,0},{8,12},{12,8},{16,20},{20,16},{24,28},{28,24},{32,36},... | collective-permute-start | bytes 15368 | tf_op jit(solution)/shard_map/ppermute | solution.py:20
  170.7 6.3 %collective-permute-start.20 = (bf16[8,320]{1,0:T(8,128)(2,1)S(1)}, bf16[8,320]{1,0:T(8,128)(2,1)S(1)}, u32[]{:S(2)}, u32[]{:S(2)}) collective-permute-start(bf16[8,320]{1,0:T(8,128)(2,1)S(1)} %shard_map.112.refs_1_), channel_id=1, source_target_pairs={{0,4},{4,0},{8,12},{12,8},{16,20},{20,16},{24,28},{28,24},{32,36},... | collective-permute-start | bytes 15368 | tf_op jit(solution)/shard_map/ppermute | solution.py:20
  177.9 2.4 %shard_map.113 = f32[16,320]{1,0:T(8,128)} custom-call(bf16[8,320]{1,0:T(8,128)(2,1)S(1)} %collective-permute-done.20.refs_0_, bf16[8,320]{1,0:T(8,128)(2,1)S(1)} %shard_map.112.refs_1_, bf16[8,320]{1,0:T(8,128)(2,1)S(1)} %collective-permute-done.21.refs_2_, s32[8,64]{1,0:T(8,128)S(1)} %get-tuple-element.31.refs_3_, bf16[3072,128]{1,0:T(8,128)(2,1)S(1)} %bitcast.26, ...), custom_call_target="tpu_custom_call" | custom-call | flops 268435456 | bytes 3292224 | tf_op jit(solution)/shard_map/pallas_call | solution.py:167
  (60 shorter events, 53.0 us)
Async XLA Ops:
  7.2 52.0 %all-to-all-start = ((bf16[4,2,320,384]{3,2,1,0:T(8,128)(2,1)}), bf16[4,2,320,384]{3,2,1,0:T(8,128)(2,1)S(1)}, u32[]{:S(2)}, u32[]{:S(2)}) async-start(bf16[4,2,320,384]{3,2,1,0:T(8,128)(2,1)} %broadcast_in_dim.33), calls=%async_computation | async-start | bytes 3932160 | tf_op jit(solution)/shard_map/all_to_all | solution.py:219
  14.3 23.5 %copy-start.3 = (bf16[768,320]{1,0:T(8,128)(2,1)S(1)}, bf16[768,320]{1,0:T(8,128)(2,1)}, u32[]{:S(2)}) copy-start(bf16[768,320]{1,0:T(8,128)(2,1)} %constant.84.clone.refs_5_) | copy-start | bytes 1474564
  15.4 22.4 %collective-permute-start.1 = (bf16[16,320]{1,0:T(8,128)(2,1)S(1)}, bf16[16,320]{1,0:T(8,128)(2,1)S(1)}, u32[]{:S(2)}, u32[]{:S(2)}) collective-permute-start(bf16[16,320]{1,0:T(8,128)(2,1)S(1)} %shard_map.100.refs_1_), channel_id=1, source_target_pairs={{0,511},{1,2},{2,1},{3,4},{4,3},{5,6},{6,5},{7,8},{8,7},{9,10},{10... | collective-permute-start | bytes 30728 | tf_op jit(solution)/shard_map/ppermute | solution.py:19
  25.8 11.9 %collective-permute-start = (bf16[16,320]{1,0:T(8,128)(2,1)S(1)}, bf16[16,320]{1,0:T(8,128)(2,1)S(1)}, u32[]{:S(2)}, u32[]{:S(2)}) collective-permute-start(bf16[16,320]{1,0:T(8,128)(2,1)S(1)} %shard_map.100.refs_1_), channel_id=1, source_target_pairs={{0,1},{1,0},{2,3},{3,2},{4,5},{5,4},{6,7},{7,6},{8,9},{9,8},{10,11... | collective-permute-start | bytes 30728 | tf_op jit(solution)/shard_map/ppermute | solution.py:20
  39.9 6.3 %collective-permute-start.3 = (bf16[16,320]{1,0:T(8,128)(2,1)S(1)}, bf16[16,320]{1,0:T(8,128)(2,1)S(1)}, u32[]{:S(2)}, u32[]{:S(2)}) collective-permute-start(bf16[16,320]{1,0:T(8,128)(2,1)S(1)} %shard_map.101.refs_1_), channel_id=1, source_target_pairs={{0,511},{1,2},{2,1},{3,4},{4,3},{5,6},{6,5},{7,8},{8,7},{9,10},{10... | collective-permute-start | bytes 30728 | tf_op jit(solution)/shard_map/ppermute | solution.py:19
  42.6 4.4 %collective-permute-start.2 = (bf16[16,320]{1,0:T(8,128)(2,1)S(1)}, bf16[16,320]{1,0:T(8,128)(2,1)S(1)}, u32[]{:S(2)}, u32[]{:S(2)}) collective-permute-start(bf16[16,320]{1,0:T(8,128)(2,1)S(1)} %shard_map.101.refs_1_), channel_id=1, source_target_pairs={{0,1},{1,0},{2,3},{3,2},{4,5},{5,4},{6,7},{7,6},{8,9},{9,8},{10,11... | collective-permute-start | bytes 30728 | tf_op jit(solution)/shard_map/ppermute | solution.py:20
  49.2 7.4 %collective-permute-start.5 = (bf16[16,320]{1,0:T(8,128)(2,1)S(1)}, bf16[16,320]{1,0:T(8,128)(2,1)S(1)}, u32[]{:S(2)}, u32[]{:S(2)}) collective-permute-start(bf16[16,320]{1,0:T(8,128)(2,1)S(1)} %get-tuple-element.25.refs_1_), channel_id=1, source_target_pairs={{0,511},{1,2},{2,1},{3,4},{4,3},{5,6},{6,5},{7,8},{8,7},{9,10},{10... | collective-permute-start | bytes 30728 | tf_op jit(solution)/shard_map/ppermute | solution.py:19
  54.7 4.4 %collective-permute-start.4 = (bf16[16,320]{1,0:T(8,128)(2,1)S(1)}, bf16[16,320]{1,0:T(8,128)(2,1)S(1)}, u32[]{:S(2)}, u32[]{:S(2)}) collective-permute-start(bf16[16,320]{1,0:T(8,128)(2,1)S(1)} %get-tuple-element.25.refs_1_), channel_id=1, source_target_pairs={{0,1},{1,0},{2,3},{3,2},{4,5},{5,4},{6,7},{7,6},{8,9},{9,8},{10,11... | collective-permute-start | bytes 30728 | tf_op jit(solution)/shard_map/ppermute | solution.py:20
  70.1 17.5 %collective-permute-start.7 = (bf16[8,320]{1,0:T(8,128)(2,1)S(1)}, bf16[8,320]{1,0:T(8,128)(2,1)S(1)}, u32[]{:S(2)}, u32[]{:S(2)}) collective-permute-start(bf16[8,320]{1,0:T(8,128)(2,1)S(1)} %get-tuple-element.30.refs_1_), channel_id=1, source_target_pairs={{0,508},{4,8},{8,4},{12,16},{16,12},{20,24},{24,20},{28,32},{32,28... | collective-permute-start | bytes 15368 | tf_op jit(solution)/shard_map/ppermute | solution.py:19
  75.0 13.4 %collective-permute-start.6 = (bf16[8,320]{1,0:T(8,128)(2,1)S(1)}, bf16[8,320]{1,0:T(8,128)(2,1)S(1)}, u32[]{:S(2)}, u32[]{:S(2)}) collective-permute-start(bf16[8,320]{1,0:T(8,128)(2,1)S(1)} %get-tuple-element.30.refs_1_), channel_id=1, source_target_pairs={{0,4},{4,0},{8,12},{12,8},{16,20},{20,16},{24,28},{28,24},{32,36},... | collective-permute-start | bytes 15368 | tf_op jit(solution)/shard_map/ppermute | solution.py:20
  90.0 8.3 %collective-permute-start.9 = (bf16[8,320]{1,0:T(8,128)(2,1)S(1)}, bf16[8,320]{1,0:T(8,128)(2,1)S(1)}, u32[]{:S(2)}, u32[]{:S(2)}) collective-permute-start(bf16[8,320]{1,0:T(8,128)(2,1)S(1)} %shard_map.105.refs_1_), channel_id=1, source_target_pairs={{0,508},{4,8},{8,4},{12,16},{16,12},{20,24},{24,20},{28,32},{32,28... | collective-permute-start | bytes 15368 | tf_op jit(solution)/shard_map/ppermute | solution.py:19
  92.0 7.2 %collective-permute-start.8 = (bf16[8,320]{1,0:T(8,128)(2,1)S(1)}, bf16[8,320]{1,0:T(8,128)(2,1)S(1)}, u32[]{:S(2)}, u32[]{:S(2)}) collective-permute-start(bf16[8,320]{1,0:T(8,128)(2,1)S(1)} %shard_map.105.refs_1_), channel_id=1, source_target_pairs={{0,4},{4,0},{8,12},{12,8},{16,20},{20,16},{24,28},{28,24},{32,36},... | collective-permute-start | bytes 15368 | tf_op jit(solution)/shard_map/ppermute | solution.py:20
  100.9 6.5 %collective-permute-start.11 = (bf16[16,320]{1,0:T(8,128)(2,1)S(1)}, bf16[16,320]{1,0:T(8,128)(2,1)S(1)}, u32[]{:S(2)}, u32[]{:S(2)}) collective-permute-start(bf16[16,320]{1,0:T(8,128)(2,1)S(1)} %shard_map.106.refs_1_), channel_id=1, source_target_pairs={{0,511},{1,2},{2,1},{3,4},{4,3},{5,6},{6,5},{7,8},{8,7},{9,10},{10... | collective-permute-start | bytes 30728 | tf_op jit(solution)/shard_map/ppermute | solution.py:19
  105.5 4.7 %collective-permute-start.10 = (bf16[16,320]{1,0:T(8,128)(2,1)S(1)}, bf16[16,320]{1,0:T(8,128)(2,1)S(1)}, u32[]{:S(2)}, u32[]{:S(2)}) collective-permute-start(bf16[16,320]{1,0:T(8,128)(2,1)S(1)} %shard_map.106.refs_1_), channel_id=1, source_target_pairs={{0,1},{1,0},{2,3},{3,2},{4,5},{5,4},{6,7},{7,6},{8,9},{9,8},{10,11... | collective-permute-start | bytes 30728 | tf_op jit(solution)/shard_map/ppermute | solution.py:20
  112.4 6.3 %collective-permute-start.13 = (bf16[16,320]{1,0:T(8,128)(2,1)S(1)}, bf16[16,320]{1,0:T(8,128)(2,1)S(1)}, u32[]{:S(2)}, u32[]{:S(2)}) collective-permute-start(bf16[16,320]{1,0:T(8,128)(2,1)S(1)} %shard_map.107.refs_1_), channel_id=1, source_target_pairs={{0,511},{1,2},{2,1},{3,4},{4,3},{5,6},{6,5},{7,8},{8,7},{9,10},{10... | collective-permute-start | bytes 30728 | tf_op jit(solution)/shard_map/ppermute | solution.py:19
  115.6 4.4 %collective-permute-start.12 = (bf16[16,320]{1,0:T(8,128)(2,1)S(1)}, bf16[16,320]{1,0:T(8,128)(2,1)S(1)}, u32[]{:S(2)}, u32[]{:S(2)}) collective-permute-start(bf16[16,320]{1,0:T(8,128)(2,1)S(1)} %shard_map.107.refs_1_), channel_id=1, source_target_pairs={{0,1},{1,0},{2,3},{3,2},{4,5},{5,4},{6,7},{7,6},{8,9},{9,8},{10,11... | collective-permute-start | bytes 30728 | tf_op jit(solution)/shard_map/ppermute | solution.py:20
  122.2 6.9 %collective-permute-start.15 = (bf16[16,320]{1,0:T(8,128)(2,1)S(1)}, bf16[16,320]{1,0:T(8,128)(2,1)S(1)}, u32[]{:S(2)}, u32[]{:S(2)}) collective-permute-start(bf16[16,320]{1,0:T(8,128)(2,1)S(1)} %shard_map.108.refs_1_), channel_id=1, source_target_pairs={{0,511},{1,2},{2,1},{3,4},{4,3},{5,6},{6,5},{7,8},{8,7},{9,10},{10... | collective-permute-start | bytes 30728 | tf_op jit(solution)/shard_map/ppermute | solution.py:19
  127.2 4.4 %collective-permute-start.14 = (bf16[16,320]{1,0:T(8,128)(2,1)S(1)}, bf16[16,320]{1,0:T(8,128)(2,1)S(1)}, u32[]{:S(2)}, u32[]{:S(2)}) collective-permute-start(bf16[16,320]{1,0:T(8,128)(2,1)S(1)} %shard_map.108.refs_1_), channel_id=1, source_target_pairs={{0,1},{1,0},{2,3},{3,2},{4,5},{5,4},{6,7},{7,6},{8,9},{9,8},{10,11... | collective-permute-start | bytes 30728 | tf_op jit(solution)/shard_map/ppermute | solution.py:20
  133.8 8.5 %collective-permute-start.17 = (bf16[16,320]{1,0:T(8,128)(2,1)S(1)}, bf16[16,320]{1,0:T(8,128)(2,1)S(1)}, u32[]{:S(2)}, u32[]{:S(2)}) collective-permute-start(bf16[16,320]{1,0:T(8,128)(2,1)S(1)} %get-tuple-element.34.refs_1_), channel_id=1, source_target_pairs={{0,511},{1,2},{2,1},{3,4},{4,3},{5,6},{6,5},{7,8},{8,7},{9,10},{10... | collective-permute-start | bytes 30728 | tf_op jit(solution)/shard_map/ppermute | solution.py:19
  140.3 4.4 %collective-permute-start.16 = (bf16[16,320]{1,0:T(8,128)(2,1)S(1)}, bf16[16,320]{1,0:T(8,128)(2,1)S(1)}, u32[]{:S(2)}, u32[]{:S(2)}) collective-permute-start(bf16[16,320]{1,0:T(8,128)(2,1)S(1)} %get-tuple-element.34.refs_1_), channel_id=1, source_target_pairs={{0,1},{1,0},{2,3},{3,2},{4,5},{5,4},{6,7},{7,6},{8,9},{9,8},{10,11... | collective-permute-start | bytes 30728 | tf_op jit(solution)/shard_map/ppermute | solution.py:20
  153.3 13.0 %collective-permute-start.19 = (bf16[8,320]{1,0:T(8,128)(2,1)S(1)}, bf16[8,320]{1,0:T(8,128)(2,1)S(1)}, u32[]{:S(2)}, u32[]{:S(2)}) collective-permute-start(bf16[8,320]{1,0:T(8,128)(2,1)S(1)} %get-tuple-element.36.refs_1_), channel_id=1, source_target_pairs={{0,508},{4,8},{8,4},{12,16},{16,12},{20,24},{24,20},{28,32},{32,28... | collective-permute-start | bytes 15368 | tf_op jit(solution)/shard_map/ppermute | solution.py:19
  155.3 11.8 %collective-permute-start.18 = (bf16[8,320]{1,0:T(8,128)(2,1)S(1)}, bf16[8,320]{1,0:T(8,128)(2,1)S(1)}, u32[]{:S(2)}, u32[]{:S(2)}) collective-permute-start(bf16[8,320]{1,0:T(8,128)(2,1)S(1)} %get-tuple-element.36.refs_1_), channel_id=1, source_target_pairs={{0,4},{4,0},{8,12},{12,8},{16,20},{20,16},{24,28},{28,24},{32,36},... | collective-permute-start | bytes 15368 | tf_op jit(solution)/shard_map/ppermute | solution.py:20
  168.8 8.3 %collective-permute-start.21 = (bf16[8,320]{1,0:T(8,128)(2,1)S(1)}, bf16[8,320]{1,0:T(8,128)(2,1)S(1)}, u32[]{:S(2)}, u32[]{:S(2)}) collective-permute-start(bf16[8,320]{1,0:T(8,128)(2,1)S(1)} %shard_map.112.refs_1_), channel_id=1, source_target_pairs={{0,508},{4,8},{8,4},{12,16},{16,12},{20,24},{24,20},{28,32},{32,28... | collective-permute-start | bytes 15368 | tf_op jit(solution)/shard_map/ppermute | solution.py:19
  170.7 7.1 %collective-permute-start.20 = (bf16[8,320]{1,0:T(8,128)(2,1)S(1)}, bf16[8,320]{1,0:T(8,128)(2,1)S(1)}, u32[]{:S(2)}, u32[]{:S(2)}) collective-permute-start(bf16[8,320]{1,0:T(8,128)(2,1)S(1)} %shard_map.112.refs_1_), channel_id=1, source_target_pairs={{0,4},{4,0},{8,12},{12,8},{16,20},{20,16},{24,28},{28,24},{32,36},... | collective-permute-start | bytes 15368 | tf_op jit(solution)/shard_map/ppermute | solution.py:20
  (4 other events, 20.3 us)

commit v3 on v2

--- a/solution.py
+++ b/solution.py
@@ -72,20 +72,68 @@
 
 
 def apply_inverse(inverse_ref, vector):
-    count, dofs = vector.shape
+    count = vector.shape[0]
     row = lax.broadcasted_iota(jnp.int32, vector.shape, 0)
     result = jnp.zeros(vector.shape, jnp.float32)
     for e in range(count):
         product = lax.dot_general(
-            vector, inverse_ref[e][:, :dofs], (((1,), (1,)), ((), ())), preferred_element_type=jnp.float32
+            vector, inverse_ref[e], (((1,), (1,)), ((), ())), preferred_element_type=jnp.float32
         )
         result = jnp.where(row == e, product, result)
     return result
 
 
-def first_kernel(right_ref, inverse_ref, state_ref):
+def pool_rows(links, count, position):
+    shift = count.bit_length() - 1
+    owner, within = links >> shift, links & (count - 1)
+    place = jnp.where(owner == position, 1, jnp.where(owner == (position ^ 1), 0, 2))
+    return jnp.where(links >= 0, place * count + within, -1)
+
+
+def first_kernel(
+    right_ref,
+    inverse_ref,
+    faces_ref,
+    links_ref,
+    coarse_links_ref,
+    coarse_faces_ref,
+    operators_in_ref,
+    state_ref,
+    index_ref,
+    lists_ref,
+    operators_ref,
+):
+    tele, column = lax.axis_index("tele"), lax.axis_index("fine")
+    tele_size = lax.axis_size("tele")
     lowered = right_ref[...].astype(jnp.bfloat16)
     state_ref[...] = apply_inverse(inverse_ref, lowered).astype(jnp.bfloat16)
+
+    fine_rows = right_ref.shape[0]
+    rows = pool_rows(links_ref[...], fine_rows, column * tele_size + tele)
+    index = jnp.concatenate([rows.astype(jnp.float32), faces_ref[...].astype(jnp.float32)], axis=0)
+    index_ref[...] = index.T.astype(jnp.int32)
+
+    own = coarse_links_ref.shape[0]
+    count = own * tele_size
+    rows = pool_rows(coarse_links_ref[...], count, column).astype(jnp.float32)
+    kinds = coarse_faces_ref[...].astype(jnp.float32)
+    lists_ref[...] = jnp.zeros(lists_ref.shape, jnp.float32)
+    row = lax.broadcasted_iota(jnp.int32, (count, rows.shape[1]), 0)
+    for part, values in enumerate((rows, kinds)):
+        placed = jnp.zeros(row.shape, jnp.float32)
+        for c in range(own):
+            placed = jnp.where(row == own * tele + c, values[c : c + 1], placed)
+        lists_ref[:, part * 6 : part * 6 + 6] = placed
+
+    types, size, _ = operators_in_ref.shape
+    unit = lax.broadcasted_iota(jnp.int32, (LANES, size), 0) == lax.broadcasted_iota(jnp.int32, (LANES, size), 1)
+    unit = jnp.where(unit, 1.0, 0.0).astype(jnp.bfloat16)
+    operators_ref[...] = jnp.zeros(operators_ref.shape, jnp.bfloat16)
+    for q in range(types):
+        turned = lax.dot_general(
+            unit, operators_in_ref[q], (((1,), (1,)), ((), ())), preferred_element_type=jnp.float32
+        )
+        operators_ref[q * LANES : (q + 1) * LANES, :size] = turned.astype(jnp.bfloat16)
 
 
 def sweep_kernel(
@@ -102,29 +150,28 @@
 
 
 def restrict_kernel(
-    prev_ref, own_ref, next_ref, index_ref, operators_ref, lift_ref, lowered_ref, target_ref, *rest
-):
-    out_ref = rest[-1] if len(rest) == 1 else rest[1]
+    prev_ref, own_ref, next_ref, index_ref, operators_ref, lift_ref, lowered_ref, target_ref, lists_ref, out_ref
+):
     states = [prev_ref[...], own_ref[...], next_ref[...]]
     coupled = coupling(states, index_ref[...], operators_ref[...], lift_ref[...])
     residual = lowered_ref[...].astype(jnp.float32) - coupled
-    rows = out_ref.shape[1]
-    member = target_ref[...] == lax.broadcasted_iota(jnp.int32, (rows, residual.shape[0]), 0)
+    rows, dofs = out_ref.shape[1], residual.shape[1]
+    member = target_ref[...] & (rows - 1)
+    member = member == lax.broadcasted_iota(jnp.int32, (rows, residual.shape[0]), 0)
     partial = exact_dot(jnp.where(member, 1.0, 0.0).astype(jnp.bfloat16), residual)
     for t in range(out_ref.shape[0]):
-        out_ref[t] = partial
-    if len(rest) > 1:
-        packed_ref, _, list_ref = rest
-        dofs = residual.shape[1]
-        for c in range(rows):
-            list_ref[c : c + 1] = packed_ref[c, 0:1, dofs:].astype(jnp.int32)
-
-
-def coarse_first_kernel(parts_ref, inverse_ref, restricted_ref, state_ref):
-    restricted = parts_ref[0]
+        out_ref[t, :, :dofs] = partial
+        out_ref[t, :, dofs:] = lists_ref[...]
+
+
+def coarse_first_kernel(parts_ref, inverse_ref, restricted_ref, state_ref, index_ref):
+    total = parts_ref[0]
     for t in range(1, parts_ref.shape[0]):
-        restricted = restricted + parts_ref[t]
+        total = total + parts_ref[t]
+    dofs = restricted_ref.shape[1]
+    restricted = total[:, :dofs]
     restricted_ref[...] = restricted
+    index_ref[...] = total[:, dofs:].astype(jnp.int32)
     state_ref[...] = apply_inverse(inverse_ref, restricted.astype(jnp.bfloat16)).astype(jnp.bfloat16)
 
 
@@ -145,7 +192,8 @@
     coupled = coupling(states, index_ref[...], operators_ref[...], lift_ref[...])
     coarse = apply_inverse(inverse_ref, (right_ref[...] - coupled).astype(jnp.bfloat16))
     rows, fine = coarse.shape[0], solution_ref.shape[0]
-    member = target_ref[...] == lax.broadcasted_iota(jnp.int32, (rows, fine), 0)
+    member = target_ref[...] & (rows - 1)
+    member = member == lax.broadcasted_iota(jnp.int32, (rows, fine), 0)
     added = exact_dot(jnp.where(member, 1.0, 0.0).T.astype(jnp.bfloat16), coarse)
     out_ref[...] = (solution_ref[...] + added).astype(out_ref.dtype)
 
@@ -175,12 +223,6 @@
     return result[0] if single else result
 
 
-def local_rows(links, count, position):
-    owner, within = links // count, links % count
-    place = jnp.where(owner == position, 1, jnp.where(owner == position ^ 1, 0, 2))
-    return jnp.where(links >= 0, place * count + within, -1)
-
-
 def shards(
     right_side,
     fine_inverse,
@@ -192,35 +234,38 @@
     face_operators,
     agglomerate,
 ):
-    f32, bf16 = jnp.float32, jnp.bfloat16
+    f32, bf16, i32 = jnp.float32, jnp.bfloat16, jnp.int32
     fine_rows, dofs = right_side.shape
     tele_size = lax.axis_size("tele")
-    tele = lax.axis_index("tele")
-    column = lax.axis_index("fine")
-    coarse_own = coarse_inverse.shape[0]
-    coarse_rows = coarse_own * tele_size
-
+    coarse_rows = coarse_inverse.shape[0] * tele_size
+    types = face_operators.shape[0]
+    spare = -dofs % LANES
+
+    block_inverse = jnp.broadcast_to(coarse_inverse[None], (tele_size,) + coarse_inverse.shape)
+    right_side, block_inverse = lax.optimization_barrier((right_side, block_inverse))
+    block_inverse = lax.all_to_all(block_inverse, "tele", 0, 0, tiled=True)
+    block_inverse = block_inverse.reshape((coarse_rows,) + coarse_inverse.shape[1:])
     lift = jnp.asarray(face_table(), bf16)
-    types, face_dofs, _ = face_operators.shape
-    pad = LANES - face_dofs
-    operators = jnp.pad(face_operators.transpose(0, 2, 1), ((0, 0), (0, pad), (0, pad)))
-    operators = operators.reshape(types * LANES, LANES)
-    fine_index = jnp.concatenate([local_rows(fine_links, fine_rows, column * tele_size + tele), fine_faces], axis=1)
-    target = agglomerate % coarse_rows
-    target = target[None, :]
-
-    lists = jnp.concatenate([local_rows(coarse_links, coarse_rows, column), coarse_faces], axis=1).astype(bf16)
-    lists = jnp.pad(lists[:, None, :], ((0, 0), (0, dofs - 1), (0, -dofs % LANES - lists.shape[1])))
-    packed = jnp.concatenate([coarse_inverse, lists], axis=2)
-    packed = jnp.broadcast_to(packed[None], (tele_size,) + packed.shape)
-    right_side, operators, fine_index, target, packed = lax.optimization_barrier(
-        (right_side, operators, fine_index, target, packed)
-    )
-    packed = lax.all_to_all(packed, "tele", 0, 0, tiled=True)
-    block_inverse = packed.reshape((coarse_rows,) + packed.shape[2:])
+    target = agglomerate[None, :]
+    inverse = fine_inverse
+    state, fine_index, lists, operators = run(
+        first_kernel,
+        [
+            ((fine_rows, dofs), bf16),
+            ((fine_rows, 12), i32),
+            ((coarse_rows, spare), f32),
+            ((types * LANES, LANES), bf16),
+        ],
+        right_side,
+        inverse,
+        fine_faces.T,
+        fine_links.T,
+        coarse_links,
+        coarse_faces,
+        face_operators,
+        held=(1,),
+    )
     shared = (operators, lift)
-    inverse = fine_inverse
-    state = run(first_kernel, ((fine_rows, dofs), bf16), right_side, inverse, held=(1,))
 
     def halo(block, axis):
         inner, outer = swapped(block, axis)
@@ -228,7 +273,6 @@
 
     both = ("fine", "tele")
     for cycle in range(CYCLES):
-        keep = (inverse,) if cycle < CYCLES - 1 else ()
         for sweep in range(SWEEPS):
             if cycle == 0 and sweep == 0:
                 continue
@@ -240,23 +284,25 @@
             )
             state = result[0]
         solution, lowered = result[1], result[2]
-        operands = (*halo(state, both), fine_index, *shared, lowered, target)
-        part_shape = ((tele_size, coarse_rows, dofs), f32)
-        if cycle == 0:
-            lists_shape = ((coarse_rows, block_inverse.shape[2] - dofs), jnp.int32)
-            parts, coarse_index = run(
-                restrict_kernel, [part_shape, lists_shape], *operands, block_inverse, held=(5, 8), keep=keep
-            )
-        else:
-            parts = run(restrict_kernel, part_shape, *operands, held=(5,), keep=keep)
+        parts = run(
+            restrict_kernel,
+            ((tele_size, coarse_rows, dofs + spare), f32),
+            *halo(state, both),
+            fine_index,
+            *shared,
+            lowered,
+            target,
+            lists,
+            held=(5,),
+            keep=(block_inverse,),
+        )
         parts = lax.all_to_all(parts, "tele", 0, 0, tiled=True)
-        restricted, coarse = run(
+        restricted, coarse, coarse_index = run(
             coarse_first_kernel,
-            [((coarse_rows, dofs), f32), ((coarse_rows, dofs), bf16)],
+            [((coarse_rows, dofs), f32), ((coarse_rows, dofs), bf16), ((coarse_rows, spare), i32)],
             parts,
             block_inverse,
             held=(1,),
-            keep=keep,
         )
         for sweep in range(SWEEPS - 2):
             coarse = run(
@@ -268,7 +314,6 @@
                 restricted,
                 block_inverse,
                 held=(5, 7),
-                keep=keep,
             )[0]
         last = cycle == CYCLES - 1
         state = run(
@@ -282,7 +327,6 @@
             target,
             solution,
             held=(5, 7),
-            keep=keep,
         )
     return state
 

time: 181 us -> 175 us (0.967)
  local copies, waits for them, and re-layouts: 8.71 us -> 5.69 us
  other arithmetic: 2.66 us -> 0 us
    unnamed x14 -> x20, local copies, waits for them, and re-layouts: 7.04 us -> 3.18 us
    concatenate x4 -> x0, other arithmetic: 1.98 us -> none  [the longest x1 1.11 us: shards(): packed = jnp.concatenate([coarse_inverse, lists], axis=2)]
where the time goes in v3:
time: 175 us; the launch traced here: 174 us
  starting transfers between devices  104 us (59%)
  waiting for transfers between devices  27.1 us (15%)
  Pallas kernels  23.5 us (13%)
  blocking collectives  13.5 us (8%)
  local copies, waits for them, and re-layouts  5.69 us (3%)
    ppermute x11, starting transfers between devices, swapped(): inner = lax.ppermute(block, axis, [(i, i ^ 1) for i in range(count)])  49.7 us
    ppermute x11, starting transfers between devices, swapped(): lax.ppermute(block, axis, [(i, (i - 1 if i % 2 == 0 else i + 1) % count)...  48.8 us
    pallas_call x14, Pallas kernels, run(): pl.pallas_call(body, out_shape=[jax.ShapeDtypeStruct(s, d) for s, d in sh...  23.5 us
    ppermute x11, waiting for transfers between devices, swapped(): inner = lax.ppermute(block, axis, [(i, i ^ 1) for i in range(count)])  15.6 us
    all_to_all x2, blocking collectives, shards(): parts = lax.all_to_all(parts, 'tele', 0, 0, tiled=True)  13.5 us
    ppermute x11, waiting for transfers between devices, swapped(): lax.ppermute(block, axis, [(i, (i - 1 if i % 2 == 0 else i + 1) % count)...  11.5 us
    all_to_all x1, starting transfers between devices, shards(): block_inverse = lax.all_to_all(block_inverse, 'tele', 0, 0, tiled=True)  4.99 us
  transfers between devices with their start and end apart: 23, of which 13 were waited for; matrix products, arithmetic and copies ran while one was open for 0% of the time, Pallas kernels for 3%

profile of v3, /device:TPU:1, one launch (start us, length us, event | category | flops | bytes accessed | tf_op | source)
XLA Modules:
  0.0 173.7 jit_solution(16746824295939673746)
XLA Ops:
  0.0 2.5 %broadcast_in_dim.4 = bf16[4,2,320,320]{3,2,1,0:T(8,128)(2,1)} broadcast(bf16[2,320,320]{2,1,0:T(8,128)(2,1)} %param.14), dimensions={1,2,3} | broadcast | bytes 2048000 | tf_op jit(solution)/shard_map/broadcast_in_dim | solution.py:244
  2.5 5.0 %all-to-all-start = ((bf16[4,2,320,320]{3,2,1,0:T(8,128)(2,1)}), bf16[4,2,320,320]{3,2,1,0:T(8,128)(2,1)S(1)}, u32[]{:S(2)}, u32[]{:S(2)}) async-start(bf16[4,2,320,320]{3,2,1,0:T(8,128)(2,1)} %broadcast_in_dim.4), calls=%async_computation | async-start | bytes 3932160 | tf_op jit(solution)/shard_map/all_to_all | solution.py:246
  12.3 10.4 %collective-permute-start.1 = (bf16[16,320]{1,0:T(8,128)(2,1)S(1)}, bf16[16,320]{1,0:T(8,128)(2,1)S(1)}, u32[]{:S(2)}, u32[]{:S(2)}) collective-permute-start(bf16[16,320]{1,0:T(8,128)(2,1)S(1)} %get-tuple-element.24.refs_1_), channel_id=1, source_target_pairs={{0,511},{1,2},{2,1},{3,4},{4,3},{5,6},{6,5},{7,8},{8,7},{9,10},{10... | collective-permute-start | bytes 30728 | tf_op jit(solution)/shard_map/ppermute | solution.py:19
  24.5 8.6 %collective-permute-done.1.refs_2_ = bf16[16,320]{1,0:T(8,128)(2,1)S(1)} collective-permute-done((bf16[16,320]{1,0:T(8,128)(2,1)S(1)}, bf16[16,320]{1,0:T(8,128)(2,1)S(1)}, u32[]{:S(2)}, u32[]{:S(2)}) %collective-permute-start.1) | collective-permute-done | bytes 10272 | tf_op jit(solution)/shard_map/ppermute | solution.py:19
  33.1 2.2 %shard_map.101.refs_1_ = bf16[16,320]{1,0:T(8,128)(2,1)S(1)} custom-call(bf16[16,320]{1,0:T(8,128)(2,1)S(1)} %collective-permute-done.refs_0_, bf16[16,320]{1,0:T(8,128)(2,1)S(1)} %get-tuple-element.24.refs_1_, bf16[16,320]{1,0:T(8,128)(2,1)S(1)} %collective-permute-done.1.refs_2_, s32[16,12]{1,0:T(8,128)S(1)} %get-tuple-element.25.refs_3_, ...), custom_call_target="tpu_custom_call" | custom-call | flops 268435456 | bytes 4606720 | tf_op jit(solution)/shard_map/pallas_call | solution.py:215
  35.3 2.8 %collective-permute-start.3 = (bf16[16,320]{1,0:T(8,128)(2,1)S(1)}, bf16[16,320]{1,0:T(8,128)(2,1)S(1)}, u32[]{:S(2)}, u32[]{:S(2)}) collective-permute-start(bf16[16,320]{1,0:T(8,128)(2,1)S(1)} %shard_map.101.refs_1_), channel_id=1, source_target_pairs={{0,511},{1,2},{2,1},{3,4},{4,3},{5,6},{6,5},{7,8},{8,7},{9,10},{10... | collective-permute-start | bytes 30728 | tf_op jit(solution)/shard_map/ppermute | solution.py:19
  44.8 5.4 %collective-permute-start.5 = (bf16[16,320]{1,0:T(8,128)(2,1)S(1)}, bf16[16,320]{1,0:T(8,128)(2,1)S(1)}, u32[]{:S(2)}, u32[]{:S(2)}) collective-permute-start(bf16[16,320]{1,0:T(8,128)(2,1)S(1)} %get-tuple-element.27.refs_1_), channel_id=1, source_target_pairs={{0,511},{1,2},{2,1},{3,4},{4,3},{5,6},{6,5},{7,8},{8,7},{9,10},{10... | collective-permute-start | bytes 30728 | tf_op jit(solution)/shard_map/ppermute | solution.py:19
  52.1 2.5 %collective-permute-done.4.refs_0_ = bf16[16,320]{1,0:T(8,128)(2,1)S(1)} collective-permute-done((bf16[16,320]{1,0:T(8,128)(2,1)S(1)}, bf16[16,320]{1,0:T(8,128)(2,1)S(1)}, u32[]{:S(2)}, u32[]{:S(2)}) %collective-permute-start.4) | collective-permute-done | bytes 10272 | tf_op jit(solution)/shard_map/ppermute | solution.py:20
  55.8 6.8 %all_to_all.15.refs_0_ = f32[4,8,384]{2,1,0:T(8,128)S(1)} all-to-all(f32[4,8,384]{2,1,0:T(8,128)S(1)} %shard_map.103), channel_id=1, replica_groups=mesh['fine'=128,'tele'=4] {'tele'}, dimensions={0} | all-to-all | bytes 98304 | tf_op jit(solution)/shard_map/all_to_all | solution.py:299
  63.2 5.2 %collective-permute-start.7 = (bf16[8,320]{1,0:T(8,128)(2,1)S(1)}, bf16[8,320]{1,0:T(8,128)(2,1)S(1)}, u32[]{:S(2)}, u32[]{:S(2)}) collective-permute-start(bf16[8,320]{1,0:T(8,128)(2,1)S(1)} %get-tuple-element.31.refs_1_), channel_id=1, source_target_pairs={{0,508},{4,8},{8,4},{12,16},{16,12},{20,24},{24,20},{28,32},{32,28... | collective-permute-start | bytes 15368 | tf_op jit(solution)/shard_map/ppermute | solution.py:19
  68.4 12.5 %collective-permute-start.6 = (bf16[8,320]{1,0:T(8,128)(2,1)S(1)}, bf16[8,320]{1,0:T(8,128)(2,1)S(1)}, u32[]{:S(2)}, u32[]{:S(2)}) collective-permute-start(bf16[8,320]{1,0:T(8,128)(2,1)S(1)} %get-tuple-element.31.refs_1_), channel_id=1, source_target_pairs={{0,4},{4,0},{8,12},{12,8},{16,20},{20,16},{24,28},{28,24},{32,36},... | collective-permute-start | bytes 15368 | tf_op jit(solution)/shard_map/ppermute | solution.py:20
  85.4 6.4 %collective-permute-start.8 = (bf16[8,320]{1,0:T(8,128)(2,1)S(1)}, bf16[8,320]{1,0:T(8,128)(2,1)S(1)}, u32[]{:S(2)}, u32[]{:S(2)}) collective-permute-start(bf16[8,320]{1,0:T(8,128)(2,1)S(1)} %shard_map.105.refs_1_), channel_id=1, source_target_pairs={{0,4},{4,0},{8,12},{12,8},{16,20},{20,16},{24,28},{28,24},{32,36},... | collective-permute-start | bytes 15368 | tf_op jit(solution)/shard_map/ppermute | solution.py:20
  94.4 4.6 %collective-permute-start.11 = (bf16[16,320]{1,0:T(8,128)(2,1)S(1)}, bf16[16,320]{1,0:T(8,128)(2,1)S(1)}, u32[]{:S(2)}, u32[]{:S(2)}) collective-permute-start(bf16[16,320]{1,0:T(8,128)(2,1)S(1)} %shard_map.106.refs_1_), channel_id=1, source_target_pairs={{0,511},{1,2},{2,1},{3,4},{4,3},{5,6},{6,5},{7,8},{8,7},{9,10},{10... | collective-permute-start | bytes 30728 | tf_op jit(solution)/shard_map/ppermute | solution.py:19
  100.9 2.8 %collective-permute-done.10.refs_0_ = bf16[16,320]{1,0:T(8,128)(2,1)S(1)} collective-permute-done((bf16[16,320]{1,0:T(8,128)(2,1)S(1)}, bf16[16,320]{1,0:T(8,128)(2,1)S(1)}, u32[]{:S(2)}, u32[]{:S(2)}) %collective-permute-start.10) | collective-permute-done | bytes 10272 | tf_op jit(solution)/shard_map/ppermute | solution.py:20
  103.7 2.2 %shard_map.107.refs_1_ = bf16[16,320]{1,0:T(8,128)(2,1)S(1)} custom-call(bf16[16,320]{1,0:T(8,128)(2,1)S(1)} %collective-permute-done.10.refs_0_, bf16[16,320]{1,0:T(8,128)(2,1)S(1)} %shard_map.106.refs_1_, bf16[16,320]{1,0:T(8,128)(2,1)S(1)} %collective-permute-done.11.refs_2_, s32[16,12]{1,0:T(8,128)S(1)} %get-tuple-element.25.refs_3_, ...), custom_call_target="tpu_custom_call" | custom-call | flops 268435456 | bytes 4606720 | tf_op jit(solution)/shard_map/pallas_call | solution.py:215
  105.8 3.2 %collective-permute-start.13 = (bf16[16,320]{1,0:T(8,128)(2,1)S(1)}, bf16[16,320]{1,0:T(8,128)(2,1)S(1)}, u32[]{:S(2)}, u32[]{:S(2)}) collective-permute-start(bf16[16,320]{1,0:T(8,128)(2,1)S(1)} %shard_map.107.refs_1_), channel_id=1, source_target_pairs={{0,511},{1,2},{2,1},{3,4},{4,3},{5,6},{6,5},{7,8},{8,7},{9,10},{10... | collective-permute-start | bytes 30728 | tf_op jit(solution)/shard_map/ppermute | solution.py:19
  115.6 4.9 %collective-permute-start.15 = (bf16[16,320]{1,0:T(8,128)(2,1)S(1)}, bf16[16,320]{1,0:T(8,128)(2,1)S(1)}, u32[]{:S(2)}, u32[]{:S(2)}) collective-permute-start(bf16[16,320]{1,0:T(8,128)(2,1)S(1)} %shard_map.108.refs_1_), channel_id=1, source_target_pairs={{0,511},{1,2},{2,1},{3,4},{4,3},{5,6},{6,5},{7,8},{8,7},{9,10},{10... | collective-permute-start | bytes 30728 | tf_op jit(solution)/shard_map/ppermute | solution.py:19
  122.5 2.5 %collective-permute-done.14.refs_0_ = bf16[16,320]{1,0:T(8,128)(2,1)S(1)} collective-permute-done((bf16[16,320]{1,0:T(8,128)(2,1)S(1)}, bf16[16,320]{1,0:T(8,128)(2,1)S(1)}, u32[]{:S(2)}, u32[]{:S(2)}) %collective-permute-start.14) | collective-permute-done | bytes 10272 | tf_op jit(solution)/shard_map/ppermute | solution.py:20
  127.2 6.5 %collective-permute-start.17 = (bf16[16,320]{1,0:T(8,128)(2,1)S(1)}, bf16[16,320]{1,0:T(8,128)(2,1)S(1)}, u32[]{:S(2)}, u32[]{:S(2)}) collective-permute-start(bf16[16,320]{1,0:T(8,128)(2,1)S(1)} %get-tuple-element.35.refs_1_), channel_id=1, source_target_pairs={{0,511},{1,2},{2,1},{3,4},{4,3},{5,6},{6,5},{7,8},{8,7},{9,10},{10... | collective-permute-start | bytes 30728 | tf_op jit(solution)/shard_map/ppermute | solution.py:19
  135.7 2.5 %collective-permute-done.16.refs_0_ = bf16[16,320]{1,0:T(8,128)(2,1)S(1)} collective-permute-done((bf16[16,320]{1,0:T(8,128)(2,1)S(1)}, bf16[16,320]{1,0:T(8,128)(2,1)S(1)}, u32[]{:S(2)}, u32[]{:S(2)}) %collective-permute-start.16) | collective-permute-done | bytes 10272 | tf_op jit(solution)/shard_map/ppermute | solution.py:20
  139.3 6.8 %all_to_all.16.refs_0_ = f32[4,8,384]{2,1,0:T(8,128)S(1)} all-to-all(f32[4,8,384]{2,1,0:T(8,128)S(1)} %shard_map.110), channel_id=1, replica_groups=mesh['fine'=128,'tele'=4] {'tele'}, dimensions={0} | all-to-all | bytes 98304 | tf_op jit(solution)/shard_map/all_to_all | solution.py:299
  148.7 11.0 %collective-permute-start.18 = (bf16[8,320]{1,0:T(8,128)(2,1)S(1)}, bf16[8,320]{1,0:T(8,128)(2,1)S(1)}, u32[]{:S(2)}, u32[]{:S(2)}) collective-permute-start(bf16[8,320]{1,0:T(8,128)(2,1)S(1)} %get-tuple-element.37.refs_1_), channel_id=1, source_target_pairs={{0,4},{4,0},{8,12},{12,8},{16,20},{20,16},{24,28},{28,24},{32,36},... | collective-permute-start | bytes 15368 | tf_op jit(solution)/shard_map/ppermute | solution.py:20
  164.2 6.3 %collective-permute-start.20 = (bf16[8,320]{1,0:T(8,128)(2,1)S(1)}, bf16[8,320]{1,0:T(8,128)(2,1)S(1)}, u32[]{:S(2)}, u32[]{:S(2)}) collective-permute-start(bf16[8,320]{1,0:T(8,128)(2,1)S(1)} %shard_map.112.refs_1_), channel_id=1, source_target_pairs={{0,4},{4,0},{8,12},{12,8},{16,20},{20,16},{24,28},{28,24},{32,36},... | collective-permute-start | bytes 15368 | tf_op jit(solution)/shard_map/ppermute | solution.py:20
  171.3 2.4 %shard_map.113 = f32[16,320]{1,0:T(8,128)} custom-call(bf16[8,320]{1,0:T(8,128)(2,1)S(1)} %collective-permute-done.20.refs_0_, bf16[8,320]{1,0:T(8,128)(2,1)S(1)} %shard_map.112.refs_1_, bf16[8,320]{1,0:T(8,128)(2,1)S(1)} %collective-permute-done.21.refs_2_, s32[8,64]{1,0:T(8,128)S(1)} %get-tuple-element.38.refs_3_, ...), custom_call_target="tpu_custom_call" | custom-call | flops 268435456 | bytes 2964544 | tf_op jit(solution)/shard_map/pallas_call | solution.py:215
  (59 shorter events, 47.4 us)
Async XLA Ops:
  2.5 52.1 %all-to-all-start = ((bf16[4,2,320,320]{3,2,1,0:T(8,128)(2,1)}), bf16[4,2,320,320]{3,2,1,0:T(8,128)(2,1)S(1)}, u32[]{:S(2)}, u32[]{:S(2)}) async-start(bf16[4,2,320,320]{3,2,1,0:T(8,128)(2,1)} %broadcast_in_dim.4), calls=%async_computation | async-start | bytes 3932160 | tf_op jit(solution)/shard_map/all_to_all | solution.py:246
  10.7 22.4 %copy-start.2 = (bf16[768,320]{1,0:T(8,128)(2,1)S(1)}, bf16[768,320]{1,0:T(8,128)(2,1)}, u32[]{:S(2)}) copy-start(bf16[768,320]{1,0:T(8,128)(2,1)} %constant.2.clone.refs_5_) | copy-start | bytes 1474564
  12.3 20.9 %collective-permute-start.1 = (bf16[16,320]{1,0:T(8,128)(2,1)S(1)}, bf16[16,320]{1,0:T(8,128)(2,1)S(1)}, u32[]{:S(2)}, u32[]{:S(2)}) collective-permute-start(bf16[16,320]{1,0:T(8,128)(2,1)S(1)} %get-tuple-element.24.refs_1_), channel_id=1, source_target_pairs={{0,511},{1,2},{2,1},{3,4},{4,3},{5,6},{6,5},{7,8},{8,7},{9,10},{10... | collective-permute-start | bytes 30728 | tf_op jit(solution)/shard_map/ppermute | solution.py:19
  22.6 10.5 %collective-permute-start = (bf16[16,320]{1,0:T(8,128)(2,1)S(1)}, bf16[16,320]{1,0:T(8,128)(2,1)S(1)}, u32[]{:S(2)}, u32[]{:S(2)}) collective-permute-start(bf16[16,320]{1,0:T(8,128)(2,1)S(1)} %get-tuple-element.24.refs_1_), channel_id=1, source_target_pairs={{0,1},{1,0},{2,3},{3,2},{4,5},{5,4},{6,7},{7,6},{8,9},{9,8},{10,11... | collective-permute-start | bytes 30728 | tf_op jit(solution)/shard_map/ppermute | solution.py:20
  35.3 6.4 %collective-permute-start.3 = (bf16[16,320]{1,0:T(8,128)(2,1)S(1)}, bf16[16,320]{1,0:T(8,128)(2,1)S(1)}, u32[]{:S(2)}, u32[]{:S(2)}) collective-permute-start(bf16[16,320]{1,0:T(8,128)(2,1)S(1)} %shard_map.101.refs_1_), channel_id=1, source_target_pairs={{0,511},{1,2},{2,1},{3,4},{4,3},{5,6},{6,5},{7,8},{8,7},{9,10},{10... | collective-permute-start | bytes 30728 | tf_op jit(solution)/shard_map/ppermute | solution.py:19
  38.2 4.4 %collective-permute-start.2 = (bf16[16,320]{1,0:T(8,128)(2,1)S(1)}, bf16[16,320]{1,0:T(8,128)(2,1)S(1)}, u32[]{:S(2)}, u32[]{:S(2)}) collective-permute-start(bf16[16,320]{1,0:T(8,128)(2,1)S(1)} %shard_map.101.refs_1_), channel_id=1, source_target_pairs={{0,1},{1,0},{2,3},{3,2},{4,5},{5,4},{6,7},{7,6},{8,9},{9,8},{10,11... | collective-permute-start | bytes 30728 | tf_op jit(solution)/shard_map/ppermute | solution.py:20
  44.8 7.4 %collective-permute-start.5 = (bf16[16,320]{1,0:T(8,128)(2,1)S(1)}, bf16[16,320]{1,0:T(8,128)(2,1)S(1)}, u32[]{:S(2)}, u32[]{:S(2)}) collective-permute-start(bf16[16,320]{1,0:T(8,128)(2,1)S(1)} %get-tuple-element.27.refs_1_), channel_id=1, source_target_pairs={{0,511},{1,2},{2,1},{3,4},{4,3},{5,6},{6,5},{7,8},{8,7},{9,10},{10... | collective-permute-start | bytes 30728 | tf_op jit(solution)/shard_map/ppermute | solution.py:19
  50.2 4.4 %collective-permute-start.4 = (bf16[16,320]{1,0:T(8,128)(2,1)S(1)}, bf16[16,320]{1,0:T(8,128)(2,1)S(1)}, u32[]{:S(2)}, u32[]{:S(2)}) collective-permute-start(bf16[16,320]{1,0:T(8,128)(2,1)S(1)} %get-tuple-element.27.refs_1_), channel_id=1, source_target_pairs={{0,1},{1,0},{2,3},{3,2},{4,5},{5,4},{6,7},{7,6},{8,9},{9,8},{10,11... | collective-permute-start | bytes 30728 | tf_op jit(solution)/shard_map/ppermute | solution.py:20
  63.2 17.8 %collective-permute-start.7 = (bf16[8,320]{1,0:T(8,128)(2,1)S(1)}, bf16[8,320]{1,0:T(8,128)(2,1)S(1)}, u32[]{:S(2)}, u32[]{:S(2)}) collective-permute-start(bf16[8,320]{1,0:T(8,128)(2,1)S(1)} %get-tuple-element.31.refs_1_), channel_id=1, source_target_pairs={{0,508},{4,8},{8,4},{12,16},{16,12},{20,24},{24,20},{28,32},{32,28... | collective-permute-start | bytes 15368 | tf_op jit(solution)/shard_map/ppermute | solution.py:19
  68.4 13.4 %collective-permute-start.6 = (bf16[8,320]{1,0:T(8,128)(2,1)S(1)}, bf16[8,320]{1,0:T(8,128)(2,1)S(1)}, u32[]{:S(2)}, u32[]{:S(2)}) collective-permute-start(bf16[8,320]{1,0:T(8,128)(2,1)S(1)} %get-tuple-element.31.refs_1_), channel_id=1, source_target_pairs={{0,4},{4,0},{8,12},{12,8},{16,20},{20,16},{24,28},{28,24},{32,36},... | collective-permute-start | bytes 15368 | tf_op jit(solution)/shard_map/ppermute | solution.py:20
  83.4 8.3 %collective-permute-start.9 = (bf16[8,320]{1,0:T(8,128)(2,1)S(1)}, bf16[8,320]{1,0:T(8,128)(2,1)S(1)}, u32[]{:S(2)}, u32[]{:S(2)}) collective-permute-start(bf16[8,320]{1,0:T(8,128)(2,1)S(1)} %shard_map.105.refs_1_), channel_id=1, source_target_pairs={{0,508},{4,8},{8,4},{12,16},{16,12},{20,24},{24,20},{28,32},{32,28... | collective-permute-start | bytes 15368 | tf_op jit(solution)/shard_map/ppermute | solution.py:19
  85.4 7.2 %collective-permute-start.8 = (bf16[8,320]{1,0:T(8,128)(2,1)S(1)}, bf16[8,320]{1,0:T(8,128)(2,1)S(1)}, u32[]{:S(2)}, u32[]{:S(2)}) collective-permute-start(bf16[8,320]{1,0:T(8,128)(2,1)S(1)} %shard_map.105.refs_1_), channel_id=1, source_target_pairs={{0,4},{4,0},{8,12},{12,8},{16,20},{20,16},{24,28},{28,24},{32,36},... | collective-permute-start | bytes 15368 | tf_op jit(solution)/shard_map/ppermute | solution.py:20
  94.4 6.5 %collective-permute-start.11 = (bf16[16,320]{1,0:T(8,128)(2,1)S(1)}, bf16[16,320]{1,0:T(8,128)(2,1)S(1)}, u32[]{:S(2)}, u32[]{:S(2)}) collective-permute-start(bf16[16,320]{1,0:T(8,128)(2,1)S(1)} %shard_map.106.refs_1_), channel_id=1, source_target_pairs={{0,511},{1,2},{2,1},{3,4},{4,3},{5,6},{6,5},{7,8},{8,7},{9,10},{10... | collective-permute-start | bytes 30728 | tf_op jit(solution)/shard_map/ppermute | solution.py:19
  98.9 4.7 %collective-permute-start.10 = (bf16[16,320]{1,0:T(8,128)(2,1)S(1)}, bf16[16,320]{1,0:T(8,128)(2,1)S(1)}, u32[]{:S(2)}, u32[]{:S(2)}) collective-permute-start(bf16[16,320]{1,0:T(8,128)(2,1)S(1)} %shard_map.106.refs_1_), channel_id=1, source_target_pairs={{0,1},{1,0},{2,3},{3,2},{4,5},{5,4},{6,7},{7,6},{8,9},{9,8},{10,11... | collective-permute-start | bytes 30728 | tf_op jit(solution)/shard_map/ppermute | solution.py:20
  105.8 6.3 %collective-permute-start.13 = (bf16[16,320]{1,0:T(8,128)(2,1)S(1)}, bf16[16,320]{1,0:T(8,128)(2,1)S(1)}, u32[]{:S(2)}, u32[]{:S(2)}) collective-permute-start(bf16[16,320]{1,0:T(8,128)(2,1)S(1)} %shard_map.107.refs_1_), channel_id=1, source_target_pairs={{0,511},{1,2},{2,1},{3,4},{4,3},{5,6},{6,5},{7,8},{8,7},{9,10},{10... | collective-permute-start | bytes 30728 | tf_op jit(solution)/shard_map/ppermute | solution.py:19
  109.0 4.4 %collective-permute-start.12 = (bf16[16,320]{1,0:T(8,128)(2,1)S(1)}, bf16[16,320]{1,0:T(8,128)(2,1)S(1)}, u32[]{:S(2)}, u32[]{:S(2)}) collective-permute-start(bf16[16,320]{1,0:T(8,128)(2,1)S(1)} %shard_map.107.refs_1_), channel_id=1, source_target_pairs={{0,1},{1,0},{2,3},{3,2},{4,5},{5,4},{6,7},{7,6},{8,9},{9,8},{10,11... | collective-permute-start | bytes 30728 | tf_op jit(solution)/shard_map/ppermute | solution.py:20
  115.6 6.9 %collective-permute-start.15 = (bf16[16,320]{1,0:T(8,128)(2,1)S(1)}, bf16[16,320]{1,0:T(8,128)(2,1)S(1)}, u32[]{:S(2)}, u32[]{:S(2)}) collective-permute-start(bf16[16,320]{1,0:T(8,128)(2,1)S(1)} %shard_map.108.refs_1_), channel_id=1, source_target_pairs={{0,511},{1,2},{2,1},{3,4},{4,3},{5,6},{6,5},{7,8},{8,7},{9,10},{10... | collective-permute-start | bytes 30728 | tf_op jit(solution)/shard_map/ppermute | solution.py:19
  120.6 4.4 %collective-permute-start.14 = (bf16[16,320]{1,0:T(8,128)(2,1)S(1)}, bf16[16,320]{1,0:T(8,128)(2,1)S(1)}, u32[]{:S(2)}, u32[]{:S(2)}) collective-permute-start(bf16[16,320]{1,0:T(8,128)(2,1)S(1)} %shard_map.108.refs_1_), channel_id=1, source_target_pairs={{0,1},{1,0},{2,3},{3,2},{4,5},{5,4},{6,7},{7,6},{8,9},{9,8},{10,11... | collective-permute-start | bytes 30728 | tf_op jit(solution)/shard_map/ppermute | solution.py:20
  127.2 8.5 %collective-permute-start.17 = (bf16[16,320]{1,0:T(8,128)(2,1)S(1)}, bf16[16,320]{1,0:T(8,128)(2,1)S(1)}, u32[]{:S(2)}, u32[]{:S(2)}) collective-permute-start(bf16[16,320]{1,0:T(8,128)(2,1)S(1)} %get-tuple-element.35.refs_1_), channel_id=1, source_target_pairs={{0,511},{1,2},{2,1},{3,4},{4,3},{5,6},{6,5},{7,8},{8,7},{9,10},{10... | collective-permute-start | bytes 30728 | tf_op jit(solution)/shard_map/ppermute | solution.py:19
  133.7 4.4 %collective-permute-start.16 = (bf16[16,320]{1,0:T(8,128)(2,1)S(1)}, bf16[16,320]{1,0:T(8,128)(2,1)S(1)}, u32[]{:S(2)}, u32[]{:S(2)}) collective-permute-start(bf16[16,320]{1,0:T(8,128)(2,1)S(1)} %get-tuple-element.35.refs_1_), channel_id=1, source_target_pairs={{0,1},{1,0},{2,3},{3,2},{4,5},{5,4},{6,7},{7,6},{8,9},{9,8},{10,11... | collective-permute-start | bytes 30728 | tf_op jit(solution)/shard_map/ppermute | solution.py:20
  146.7 13.0 %collective-permute-start.19 = (bf16[8,320]{1,0:T(8,128)(2,1)S(1)}, bf16[8,320]{1,0:T(8,128)(2,1)S(1)}, u32[]{:S(2)}, u32[]{:S(2)}) collective-permute-start(bf16[8,320]{1,0:T(8,128)(2,1)S(1)} %get-tuple-element.37.refs_1_), channel_id=1, source_target_pairs={{0,508},{4,8},{8,4},{12,16},{16,12},{20,24},{24,20},{28,32},{32,28... | collective-permute-start | bytes 15368 | tf_op jit(solution)/shard_map/ppermute | solution.py:19
  148.7 11.8 %collective-permute-start.18 = (bf16[8,320]{1,0:T(8,128)(2,1)S(1)}, bf16[8,320]{1,0:T(8,128)(2,1)S(1)}, u32[]{:S(2)}, u32[]{:S(2)}) collective-permute-start(bf16[8,320]{1,0:T(8,128)(2,1)S(1)} %get-tuple-element.37.refs_1_), channel_id=1, source_target_pairs={{0,4},{4,0},{8,12},{12,8},{16,20},{20,16},{24,28},{28,24},{32,36},... | collective-permute-start | bytes 15368 | tf_op jit(solution)/shard_map/ppermute | solution.py:20
  162.2 8.3 %collective-permute-start.21 = (bf16[8,320]{1,0:T(8,128)(2,1)S(1)}, bf16[8,320]{1,0:T(8,128)(2,1)S(1)}, u32[]{:S(2)}, u32[]{:S(2)}) collective-permute-start(bf16[8,320]{1,0:T(8,128)(2,1)S(1)} %shard_map.112.refs_1_), channel_id=1, source_target_pairs={{0,508},{4,8},{8,4},{12,16},{16,12},{20,24},{24,20},{28,32},{32,28... | collective-permute-start | bytes 15368 | tf_op jit(solution)/shard_map/ppermute | solution.py:19
  164.2 7.1 %collective-permute-start.20 = (bf16[8,320]{1,0:T(8,128)(2,1)S(1)}, bf16[8,320]{1,0:T(8,128)(2,1)S(1)}, u32[]{:S(2)}, u32[]{:S(2)}) collective-permute-start(bf16[8,320]{1,0:T(8,128)(2,1)S(1)} %shard_map.112.refs_1_), channel_id=1, source_target_pairs={{0,4},{4,0},{8,12},{12,8},{16,20},{20,16},{24,28},{28,24},{32,36},... | collective-permute-start | bytes 15368 | tf_op jit(solution)/shard_map/ppermute | solution.py:20
  (9 other events, 69.4 us)

commit v4 on v3

v4 whole, which is shorter than its diff:
```python
import functools

import jax
import jax.numpy as jnp
import numpy as np
from jax import lax
from jax.experimental import pallas as pl
from jax.experimental.pallas import tpu as pltpu
from jax.sharding import PartitionSpec as P

FIELDS = 5
NODES = 4
SWEEPS = 3
CYCLES = 2
LANES = 128
OPPOSITE = (1, 0, 3, 2, 5, 4)


def swapped(block, axis):
    count = lax.axis_size(axis)
    outer = lax.ppermute(block, axis, [(i, (i - 1 if i % 2 == 0 else i + 1) % count) for i in range(count)])
    inner = lax.ppermute(block, axis, [(i, i ^ 1) for i in range(count)])
    return inner, outer


def face_table():
    cube = np.arange(FIELDS * NODES**3).reshape(FIELDS, NODES, NODES, NODES)
    far = NODES - 1
    faces = (cube[:, 0], cube[:, far], cube[:, :, 0], cube[:, :, far], cube[..., 0], cube[..., far])
    table = np.zeros((6 * LANES, cube.size), np.float32)
    for k, face in enumerate(faces):
        nodes = face.reshape(-1)
        table[k * LANES + np.arange(nodes.size), nodes] = 1.0
    return table


def halves(value):
    high = value.astype(jnp.bfloat16)
    low = (value - high.astype(jnp.float32)).astype(jnp.bfloat16)
    return high, low


def exact_dot(left, right):
    high, low = halves(right)
    return jnp.dot(left, high, preferred_element_type=jnp.float32) + jnp.dot(
        left, low, preferred_element_type=jnp.float32
    )


def coupling(states, index, operators, lift):
    count = states[0].shape[0]
    pool = jnp.concatenate([state.astype(jnp.float32) for state in states], axis=0).astype(jnp.bfloat16)
    traces = lax.dot_general(pool, lift, (((1,), (1,)), ((), ())), preferred_element_type=jnp.float32)
    traces = traces.astype(jnp.bfloat16)
    column = lax.broadcasted_iota(jnp.int32, (count, pool.shape[0]), 1)
    face_rows, kinds = [], []
    for k in range(6):
        chosen = jnp.where(index[:, k : k + 1] == column, 1.0, 0.0).astype(jnp.bfloat16)
        across = traces[:, OPPOSITE[k] * LANES : (OPPOSITE[k] + 1) * LANES]
        face_rows.append(jnp.dot(chosen, across, preferred_element_type=jnp.float32))
        kinds.append(jnp.broadcast_to(index[:, 6 + k : 7 + k], (count, LANES)))
    face_rows = jnp.concatenate(face_rows, axis=0)
    kinds = jnp.concatenate(kinds, axis=0)
    types = operators.shape[0] // LANES
    spread = jnp.concatenate(
        [jnp.where(kinds == q, face_rows, 0.0).astype(jnp.bfloat16) for q in range(types)], axis=1
    )
    coupled = jnp.dot(spread, operators, preferred_element_type=jnp.float32)
    side_by_side = jnp.concatenate([coupled[k * count : (k + 1) * count] for k in range(6)], axis=1)
    high = side_by_side.astype(jnp.bfloat16).astype(jnp.float32)
    terms = jnp.concatenate([high, side_by_side - high], axis=0).astype(jnp.bfloat16)
    lifted = jnp.dot(terms, lift, preferred_element_type=jnp.float32)
    return lifted[:count] + lifted[count:]


def apply_inverse(blocks, vector):
    row = lax.broadcasted_iota(jnp.int32, vector.shape, 0)
    result = jnp.zeros(vector.shape, jnp.float32)
    first = 0
    for block in blocks:
        for e in range(block.shape[0]):
            product = lax.dot_general(
                vector, block[e], (((1,), (1,)), ((), ())), preferred_element_type=jnp.float32
            )
            result = jnp.where(row == first + e, product, result)
        first += block.shape[0]
    return result


def pool_rows(links, count, position, turn=0):
    shift = count.bit_length() - 1
    owner, within = links >> shift, (links - turn) & (count - 1)
    place = jnp.where(owner == position, 1, jnp.where(owner == (position ^ 1), 0, 2))
    return jnp.where(links >= 0, place * count + within, -1)


def first_kernel(*refs, count):
    sources, (state_ref, index_ref, lists_ref, operators_ref, inverse_ref) = refs[:count], refs[count : count + 5]
    targets, (sems, block_sems) = refs[count + 5 : -2], refs[-2:]
    right_ref, links_ref, faces_ref, coarse_links_ref, coarse_faces_ref, operators_in_ref = targets
    whole = [pltpu.make_async_copy(sources[i], targets[i], sems.at[i]) for i in range(count - 1)]
    blocks = [
        pltpu.make_async_copy(sources[-1].at[e], inverse_ref.at[e], block_sems.at[e])
        for e in range(inverse_ref.shape[0])
    ]
    for copy in [whole[0], *blocks, *whole[1:]]:
        copy.start()

    tele, column = lax.axis_index("tele"), lax.axis_index("fine")
    tele_size = lax.axis_size("tele")
    whole[0].wait()
    lowered = right_ref[...].astype(jnp.bfloat16)
    row = lax.broadcasted_iota(jnp.int32, lowered.shape, 0)
    result = jnp.zeros(lowered.shape, jnp.float32)
    for e, copy in enumerate(blocks):
        copy.wait()
        product = lax.dot_general(
            lowered, inverse_ref[e], (((1,), (1,)), ((), ())), preferred_element_type=jnp.float32
        )
        result = jnp.where(row == e, product, result)
    state_ref[...] = result.astype(jnp.bfloat16)
    for copy in whole[1:]:
        copy.wait()

    fine_rows = right_ref.shape[0]
    rows = pool_rows(links_ref[...], fine_rows, column * tele_size + tele)
    index = jnp.concatenate([rows.astype(jnp.float32), faces_ref[...].astype(jnp.float32)], axis=0)
    index_ref[...] = index.T.astype(jnp.int32)

    own = coarse_links_ref.shape[0]
    count = own * tele_size
    kinds = coarse_faces_ref[...].astype(jnp.float32)
    lists_ref[...] = jnp.zeros(lists_ref.shape, jnp.float32)
    row = lax.broadcasted_iota(jnp.int32, (count, kinds.shape[1]), 0)
    for t in range(tele_size):
        rows = pool_rows(coarse_links_ref[...], count, column, own * t).astype(jnp.float32)
        for part, values in enumerate((rows, kinds)):
            placed = jnp.zeros(row.shape, jnp.float32)
            for c in range(own):
                placed = jnp.where(row == ((own * (tele - t) + c) & (count - 1)), values[c : c + 1], placed)
            lists_ref[t, :, part * 6 : part * 6 + 6] = placed

    types, size, _ = operators_in_ref.shape
    unit = lax.broadcasted_iota(jnp.int32, (LANES, size), 0) == lax.broadcasted_iota(jnp.int32, (LANES, size), 1)
    unit = jnp.where(unit, 1.0, 0.0).astype(jnp.bfloat16)
    operators_ref[...] = jnp.zeros(operators_ref.shape, jnp.bfloat16)
    for q in range(types):
        turned = lax.dot_general(
            unit, operators_in_ref[q], (((1,), (1,)), ((), ())), preferred_element_type=jnp.float32
        )
        operators_ref[q * LANES : (q + 1) * LANES, :size] = turned.astype(jnp.bfloat16)


def take_kernel(before_ref, after_ref, low_ref, high_ref):
    low_ref[...] = before_ref[0:1]
    high_ref[...] = after_ref[1:2]


def sweep(refs, blocks):
    prev_ref, own_ref, next_ref, index_ref, operators_ref, lift_ref, right_ref = refs
    states = [prev_ref[...], own_ref[...], next_ref[...]]
    coupled = coupling(states, index_ref[...], operators_ref[...], lift_ref[...])
    lowered = (right_ref[...] - coupled).astype(jnp.bfloat16)
    return apply_inverse(blocks, lowered), lowered


def sweep_kernel(*refs, blocks):
    result, lowered = sweep(refs[:7], refs[7 : 7 + blocks])
    outs = refs[7 + blocks :]
    outs[0][...] = result.astype(jnp.bfloat16)
    if len(outs) > 1:
        outs[1][...] = result
        outs[2][...] = lowered


def restrict_kernel(
    prev_ref, own_ref, next_ref, index_ref, operators_ref, lift_ref, lowered_ref, target_ref, lists_ref, out_ref
):
    states = [prev_ref[...], own_ref[...], next_ref[...]]
    coupled = coupling(states, index_ref[...], operators_ref[...], lift_ref[...])
    residual = lowered_ref[...].astype(jnp.float32) - coupled
    tele_size, rows, dofs = out_ref.shape[0], out_ref.shape[1], residual.shape[1]
    shape = (tele_size * rows, residual.shape[0])
    row = lax.broadcasted_iota(jnp.int32, shape, 0)
    element = (row + (row >> (rows.bit_length() - 1)) * (rows // tele_size)) & (rows - 1)
    member = jnp.where((target_ref[...] & (rows - 1)) == element, 1.0, 0.0).astype(jnp.bfloat16)
    partial = exact_dot(member, residual)
    for t in range(tele_size):
        out_ref[t, :, :dofs] = partial[t * rows : (t + 1) * rows]
        out_ref[t, :, dofs:] = lists_ref[t]


def coarse_first_kernel(*refs, blocks):
    parts_ref, inverses, (restricted_ref, state_ref, index_ref) = refs[0], refs[1 : 1 + blocks], refs[1 + blocks :]
    total = parts_ref[0]
    for t in range(1, parts_ref.shape[0]):
        total = total + parts_ref[t]
    dofs = restricted_ref.shape[1]
    restricted = total[:, :dofs]
    restricted_ref[...] = restricted
    index_ref[...] = total[:, dofs:].astype(jnp.int32)
    state_ref[...] = apply_inverse(inverses, restricted.astype(jnp.bfloat16)).astype(jnp.bfloat16)


def correct_kernel(*refs, blocks):
    coarse, _ = sweep(refs[:7], refs[7 : 7 + blocks])
    target_ref, solution_ref, out_ref = refs[7 + blocks :]
    rows, fine = coarse.shape[0], solution_ref.shape[0]
    turn = lax.axis_index("tele") * (rows // lax.axis_size("tele"))
    member = ((target_ref[...] - turn) & (rows - 1)) == lax.broadcasted_iota(jnp.int32, (rows, fine), 0)
    added = exact_dot(jnp.where(member, 1.0, 0.0).T.astype(jnp.bfloat16), coarse)
    out_ref[...] = (solution_ref[...] + added).astype(out_ref.dtype)


def run(kernel, outs, *operands, held=(), keep=(), hbm=(), pinned=(), scratch=()):
    count = len(operands)

    def body(*refs):
        kernel(*refs[:count], *refs[count + len(keep) :])

    single = not isinstance(outs, list)
    shapes = [outs] if single else outs
    vmem = pl.BlockSpec(memory_space=pltpu.VMEM)
    moved = sum(o.size * o.dtype.itemsize for o in operands)
    operands = [
        pltpu.with_memory_space_constraint(o, pltpu.HBM if i in hbm else pltpu.VMEM) if i in held or i in hbm else o
        for i, o in enumerate(operands)
    ]
    operands += [pltpu.with_memory_space_constraint(o, pltpu.VMEM) for o in keep]
    result = pl.pallas_call(
        body,
        out_shape=[pltpu.VMEM(s, d) if i in pinned else jax.ShapeDtypeStruct(s, d) for i, (s, d) in enumerate(shapes)],
        in_specs=[pl.BlockSpec(memory_space=pltpu.HBM) if i in hbm else vmem for i in range(len(operands))],
        out_specs=[vmem] * len(shapes),
        scratch_shapes=scratch,
        compiler_params=pltpu.CompilerParams(vmem_limit_bytes=20 << 20),
        cost_estimate=pl.CostEstimate(flops=1 << 28, bytes_accessed=moved, transcendentals=0),
    )(*operands)
    return result[0] if single else result


def shards(
    right_side,
    fine_inverse,
    fine_links,
    fine_faces,
    coarse_inverse,
    coarse_links,
    coarse_faces,
    face_operators,
    agglomerate,
):
    f32, bf16, i32 = jnp.float32, jnp.bfloat16, jnp.int32
    fine_rows, dofs = right_side.shape
    tele_size = lax.axis_size("tele")
    coarse_rows = coarse_inverse.shape[0] * tele_size
    types = face_operators.shape[0]
    spare = -dofs % LANES

    def along(block, distance):
        return lax.ppermute(block, "tele", [(i, (i + distance) % tele_size) for i in range(tele_size)])

    before, after = along(coarse_inverse, 1), along(coarse_inverse, -1)
    lift = jnp.asarray(face_table(), bf16)
    target = agglomerate[None, :]
    operands = (
        right_side,
        fine_links.T,
        fine_faces.T,
        coarse_links,
        coarse_faces,
        face_operators,
        fine_inverse,
    )
    state, fine_index, lists, operators, inverse = run(
        functools.partial(first_kernel, count=len(operands)),
        [
            ((fine_rows, dofs), bf16),
            ((fine_rows, 12), i32),
            ((tele_size, coarse_rows, spare), f32),
            ((types * LANES, LANES), bf16),
            (fine_inverse.shape, bf16),
        ],
        *operands,
        hbm=range(len(operands)),
        pinned=(3, 4),
        scratch=[pltpu.VMEM(o.shape, o.dtype) for o in operands[:-1]]
        + [pltpu.SemaphoreType.DMA((len(operands),)), pltpu.SemaphoreType.DMA((fine_rows,))],
    )
    shared = (operators, lift)

    def halo(block, axis):
        inner, outer = swapped(block, axis)
        return inner, block, outer

    both = ("fine", "tele")
    for cycle in range(CYCLES):
        for sweep in range(SWEEPS):
            if cycle == 0 and sweep == 0:
                continue
            outs = [((fine_rows, dofs), bf16)]
            if sweep == SWEEPS - 1:
                outs += [((fine_rows, dofs), f32), ((fine_rows, dofs), bf16)]
            result = run(
                functools.partial(sweep_kernel, blocks=1),
                outs,
                *halo(state, both),
                fine_index,
                *shared,
                right_side,
                inverse,
                held=(5, 7),
            )
            state = result[0]
            if cycle == 0 and sweep == 1:
                before, after, state = lax.optimization_barrier((before, after, state))
                far_low, far_high = run(take_kernel, [((1,) + before.shape[1:], bf16)] * 2, before, after)
                far_low, far_high = along(far_low, 1), along(far_high, -1)
                blocks = (coarse_inverse, after, far_low, far_high, before)
        solution, lowered = result[1], result[2]
        parts = run(
            restrict_kernel,
            ((tele_size, coarse_rows, dofs + spare), f32),
            *halo(state, both),
            fine_index,
            *shared,
            lowered,
            target,
            lists,
            held=(5,),
        )
        parts = lax.all_to_all(parts, "tele", 0, 0, tiled=True)
        restricted, coarse, coarse_index = run(
            functools.partial(coarse_first_kernel, blocks=len(blocks)),
            [((coarse_rows, dofs), f32), ((coarse_rows, dofs), bf16), ((coarse_rows, spare), i32)],
            parts,
            *blocks,
            held=range(1, 1 + len(blocks)),
        )
        for sweep in range(SWEEPS - 2):
            coarse = run(
                functools.partial(sweep_kernel, blocks=len(blocks)),
                [((coarse_rows, dofs), bf16)],
                *halo(coarse, "fine"),
                coarse_index,
                *shared,
                restricted,
                *blocks,
                held=(5, *range(7, 7 + len(blocks))),
            )[0]
        last = cycle == CYCLES - 1
        state = run(
            functools.partial(correct_kernel, blocks=len(blocks)),
            ((fine_rows, dofs), f32 if last else bf16),
            *halo(coarse, "fine"),
            coarse_index,
            *shared,
            restricted,
            *blocks,
            target,
            solution,
            held=(5, *range(7, 7 + len(blocks))),
        )
    return state


def solution(mesh):
    both = P(("fine", "tele"))
    return jax.shard_map(
        shards,
        mesh=mesh,
        in_specs=(both, both, both, both, both, both, both, P(), both),
        out_specs=both,
        check_vma=False,
    )
```

time: 175 us -> 190 us (1.086)
  starting transfers between devices: 104 us -> 126 us
  local copies, waits for them, and re-layouts: 5.69 us -> 0.02 us
  waiting for transfers between devices: 27.1 us -> 21.6 us
  Pallas kernels: 23.5 us -> 26.1 us
    ppermute x11, waiting for transfers between devices: 15.6 us -> 0.03 us  [swapped(): inner = lax.ppermute(block, axis, [(i, i ^ 1) for i in range(count)])]
    ppermute x0 -> x4, starting transfers between devices: none -> 13.9 us  [along(): lax.ppermute(block, 'tele', [(i, (i + distance) % tele_size) for i in ran...]
    ppermute x11, starting transfers between devices: 48.8 us -> 62.4 us  [swapped(): lax.ppermute(block, axis, [(i, (i - 1 if i % 2 == 0 else i + 1) % count)...]
    ppermute x11, waiting for transfers between devices: 11.5 us -> 21.5 us  [swapped(): lax.ppermute(block, axis, [(i, (i - 1 if i % 2 == 0 else i + 1) % count)...]
    all_to_all x1 -> x0, starting transfers between devices: 4.99 us -> none  [shards(): block_inverse = lax.all_to_all(block_inverse, 'tele', 0, 0, tiled=True)]
    unnamed x20 -> x8, local copies, waits for them, and re-layouts: 3.18 us -> 0.02 us
    pallas_call x14 -> x15, Pallas kernels: 23.5 us -> 26.1 us  [run(): pl.pallas_call(body, out_shape=[pltpu.VMEM(s, d) if i in pinned else jax....]
    broadcast_in_dim x1 -> x0, local copies, waits for them, and re-layouts: 2.51 us -> none  [shards(): jnp.broadcast_to(coarse_inverse[None], (tele_size,) + coarse_inverse.shape)]
  transfers between devices with their start and end apart: 23 -> 26, of which waited for: 13 -> 11; matrix products, arithmetic and copies ran while one was open for 0% -> 0% of each run, Pallas kernels for 3% -> 6%
where the time goes in v4:
time: 190 us; the launch traced here: 188 us
  starting transfers between devices  126 us (66%)
  Pallas kernels  26.1 us (14%)
  waiting for transfers between devices  21.6 us (11%)
  blocking collectives  14.1 us (7%)
    ppermute x11, starting transfers between devices, swapped(): lax.ppermute(block, axis, [(i, (i - 1 if i % 2 == 0 else i + 1) % count)...  62.4 us
    ppermute x11, starting transfers between devices, swapped(): inner = lax.ppermute(block, axis, [(i, i ^ 1) for i in range(count)])  49.6 us
    pallas_call x15, Pallas kernels, run(): pl.pallas_call(body, out_shape=[pltpu.VMEM(s, d) if i in pinned else jax....  26.1 us
    ppermute x11, waiting for transfers between devices, swapped(): lax.ppermute(block, axis, [(i, (i - 1 if i % 2 == 0 else i + 1) % count)...  21.5 us
    all_to_all x2, blocking collectives, shards(): parts = lax.all_to_all(parts, 'tele', 0, 0, tiled=True)  14.1 us
    ppermute x4, starting transfers between devices, along(): lax.ppermute(block, 'tele', [(i, (i + distance) % tele_size) for i in ran...  13.9 us
  transfers between devices with their start and end apart: 26, of which 11 were waited for; matrix products, arithmetic and copies ran while one was open for 0% of the time, Pallas kernels for 6%

profile of v4, /device:TPU:1, one launch (start us, length us, event | category | flops | bytes accessed | tf_op | source)
XLA Modules:
  0.0 188.5 jit_solution(653691680738913456)
XLA Ops:
  0.0 4.1 %collective-permute-start = (bf16[2,320,320]{2,1,0:T(8,128)(2,1)}, bf16[2,320,320]{2,1,0:T(8,128)(2,1)S(1)}, u32[]{:S(2)}, u32[]{:S(2)}) collective-permute-start(bf16[2,320,320]{2,1,0:T(8,128)(2,1)} %refs_7_.7), channel_id=1, source_target_pairs={{0,1},{1,2},{2,3},{3,0},{4,5},{5,6},{6,7},{7,4},{8,9},{9,10},{10,1... | collective-permute-start | bytes 1228808 | tf_op jit(solution)/shard_map/ppermute | solution.py:261
  4.1 3.2 %collective-permute-start.1 = (bf16[2,320,320]{2,1,0:T(8,128)(2,1)}, bf16[2,320,320]{2,1,0:T(8,128)(2,1)S(1)}, u32[]{:S(2)}, u32[]{:S(2)}) collective-permute-start(bf16[2,320,320]{2,1,0:T(8,128)(2,1)} %refs_7_.7), channel_id=1, source_target_pairs={{0,3},{1,0},{2,1},{3,2},{4,7},{5,4},{6,5},{7,6},{8,11},{9,8},{10,9... | collective-permute-start | bytes 1228808 | tf_op jit(solution)/shard_map/ppermute | solution.py:261
  7.3 5.7 %shard_map.100 = (bf16[16,320]{1,0:T(8,128)(2,1)S(1)}, s32[16,12]{1,0:T(8,128)S(1)}, f32[4,8,64]{2,1,0:T(8,128)S(1)}, bf16[3072,128]{1,0:T(8,128)(2,1)S(1)}, bf16[16,320,320]{2,1,0:T(8,128)(2,1)S(1)}) custom-call(f32[16,320]{1,0:T(8,128)} %refs_6_.11, s32[6,16]{1,0:T(8,128)} %bitcast.7, s32[6,16]{1,0:T(8,128)} %bitcast.8, s32[2,6]{1,0:T(2,128)} %refs_3_.1, ...), custom_call_target="tpu_custom_call" | custom-call | flops 268435456 | bytes 3605344 | tf_op jit(solution)/shard_map/pallas_call | solution.py:230
  13.0 2.1 %collective-permute-start.2 = (bf16[16,320]{1,0:T(8,128)(2,1)S(1)}, bf16[16,320]{1,0:T(8,128)(2,1)S(1)}, u32[]{:S(2)}, u32[]{:S(2)}) collective-permute-start(bf16[16,320]{1,0:T(8,128)(2,1)S(1)} %get-tuple-element.27.refs_1_), channel_id=1, source_target_pairs={{0,1},{1,0},{2,3},{3,2},{4,5},{5,4},{6,7},{7,6},{8,9},{9,8},{10,11... | collective-permute-start | bytes 30728 | tf_op jit(solution)/shard_map/ppermute | solution.py:22
  15.1 8.1 %collective-permute-start.3 = (bf16[16,320]{1,0:T(8,128)(2,1)S(1)}, bf16[16,320]{1,0:T(8,128)(2,1)S(1)}, u32[]{:S(2)}, u32[]{:S(2)}) collective-permute-start(bf16[16,320]{1,0:T(8,128)(2,1)S(1)} %get-tuple-element.27.refs_1_), channel_id=1, source_target_pairs={{0,511},{1,2},{2,1},{3,4},{4,3},{5,6},{6,5},{7,8},{8,7},{9,10},{10... | collective-permute-start | bytes 30728 | tf_op jit(solution)/shard_map/ppermute | solution.py:21
  28.9 4.6 %collective-permute-start.9 = (bf16[1,320,320]{2,1,0:T(8,128)(2,1)S(1)}, bf16[1,320,320]{2,1,0:T(8,128)(2,1)S(1)}, u32[]{:S(2)}, u32[]{:S(2)}) collective-permute-start(bf16[1,320,320]{2,1,0:T(8,128)(2,1)S(1)} %get-tuple-element.38), channel_id=1, source_target_pairs={{0,3},{1,0},{2,1},{3,2},{4,7},{5,4},{6,5},{7,6},{8,11},{9,8},{10,9... | collective-permute-start | bytes 614408 | tf_op jit(solution)/shard_map/ppermute | solution.py:261
  35.4 9.6 %collective-permute-start.5 = (bf16[16,320]{1,0:T(8,128)(2,1)S(1)}, bf16[16,320]{1,0:T(8,128)(2,1)S(1)}, u32[]{:S(2)}, u32[]{:S(2)}) collective-permute-start(bf16[16,320]{1,0:T(8,128)(2,1)S(1)} %shard_map.101.refs_1_), channel_id=1, source_target_pairs={{0,511},{1,2},{2,1},{3,4},{4,3},{5,6},{6,5},{7,8},{8,7},{9,10},{10... | collective-permute-start | bytes 30728 | tf_op jit(solution)/shard_map/ppermute | solution.py:21
  50.4 6.8 %collective-permute-start.7 = (bf16[16,320]{1,0:T(8,128)(2,1)S(1)}, bf16[16,320]{1,0:T(8,128)(2,1)S(1)}, u32[]{:S(2)}, u32[]{:S(2)}) collective-permute-start(bf16[16,320]{1,0:T(8,128)(2,1)S(1)} %get-tuple-element.32.refs_1_), channel_id=1, source_target_pairs={{0,511},{1,2},{2,1},{3,4},{4,3},{5,6},{6,5},{7,8},{8,7},{9,10},{10... | collective-permute-start | bytes 30728 | tf_op jit(solution)/shard_map/ppermute | solution.py:21
  59.7 7.1 %all_to_all.10.refs_0_ = f32[4,8,384]{2,1,0:T(8,128)S(1)} all-to-all(f32[4,8,384]{2,1,0:T(8,128)S(1)} %shard_map.103), channel_id=1, replica_groups=mesh['fine'=128,'tele'=4] {'tele'}, dimensions={0} | all-to-all | bytes 98304 | tf_op jit(solution)/shard_map/all_to_all | solution.py:332
  67.4 12.6 %collective-permute-start.10 = (bf16[8,320]{1,0:T(8,128)(2,1)S(1)}, bf16[8,320]{1,0:T(8,128)(2,1)S(1)}, u32[]{:S(2)}, u32[]{:S(2)}) collective-permute-start(bf16[8,320]{1,0:T(8,128)(2,1)S(1)} %get-tuple-element.39.refs_1_), channel_id=1, source_target_pairs={{0,4},{4,0},{8,12},{12,8},{16,20},{20,16},{24,28},{28,24},{32,36},... | collective-permute-start | bytes 15368 | tf_op jit(solution)/shard_map/ppermute | solution.py:22
  81.9 3.0 %collective-permute-done.11.refs_2_ = bf16[8,320]{1,0:T(8,128)(2,1)S(1)} collective-permute-done((bf16[8,320]{1,0:T(8,128)(2,1)S(1)}, bf16[8,320]{1,0:T(8,128)(2,1)S(1)}, u32[]{:S(2)}, u32[]{:S(2)}) %collective-permute-start.11) | collective-permute-done | bytes 5152 | tf_op jit(solution)/shard_map/ppermute | solution.py:21
  86.4 5.3 %collective-permute-start.12 = (bf16[8,320]{1,0:T(8,128)(2,1)S(1)}, bf16[8,320]{1,0:T(8,128)(2,1)S(1)}, u32[]{:S(2)}, u32[]{:S(2)}) collective-permute-start(bf16[8,320]{1,0:T(8,128)(2,1)S(1)} %shard_map.106.refs_1_), channel_id=1, source_target_pairs={{0,4},{4,0},{8,12},{12,8},{16,20},{20,16},{24,28},{28,24},{32,36},... | collective-permute-start | bytes 15368 | tf_op jit(solution)/shard_map/ppermute | solution.py:22
  93.6 3.0 %collective-permute-done.13.refs_2_ = bf16[8,320]{1,0:T(8,128)(2,1)S(1)} collective-permute-done((bf16[8,320]{1,0:T(8,128)(2,1)S(1)}, bf16[8,320]{1,0:T(8,128)(2,1)S(1)}, u32[]{:S(2)}, u32[]{:S(2)}) %collective-permute-start.13) | collective-permute-done | bytes 5152 | tf_op jit(solution)/shard_map/ppermute | solution.py:21
  98.3 2.2 %collective-permute-start.14 = (bf16[16,320]{1,0:T(8,128)(2,1)S(1)}, bf16[16,320]{1,0:T(8,128)(2,1)S(1)}, u32[]{:S(2)}, u32[]{:S(2)}) collective-permute-start(bf16[16,320]{1,0:T(8,128)(2,1)S(1)} %shard_map.107.refs_1_), channel_id=1, source_target_pairs={{0,1},{1,0},{2,3},{3,2},{4,5},{5,4},{6,7},{7,6},{8,9},{9,8},{10,11... | collective-permute-start | bytes 30728 | tf_op jit(solution)/shard_map/ppermute | solution.py:22
  100.5 6.2 %collective-permute-start.15 = (bf16[16,320]{1,0:T(8,128)(2,1)S(1)}, bf16[16,320]{1,0:T(8,128)(2,1)S(1)}, u32[]{:S(2)}, u32[]{:S(2)}) collective-permute-start(bf16[16,320]{1,0:T(8,128)(2,1)S(1)} %shard_map.107.refs_1_), channel_id=1, source_target_pairs={{0,511},{1,2},{2,1},{3,4},{4,3},{5,6},{6,5},{7,8},{8,7},{9,10},{10... | collective-permute-start | bytes 30728 | tf_op jit(solution)/shard_map/ppermute | solution.py:21
  112.1 5.8 %collective-permute-start.17 = (bf16[16,320]{1,0:T(8,128)(2,1)S(1)}, bf16[16,320]{1,0:T(8,128)(2,1)S(1)}, u32[]{:S(2)}, u32[]{:S(2)}) collective-permute-start(bf16[16,320]{1,0:T(8,128)(2,1)S(1)} %shard_map.108.refs_1_), channel_id=1, source_target_pairs={{0,511},{1,2},{2,1},{3,4},{4,3},{5,6},{6,5},{7,8},{8,7},{9,10},{10... | collective-permute-start | bytes 30728 | tf_op jit(solution)/shard_map/ppermute | solution.py:21
  123.3 9.1 %collective-permute-start.19 = (bf16[16,320]{1,0:T(8,128)(2,1)S(1)}, bf16[16,320]{1,0:T(8,128)(2,1)S(1)}, u32[]{:S(2)}, u32[]{:S(2)}) collective-permute-start(bf16[16,320]{1,0:T(8,128)(2,1)S(1)} %shard_map.109.refs_1_), channel_id=1, source_target_pairs={{0,511},{1,2},{2,1},{3,4},{4,3},{5,6},{6,5},{7,8},{8,7},{9,10},{10... | collective-permute-start | bytes 30728 | tf_op jit(solution)/shard_map/ppermute | solution.py:21
  137.7 9.1 %collective-permute-start.21 = (bf16[16,320]{1,0:T(8,128)(2,1)S(1)}, bf16[16,320]{1,0:T(8,128)(2,1)S(1)}, u32[]{:S(2)}, u32[]{:S(2)}) collective-permute-start(bf16[16,320]{1,0:T(8,128)(2,1)S(1)} %get-tuple-element.43.refs_1_), channel_id=1, source_target_pairs={{0,511},{1,2},{2,1},{3,4},{4,3},{5,6},{6,5},{7,8},{8,7},{9,10},{10... | collective-permute-start | bytes 30728 | tf_op jit(solution)/shard_map/ppermute | solution.py:21
  149.3 7.1 %all_to_all.11.refs_0_ = f32[4,8,384]{2,1,0:T(8,128)S(1)} all-to-all(f32[4,8,384]{2,1,0:T(8,128)S(1)} %shard_map.111), channel_id=1, replica_groups=mesh['fine'=128,'tele'=4] {'tele'}, dimensions={0} | all-to-all | bytes 98304 | tf_op jit(solution)/shard_map/all_to_all | solution.py:332
  157.0 12.6 %collective-permute-start.22 = (bf16[8,320]{1,0:T(8,128)(2,1)S(1)}, bf16[8,320]{1,0:T(8,128)(2,1)S(1)}, u32[]{:S(2)}, u32[]{:S(2)}) collective-permute-start(bf16[8,320]{1,0:T(8,128)(2,1)S(1)} %get-tuple-element.45.refs_1_), channel_id=1, source_target_pairs={{0,4},{4,0},{8,12},{12,8},{16,20},{20,16},{24,28},{28,24},{32,36},... | collective-permute-start | bytes 15368 | tf_op jit(solution)/shard_map/ppermute | solution.py:22
  171.5 3.0 %collective-permute-done.23.refs_2_ = bf16[8,320]{1,0:T(8,128)(2,1)S(1)} collective-permute-done((bf16[8,320]{1,0:T(8,128)(2,1)S(1)}, bf16[8,320]{1,0:T(8,128)(2,1)S(1)}, u32[]{:S(2)}, u32[]{:S(2)}) %collective-permute-start.23) | collective-permute-done | bytes 5152 | tf_op jit(solution)/shard_map/ppermute | solution.py:21
  176.0 5.3 %collective-permute-start.24 = (bf16[8,320]{1,0:T(8,128)(2,1)S(1)}, bf16[8,320]{1,0:T(8,128)(2,1)S(1)}, u32[]{:S(2)}, u32[]{:S(2)}) collective-permute-start(bf16[8,320]{1,0:T(8,128)(2,1)S(1)} %shard_map.113.refs_1_), channel_id=1, source_target_pairs={{0,4},{4,0},{8,12},{12,8},{16,20},{20,16},{24,28},{28,24},{32,36},... | collective-permute-start | bytes 15368 | tf_op jit(solution)/shard_map/ppermute | solution.py:22
  183.2 3.0 %collective-permute-done.25.refs_2_ = bf16[8,320]{1,0:T(8,128)(2,1)S(1)} collective-permute-done((bf16[8,320]{1,0:T(8,128)(2,1)S(1)}, bf16[8,320]{1,0:T(8,128)(2,1)S(1)}, u32[]{:S(2)}, u32[]{:S(2)}) %collective-permute-start.25) | collective-permute-done | bytes 5152 | tf_op jit(solution)/shard_map/ppermute | solution.py:21
  186.2 2.3 %shard_map.114 = f32[16,320]{1,0:T(8,128)} custom-call(bf16[8,320]{1,0:T(8,128)(2,1)S(1)} %collective-permute-done.24.refs_0_, bf16[8,320]{1,0:T(8,128)(2,1)S(1)} %shard_map.113.refs_1_, bf16[8,320]{1,0:T(8,128)(2,1)S(1)} %collective-permute-done.25.refs_2_, s32[8,64]{1,0:T(8,128)S(1)} %get-tuple-element.46.refs_3_, ...), custom_call_target="tpu_custom_call" | custom-call | flops 268435456 | bytes 2964544 | tf_op jit(solution)/shard_map/pallas_call | solution.py:230
  (53 shorter events, 47.1 us)
Async XLA Ops:
  0.0 26.7 %collective-permute-start = (bf16[2,320,320]{2,1,0:T(8,128)(2,1)}, bf16[2,320,320]{2,1,0:T(8,128)(2,1)S(1)}, u32[]{:S(2)}, u32[]{:S(2)}) collective-permute-start(bf16[2,320,320]{2,1,0:T(8,128)(2,1)} %refs_7_.7), channel_id=1, source_target_pairs={{0,1},{1,2},{2,3},{3,0},{4,5},{5,6},{6,7},{7,4},{8,9},{9,10},{10,1... | collective-permute-start | bytes 1228808 | tf_op jit(solution)/shard_map/ppermute | solution.py:261
  4.1 22.7 %collective-permute-start.1 = (bf16[2,320,320]{2,1,0:T(8,128)(2,1)}, bf16[2,320,320]{2,1,0:T(8,128)(2,1)S(1)}, u32[]{:S(2)}, u32[]{:S(2)}) collective-permute-start(bf16[2,320,320]{2,1,0:T(8,128)(2,1)} %refs_7_.7), channel_id=1, source_target_pairs={{0,3},{1,0},{2,1},{3,2},{4,7},{5,4},{6,5},{7,6},{8,11},{9,8},{10,9... | collective-permute-start | bytes 1228808 | tf_op jit(solution)/shard_map/ppermute | solution.py:261
  13.0 10.3 %collective-permute-start.2 = (bf16[16,320]{1,0:T(8,128)(2,1)S(1)}, bf16[16,320]{1,0:T(8,128)(2,1)S(1)}, u32[]{:S(2)}, u32[]{:S(2)}) collective-permute-start(bf16[16,320]{1,0:T(8,128)(2,1)S(1)} %get-tuple-element.27.refs_1_), channel_id=1, source_target_pairs={{0,1},{1,0},{2,3},{3,2},{4,5},{5,4},{6,7},{7,6},{8,9},{9,8},{10,11... | collective-permute-start | bytes 30728 | tf_op jit(solution)/shard_map/ppermute | solution.py:22
  15.1 9.5 %collective-permute-start.3 = (bf16[16,320]{1,0:T(8,128)(2,1)S(1)}, bf16[16,320]{1,0:T(8,128)(2,1)S(1)}, u32[]{:S(2)}, u32[]{:S(2)}) collective-permute-start(bf16[16,320]{1,0:T(8,128)(2,1)S(1)} %get-tuple-element.27.refs_1_), channel_id=1, source_target_pairs={{0,511},{1,2},{2,1},{3,4},{4,3},{5,6},{6,5},{7,8},{8,7},{9,10},{10... | collective-permute-start | bytes 30728 | tf_op jit(solution)/shard_map/ppermute | solution.py:21
  26.8 39.9 %collective-permute-start.8 = (bf16[1,320,320]{2,1,0:T(8,128)(2,1)S(1)}, bf16[1,320,320]{2,1,0:T(8,128)(2,1)S(1)}, u32[]{:S(2)}, u32[]{:S(2)}) collective-permute-start(bf16[1,320,320]{2,1,0:T(8,128)(2,1)S(1)} %get-tuple-element.37), channel_id=1, source_target_pairs={{0,1},{1,2},{2,3},{3,0},{4,5},{5,6},{6,7},{7,4},{8,9},{9,10},{10,1... | collective-permute-start | bytes 614408 | tf_op jit(solution)/shard_map/ppermute | solution.py:261
  28.9 37.9 %collective-permute-start.9 = (bf16[1,320,320]{2,1,0:T(8,128)(2,1)S(1)}, bf16[1,320,320]{2,1,0:T(8,128)(2,1)S(1)}, u32[]{:S(2)}, u32[]{:S(2)}) collective-permute-start(bf16[1,320,320]{2,1,0:T(8,128)(2,1)S(1)} %get-tuple-element.38), channel_id=1, source_target_pairs={{0,3},{1,0},{2,1},{3,2},{4,7},{5,4},{6,5},{7,6},{8,11},{9,8},{10,9... | collective-permute-start | bytes 614408 | tf_op jit(solution)/shard_map/ppermute | solution.py:261
  33.5 11.6 %collective-permute-start.4 = (bf16[16,320]{1,0:T(8,128)(2,1)S(1)}, bf16[16,320]{1,0:T(8,128)(2,1)S(1)}, u32[]{:S(2)}, u32[]{:S(2)}) collective-permute-start(bf16[16,320]{1,0:T(8,128)(2,1)S(1)} %shard_map.101.refs_1_), channel_id=1, source_target_pairs={{0,1},{1,0},{2,3},{3,2},{4,5},{5,4},{6,7},{7,6},{8,9},{9,8},{10,11... | collective-permute-start | bytes 30728 | tf_op jit(solution)/shard_map/ppermute | solution.py:22
  35.4 11.0 %collective-permute-start.5 = (bf16[16,320]{1,0:T(8,128)(2,1)S(1)}, bf16[16,320]{1,0:T(8,128)(2,1)S(1)}, u32[]{:S(2)}, u32[]{:S(2)}) collective-permute-start(bf16[16,320]{1,0:T(8,128)(2,1)S(1)} %shard_map.101.refs_1_), channel_id=1, source_target_pairs={{0,511},{1,2},{2,1},{3,4},{4,3},{5,6},{6,5},{7,8},{8,7},{9,10},{10... | collective-permute-start | bytes 30728 | tf_op jit(solution)/shard_map/ppermute | solution.py:21
  48.5 8.8 %collective-permute-start.6 = (bf16[16,320]{1,0:T(8,128)(2,1)S(1)}, bf16[16,320]{1,0:T(8,128)(2,1)S(1)}, u32[]{:S(2)}, u32[]{:S(2)}) collective-permute-start(bf16[16,320]{1,0:T(8,128)(2,1)S(1)} %get-tuple-element.32.refs_1_), channel_id=1, source_target_pairs={{0,1},{1,0},{2,3},{3,2},{4,5},{5,4},{6,7},{7,6},{8,9},{9,8},{10,11... | collective-permute-start | bytes 30728 | tf_op jit(solution)/shard_map/ppermute | solution.py:22
  50.4 8.2 %collective-permute-start.7 = (bf16[16,320]{1,0:T(8,128)(2,1)S(1)}, bf16[16,320]{1,0:T(8,128)(2,1)S(1)}, u32[]{:S(2)}, u32[]{:S(2)}) collective-permute-start(bf16[16,320]{1,0:T(8,128)(2,1)S(1)} %get-tuple-element.32.refs_1_), channel_id=1, source_target_pairs={{0,511},{1,2},{2,1},{3,4},{4,3},{5,6},{6,5},{7,8},{8,7},{9,10},{10... | collective-permute-start | bytes 30728 | tf_op jit(solution)/shard_map/ppermute | solution.py:21
  67.4 14.5 %collective-permute-start.10 = (bf16[8,320]{1,0:T(8,128)(2,1)S(1)}, bf16[8,320]{1,0:T(8,128)(2,1)S(1)}, u32[]{:S(2)}, u32[]{:S(2)}) collective-permute-start(bf16[8,320]{1,0:T(8,128)(2,1)S(1)} %get-tuple-element.39.refs_1_), channel_id=1, source_target_pairs={{0,4},{4,0},{8,12},{12,8},{16,20},{20,16},{24,28},{28,24},{32,36},... | collective-permute-start | bytes 15368 | tf_op jit(solution)/shard_map/ppermute | solution.py:22
  80.0 4.9 %collective-permute-start.11 = (bf16[8,320]{1,0:T(8,128)(2,1)S(1)}, bf16[8,320]{1,0:T(8,128)(2,1)S(1)}, u32[]{:S(2)}, u32[]{:S(2)}) collective-permute-start(bf16[8,320]{1,0:T(8,128)(2,1)S(1)} %get-tuple-element.39.refs_1_), channel_id=1, source_target_pairs={{0,508},{4,8},{8,4},{12,16},{16,12},{20,24},{24,20},{28,32},{32,28... | collective-permute-start | bytes 15368 | tf_op jit(solution)/shard_map/ppermute | solution.py:21
  86.4 7.2 %collective-permute-start.12 = (bf16[8,320]{1,0:T(8,128)(2,1)S(1)}, bf16[8,320]{1,0:T(8,128)(2,1)S(1)}, u32[]{:S(2)}, u32[]{:S(2)}) collective-permute-start(bf16[8,320]{1,0:T(8,128)(2,1)S(1)} %shard_map.106.refs_1_), channel_id=1, source_target_pairs={{0,4},{4,0},{8,12},{12,8},{16,20},{20,16},{24,28},{28,24},{32,36},... | collective-permute-start | bytes 15368 | tf_op jit(solution)/shard_map/ppermute | solution.py:22
  91.7 4.9 %collective-permute-start.13 = (bf16[8,320]{1,0:T(8,128)(2,1)S(1)}, bf16[8,320]{1,0:T(8,128)(2,1)S(1)}, u32[]{:S(2)}, u32[]{:S(2)}) collective-permute-start(bf16[8,320]{1,0:T(8,128)(2,1)S(1)} %shard_map.106.refs_1_), channel_id=1, source_target_pairs={{0,508},{4,8},{8,4},{12,16},{16,12},{20,24},{24,20},{28,32},{32,28... | collective-permute-start | bytes 15368 | tf_op jit(solution)/shard_map/ppermute | solution.py:21
  98.3 8.4 %collective-permute-start.14 = (bf16[16,320]{1,0:T(8,128)(2,1)S(1)}, bf16[16,320]{1,0:T(8,128)(2,1)S(1)}, u32[]{:S(2)}, u32[]{:S(2)}) collective-permute-start(bf16[16,320]{1,0:T(8,128)(2,1)S(1)} %shard_map.107.refs_1_), channel_id=1, source_target_pairs={{0,1},{1,0},{2,3},{3,2},{4,5},{5,4},{6,7},{7,6},{8,9},{9,8},{10,11... | collective-permute-start | bytes 30728 | tf_op jit(solution)/shard_map/ppermute | solution.py:22
  100.5 7.5 %collective-permute-start.15 = (bf16[16,320]{1,0:T(8,128)(2,1)S(1)}, bf16[16,320]{1,0:T(8,128)(2,1)S(1)}, u32[]{:S(2)}, u32[]{:S(2)}) collective-permute-start(bf16[16,320]{1,0:T(8,128)(2,1)S(1)} %shard_map.107.refs_1_), channel_id=1, source_target_pairs={{0,511},{1,2},{2,1},{3,4},{4,3},{5,6},{6,5},{7,8},{8,7},{9,10},{10... | collective-permute-start | bytes 30728 | tf_op jit(solution)/shard_map/ppermute | solution.py:21
  110.1 7.8 %collective-permute-start.16 = (bf16[16,320]{1,0:T(8,128)(2,1)S(1)}, bf16[16,320]{1,0:T(8,128)(2,1)S(1)}, u32[]{:S(2)}, u32[]{:S(2)}) collective-permute-start(bf16[16,320]{1,0:T(8,128)(2,1)S(1)} %shard_map.108.refs_1_), channel_id=1, source_target_pairs={{0,1},{1,0},{2,3},{3,2},{4,5},{5,4},{6,7},{7,6},{8,9},{9,8},{10,11... | collective-permute-start | bytes 30728 | tf_op jit(solution)/shard_map/ppermute | solution.py:22
  112.1 7.2 %collective-permute-start.17 = (bf16[16,320]{1,0:T(8,128)(2,1)S(1)}, bf16[16,320]{1,0:T(8,128)(2,1)S(1)}, u32[]{:S(2)}, u32[]{:S(2)}) collective-permute-start(bf16[16,320]{1,0:T(8,128)(2,1)S(1)} %shard_map.108.refs_1_), channel_id=1, source_target_pairs={{0,511},{1,2},{2,1},{3,4},{4,3},{5,6},{6,5},{7,8},{8,7},{9,10},{10... | collective-permute-start | bytes 30728 | tf_op jit(solution)/shard_map/ppermute | solution.py:21
  121.3 11.0 %collective-permute-start.18 = (bf16[16,320]{1,0:T(8,128)(2,1)S(1)}, bf16[16,320]{1,0:T(8,128)(2,1)S(1)}, u32[]{:S(2)}, u32[]{:S(2)}) collective-permute-start(bf16[16,320]{1,0:T(8,128)(2,1)S(1)} %shard_map.109.refs_1_), channel_id=1, source_target_pairs={{0,1},{1,0},{2,3},{3,2},{4,5},{5,4},{6,7},{7,6},{8,9},{9,8},{10,11... | collective-permute-start | bytes 30728 | tf_op jit(solution)/shard_map/ppermute | solution.py:22
  123.3 10.4 %collective-permute-start.19 = (bf16[16,320]{1,0:T(8,128)(2,1)S(1)}, bf16[16,320]{1,0:T(8,128)(2,1)S(1)}, u32[]{:S(2)}, u32[]{:S(2)}) collective-permute-start(bf16[16,320]{1,0:T(8,128)(2,1)S(1)} %shard_map.109.refs_1_), channel_id=1, source_target_pairs={{0,511},{1,2},{2,1},{3,4},{4,3},{5,6},{6,5},{7,8},{8,7},{9,10},{10... | collective-permute-start | bytes 30728 | tf_op jit(solution)/shard_map/ppermute | solution.py:21
  135.8 11.0 %collective-permute-start.20 = (bf16[16,320]{1,0:T(8,128)(2,1)S(1)}, bf16[16,320]{1,0:T(8,128)(2,1)S(1)}, u32[]{:S(2)}, u32[]{:S(2)}) collective-permute-start(bf16[16,320]{1,0:T(8,128)(2,1)S(1)} %get-tuple-element.43.refs_1_), channel_id=1, source_target_pairs={{0,1},{1,0},{2,3},{3,2},{4,5},{5,4},{6,7},{7,6},{8,9},{9,8},{10,11... | collective-permute-start | bytes 30728 | tf_op jit(solution)/shard_map/ppermute | solution.py:22
  137.7 10.4 %collective-permute-start.21 = (bf16[16,320]{1,0:T(8,128)(2,1)S(1)}, bf16[16,320]{1,0:T(8,128)(2,1)S(1)}, u32[]{:S(2)}, u32[]{:S(2)}) collective-permute-start(bf16[16,320]{1,0:T(8,128)(2,1)S(1)} %get-tuple-element.43.refs_1_), channel_id=1, source_target_pairs={{0,511},{1,2},{2,1},{3,4},{4,3},{5,6},{6,5},{7,8},{8,7},{9,10},{10... | collective-permute-start | bytes 30728 | tf_op jit(solution)/shard_map/ppermute | solution.py:21
  157.0 14.5 %collective-permute-start.22 = (bf16[8,320]{1,0:T(8,128)(2,1)S(1)}, bf16[8,320]{1,0:T(8,128)(2,1)S(1)}, u32[]{:S(2)}, u32[]{:S(2)}) collective-permute-start(bf16[8,320]{1,0:T(8,128)(2,1)S(1)} %get-tuple-element.45.refs_1_), channel_id=1, source_target_pairs={{0,4},{4,0},{8,12},{12,8},{16,20},{20,16},{24,28},{28,24},{32,36},... | collective-permute-start | bytes 15368 | tf_op jit(solution)/shard_map/ppermute | solution.py:22
  176.0 7.2 %collective-permute-start.24 = (bf16[8,320]{1,0:T(8,128)(2,1)S(1)}, bf16[8,320]{1,0:T(8,128)(2,1)S(1)}, u32[]{:S(2)}, u32[]{:S(2)}) collective-permute-start(bf16[8,320]{1,0:T(8,128)(2,1)S(1)} %shard_map.113.refs_1_), channel_id=1, source_target_pairs={{0,4},{4,0},{8,12},{12,8},{16,20},{20,16},{24,28},{28,24},{32,36},... | collective-permute-start | bytes 15368 | tf_op jit(solution)/shard_map/ppermute | solution.py:22
  (6 other events, 131.1 us)

commit v5 on v4

--- a/solution.py
+++ b/solution.py
@@ -18,8 +18,8 @@
 
 def swapped(block, axis):
     count = lax.axis_size(axis)
+    inner = lax.ppermute(block, axis, [(i, i ^ 1) for i in range(count)])
     outer = lax.ppermute(block, axis, [(i, (i - 1 if i % 2 == 0 else i + 1) % count) for i in range(count)])
-    inner = lax.ppermute(block, axis, [(i, i ^ 1) for i in range(count)])
     return inner, outer
 
 
@@ -89,8 +89,8 @@
 
 def pool_rows(links, count, position, turn=0):
     shift = count.bit_length() - 1
-    owner, within = links >> shift, (links - turn) & (count - 1)
-    place = jnp.where(owner == position, 1, jnp.where(owner == (position ^ 1), 0, 2))
+    owner, within = links >> shift, (links & (count - 1)) ^ turn
+    place = jnp.where(owner == position, 1, jnp.where(owner == (position ^ 1), 2, 0))
     return jnp.where(links >= 0, place * count + within, -1)
 
 
@@ -99,9 +99,12 @@
     targets, (sems, block_sems) = refs[count + 5 : -2], refs[-2:]
     right_ref, links_ref, faces_ref, coarse_links_ref, coarse_faces_ref, operators_in_ref = targets
     whole = [pltpu.make_async_copy(sources[i], targets[i], sems.at[i]) for i in range(count - 1)]
+    step = inverse_ref.shape[0] // block_sems.shape[0]
     blocks = [
-        pltpu.make_async_copy(sources[-1].at[e], inverse_ref.at[e], block_sems.at[e])
-        for e in range(inverse_ref.shape[0])
+        pltpu.make_async_copy(
+            sources[-1].at[i * step : (i + 1) * step], inverse_ref.at[i * step : (i + 1) * step], block_sems.at[i]
+        )
+        for i in range(block_sems.shape[0])
     ]
     for copy in [whole[0], *blocks, *whole[1:]]:
         copy.start()
@@ -112,8 +115,9 @@
     lowered = right_ref[...].astype(jnp.bfloat16)
     row = lax.broadcasted_iota(jnp.int32, lowered.shape, 0)
     result = jnp.zeros(lowered.shape, jnp.float32)
-    for e, copy in enumerate(blocks):
-        copy.wait()
+    for e in range(inverse_ref.shape[0]):
+        if e % step == 0:
+            blocks[e // step].wait()
         product = lax.dot_general(
             lowered, inverse_ref[e], (((1,), (1,)), ((), ())), preferred_element_type=jnp.float32
         )
@@ -137,7 +141,7 @@
         for part, values in enumerate((rows, kinds)):
             placed = jnp.zeros(row.shape, jnp.float32)
             for c in range(own):
-                placed = jnp.where(row == ((own * (tele - t) + c) & (count - 1)), values[c : c + 1], placed)
+                placed = jnp.where(row == ((own * tele + c) ^ (own * t)), values[c : c + 1], placed)
             lists_ref[t, :, part * 6 : part * 6 + 6] = placed
 
     types, size, _ = operators_in_ref.shape
@@ -182,7 +186,7 @@
     tele_size, rows, dofs = out_ref.shape[0], out_ref.shape[1], residual.shape[1]
     shape = (tele_size * rows, residual.shape[0])
     row = lax.broadcasted_iota(jnp.int32, shape, 0)
-    element = (row + (row >> (rows.bit_length() - 1)) * (rows // tele_size)) & (rows - 1)
+    element = (row & (rows - 1)) ^ ((row >> (rows.bit_length() - 1)) * (rows // tele_size))
     member = jnp.where((target_ref[...] & (rows - 1)) == element, 1.0, 0.0).astype(jnp.bfloat16)
     partial = exact_dot(member, residual)
     for t in range(tele_size):
@@ -207,7 +211,7 @@
     target_ref, solution_ref, out_ref = refs[7 + blocks :]
     rows, fine = coarse.shape[0], solution_ref.shape[0]
     turn = lax.axis_index("tele") * (rows // lax.axis_size("tele"))
-    member = ((target_ref[...] - turn) & (rows - 1)) == lax.broadcasted_iota(jnp.int32, (rows, fine), 0)
+    member = ((target_ref[...] & (rows - 1)) ^ turn) == lax.broadcasted_iota(jnp.int32, (rows, fine), 0)
     added = exact_dot(jnp.where(member, 1.0, 0.0).T.astype(jnp.bfloat16), coarse)
     out_ref[...] = (solution_ref[...] + added).astype(out_ref.dtype)
 
@@ -257,10 +261,9 @@
     types = face_operators.shape[0]
     spare = -dofs % LANES
 
-    def along(block, distance):
-        return lax.ppermute(block, "tele", [(i, (i + distance) % tele_size) for i in range(tele_size)])
-
-    before, after = along(coarse_inverse, 1), along(coarse_inverse, -1)
+    def across(block, bits):
+        return lax.ppermute(block, "tele", [(i, i ^ bits) for i in range(tele_size)])
+
     lift = jnp.asarray(face_table(), bf16)
     target = agglomerate[None, :]
     operands = (
@@ -285,13 +288,15 @@
         hbm=range(len(operands)),
         pinned=(3, 4),
         scratch=[pltpu.VMEM(o.shape, o.dtype) for o in operands[:-1]]
-        + [pltpu.SemaphoreType.DMA((len(operands),)), pltpu.SemaphoreType.DMA((fine_rows,))],
+        + [pltpu.SemaphoreType.DMA((len(operands),)), pltpu.SemaphoreType.DMA((4,))],
     )
     shared = (operators, lift)
+    own, state = lax.optimization_barrier((coarse_inverse, state))
+    near, other = across(own, 1), across(own, tele_size - 1)
 
     def halo(block, axis):
         inner, outer = swapped(block, axis)
-        return inner, block, outer
+        return outer, block, inner
 
     both = ("fine", "tele")
     for cycle in range(CYCLES):
@@ -313,10 +318,10 @@
             )
             state = result[0]
             if cycle == 0 and sweep == 1:
-                before, after, state = lax.optimization_barrier((before, after, state))
-                far_low, far_high = run(take_kernel, [((1,) + before.shape[1:], bf16)] * 2, before, after)
-                far_low, far_high = along(far_low, 1), along(far_high, -1)
-                blocks = (coarse_inverse, after, far_low, far_high, before)
+                near, other, state = lax.optimization_barrier((near, other, state))
+                far_low, far_high = run(take_kernel, [((1,) + near.shape[1:], bf16)] * 2, other, near)
+                far_low, far_high = across(far_low, 1), across(far_high, tele_size - 1)
+                blocks = (coarse_inverse, near, far_low, far_high, other)
         solution, lowered = result[1], result[2]
         parts = run(
             restrict_kernel,

time: 190 us -> 171 us (0.900)
  starting transfers between devices: 126 us -> 111 us
  Pallas kernels: 26.1 us -> 23.8 us
    ppermute x11, waiting for transfers between devices: 0.03 us -> 15.8 us  [swapped(): inner = lax.ppermute(block, axis, [(i, i ^ 1) for i in range(count)])]
    ppermute x11, waiting for transfers between devices: 21.5 us -> 5.98 us  [swapped(): lax.ppermute(block, axis, [(i, (i - 1 if i % 2 == 0 else i + 1) % count)...]
    ppermute x11, starting transfers between devices: 62.4 us -> 49.7 us  [swapped(): lax.ppermute(block, axis, [(i, (i - 1 if i % 2 == 0 else i + 1) % count)...]
    ppermute x4, starting transfers between devices: 13.9 us -> 11.5 us  [across(): lax.ppermute(block, 'tele', [(i, i ^ bits) for i in range(tele_size)])]
    pallas_call x15, Pallas kernels: 26.1 us -> 23.8 us  [run(): pl.pallas_call(body, out_shape=[pltpu.VMEM(s, d) if i in pinned else jax....]
  transfers between devices with their start and end apart: 26 -> 26, of which waited for: 11 -> 14; matrix products, arithmetic and copies ran while one was open for 0% -> 0% of each run, Pallas kernels for 6% -> 3%
where the time goes in v5:
time: 171 us; the launch traced here: 170 us
  starting transfers between devices  111 us (65%)
  Pallas kernels  23.8 us (14%)
  waiting for transfers between devices  21.8 us (13%)
  blocking collectives  13.5 us (8%)
    ppermute x11, starting transfers between devices, swapped(): lax.ppermute(block, axis, [(i, (i - 1 if i % 2 == 0 else i + 1) % count)...  49.7 us
    ppermute x11, starting transfers between devices, swapped(): inner = lax.ppermute(block, axis, [(i, i ^ 1) for i in range(count)])  49.5 us
    pallas_call x15, Pallas kernels, run(): pl.pallas_call(body, out_shape=[pltpu.VMEM(s, d) if i in pinned else jax....  23.8 us
    ppermute x11, waiting for transfers between devices, swapped(): inner = lax.ppermute(block, axis, [(i, i ^ 1) for i in range(count)])  15.8 us
    all_to_all x2, blocking collectives, shards(): parts = lax.all_to_all(parts, 'tele', 0, 0, tiled=True)  13.5 us
    ppermute x4, starting transfers between devices, across(): lax.ppermute(block, 'tele', [(i, i ^ bits) for i in range(tele_size)])  11.5 us
    ppermute x11, waiting for transfers between devices, swapped(): lax.ppermute(block, axis, [(i, (i - 1 if i % 2 == 0 else i + 1) % count)...  5.98 us
  transfers between devices with their start and end apart: 26, of which 14 were waited for; matrix products, arithmetic and copies ran while one was open for 0% of the time, Pallas kernels for 3%

profile of v5, /device:TPU:1, one launch (start us, length us, event | category | flops | bytes accessed | tf_op | source)
XLA Modules:
  0.0 170.5 jit_solution(5897712890153199834)
XLA Ops:
  0.0 3.4 %shard_map.100 = (bf16[16,320]{1,0:T(8,128)(2,1)S(1)}, s32[16,12]{1,0:T(8,128)S(1)}, f32[4,8,64]{2,1,0:T(8,128)S(1)}, bf16[3072,128]{1,0:T(8,128)(2,1)S(1)}, bf16[16,320,320]{2,1,0:T(8,128)(2,1)S(1)}) custom-call(f32[16,320]{1,0:T(8,128)} %refs_6_.11, s32[6,16]{1,0:T(8,128)} %bitcast.7, s32[6,16]{1,0:T(8,128)} %bitcast.8, s32[2,6]{1,0:T(2,128)} %refs_3_.1, ...), custom_call_target="tpu_custom_call" | custom-call | flops 268435456 | bytes 3605344 | tf_op jit(solution)/shard_map/pallas_call | solution.py:234
  3.4 3.9 %collective-permute-start = (bf16[2,320,320]{2,1,0:T(8,128)(2,1)S(1)}, bf16[2,320,320]{2,1,0:T(8,128)(2,1)S(1)}, u32[]{:S(2)}, u32[]{:S(2)}) collective-permute-start(bf16[2,320,320]{2,1,0:T(8,128)(2,1)S(1)} %copy-done.1), channel_id=1, source_target_pairs={{0,1},{1,0},{2,3},{3,2},{4,5},{5,4},{6,7},{7,6},{8,9},{9,8},{10,11... | collective-permute-start | bytes 1228808 | tf_op jit(solution)/shard_map/ppermute | solution.py:265
  7.4 3.7 %collective-permute-start.1 = (bf16[2,320,320]{2,1,0:T(8,128)(2,1)S(1)}, bf16[2,320,320]{2,1,0:T(8,128)(2,1)S(1)}, u32[]{:S(2)}, u32[]{:S(2)}) collective-permute-start(bf16[2,320,320]{2,1,0:T(8,128)(2,1)S(1)} %copy-done.1), channel_id=1, source_target_pairs={{0,3},{1,2},{2,1},{3,0},{4,7},{5,6},{6,5},{7,4},{8,11},{9,10},{10,... | collective-permute-start | bytes 1228808 | tf_op jit(solution)/shard_map/ppermute | solution.py:265
  11.1 7.8 %collective-permute-start.2 = (bf16[16,320]{1,0:T(8,128)(2,1)S(1)}, bf16[16,320]{1,0:T(8,128)(2,1)S(1)}, u32[]{:S(2)}, u32[]{:S(2)}) collective-permute-start(bf16[16,320]{1,0:T(8,128)(2,1)S(1)} %get-tuple-element.31.refs_1_), channel_id=1, source_target_pairs={{0,511},{1,2},{2,1},{3,4},{4,3},{5,6},{6,5},{7,8},{8,7},{9,10},{10... | collective-permute-start | bytes 30728 | tf_op jit(solution)/shard_map/ppermute | solution.py:22
  20.8 2.9 %collective-permute-done.2.refs_0_ = bf16[16,320]{1,0:T(8,128)(2,1)S(1)} collective-permute-done((bf16[16,320]{1,0:T(8,128)(2,1)S(1)}, bf16[16,320]{1,0:T(8,128)(2,1)S(1)}, u32[]{:S(2)}, u32[]{:S(2)}) %collective-permute-start.2) | collective-permute-done | bytes 10272 | tf_op jit(solution)/shard_map/ppermute | solution.py:22
  23.8 2.0 %shard_map.101.refs_1_ = bf16[16,320]{1,0:T(8,128)(2,1)S(1)} custom-call(bf16[16,320]{1,0:T(8,128)(2,1)S(1)} %collective-permute-done.2.refs_0_, bf16[16,320]{1,0:T(8,128)(2,1)S(1)} %get-tuple-element.31.refs_1_, bf16[16,320]{1,0:T(8,128)(2,1)S(1)} %collective-permute-done.3.refs_2_, s32[16,12]{1,0:T(8,128)S(1)} %get-tuple-element.32.refs_3_, ...), custom_call_target="tpu_custom_call" | custom-call | flops 268435456 | bytes 4606720 | tf_op jit(solution)/shard_map/pallas_call | solution.py:234
  29.8 12.4 %collective-permute-start.4 = (bf16[16,320]{1,0:T(8,128)(2,1)S(1)}, bf16[16,320]{1,0:T(8,128)(2,1)S(1)}, u32[]{:S(2)}, u32[]{:S(2)}) collective-permute-start(bf16[16,320]{1,0:T(8,128)(2,1)S(1)} %shard_map.101.refs_1_), channel_id=1, source_target_pairs={{0,511},{1,2},{2,1},{3,4},{4,3},{5,6},{6,5},{7,8},{8,7},{9,10},{10... | collective-permute-start | bytes 30728 | tf_op jit(solution)/shard_map/ppermute | solution.py:22
  44.4 2.5 %collective-permute-done.5.refs_2_ = bf16[16,320]{1,0:T(8,128)(2,1)S(1)} collective-permute-done((bf16[16,320]{1,0:T(8,128)(2,1)S(1)}, bf16[16,320]{1,0:T(8,128)(2,1)S(1)}, u32[]{:S(2)}, u32[]{:S(2)}) %collective-permute-start.5) | collective-permute-done | bytes 10272 | tf_op jit(solution)/shard_map/ppermute | solution.py:21
  49.0 2.8 %collective-permute-start.6 = (bf16[16,320]{1,0:T(8,128)(2,1)S(1)}, bf16[16,320]{1,0:T(8,128)(2,1)S(1)}, u32[]{:S(2)}, u32[]{:S(2)}) collective-permute-start(bf16[16,320]{1,0:T(8,128)(2,1)S(1)} %get-tuple-element.36.refs_1_), channel_id=1, source_target_pairs={{0,511},{1,2},{2,1},{3,4},{4,3},{5,6},{6,5},{7,8},{8,7},{9,10},{10... | collective-permute-start | bytes 30728 | tf_op jit(solution)/shard_map/ppermute | solution.py:22
  57.3 6.8 %all_to_all.10.refs_0_ = f32[4,8,384]{2,1,0:T(8,128)S(1)} all-to-all(f32[4,8,384]{2,1,0:T(8,128)S(1)} %shard_map.103), channel_id=1, replica_groups=mesh['fine'=128,'tele'=4] {'tele'}, dimensions={0} | all-to-all | bytes 98304 | tf_op jit(solution)/shard_map/all_to_all | solution.py:337
  66.7 12.1 %collective-permute-start.11 = (bf16[8,320]{1,0:T(8,128)(2,1)S(1)}, bf16[8,320]{1,0:T(8,128)(2,1)S(1)}, u32[]{:S(2)}, u32[]{:S(2)}) collective-permute-start(bf16[8,320]{1,0:T(8,128)(2,1)S(1)} %get-tuple-element.43.refs_1_), channel_id=1, source_target_pairs={{0,4},{4,0},{8,12},{12,8},{16,20},{20,16},{24,28},{28,24},{32,36},... | collective-permute-start | bytes 15368 | tf_op jit(solution)/shard_map/ppermute | solution.py:21
  83.1 6.5 %collective-permute-start.13 = (bf16[8,320]{1,0:T(8,128)(2,1)S(1)}, bf16[8,320]{1,0:T(8,128)(2,1)S(1)}, u32[]{:S(2)}, u32[]{:S(2)}) collective-permute-start(bf16[8,320]{1,0:T(8,128)(2,1)S(1)} %shard_map.106.refs_1_), channel_id=1, source_target_pairs={{0,4},{4,0},{8,12},{12,8},{16,20},{20,16},{24,28},{28,24},{32,36},... | collective-permute-start | bytes 15368 | tf_op jit(solution)/shard_map/ppermute | solution.py:21
  92.0 4.6 %collective-permute-start.14 = (bf16[16,320]{1,0:T(8,128)(2,1)S(1)}, bf16[16,320]{1,0:T(8,128)(2,1)S(1)}, u32[]{:S(2)}, u32[]{:S(2)}) collective-permute-start(bf16[16,320]{1,0:T(8,128)(2,1)S(1)} %shard_map.107.refs_1_), channel_id=1, source_target_pairs={{0,511},{1,2},{2,1},{3,4},{4,3},{5,6},{6,5},{7,8},{8,7},{9,10},{10... | collective-permute-start | bytes 30728 | tf_op jit(solution)/shard_map/ppermute | solution.py:22
  98.5 2.8 %collective-permute-done.15.refs_2_ = bf16[16,320]{1,0:T(8,128)(2,1)S(1)} collective-permute-done((bf16[16,320]{1,0:T(8,128)(2,1)S(1)}, bf16[16,320]{1,0:T(8,128)(2,1)S(1)}, u32[]{:S(2)}, u32[]{:S(2)}) %collective-permute-start.15) | collective-permute-done | bytes 10272 | tf_op jit(solution)/shard_map/ppermute | solution.py:21
  101.3 2.0 %shard_map.108.refs_1_ = bf16[16,320]{1,0:T(8,128)(2,1)S(1)} custom-call(bf16[16,320]{1,0:T(8,128)(2,1)S(1)} %collective-permute-done.14.refs_0_, bf16[16,320]{1,0:T(8,128)(2,1)S(1)} %shard_map.107.refs_1_, bf16[16,320]{1,0:T(8,128)(2,1)S(1)} %collective-permute-done.15.refs_2_, s32[16,12]{1,0:T(8,128)S(1)} %get-tuple-element.32.refs_3_, ...), custom_call_target="tpu_custom_call" | custom-call | flops 268435456 | bytes 4606720 | tf_op jit(solution)/shard_map/pallas_call | solution.py:234
  103.4 3.1 %collective-permute-start.16 = (bf16[16,320]{1,0:T(8,128)(2,1)S(1)}, bf16[16,320]{1,0:T(8,128)(2,1)S(1)}, u32[]{:S(2)}, u32[]{:S(2)}) collective-permute-start(bf16[16,320]{1,0:T(8,128)(2,1)S(1)} %shard_map.108.refs_1_), channel_id=1, source_target_pairs={{0,511},{1,2},{2,1},{3,4},{4,3},{5,6},{6,5},{7,8},{8,7},{9,10},{10... | collective-permute-start | bytes 30728 | tf_op jit(solution)/shard_map/ppermute | solution.py:22
  113.0 4.9 %collective-permute-start.18 = (bf16[16,320]{1,0:T(8,128)(2,1)S(1)}, bf16[16,320]{1,0:T(8,128)(2,1)S(1)}, u32[]{:S(2)}, u32[]{:S(2)}) collective-permute-start(bf16[16,320]{1,0:T(8,128)(2,1)S(1)} %shard_map.109.refs_1_), channel_id=1, source_target_pairs={{0,511},{1,2},{2,1},{3,4},{4,3},{5,6},{6,5},{7,8},{8,7},{9,10},{10... | collective-permute-start | bytes 30728 | tf_op jit(solution)/shard_map/ppermute | solution.py:22
  119.8 2.5 %collective-permute-done.19.refs_2_ = bf16[16,320]{1,0:T(8,128)(2,1)S(1)} collective-permute-done((bf16[16,320]{1,0:T(8,128)(2,1)S(1)}, bf16[16,320]{1,0:T(8,128)(2,1)S(1)}, u32[]{:S(2)}, u32[]{:S(2)}) %collective-permute-start.19) | collective-permute-done | bytes 10272 | tf_op jit(solution)/shard_map/ppermute | solution.py:21
  124.4 6.5 %collective-permute-start.20 = (bf16[16,320]{1,0:T(8,128)(2,1)S(1)}, bf16[16,320]{1,0:T(8,128)(2,1)S(1)}, u32[]{:S(2)}, u32[]{:S(2)}) collective-permute-start(bf16[16,320]{1,0:T(8,128)(2,1)S(1)} %get-tuple-element.47.refs_1_), channel_id=1, source_target_pairs={{0,511},{1,2},{2,1},{3,4},{4,3},{5,6},{6,5},{7,8},{8,7},{9,10},{10... | collective-permute-start | bytes 30728 | tf_op jit(solution)/shard_map/ppermute | solution.py:22
  132.8 2.5 %collective-permute-done.21.refs_2_ = bf16[16,320]{1,0:T(8,128)(2,1)S(1)} collective-permute-done((bf16[16,320]{1,0:T(8,128)(2,1)S(1)}, bf16[16,320]{1,0:T(8,128)(2,1)S(1)}, u32[]{:S(2)}, u32[]{:S(2)}) %collective-permute-start.21) | collective-permute-done | bytes 10272 | tf_op jit(solution)/shard_map/ppermute | solution.py:21
  136.4 6.8 %all_to_all.11.refs_0_ = f32[4,8,384]{2,1,0:T(8,128)S(1)} all-to-all(f32[4,8,384]{2,1,0:T(8,128)S(1)} %shard_map.111), channel_id=1, replica_groups=mesh['fine'=128,'tele'=4] {'tele'}, dimensions={0} | all-to-all | bytes 98304 | tf_op jit(solution)/shard_map/all_to_all | solution.py:337
  145.8 11.0 %collective-permute-start.23 = (bf16[8,320]{1,0:T(8,128)(2,1)S(1)}, bf16[8,320]{1,0:T(8,128)(2,1)S(1)}, u32[]{:S(2)}, u32[]{:S(2)}) collective-permute-start(bf16[8,320]{1,0:T(8,128)(2,1)S(1)} %get-tuple-element.49.refs_1_), channel_id=1, source_target_pairs={{0,4},{4,0},{8,12},{12,8},{16,20},{20,16},{24,28},{28,24},{32,36},... | collective-permute-start | bytes 15368 | tf_op jit(solution)/shard_map/ppermute | solution.py:21
  161.1 6.4 %collective-permute-start.25 = (bf16[8,320]{1,0:T(8,128)(2,1)S(1)}, bf16[8,320]{1,0:T(8,128)(2,1)S(1)}, u32[]{:S(2)}, u32[]{:S(2)}) collective-permute-start(bf16[8,320]{1,0:T(8,128)(2,1)S(1)} %shard_map.113.refs_1_), channel_id=1, source_target_pairs={{0,4},{4,0},{8,12},{12,8},{16,20},{20,16},{24,28},{28,24},{32,36},... | collective-permute-start | bytes 15368 | tf_op jit(solution)/shard_map/ppermute | solution.py:21
  168.2 2.3 %shard_map.114 = f32[16,320]{1,0:T(8,128)} custom-call(bf16[8,320]{1,0:T(8,128)(2,1)S(1)} %collective-permute-done.24.refs_0_, bf16[8,320]{1,0:T(8,128)(2,1)S(1)} %shard_map.113.refs_1_, bf16[8,320]{1,0:T(8,128)(2,1)S(1)} %collective-permute-done.25.refs_2_, s32[8,64]{1,0:T(8,128)S(1)} %get-tuple-element.50.refs_3_, ...), custom_call_target="tpu_custom_call" | custom-call | flops 268435456 | bytes 2964544 | tf_op jit(solution)/shard_map/pallas_call | solution.py:234
  (53 shorter events, 47.7 us)
Async XLA Ops:
  3.4 22.4 %collective-permute-start = (bf16[2,320,320]{2,1,0:T(8,128)(2,1)S(1)}, bf16[2,320,320]{2,1,0:T(8,128)(2,1)S(1)}, u32[]{:S(2)}, u32[]{:S(2)}) collective-permute-start(bf16[2,320,320]{2,1,0:T(8,128)(2,1)S(1)} %copy-done.1), channel_id=1, source_target_pairs={{0,1},{1,0},{2,3},{3,2},{4,5},{5,4},{6,7},{7,6},{8,9},{9,8},{10,11... | collective-permute-start | bytes 1228808 | tf_op jit(solution)/shard_map/ppermute | solution.py:265
  7.4 18.5 %collective-permute-start.1 = (bf16[2,320,320]{2,1,0:T(8,128)(2,1)S(1)}, bf16[2,320,320]{2,1,0:T(8,128)(2,1)S(1)}, u32[]{:S(2)}, u32[]{:S(2)}) collective-permute-start(bf16[2,320,320]{2,1,0:T(8,128)(2,1)S(1)} %copy-done.1), channel_id=1, source_target_pairs={{0,3},{1,2},{2,1},{3,0},{4,7},{5,6},{6,5},{7,4},{8,11},{9,10},{10,... | collective-permute-start | bytes 1228808 | tf_op jit(solution)/shard_map/ppermute | solution.py:265
  11.1 12.6 %collective-permute-start.2 = (bf16[16,320]{1,0:T(8,128)(2,1)S(1)}, bf16[16,320]{1,0:T(8,128)(2,1)S(1)}, u32[]{:S(2)}, u32[]{:S(2)}) collective-permute-start(bf16[16,320]{1,0:T(8,128)(2,1)S(1)} %get-tuple-element.31.refs_1_), channel_id=1, source_target_pairs={{0,511},{1,2},{2,1},{3,4},{4,3},{5,6},{6,5},{7,8},{8,7},{9,10},{10... | collective-permute-start | bytes 30728 | tf_op jit(solution)/shard_map/ppermute | solution.py:22
  18.9 4.9 %collective-permute-start.3 = (bf16[16,320]{1,0:T(8,128)(2,1)S(1)}, bf16[16,320]{1,0:T(8,128)(2,1)S(1)}, u32[]{:S(2)}, u32[]{:S(2)}) collective-permute-start(bf16[16,320]{1,0:T(8,128)(2,1)S(1)} %get-tuple-element.31.refs_1_), channel_id=1, source_target_pairs={{0,1},{1,0},{2,3},{3,2},{4,5},{5,4},{6,7},{7,6},{8,9},{9,8},{10,11... | collective-permute-start | bytes 30728 | tf_op jit(solution)/shard_map/ppermute | solution.py:21
  26.0 38.1 %collective-permute-start.8 = (bf16[1,320,320]{2,1,0:T(8,128)(2,1)S(1)}, bf16[1,320,320]{2,1,0:T(8,128)(2,1)S(1)}, u32[]{:S(2)}, u32[]{:S(2)}) collective-permute-start(bf16[1,320,320]{2,1,0:T(8,128)(2,1)S(1)} %get-tuple-element.41), channel_id=1, source_target_pairs={{0,1},{1,0},{2,3},{3,2},{4,5},{5,4},{6,7},{7,6},{8,9},{9,8},{10,11... | collective-permute-start | bytes 614408 | tf_op jit(solution)/shard_map/ppermute | solution.py:265
  27.9 36.2 %collective-permute-start.9 = (bf16[1,320,320]{2,1,0:T(8,128)(2,1)S(1)}, bf16[1,320,320]{2,1,0:T(8,128)(2,1)S(1)}, u32[]{:S(2)}, u32[]{:S(2)}) collective-permute-start(bf16[1,320,320]{2,1,0:T(8,128)(2,1)S(1)} %get-tuple-element.42), channel_id=1, source_target_pairs={{0,3},{1,2},{2,1},{3,0},{4,7},{5,6},{6,5},{7,4},{8,11},{9,10},{10,... | collective-permute-start | bytes 614408 | tf_op jit(solution)/shard_map/ppermute | solution.py:265
  29.8 14.6 %collective-permute-start.4 = (bf16[16,320]{1,0:T(8,128)(2,1)S(1)}, bf16[16,320]{1,0:T(8,128)(2,1)S(1)}, u32[]{:S(2)}, u32[]{:S(2)}) collective-permute-start(bf16[16,320]{1,0:T(8,128)(2,1)S(1)} %shard_map.101.refs_1_), channel_id=1, source_target_pairs={{0,511},{1,2},{2,1},{3,4},{4,3},{5,6},{6,5},{7,8},{8,7},{9,10},{10... | collective-permute-start | bytes 30728 | tf_op jit(solution)/shard_map/ppermute | solution.py:22
  42.2 4.7 %collective-permute-start.5 = (bf16[16,320]{1,0:T(8,128)(2,1)S(1)}, bf16[16,320]{1,0:T(8,128)(2,1)S(1)}, u32[]{:S(2)}, u32[]{:S(2)}) collective-permute-start(bf16[16,320]{1,0:T(8,128)(2,1)S(1)} %shard_map.101.refs_1_), channel_id=1, source_target_pairs={{0,1},{1,0},{2,3},{3,2},{4,5},{5,4},{6,7},{7,6},{8,9},{9,8},{10,11... | collective-permute-start | bytes 30728 | tf_op jit(solution)/shard_map/ppermute | solution.py:21
  49.0 6.2 %collective-permute-start.6 = (bf16[16,320]{1,0:T(8,128)(2,1)S(1)}, bf16[16,320]{1,0:T(8,128)(2,1)S(1)}, u32[]{:S(2)}, u32[]{:S(2)}) collective-permute-start(bf16[16,320]{1,0:T(8,128)(2,1)S(1)} %get-tuple-element.36.refs_1_), channel_id=1, source_target_pairs={{0,511},{1,2},{2,1},{3,4},{4,3},{5,6},{6,5},{7,8},{8,7},{9,10},{10... | collective-permute-start | bytes 30728 | tf_op jit(solution)/shard_map/ppermute | solution.py:22
  51.8 4.4 %collective-permute-start.7 = (bf16[16,320]{1,0:T(8,128)(2,1)S(1)}, bf16[16,320]{1,0:T(8,128)(2,1)S(1)}, u32[]{:S(2)}, u32[]{:S(2)}) collective-permute-start(bf16[16,320]{1,0:T(8,128)(2,1)S(1)} %get-tuple-element.36.refs_1_), channel_id=1, source_target_pairs={{0,1},{1,0},{2,3},{3,2},{4,5},{5,4},{6,7},{7,6},{8,9},{9,8},{10,11... | collective-permute-start | bytes 30728 | tf_op jit(solution)/shard_map/ppermute | solution.py:21
  64.7 14.1 %collective-permute-start.10 = (bf16[8,320]{1,0:T(8,128)(2,1)S(1)}, bf16[8,320]{1,0:T(8,128)(2,1)S(1)}, u32[]{:S(2)}, u32[]{:S(2)}) collective-permute-start(bf16[8,320]{1,0:T(8,128)(2,1)S(1)} %get-tuple-element.43.refs_1_), channel_id=1, source_target_pairs={{0,508},{4,8},{8,4},{12,16},{16,12},{20,24},{24,20},{28,32},{32,28... | collective-permute-start | bytes 15368 | tf_op jit(solution)/shard_map/ppermute | solution.py:22
  66.7 13.0 %collective-permute-start.11 = (bf16[8,320]{1,0:T(8,128)(2,1)S(1)}, bf16[8,320]{1,0:T(8,128)(2,1)S(1)}, u32[]{:S(2)}, u32[]{:S(2)}) collective-permute-start(bf16[8,320]{1,0:T(8,128)(2,1)S(1)} %get-tuple-element.43.refs_1_), channel_id=1, source_target_pairs={{0,4},{4,0},{8,12},{12,8},{16,20},{20,16},{24,28},{28,24},{32,36},... | collective-permute-start | bytes 15368 | tf_op jit(solution)/shard_map/ppermute | solution.py:21
  81.1 8.4 %collective-permute-start.12 = (bf16[8,320]{1,0:T(8,128)(2,1)S(1)}, bf16[8,320]{1,0:T(8,128)(2,1)S(1)}, u32[]{:S(2)}, u32[]{:S(2)}) collective-permute-start(bf16[8,320]{1,0:T(8,128)(2,1)S(1)} %shard_map.106.refs_1_), channel_id=1, source_target_pairs={{0,508},{4,8},{8,4},{12,16},{16,12},{20,24},{24,20},{28,32},{32,28... | collective-permute-start | bytes 15368 | tf_op jit(solution)/shard_map/ppermute | solution.py:22
  83.1 7.3 %collective-permute-start.13 = (bf16[8,320]{1,0:T(8,128)(2,1)S(1)}, bf16[8,320]{1,0:T(8,128)(2,1)S(1)}, u32[]{:S(2)}, u32[]{:S(2)}) collective-permute-start(bf16[8,320]{1,0:T(8,128)(2,1)S(1)} %shard_map.106.refs_1_), channel_id=1, source_target_pairs={{0,4},{4,0},{8,12},{12,8},{16,20},{20,16},{24,28},{28,24},{32,36},... | collective-permute-start | bytes 15368 | tf_op jit(solution)/shard_map/ppermute | solution.py:21
  92.0 6.5 %collective-permute-start.14 = (bf16[16,320]{1,0:T(8,128)(2,1)S(1)}, bf16[16,320]{1,0:T(8,128)(2,1)S(1)}, u32[]{:S(2)}, u32[]{:S(2)}) collective-permute-start(bf16[16,320]{1,0:T(8,128)(2,1)S(1)} %shard_map.107.refs_1_), channel_id=1, source_target_pairs={{0,511},{1,2},{2,1},{3,4},{4,3},{5,6},{6,5},{7,8},{8,7},{9,10},{10... | collective-permute-start | bytes 30728 | tf_op jit(solution)/shard_map/ppermute | solution.py:22
  96.6 4.7 %collective-permute-start.15 = (bf16[16,320]{1,0:T(8,128)(2,1)S(1)}, bf16[16,320]{1,0:T(8,128)(2,1)S(1)}, u32[]{:S(2)}, u32[]{:S(2)}) collective-permute-start(bf16[16,320]{1,0:T(8,128)(2,1)S(1)} %shard_map.107.refs_1_), channel_id=1, source_target_pairs={{0,1},{1,0},{2,3},{3,2},{4,5},{5,4},{6,7},{7,6},{8,9},{9,8},{10,11... | collective-permute-start | bytes 30728 | tf_op jit(solution)/shard_map/ppermute | solution.py:21
  103.4 6.2 %collective-permute-start.16 = (bf16[16,320]{1,0:T(8,128)(2,1)S(1)}, bf16[16,320]{1,0:T(8,128)(2,1)S(1)}, u32[]{:S(2)}, u32[]{:S(2)}) collective-permute-start(bf16[16,320]{1,0:T(8,128)(2,1)S(1)} %shard_map.108.refs_1_), channel_id=1, source_target_pairs={{0,511},{1,2},{2,1},{3,4},{4,3},{5,6},{6,5},{7,8},{8,7},{9,10},{10... | collective-permute-start | bytes 30728 | tf_op jit(solution)/shard_map/ppermute | solution.py:22
  113.0 6.8 %collective-permute-start.18 = (bf16[16,320]{1,0:T(8,128)(2,1)S(1)}, bf16[16,320]{1,0:T(8,128)(2,1)S(1)}, u32[]{:S(2)}, u32[]{:S(2)}) collective-permute-start(bf16[16,320]{1,0:T(8,128)(2,1)S(1)} %shard_map.109.refs_1_), channel_id=1, source_target_pairs={{0,511},{1,2},{2,1},{3,4},{4,3},{5,6},{6,5},{7,8},{8,7},{9,10},{10... | collective-permute-start | bytes 30728 | tf_op jit(solution)/shard_map/ppermute | solution.py:22
  117.9 4.4 %collective-permute-start.19 = (bf16[16,320]{1,0:T(8,128)(2,1)S(1)}, bf16[16,320]{1,0:T(8,128)(2,1)S(1)}, u32[]{:S(2)}, u32[]{:S(2)}) collective-permute-start(bf16[16,320]{1,0:T(8,128)(2,1)S(1)} %shard_map.109.refs_1_), channel_id=1, source_target_pairs={{0,1},{1,0},{2,3},{3,2},{4,5},{5,4},{6,7},{7,6},{8,9},{9,8},{10,11... | collective-permute-start | bytes 30728 | tf_op jit(solution)/shard_map/ppermute | solution.py:21
  124.4 8.4 %collective-permute-start.20 = (bf16[16,320]{1,0:T(8,128)(2,1)S(1)}, bf16[16,320]{1,0:T(8,128)(2,1)S(1)}, u32[]{:S(2)}, u32[]{:S(2)}) collective-permute-start(bf16[16,320]{1,0:T(8,128)(2,1)S(1)} %get-tuple-element.47.refs_1_), channel_id=1, source_target_pairs={{0,511},{1,2},{2,1},{3,4},{4,3},{5,6},{6,5},{7,8},{8,7},{9,10},{10... | collective-permute-start | bytes 30728 | tf_op jit(solution)/shard_map/ppermute | solution.py:22
  143.8 13.0 %collective-permute-start.22 = (bf16[8,320]{1,0:T(8,128)(2,1)S(1)}, bf16[8,320]{1,0:T(8,128)(2,1)S(1)}, u32[]{:S(2)}, u32[]{:S(2)}) collective-permute-start(bf16[8,320]{1,0:T(8,128)(2,1)S(1)} %get-tuple-element.49.refs_1_), channel_id=1, source_target_pairs={{0,508},{4,8},{8,4},{12,16},{16,12},{20,24},{24,20},{28,32},{32,28... | collective-permute-start | bytes 15368 | tf_op jit(solution)/shard_map/ppermute | solution.py:22
  145.8 11.8 %collective-permute-start.23 = (bf16[8,320]{1,0:T(8,128)(2,1)S(1)}, bf16[8,320]{1,0:T(8,128)(2,1)S(1)}, u32[]{:S(2)}, u32[]{:S(2)}) collective-permute-start(bf16[8,320]{1,0:T(8,128)(2,1)S(1)} %get-tuple-element.49.refs_1_), channel_id=1, source_target_pairs={{0,4},{4,0},{8,12},{12,8},{16,20},{20,16},{24,28},{28,24},{32,36},... | collective-permute-start | bytes 15368 | tf_op jit(solution)/shard_map/ppermute | solution.py:21
  159.1 8.3 %collective-permute-start.24 = (bf16[8,320]{1,0:T(8,128)(2,1)S(1)}, bf16[8,320]{1,0:T(8,128)(2,1)S(1)}, u32[]{:S(2)}, u32[]{:S(2)}) collective-permute-start(bf16[8,320]{1,0:T(8,128)(2,1)S(1)} %shard_map.113.refs_1_), channel_id=1, source_target_pairs={{0,508},{4,8},{8,4},{12,16},{16,12},{20,24},{24,20},{28,32},{32,28... | collective-permute-start | bytes 15368 | tf_op jit(solution)/shard_map/ppermute | solution.py:22
  161.1 7.2 %collective-permute-start.25 = (bf16[8,320]{1,0:T(8,128)(2,1)S(1)}, bf16[8,320]{1,0:T(8,128)(2,1)S(1)}, u32[]{:S(2)}, u32[]{:S(2)}) collective-permute-start(bf16[8,320]{1,0:T(8,128)(2,1)S(1)} %shard_map.113.refs_1_), channel_id=1, source_target_pairs={{0,4},{4,0},{8,12},{12,8},{16,20},{20,16},{24,28},{28,24},{32,36},... | collective-permute-start | bytes 15368 | tf_op jit(solution)/shard_map/ppermute | solution.py:21
  (6 other events, 90.2 us)

commit v6 on v5

--- a/solution.py
+++ b/solution.py
@@ -106,24 +106,12 @@
         )
         for i in range(block_sems.shape[0])
     ]
-    for copy in [whole[0], *blocks, *whole[1:]]:
+    for copy in whole + blocks:
         copy.start()
 
     tele, column = lax.axis_index("tele"), lax.axis_index("fine")
     tele_size = lax.axis_size("tele")
-    whole[0].wait()
-    lowered = right_ref[...].astype(jnp.bfloat16)
-    row = lax.broadcasted_iota(jnp.int32, lowered.shape, 0)
-    result = jnp.zeros(lowered.shape, jnp.float32)
-    for e in range(inverse_ref.shape[0]):
-        if e % step == 0:
-            blocks[e // step].wait()
-        product = lax.dot_general(
-            lowered, inverse_ref[e], (((1,), (1,)), ((), ())), preferred_element_type=jnp.float32
-        )
-        result = jnp.where(row == e, product, result)
-    state_ref[...] = result.astype(jnp.bfloat16)
-    for copy in whole[1:]:
+    for copy in whole:
         copy.wait()
 
     fine_rows = right_ref.shape[0]
@@ -153,6 +141,18 @@
             unit, operators_in_ref[q], (((1,), (1,)), ((), ())), preferred_element_type=jnp.float32
         )
         operators_ref[q * LANES : (q + 1) * LANES, :size] = turned.astype(jnp.bfloat16)
+
+    lowered = right_ref[...].astype(jnp.bfloat16)
+    row = lax.broadcasted_iota(jnp.int32, lowered.shape, 0)
+    result = jnp.zeros(lowered.shape, jnp.float32)
+    for e in range(inverse_ref.shape[0]):
+        if e % step == 0:
+            blocks[e // step].wait()
+        product = lax.dot_general(
+            lowered, inverse_ref[e], (((1,), (1,)), ((), ())), preferred_element_type=jnp.float32
+        )
+        result = jnp.where(row == e, product, result)
+    state_ref[...] = result.astype(jnp.bfloat16)
 
 
 def take_kernel(before_ref, after_ref, low_ref, high_ref):
@@ -238,7 +238,7 @@
         out_specs=[vmem] * len(shapes),
         scratch_shapes=scratch,
         compiler_params=pltpu.CompilerParams(vmem_limit_bytes=20 << 20),
-        cost_estimate=pl.CostEstimate(flops=1 << 28, bytes_accessed=moved, transcendentals=0),
+        cost_estimate=pl.CostEstimate(flops=1 << 32, bytes_accessed=moved, transcendentals=0),
     )(*operands)
     return result[0] if single else result
 
@@ -291,8 +291,6 @@
         + [pltpu.SemaphoreType.DMA((len(operands),)), pltpu.SemaphoreType.DMA((4,))],
     )
     shared = (operators, lift)
-    own, state = lax.optimization_barrier((coarse_inverse, state))
-    near, other = across(own, 1), across(own, tele_size - 1)
 
     def halo(block, axis):
         inner, outer = swapped(block, axis)
@@ -303,13 +301,24 @@
         for sweep in range(SWEEPS):
             if cycle == 0 and sweep == 0:
                 continue
+            outer, own, inner = halo(state, both)
+            if cycle == 0 and sweep == 1:
+                sent, inner = lax.optimization_barrier((coarse_inverse, inner))
+                near, other = across(sent, 1), across(sent, tele_size - 1)
+            if cycle == 0 and sweep == 2:
+                near, other, outer = lax.optimization_barrier((near, other, outer))
+                far_low, far_high = run(take_kernel, [((1,) + near.shape[1:], bf16)] * 2, other, near)
+                far_low, far_high = across(far_low, 1), across(far_high, tele_size - 1)
+                blocks = (coarse_inverse, near, far_low, far_high, other)
             outs = [((fine_rows, dofs), bf16)]
             if sweep == SWEEPS - 1:
                 outs += [((fine_rows, dofs), f32), ((fine_rows, dofs), bf16)]
             result = run(
                 functools.partial(sweep_kernel, blocks=1),
                 outs,
-                *halo(state, both),
+                outer,
+                own,
+                inner,
                 fine_index,
                 *shared,
                 right_side,
@@ -317,11 +326,6 @@
                 held=(5, 7),
             )
             state = result[0]
-            if cycle == 0 and sweep == 1:
-                near, other, state = lax.optimization_barrier((near, other, state))
-                far_low, far_high = run(take_kernel, [((1,) + near.shape[1:], bf16)] * 2, other, near)
-                far_low, far_high = across(far_low, 1), across(far_high, tele_size - 1)
-                blocks = (coarse_inverse, near, far_low, far_high, other)
         solution, lowered = result[1], result[2]
         parts = run(
             restrict_kernel,

time: 171 us -> 166 us (0.971)
  waiting for transfers between devices: 21.8 us -> 16.3 us
  starting transfers between devices: 111 us -> 108 us
    ppermute x11, waiting for transfers between devices: 5.98 us -> 2.16 us  [swapped(): lax.ppermute(block, axis, [(i, (i - 1 if i % 2 == 0 else i + 1) % count)...]
    ppermute x11, starting transfers between devices: 49.7 us -> 47.7 us  [swapped(): lax.ppermute(block, axis, [(i, (i - 1 if i % 2 == 0 else i + 1) % count)...]
  transfers between devices with their start and end apart: 26 -> 26, of which waited for: 14 -> 11; matrix products, arithmetic and copies ran while one was open for 0% -> 0% of each run, Pallas kernels for 3% -> 2%
where the time goes in v6:
time: 166 us; the launch traced here: 165 us
  starting transfers between devices  108 us (65%)
  Pallas kernels  24.6 us (15%)
  waiting for transfers between devices  16.3 us (10%)
  blocking collectives  14.9 us (9%)
    ppermute x11, starting transfers between devices, swapped(): inner = lax.ppermute(block, axis, [(i, i ^ 1) for i in range(count)])  49.2 us
    ppermute x11, starting transfers between devices, swapped(): lax.ppermute(block, axis, [(i, (i - 1 if i % 2 == 0 else i + 1) % count)...  47.7 us
    pallas_call x15, Pallas kernels, run(): pl.pallas_call(body, out_shape=[pltpu.VMEM(s, d) if i in pinned else jax....  24.6 us
    all_to_all x2, blocking collectives, shards(): parts = lax.all_to_all(parts, 'tele', 0, 0, tiled=True)  14.9 us
    ppermute x11, waiting for transfers between devices, swapped(): inner = lax.ppermute(block, axis, [(i, i ^ 1) for i in range(count)])  14.1 us
    ppermute x4, starting transfers between devices, across(): lax.ppermute(block, 'tele', [(i, i ^ bits) for i in range(tele_size)])  11.3 us
  transfers between devices with their start and end apart: 26, of which 11 were waited for; matrix products, arithmetic and copies ran while one was open for 0% of the time, Pallas kernels for 2%

profile of v6, /device:TPU:1, one launch (start us, length us, event | category | flops | bytes accessed | tf_op | source)
XLA Modules:
  0.0 164.8 jit_solution(14887184897428270469)
XLA Ops:
  0.0 4.2 %shard_map.100 = (bf16[16,320]{1,0:T(8,128)(2,1)S(1)}, s32[16,12]{1,0:T(8,128)S(1)}, f32[4,8,64]{2,1,0:T(8,128)S(1)}, bf16[3072,128]{1,0:T(8,128)(2,1)S(1)}, bf16[16,320,320]{2,1,0:T(8,128)(2,1)S(1)}) custom-call(f32[16,320]{1,0:T(8,128)} %refs_6_.11, s32[6,16]{1,0:T(8,128)} %bitcast.7, s32[6,16]{1,0:T(8,128)} %bitcast.8, s32[2,6]{1,0:T(2,128)} %refs_3_.1, ...), custom_call_target="tpu_custom_call" | custom-call | flops 4294967296 | bytes 3605344 | tf_op jit(solution)/shard_map/pallas_call | solution.py:234
  4.2 3.9 %collective-permute-start = (bf16[16,320]{1,0:T(8,128)(2,1)S(1)}, bf16[16,320]{1,0:T(8,128)(2,1)S(1)}, u32[]{:S(2)}, u32[]{:S(2)}) collective-permute-start(bf16[16,320]{1,0:T(8,128)(2,1)S(1)} %get-tuple-element.29.refs_1_), channel_id=1, source_target_pairs={{0,1},{1,0},{2,3},{3,2},{4,5},{5,4},{6,7},{7,6},{8,9},{9,8},{10,11... | collective-permute-start | bytes 30728 | tf_op jit(solution)/shard_map/ppermute | solution.py:21
  8.1 4.6 %collective-permute-start.3 = (bf16[16,320]{1,0:T(8,128)(2,1)S(1)}, bf16[16,320]{1,0:T(8,128)(2,1)S(1)}, u32[]{:S(2)}, u32[]{:S(2)}) collective-permute-start(bf16[16,320]{1,0:T(8,128)(2,1)S(1)} %get-tuple-element.29.refs_1_), channel_id=1, source_target_pairs={{0,511},{1,2},{2,1},{3,4},{4,3},{5,6},{6,5},{7,8},{8,7},{9,10},{10... | collective-permute-start | bytes 30728 | tf_op jit(solution)/shard_map/ppermute | solution.py:22
  14.6 4.1 %collective-permute-start.2 = (bf16[2,320,320]{2,1,0:T(8,128)(2,1)S(1)}, bf16[2,320,320]{2,1,0:T(8,128)(2,1)S(1)}, u32[]{:S(2)}, u32[]{:S(2)}) collective-permute-start(bf16[2,320,320]{2,1,0:T(8,128)(2,1)S(1)} %copy-done), channel_id=1, source_target_pairs={{0,3},{1,2},{2,1},{3,0},{4,7},{5,6},{6,5},{7,4},{8,11},{9,10},{10,... | collective-permute-start | bytes 1228808 | tf_op jit(solution)/shard_map/ppermute | solution.py:265
  18.8 2.0 %shard_map.101.refs_1_ = bf16[16,320]{1,0:T(8,128)(2,1)S(1)} custom-call(bf16[16,320]{1,0:T(8,128)(2,1)S(1)} %collective-permute-done.3.refs_0_, bf16[16,320]{1,0:T(8,128)(2,1)S(1)} %get-tuple-element.29.refs_1_, bf16[16,320]{1,0:T(8,128)(2,1)S(1)} %collective-permute-done.refs_2_, s32[16,12]{1,0:T(8,128)S(1)} %get-tuple-element.32.refs_3_, ...), custom_call_target="tpu_custom_call" | custom-call | flops 4294967296 | bytes 4606720 | tf_op jit(solution)/shard_map/pallas_call | solution.py:234
  20.9 13.5 %collective-permute-start.4 = (bf16[16,320]{1,0:T(8,128)(2,1)S(1)}, bf16[16,320]{1,0:T(8,128)(2,1)S(1)}, u32[]{:S(2)}, u32[]{:S(2)}) collective-permute-start(bf16[16,320]{1,0:T(8,128)(2,1)S(1)} %shard_map.101.refs_1_), channel_id=1, source_target_pairs={{0,511},{1,2},{2,1},{3,4},{4,3},{5,6},{6,5},{7,8},{8,7},{9,10},{10... | collective-permute-start | bytes 30728 | tf_op jit(solution)/shard_map/ppermute | solution.py:22
  39.1 2.0 %shard_map.102 = (bf16[16,320]{1,0:T(8,128)(2,1)S(1)}, f32[16,320]{1,0:T(8,128)S(1)}, bf16[16,320]{1,0:T(8,128)(2,1)S(1)}) custom-call(bf16[16,320]{1,0:T(8,128)(2,1)S(1)} %collective-permute-done.4.refs_0_, bf16[16,320]{1,0:T(8,128)(2,1)S(1)} %shard_map.101.refs_1_, bf16[16,320]{1,0:T(8,128)(2,1)S(1)} %collective-permute-done.5.refs_2_, ...), custom_call_target="tpu_custom_call" | custom-call | flops 4294967296 | bytes 4606720 | tf_op jit(solution)/shard_map/pallas_call | solution.py:234
  41.2 2.9 %collective-permute-start.6 = (bf16[16,320]{1,0:T(8,128)(2,1)S(1)}, bf16[16,320]{1,0:T(8,128)(2,1)S(1)}, u32[]{:S(2)}, u32[]{:S(2)}) collective-permute-start(bf16[16,320]{1,0:T(8,128)(2,1)S(1)} %get-tuple-element.36.refs_1_), channel_id=1, source_target_pairs={{0,511},{1,2},{2,1},{3,4},{4,3},{5,6},{6,5},{7,8},{8,7},{9,10},{10... | collective-permute-start | bytes 30728 | tf_op jit(solution)/shard_map/ppermute | solution.py:22
  46.1 3.4 %collective-permute-start.8 = (bf16[1,320,320]{2,1,0:T(8,128)(2,1)S(1)}, bf16[1,320,320]{2,1,0:T(8,128)(2,1)S(1)}, u32[]{:S(2)}, u32[]{:S(2)}) collective-permute-start(bf16[1,320,320]{2,1,0:T(8,128)(2,1)S(1)} %get-tuple-element.41), channel_id=1, source_target_pairs={{0,1},{1,0},{2,3},{3,2},{4,5},{5,4},{6,7},{7,6},{8,9},{9,8},{10,11... | collective-permute-start | bytes 614408 | tf_op jit(solution)/shard_map/ppermute | solution.py:265
  52.5 8.1 %all_to_all.10.refs_0_ = f32[4,8,384]{2,1,0:T(8,128)S(1)} all-to-all(f32[4,8,384]{2,1,0:T(8,128)S(1)} %shard_map.103), channel_id=1, replica_groups=mesh['fine'=128,'tele'=4] {'tele'}, dimensions={0} | all-to-all | bytes 98304 | tf_op jit(solution)/shard_map/all_to_all | solution.py:341
  63.3 9.9 %collective-permute-start.11 = (bf16[8,320]{1,0:T(8,128)(2,1)S(1)}, bf16[8,320]{1,0:T(8,128)(2,1)S(1)}, u32[]{:S(2)}, u32[]{:S(2)}) collective-permute-start(bf16[8,320]{1,0:T(8,128)(2,1)S(1)} %get-tuple-element.43.refs_1_), channel_id=1, source_target_pairs={{0,4},{4,0},{8,12},{12,8},{16,20},{20,16},{24,28},{28,24},{32,36},... | collective-permute-start | bytes 15368 | tf_op jit(solution)/shard_map/ppermute | solution.py:21
  77.4 6.5 %collective-permute-start.13 = (bf16[8,320]{1,0:T(8,128)(2,1)S(1)}, bf16[8,320]{1,0:T(8,128)(2,1)S(1)}, u32[]{:S(2)}, u32[]{:S(2)}) collective-permute-start(bf16[8,320]{1,0:T(8,128)(2,1)S(1)} %shard_map.106.refs_1_), channel_id=1, source_target_pairs={{0,4},{4,0},{8,12},{12,8},{16,20},{20,16},{24,28},{28,24},{32,36},... | collective-permute-start | bytes 15368 | tf_op jit(solution)/shard_map/ppermute | solution.py:21
  86.3 4.6 %collective-permute-start.14 = (bf16[16,320]{1,0:T(8,128)(2,1)S(1)}, bf16[16,320]{1,0:T(8,128)(2,1)S(1)}, u32[]{:S(2)}, u32[]{:S(2)}) collective-permute-start(bf16[16,320]{1,0:T(8,128)(2,1)S(1)} %shard_map.107.refs_1_), channel_id=1, source_target_pairs={{0,511},{1,2},{2,1},{3,4},{4,3},{5,6},{6,5},{7,8},{8,7},{9,10},{10... | collective-permute-start | bytes 30728 | tf_op jit(solution)/shard_map/ppermute | solution.py:22
  92.8 2.8 %collective-permute-done.15.refs_2_ = bf16[16,320]{1,0:T(8,128)(2,1)S(1)} collective-permute-done((bf16[16,320]{1,0:T(8,128)(2,1)S(1)}, bf16[16,320]{1,0:T(8,128)(2,1)S(1)}, u32[]{:S(2)}, u32[]{:S(2)}) %collective-permute-start.15) | collective-permute-done | bytes 10272 | tf_op jit(solution)/shard_map/ppermute | solution.py:21
  97.7 3.1 %collective-permute-start.16 = (bf16[16,320]{1,0:T(8,128)(2,1)S(1)}, bf16[16,320]{1,0:T(8,128)(2,1)S(1)}, u32[]{:S(2)}, u32[]{:S(2)}) collective-permute-start(bf16[16,320]{1,0:T(8,128)(2,1)S(1)} %shard_map.108.refs_1_), channel_id=1, source_target_pairs={{0,511},{1,2},{2,1},{3,4},{4,3},{5,6},{6,5},{7,8},{8,7},{9,10},{10... | collective-permute-start | bytes 30728 | tf_op jit(solution)/shard_map/ppermute | solution.py:22
  105.2 2.0 %shard_map.109.refs_1_ = bf16[16,320]{1,0:T(8,128)(2,1)S(1)} custom-call(bf16[16,320]{1,0:T(8,128)(2,1)S(1)} %collective-permute-done.16.refs_0_, bf16[16,320]{1,0:T(8,128)(2,1)S(1)} %shard_map.108.refs_1_, bf16[16,320]{1,0:T(8,128)(2,1)S(1)} %collective-permute-done.17.refs_2_, s32[16,12]{1,0:T(8,128)S(1)} %get-tuple-element.32.refs_3_, ...), custom_call_target="tpu_custom_call" | custom-call | flops 4294967296 | bytes 4606720 | tf_op jit(solution)/shard_map/pallas_call | solution.py:234
  107.3 4.9 %collective-permute-start.18 = (bf16[16,320]{1,0:T(8,128)(2,1)S(1)}, bf16[16,320]{1,0:T(8,128)(2,1)S(1)}, u32[]{:S(2)}, u32[]{:S(2)}) collective-permute-start(bf16[16,320]{1,0:T(8,128)(2,1)S(1)} %shard_map.109.refs_1_), channel_id=1, source_target_pairs={{0,511},{1,2},{2,1},{3,4},{4,3},{5,6},{6,5},{7,8},{8,7},{9,10},{10... | collective-permute-start | bytes 30728 | tf_op jit(solution)/shard_map/ppermute | solution.py:22
  114.1 2.5 %collective-permute-done.19.refs_2_ = bf16[16,320]{1,0:T(8,128)(2,1)S(1)} collective-permute-done((bf16[16,320]{1,0:T(8,128)(2,1)S(1)}, bf16[16,320]{1,0:T(8,128)(2,1)S(1)}, u32[]{:S(2)}, u32[]{:S(2)}) %collective-permute-start.19) | collective-permute-done | bytes 10272 | tf_op jit(solution)/shard_map/ppermute | solution.py:21
  118.7 6.5 %collective-permute-start.20 = (bf16[16,320]{1,0:T(8,128)(2,1)S(1)}, bf16[16,320]{1,0:T(8,128)(2,1)S(1)}, u32[]{:S(2)}, u32[]{:S(2)}) collective-permute-start(bf16[16,320]{1,0:T(8,128)(2,1)S(1)} %get-tuple-element.47.refs_1_), channel_id=1, source_target_pairs={{0,511},{1,2},{2,1},{3,4},{4,3},{5,6},{6,5},{7,8},{8,7},{9,10},{10... | collective-permute-start | bytes 30728 | tf_op jit(solution)/shard_map/ppermute | solution.py:22
  127.1 2.5 %collective-permute-done.21.refs_2_ = bf16[16,320]{1,0:T(8,128)(2,1)S(1)} collective-permute-done((bf16[16,320]{1,0:T(8,128)(2,1)S(1)}, bf16[16,320]{1,0:T(8,128)(2,1)S(1)}, u32[]{:S(2)}, u32[]{:S(2)}) %collective-permute-start.21) | collective-permute-done | bytes 10272 | tf_op jit(solution)/shard_map/ppermute | solution.py:21
  130.7 6.8 %all_to_all.11.refs_0_ = f32[4,8,384]{2,1,0:T(8,128)S(1)} all-to-all(f32[4,8,384]{2,1,0:T(8,128)S(1)} %shard_map.111), channel_id=1, replica_groups=mesh['fine'=128,'tele'=4] {'tele'}, dimensions={0} | all-to-all | bytes 98304 | tf_op jit(solution)/shard_map/all_to_all | solution.py:341
  140.1 11.0 %collective-permute-start.23 = (bf16[8,320]{1,0:T(8,128)(2,1)S(1)}, bf16[8,320]{1,0:T(8,128)(2,1)S(1)}, u32[]{:S(2)}, u32[]{:S(2)}) collective-permute-start(bf16[8,320]{1,0:T(8,128)(2,1)S(1)} %get-tuple-element.49.refs_1_), channel_id=1, source_target_pairs={{0,4},{4,0},{8,12},{12,8},{16,20},{20,16},{24,28},{28,24},{32,36},... | collective-permute-start | bytes 15368 | tf_op jit(solution)/shard_map/ppermute | solution.py:21
  155.3 6.4 %collective-permute-start.25 = (bf16[8,320]{1,0:T(8,128)(2,1)S(1)}, bf16[8,320]{1,0:T(8,128)(2,1)S(1)}, u32[]{:S(2)}, u32[]{:S(2)}) collective-permute-start(bf16[8,320]{1,0:T(8,128)(2,1)S(1)} %shard_map.113.refs_1_), channel_id=1, source_target_pairs={{0,4},{4,0},{8,12},{12,8},{16,20},{20,16},{24,28},{28,24},{32,36},... | collective-permute-start | bytes 15368 | tf_op jit(solution)/shard_map/ppermute | solution.py:21
  162.5 2.3 %shard_map.114 = f32[16,320]{1,0:T(8,128)} custom-call(bf16[8,320]{1,0:T(8,128)(2,1)S(1)} %collective-permute-done.24.refs_0_, bf16[8,320]{1,0:T(8,128)(2,1)S(1)} %shard_map.113.refs_1_, bf16[8,320]{1,0:T(8,128)(2,1)S(1)} %collective-permute-done.25.refs_2_, s32[8,64]{1,0:T(8,128)S(1)} %get-tuple-element.50.refs_3_, ...), custom_call_target="tpu_custom_call" | custom-call | flops 4294967296 | bytes 2964544 | tf_op jit(solution)/shard_map/pallas_call | solution.py:234
  (53 shorter events, 43.8 us)
Async XLA Ops:
  4.2 8.5 %collective-permute-start = (bf16[16,320]{1,0:T(8,128)(2,1)S(1)}, bf16[16,320]{1,0:T(8,128)(2,1)S(1)}, u32[]{:S(2)}, u32[]{:S(2)}) collective-permute-start(bf16[16,320]{1,0:T(8,128)(2,1)S(1)} %get-tuple-element.29.refs_1_), channel_id=1, source_target_pairs={{0,1},{1,0},{2,3},{3,2},{4,5},{5,4},{6,7},{7,6},{8,9},{9,8},{10,11... | collective-permute-start | bytes 30728 | tf_op jit(solution)/shard_map/ppermute | solution.py:21
  8.1 10.7 %collective-permute-start.3 = (bf16[16,320]{1,0:T(8,128)(2,1)S(1)}, bf16[16,320]{1,0:T(8,128)(2,1)S(1)}, u32[]{:S(2)}, u32[]{:S(2)}) collective-permute-start(bf16[16,320]{1,0:T(8,128)(2,1)S(1)} %get-tuple-element.29.refs_1_), channel_id=1, source_target_pairs={{0,511},{1,2},{2,1},{3,4},{4,3},{5,6},{6,5},{7,8},{8,7},{9,10},{10... | collective-permute-start | bytes 30728 | tf_op jit(solution)/shard_map/ppermute | solution.py:22
  12.7 24.6 %collective-permute-start.1 = (bf16[2,320,320]{2,1,0:T(8,128)(2,1)S(1)}, bf16[2,320,320]{2,1,0:T(8,128)(2,1)S(1)}, u32[]{:S(2)}, u32[]{:S(2)}) collective-permute-start(bf16[2,320,320]{2,1,0:T(8,128)(2,1)S(1)} %copy-done), channel_id=1, source_target_pairs={{0,1},{1,0},{2,3},{3,2},{4,5},{5,4},{6,7},{7,6},{8,9},{9,8},{10,11... | collective-permute-start | bytes 1228808 | tf_op jit(solution)/shard_map/ppermute | solution.py:265
  14.6 22.6 %collective-permute-start.2 = (bf16[2,320,320]{2,1,0:T(8,128)(2,1)S(1)}, bf16[2,320,320]{2,1,0:T(8,128)(2,1)S(1)}, u32[]{:S(2)}, u32[]{:S(2)}) collective-permute-start(bf16[2,320,320]{2,1,0:T(8,128)(2,1)S(1)} %copy-done), channel_id=1, source_target_pairs={{0,3},{1,2},{2,1},{3,0},{4,7},{5,6},{6,5},{7,4},{8,11},{9,10},{10,... | collective-permute-start | bytes 1228808 | tf_op jit(solution)/shard_map/ppermute | solution.py:265
  20.9 16.4 %collective-permute-start.4 = (bf16[16,320]{1,0:T(8,128)(2,1)S(1)}, bf16[16,320]{1,0:T(8,128)(2,1)S(1)}, u32[]{:S(2)}, u32[]{:S(2)}) collective-permute-start(bf16[16,320]{1,0:T(8,128)(2,1)S(1)} %shard_map.101.refs_1_), channel_id=1, source_target_pairs={{0,511},{1,2},{2,1},{3,4},{4,3},{5,6},{6,5},{7,8},{8,7},{9,10},{10... | collective-permute-start | bytes 30728 | tf_op jit(solution)/shard_map/ppermute | solution.py:22
  34.4 4.7 %collective-permute-start.5 = (bf16[16,320]{1,0:T(8,128)(2,1)S(1)}, bf16[16,320]{1,0:T(8,128)(2,1)S(1)}, u32[]{:S(2)}, u32[]{:S(2)}) collective-permute-start(bf16[16,320]{1,0:T(8,128)(2,1)S(1)} %shard_map.101.refs_1_), channel_id=1, source_target_pairs={{0,1},{1,0},{2,3},{3,2},{4,5},{5,4},{6,7},{7,6},{8,9},{9,8},{10,11... | collective-permute-start | bytes 30728 | tf_op jit(solution)/shard_map/ppermute | solution.py:21
  41.2 10.2 %collective-permute-start.6 = (bf16[16,320]{1,0:T(8,128)(2,1)S(1)}, bf16[16,320]{1,0:T(8,128)(2,1)S(1)}, u32[]{:S(2)}, u32[]{:S(2)}) collective-permute-start(bf16[16,320]{1,0:T(8,128)(2,1)S(1)} %get-tuple-element.36.refs_1_), channel_id=1, source_target_pairs={{0,511},{1,2},{2,1},{3,4},{4,3},{5,6},{6,5},{7,8},{8,7},{9,10},{10... | collective-permute-start | bytes 30728 | tf_op jit(solution)/shard_map/ppermute | solution.py:22
  44.2 7.3 %collective-permute-start.7 = (bf16[16,320]{1,0:T(8,128)(2,1)S(1)}, bf16[16,320]{1,0:T(8,128)(2,1)S(1)}, u32[]{:S(2)}, u32[]{:S(2)}) collective-permute-start(bf16[16,320]{1,0:T(8,128)(2,1)S(1)} %get-tuple-element.36.refs_1_), channel_id=1, source_target_pairs={{0,1},{1,0},{2,3},{3,2},{4,5},{5,4},{6,7},{7,6},{8,9},{9,8},{10,11... | collective-permute-start | bytes 30728 | tf_op jit(solution)/shard_map/ppermute | solution.py:21
  46.1 14.5 %collective-permute-start.8 = (bf16[1,320,320]{2,1,0:T(8,128)(2,1)S(1)}, bf16[1,320,320]{2,1,0:T(8,128)(2,1)S(1)}, u32[]{:S(2)}, u32[]{:S(2)}) collective-permute-start(bf16[1,320,320]{2,1,0:T(8,128)(2,1)S(1)} %get-tuple-element.41), channel_id=1, source_target_pairs={{0,1},{1,0},{2,3},{3,2},{4,5},{5,4},{6,7},{7,6},{8,9},{9,8},{10,11... | collective-permute-start | bytes 614408 | tf_op jit(solution)/shard_map/ppermute | solution.py:265
  49.5 11.2 %collective-permute-start.9 = (bf16[1,320,320]{2,1,0:T(8,128)(2,1)S(1)}, bf16[1,320,320]{2,1,0:T(8,128)(2,1)S(1)}, u32[]{:S(2)}, u32[]{:S(2)}) collective-permute-start(bf16[1,320,320]{2,1,0:T(8,128)(2,1)S(1)} %get-tuple-element.42), channel_id=1, source_target_pairs={{0,3},{1,2},{2,1},{3,0},{4,7},{5,6},{6,5},{7,4},{8,11},{9,10},{10,... | collective-permute-start | bytes 614408 | tf_op jit(solution)/shard_map/ppermute | solution.py:265
  61.3 11.8 %collective-permute-start.10 = (bf16[8,320]{1,0:T(8,128)(2,1)S(1)}, bf16[8,320]{1,0:T(8,128)(2,1)S(1)}, u32[]{:S(2)}, u32[]{:S(2)}) collective-permute-start(bf16[8,320]{1,0:T(8,128)(2,1)S(1)} %get-tuple-element.43.refs_1_), channel_id=1, source_target_pairs={{0,508},{4,8},{8,4},{12,16},{16,12},{20,24},{24,20},{28,32},{32,28... | collective-permute-start | bytes 15368 | tf_op jit(solution)/shard_map/ppermute | solution.py:22
  63.3 10.7 %collective-permute-start.11 = (bf16[8,320]{1,0:T(8,128)(2,1)S(1)}, bf16[8,320]{1,0:T(8,128)(2,1)S(1)}, u32[]{:S(2)}, u32[]{:S(2)}) collective-permute-start(bf16[8,320]{1,0:T(8,128)(2,1)S(1)} %get-tuple-element.43.refs_1_), channel_id=1, source_target_pairs={{0,4},{4,0},{8,12},{12,8},{16,20},{20,16},{24,28},{28,24},{32,36},... | collective-permute-start | bytes 15368 | tf_op jit(solution)/shard_map/ppermute | solution.py:21
  75.4 8.4 %collective-permute-start.12 = (bf16[8,320]{1,0:T(8,128)(2,1)S(1)}, bf16[8,320]{1,0:T(8,128)(2,1)S(1)}, u32[]{:S(2)}, u32[]{:S(2)}) collective-permute-start(bf16[8,320]{1,0:T(8,128)(2,1)S(1)} %shard_map.106.refs_1_), channel_id=1, source_target_pairs={{0,508},{4,8},{8,4},{12,16},{16,12},{20,24},{24,20},{28,32},{32,28... | collective-permute-start | bytes 15368 | tf_op jit(solution)/shard_map/ppermute | solution.py:22
  77.4 7.3 %collective-permute-start.13 = (bf16[8,320]{1,0:T(8,128)(2,1)S(1)}, bf16[8,320]{1,0:T(8,128)(2,1)S(1)}, u32[]{:S(2)}, u32[]{:S(2)}) collective-permute-start(bf16[8,320]{1,0:T(8,128)(2,1)S(1)} %shard_map.106.refs_1_), channel_id=1, source_target_pairs={{0,4},{4,0},{8,12},{12,8},{16,20},{20,16},{24,28},{28,24},{32,36},... | collective-permute-start | bytes 15368 | tf_op jit(solution)/shard_map/ppermute | solution.py:21
  86.3 6.5 %collective-permute-start.14 = (bf16[16,320]{1,0:T(8,128)(2,1)S(1)}, bf16[16,320]{1,0:T(8,128)(2,1)S(1)}, u32[]{:S(2)}, u32[]{:S(2)}) collective-permute-start(bf16[16,320]{1,0:T(8,128)(2,1)S(1)} %shard_map.107.refs_1_), channel_id=1, source_target_pairs={{0,511},{1,2},{2,1},{3,4},{4,3},{5,6},{6,5},{7,8},{8,7},{9,10},{10... | collective-permute-start | bytes 30728 | tf_op jit(solution)/shard_map/ppermute | solution.py:22
  90.9 4.7 %collective-permute-start.15 = (bf16[16,320]{1,0:T(8,128)(2,1)S(1)}, bf16[16,320]{1,0:T(8,128)(2,1)S(1)}, u32[]{:S(2)}, u32[]{:S(2)}) collective-permute-start(bf16[16,320]{1,0:T(8,128)(2,1)S(1)} %shard_map.107.refs_1_), channel_id=1, source_target_pairs={{0,1},{1,0},{2,3},{3,2},{4,5},{5,4},{6,7},{7,6},{8,9},{9,8},{10,11... | collective-permute-start | bytes 30728 | tf_op jit(solution)/shard_map/ppermute | solution.py:21
  97.7 6.2 %collective-permute-start.16 = (bf16[16,320]{1,0:T(8,128)(2,1)S(1)}, bf16[16,320]{1,0:T(8,128)(2,1)S(1)}, u32[]{:S(2)}, u32[]{:S(2)}) collective-permute-start(bf16[16,320]{1,0:T(8,128)(2,1)S(1)} %shard_map.108.refs_1_), channel_id=1, source_target_pairs={{0,511},{1,2},{2,1},{3,4},{4,3},{5,6},{6,5},{7,8},{8,7},{9,10},{10... | collective-permute-start | bytes 30728 | tf_op jit(solution)/shard_map/ppermute | solution.py:22
  107.3 6.8 %collective-permute-start.18 = (bf16[16,320]{1,0:T(8,128)(2,1)S(1)}, bf16[16,320]{1,0:T(8,128)(2,1)S(1)}, u32[]{:S(2)}, u32[]{:S(2)}) collective-permute-start(bf16[16,320]{1,0:T(8,128)(2,1)S(1)} %shard_map.109.refs_1_), channel_id=1, source_target_pairs={{0,511},{1,2},{2,1},{3,4},{4,3},{5,6},{6,5},{7,8},{8,7},{9,10},{10... | collective-permute-start | bytes 30728 | tf_op jit(solution)/shard_map/ppermute | solution.py:22
  112.2 4.4 %collective-permute-start.19 = (bf16[16,320]{1,0:T(8,128)(2,1)S(1)}, bf16[16,320]{1,0:T(8,128)(2,1)S(1)}, u32[]{:S(2)}, u32[]{:S(2)}) collective-permute-start(bf16[16,320]{1,0:T(8,128)(2,1)S(1)} %shard_map.109.refs_1_), channel_id=1, source_target_pairs={{0,1},{1,0},{2,3},{3,2},{4,5},{5,4},{6,7},{7,6},{8,9},{9,8},{10,11... | collective-permute-start | bytes 30728 | tf_op jit(solution)/shard_map/ppermute | solution.py:21
  118.7 8.4 %collective-permute-start.20 = (bf16[16,320]{1,0:T(8,128)(2,1)S(1)}, bf16[16,320]{1,0:T(8,128)(2,1)S(1)}, u32[]{:S(2)}, u32[]{:S(2)}) collective-permute-start(bf16[16,320]{1,0:T(8,128)(2,1)S(1)} %get-tuple-element.47.refs_1_), channel_id=1, source_target_pairs={{0,511},{1,2},{2,1},{3,4},{4,3},{5,6},{6,5},{7,8},{8,7},{9,10},{10... | collective-permute-start | bytes 30728 | tf_op jit(solution)/shard_map/ppermute | solution.py:22
  138.1 13.0 %collective-permute-start.22 = (bf16[8,320]{1,0:T(8,128)(2,1)S(1)}, bf16[8,320]{1,0:T(8,128)(2,1)S(1)}, u32[]{:S(2)}, u32[]{:S(2)}) collective-permute-start(bf16[8,320]{1,0:T(8,128)(2,1)S(1)} %get-tuple-element.49.refs_1_), channel_id=1, source_target_pairs={{0,508},{4,8},{8,4},{12,16},{16,12},{20,24},{24,20},{28,32},{32,28... | collective-permute-start | bytes 15368 | tf_op jit(solution)/shard_map/ppermute | solution.py:22
  140.1 11.8 %collective-permute-start.23 = (bf16[8,320]{1,0:T(8,128)(2,1)S(1)}, bf16[8,320]{1,0:T(8,128)(2,1)S(1)}, u32[]{:S(2)}, u32[]{:S(2)}) collective-permute-start(bf16[8,320]{1,0:T(8,128)(2,1)S(1)} %get-tuple-element.49.refs_1_), channel_id=1, source_target_pairs={{0,4},{4,0},{8,12},{12,8},{16,20},{20,16},{24,28},{28,24},{32,36},... | collective-permute-start | bytes 15368 | tf_op jit(solution)/shard_map/ppermute | solution.py:21
  153.4 8.3 %collective-permute-start.24 = (bf16[8,320]{1,0:T(8,128)(2,1)S(1)}, bf16[8,320]{1,0:T(8,128)(2,1)S(1)}, u32[]{:S(2)}, u32[]{:S(2)}) collective-permute-start(bf16[8,320]{1,0:T(8,128)(2,1)S(1)} %shard_map.113.refs_1_), channel_id=1, source_target_pairs={{0,508},{4,8},{8,4},{12,16},{16,12},{20,24},{24,20},{28,32},{32,28... | collective-permute-start | bytes 15368 | tf_op jit(solution)/shard_map/ppermute | solution.py:22
  155.3 7.2 %collective-permute-start.25 = (bf16[8,320]{1,0:T(8,128)(2,1)S(1)}, bf16[8,320]{1,0:T(8,128)(2,1)S(1)}, u32[]{:S(2)}, u32[]{:S(2)}) collective-permute-start(bf16[8,320]{1,0:T(8,128)(2,1)S(1)} %shard_map.113.refs_1_), channel_id=1, source_target_pairs={{0,4},{4,0},{8,12},{12,8},{16,20},{20,16},{24,28},{28,24},{32,36},... | collective-permute-start | bytes 15368 | tf_op jit(solution)/shard_map/ppermute | solution.py:21
  (6 other events, 69.4 us)

commit v7 on v6

--- a/solution.py
+++ b/solution.py
@@ -61,11 +61,11 @@
         kinds.append(jnp.broadcast_to(index[:, 6 + k : 7 + k], (count, LANES)))
     face_rows = jnp.concatenate(face_rows, axis=0)
     kinds = jnp.concatenate(kinds, axis=0)
-    types = operators.shape[0] // LANES
+    types = operators.shape[1] // LANES
     spread = jnp.concatenate(
         [jnp.where(kinds == q, face_rows, 0.0).astype(jnp.bfloat16) for q in range(types)], axis=1
     )
-    coupled = jnp.dot(spread, operators, preferred_element_type=jnp.float32)
+    coupled = lax.dot_general(spread, operators, (((1,), (1,)), ((), ())), preferred_element_type=jnp.float32)
     side_by_side = jnp.concatenate([coupled[k * count : (k + 1) * count] for k in range(6)], axis=1)
     high = side_by_side.astype(jnp.bfloat16).astype(jnp.float32)
     terms = jnp.concatenate([high, side_by_side - high], axis=0).astype(jnp.bfloat16)
@@ -87,9 +87,9 @@
     return result
 
 
-def pool_rows(links, count, position, turn=0):
+def pool_rows(links, count, position):
     shift = count.bit_length() - 1
-    owner, within = links >> shift, (links & (count - 1)) ^ turn
+    owner, within = links >> shift, links & (count - 1)
     place = jnp.where(owner == position, 1, jnp.where(owner == (position ^ 1), 2, 0))
     return jnp.where(links >= 0, place * count + within, -1)
 
@@ -121,26 +121,20 @@
 
     own = coarse_links_ref.shape[0]
     count = own * tele_size
+    rows = pool_rows(coarse_links_ref[...], count, column).astype(jnp.float32)
     kinds = coarse_faces_ref[...].astype(jnp.float32)
     lists_ref[...] = jnp.zeros(lists_ref.shape, jnp.float32)
     row = lax.broadcasted_iota(jnp.int32, (count, kinds.shape[1]), 0)
-    for t in range(tele_size):
-        rows = pool_rows(coarse_links_ref[...], count, column, own * t).astype(jnp.float32)
-        for part, values in enumerate((rows, kinds)):
-            placed = jnp.zeros(row.shape, jnp.float32)
-            for c in range(own):
-                placed = jnp.where(row == ((own * tele + c) ^ (own * t)), values[c : c + 1], placed)
-            lists_ref[t, :, part * 6 : part * 6 + 6] = placed
+    for part, values in enumerate((rows, kinds)):
+        placed = jnp.zeros(row.shape, jnp.float32)
+        for c in range(own):
+            placed = jnp.where(row == own * tele + c, values[c : c + 1], placed)
+        lists_ref[:, part * 6 : part * 6 + 6] = placed
 
     types, size, _ = operators_in_ref.shape
-    unit = lax.broadcasted_iota(jnp.int32, (LANES, size), 0) == lax.broadcasted_iota(jnp.int32, (LANES, size), 1)
-    unit = jnp.where(unit, 1.0, 0.0).astype(jnp.bfloat16)
     operators_ref[...] = jnp.zeros(operators_ref.shape, jnp.bfloat16)
     for q in range(types):
-        turned = lax.dot_general(
-            unit, operators_in_ref[q], (((1,), (1,)), ((), ())), preferred_element_type=jnp.float32
-        )
-        operators_ref[q * LANES : (q + 1) * LANES, :size] = turned.astype(jnp.bfloat16)
+        operators_ref[:size, q * LANES : q * LANES + size] = operators_in_ref[q]
 
     lowered = right_ref[...].astype(jnp.bfloat16)
     row = lax.broadcasted_iota(jnp.int32, lowered.shape, 0)
@@ -189,9 +183,11 @@
     element = (row & (rows - 1)) ^ ((row >> (rows.bit_length() - 1)) * (rows // tele_size))
     member = jnp.where((target_ref[...] & (rows - 1)) == element, 1.0, 0.0).astype(jnp.bfloat16)
     partial = exact_dot(member, residual)
+    own = rows // tele_size
     for t in range(tele_size):
         out_ref[t, :, :dofs] = partial[t * rows : (t + 1) * rows]
-        out_ref[t, :, dofs:] = lists_ref[t]
+        for s in range(tele_size):
+            out_ref[t, s * own : (s + 1) * own, dofs:] = lists_ref[(s ^ t) * own : ((s ^ t) + 1) * own]
 
 
 def coarse_first_kernel(*refs, blocks):
@@ -202,7 +198,10 @@
     dofs = restricted_ref.shape[1]
     restricted = total[:, :dofs]
     restricted_ref[...] = restricted
-    index_ref[...] = total[:, dofs:].astype(jnp.int32)
+    lists = total[:, dofs:].astype(jnp.int32)
+    turn = lax.axis_index("tele") * (total.shape[0] // parts_ref.shape[0])
+    turned = (lax.broadcasted_iota(jnp.int32, lists.shape, 1) < 6) & (lists >= 0)
+    index_ref[...] = jnp.where(turned, lists ^ turn, lists)
     state_ref[...] = apply_inverse(inverses, restricted.astype(jnp.bfloat16)).astype(jnp.bfloat16)
 
 
@@ -280,8 +279,8 @@
         [
             ((fine_rows, dofs), bf16),
             ((fine_rows, 12), i32),
-            ((tele_size, coarse_rows, spare), f32),
-            ((types * LANES, LANES), bf16),
+            ((coarse_rows, spare), f32),
+            ((LANES, types * LANES), bf16),
             (fine_inverse.shape, bf16),
         ],
         *operands,
@@ -303,13 +302,8 @@
                 continue
             outer, own, inner = halo(state, both)
             if cycle == 0 and sweep == 1:
-                sent, inner = lax.optimization_barrier((coarse_inverse, inner))
+                sent, _ = lax.optimization_barrier((coarse_inverse, outer))
                 near, other = across(sent, 1), across(sent, tele_size - 1)
-            if cycle == 0 and sweep == 2:
-                near, other, outer = lax.optimization_barrier((near, other, outer))
-                far_low, far_high = run(take_kernel, [((1,) + near.shape[1:], bf16)] * 2, other, near)
-                far_low, far_high = across(far_low, 1), across(far_high, tele_size - 1)
-                blocks = (coarse_inverse, near, far_low, far_high, other)
             outs = [((fine_rows, dofs), bf16)]
             if sweep == SWEEPS - 1:
                 outs += [((fine_rows, dofs), f32), ((fine_rows, dofs), bf16)]
@@ -326,6 +320,11 @@
                 held=(5, 7),
             )
             state = result[0]
+            if cycle == 0 and sweep == 2:
+                far_shape = ((1,) + near.shape[1:], bf16)
+                far_low, far_high = run(take_kernel, [far_shape] * 2, other, near, keep=(state,))
+                far_low, far_high = across(far_low, 1), across(far_high, tele_size - 1)
+                blocks = (coarse_inverse, near, far_low, far_high, other)
         solution, lowered = result[1], result[2]
         parts = run(
             restrict_kernel,

time: 166 us -> 169 us (1.018)
  Pallas kernels: 24.6 us -> 27.3 us
    ppermute x11, starting transfers between devices: 49.2 us -> 43.1 us  [swapped(): inner = lax.ppermute(block, axis, [(i, i ^ 1) for i in range(count)])]
    ppermute x11, starting transfers between devices: 47.7 us -> 52.3 us  [swapped(): lax.ppermute(block, axis, [(i, (i - 1 if i % 2 == 0 else i + 1) % count)...]
    pallas_call x15, Pallas kernels: 24.6 us -> 27.3 us  [run(): pl.pallas_call(body, out_shape=[pltpu.VMEM(s, d) if i in pinned else jax....]
    ppermute x4, starting transfers between devices: 11.3 us -> 13.7 us  [across(): lax.ppermute(block, 'tele', [(i, i ^ bits) for i in range(tele_size)])]
  transfers between devices with their start and end apart: 26 -> 26, of which waited for: 11 -> 10; matrix products, arithmetic and copies ran while one was open for 0% -> 0% of each run, Pallas kernels for 2% -> 2%
where the time goes in v7:
time: 169 us; the launch traced here: 168 us
  starting transfers between devices  109 us (64%)
  Pallas kernels  27.3 us (16%)
  waiting for transfers between devices  16 us (9%)
  blocking collectives  14.9 us (9%)
    ppermute x11, starting transfers between devices, swapped(): lax.ppermute(block, axis, [(i, (i - 1 if i % 2 == 0 else i + 1) % count)...  52.3 us
    ppermute x11, starting transfers between devices, swapped(): inner = lax.ppermute(block, axis, [(i, i ^ 1) for i in range(count)])  43.1 us
    pallas_call x15, Pallas kernels, run(): pl.pallas_call(body, out_shape=[pltpu.VMEM(s, d) if i in pinned else jax....  27.3 us
    all_to_all x2, blocking collectives, shards(): parts = lax.all_to_all(parts, 'tele', 0, 0, tiled=True)  14.9 us
    ppermute x11, waiting for transfers between devices, swapped(): inner = lax.ppermute(block, axis, [(i, i ^ 1) for i in range(count)])  14.8 us
    ppermute x4, starting transfers between devices, across(): lax.ppermute(block, 'tele', [(i, i ^ bits) for i in range(tele_size)])  13.7 us
  transfers between devices with their start and end apart: 26, of which 10 were waited for; matrix products, arithmetic and copies ran while one was open for 0% of the time, Pallas kernels for 2%

profile of v7, /device:TPU:1, one launch (start us, length us, event | category | flops | bytes accessed | tf_op | source)
XLA Modules:
  0.0 167.9 jit_solution(14170271227686158871)
XLA Ops:
  0.0 3.8 %shard_map.100 = (bf16[16,320]{1,0:T(8,128)(2,1)S(1)}, s32[16,12]{1,0:T(8,128)S(1)}, f32[8,64]{1,0:T(8,128)S(1)}, bf16[128,3072]{1,0:T(8,128)(2,1)S(1)}, bf16[16,320,320]{2,1,0:T(8,128)(2,1)S(1)}) custom-call(f32[16,320]{1,0:T(8,128)} %refs_6_.11, s32[6,16]{1,0:T(8,128)} %bitcast.7, s32[6,16]{1,0:T(8,128)} %bitcast.8, s32[2,6]{1,0:T(2,128)} %refs_3_.1, ...), custom_call_target="tpu_custom_call" | custom-call | flops 4294967296 | bytes 3605344 | tf_op jit(solution)/shard_map/pallas_call | solution.py:233
  3.9 5.8 %collective-permute-start = (bf16[16,320]{1,0:T(8,128)(2,1)S(1)}, bf16[16,320]{1,0:T(8,128)(2,1)S(1)}, u32[]{:S(2)}, u32[]{:S(2)}) collective-permute-start(bf16[16,320]{1,0:T(8,128)(2,1)S(1)} %get-tuple-element.25.refs_1_), channel_id=1, source_target_pairs={{0,511},{1,2},{2,1},{3,4},{4,3},{5,6},{6,5},{7,8},{8,7},{9,10},{10... | collective-permute-start | bytes 30728 | tf_op jit(solution)/shard_map/ppermute | solution.py:22
  11.6 2.5 %collective-permute-done.1.refs_2_ = bf16[16,320]{1,0:T(8,128)(2,1)S(1)} collective-permute-done((bf16[16,320]{1,0:T(8,128)(2,1)S(1)}, bf16[16,320]{1,0:T(8,128)(2,1)S(1)}, u32[]{:S(2)}, u32[]{:S(2)}) %collective-permute-start.1) | collective-permute-done | bytes 10272 | tf_op jit(solution)/shard_map/ppermute | solution.py:21
  14.1 2.3 %shard_map.101.refs_1_ = bf16[16,320]{1,0:T(8,128)(2,1)S(1)} custom-call(bf16[16,320]{1,0:T(8,128)(2,1)S(1)} %collective-permute-done.refs_0_, bf16[16,320]{1,0:T(8,128)(2,1)S(1)} %get-tuple-element.25.refs_1_, bf16[16,320]{1,0:T(8,128)(2,1)S(1)} %collective-permute-done.1.refs_2_, s32[16,12]{1,0:T(8,128)S(1)} %get-tuple-element.26.refs_3_, ...), custom_call_target="tpu_custom_call" | custom-call | flops 4294967296 | bytes 4606720 | tf_op jit(solution)/shard_map/pallas_call | solution.py:233
  16.4 3.2 %collective-permute-start.2 = (bf16[16,320]{1,0:T(8,128)(2,1)S(1)}, bf16[16,320]{1,0:T(8,128)(2,1)S(1)}, u32[]{:S(2)}, u32[]{:S(2)}) collective-permute-start(bf16[16,320]{1,0:T(8,128)(2,1)S(1)} %shard_map.101.refs_1_), channel_id=1, source_target_pairs={{0,511},{1,2},{2,1},{3,4},{4,3},{5,6},{6,5},{7,8},{8,7},{9,10},{10... | collective-permute-start | bytes 30728 | tf_op jit(solution)/shard_map/ppermute | solution.py:22
  21.6 3.2 %collective-permute-start.6 = (bf16[2,320,320]{2,1,0:T(8,128)(2,1)S(1)}, bf16[2,320,320]{2,1,0:T(8,128)(2,1)S(1)}, u32[]{:S(2)}, u32[]{:S(2)}) collective-permute-start(bf16[2,320,320]{2,1,0:T(8,128)(2,1)S(1)} %copy-done), channel_id=1, source_target_pairs={{0,1},{1,0},{2,3},{3,2},{4,5},{5,4},{6,7},{7,6},{8,9},{9,8},{10,11... | collective-permute-start | bytes 1228808 | tf_op jit(solution)/shard_map/ppermute | solution.py:264
  24.9 5.2 %collective-permute-start.7 = (bf16[2,320,320]{2,1,0:T(8,128)(2,1)S(1)}, bf16[2,320,320]{2,1,0:T(8,128)(2,1)S(1)}, u32[]{:S(2)}, u32[]{:S(2)}) collective-permute-start(bf16[2,320,320]{2,1,0:T(8,128)(2,1)S(1)} %copy-done), channel_id=1, source_target_pairs={{0,3},{1,2},{2,1},{3,0},{4,7},{5,6},{6,5},{7,4},{8,11},{9,10},{10,... | collective-permute-start | bytes 1228808 | tf_op jit(solution)/shard_map/ppermute | solution.py:264
  30.1 2.3 %shard_map.102 = (bf16[16,320]{1,0:T(8,128)(2,1)S(1)}, f32[16,320]{1,0:T(8,128)S(1)}, bf16[16,320]{1,0:T(8,128)(2,1)S(1)}) custom-call(bf16[16,320]{1,0:T(8,128)(2,1)S(1)} %collective-permute-done.2.refs_0_, bf16[16,320]{1,0:T(8,128)(2,1)S(1)} %shard_map.101.refs_1_, bf16[16,320]{1,0:T(8,128)(2,1)S(1)} %collective-permute-done.3.refs_2_, ...), custom_call_target="tpu_custom_call" | custom-call | flops 4294967296 | bytes 4606720 | tf_op jit(solution)/shard_map/pallas_call | solution.py:233
  32.4 16.3 %collective-permute-start.4 = (bf16[16,320]{1,0:T(8,128)(2,1)S(1)}, bf16[16,320]{1,0:T(8,128)(2,1)S(1)}, u32[]{:S(2)}, u32[]{:S(2)}) collective-permute-start(bf16[16,320]{1,0:T(8,128)(2,1)S(1)} %get-tuple-element.29.refs_1_.refs_2_), channel_id=1, source_target_pairs={{0,511},{1,2},{2,1},{3,4},{4,3},{5,6},{6,5},{7,8},{8,7},{9,10},{10... | collective-permute-start | bytes 30728 | tf_op jit(solution)/shard_map/ppermute | solution.py:22
  50.8 3.4 %collective-permute-start.8 = (bf16[1,320,320]{2,1,0:T(8,128)(2,1)S(1)}, bf16[1,320,320]{2,1,0:T(8,128)(2,1)S(1)}, u32[]{:S(2)}, u32[]{:S(2)}) collective-permute-start(bf16[1,320,320]{2,1,0:T(8,128)(2,1)S(1)} %get-tuple-element.33), channel_id=1, source_target_pairs={{0,1},{1,0},{2,3},{3,2},{4,5},{5,4},{6,7},{7,6},{8,9},{9,8},{10,11... | collective-permute-start | bytes 614408 | tf_op jit(solution)/shard_map/ppermute | solution.py:264
  57.5 8.1 %all_to_all.10.refs_0_ = f32[4,8,384]{2,1,0:T(8,128)S(1)} all-to-all(f32[4,8,384]{2,1,0:T(8,128)S(1)} %shard_map.103), channel_id=1, replica_groups=mesh['fine'=128,'tele'=4] {'tele'}, dimensions={0} | all-to-all | bytes 98304 | tf_op jit(solution)/shard_map/all_to_all | solution.py:340
  68.2 5.2 %collective-permute-start.11 = (bf16[8,320]{1,0:T(8,128)(2,1)S(1)}, bf16[8,320]{1,0:T(8,128)(2,1)S(1)}, u32[]{:S(2)}, u32[]{:S(2)}) collective-permute-start(bf16[8,320]{1,0:T(8,128)(2,1)S(1)} %get-tuple-element.35.refs_1_), channel_id=1, source_target_pairs={{0,4},{4,0},{8,12},{12,8},{16,20},{20,16},{24,28},{28,24},{32,36},... | collective-permute-start | bytes 15368 | tf_op jit(solution)/shard_map/ppermute | solution.py:21
  77.9 7.1 %collective-permute-start.13 = (bf16[8,320]{1,0:T(8,128)(2,1)S(1)}, bf16[8,320]{1,0:T(8,128)(2,1)S(1)}, u32[]{:S(2)}, u32[]{:S(2)}) collective-permute-start(bf16[8,320]{1,0:T(8,128)(2,1)S(1)} %shard_map.106.refs_1_), channel_id=1, source_target_pairs={{0,4},{4,0},{8,12},{12,8},{16,20},{20,16},{24,28},{28,24},{32,36},... | collective-permute-start | bytes 15368 | tf_op jit(solution)/shard_map/ppermute | solution.py:21
  87.8 4.6 %collective-permute-start.14 = (bf16[16,320]{1,0:T(8,128)(2,1)S(1)}, bf16[16,320]{1,0:T(8,128)(2,1)S(1)}, u32[]{:S(2)}, u32[]{:S(2)}) collective-permute-start(bf16[16,320]{1,0:T(8,128)(2,1)S(1)} %shard_map.107.refs_1_), channel_id=1, source_target_pairs={{0,511},{1,2},{2,1},{3,4},{4,3},{5,6},{6,5},{7,8},{8,7},{9,10},{10... | collective-permute-start | bytes 30728 | tf_op jit(solution)/shard_map/ppermute | solution.py:22
  94.3 2.8 %collective-permute-done.15.refs_2_ = bf16[16,320]{1,0:T(8,128)(2,1)S(1)} collective-permute-done((bf16[16,320]{1,0:T(8,128)(2,1)S(1)}, bf16[16,320]{1,0:T(8,128)(2,1)S(1)}, u32[]{:S(2)}, u32[]{:S(2)}) %collective-permute-start.15) | collective-permute-done | bytes 10272 | tf_op jit(solution)/shard_map/ppermute | solution.py:21
  99.4 3.2 %collective-permute-start.16 = (bf16[16,320]{1,0:T(8,128)(2,1)S(1)}, bf16[16,320]{1,0:T(8,128)(2,1)S(1)}, u32[]{:S(2)}, u32[]{:S(2)}) collective-permute-start(bf16[16,320]{1,0:T(8,128)(2,1)S(1)} %shard_map.108.refs_1_), channel_id=1, source_target_pairs={{0,511},{1,2},{2,1},{3,4},{4,3},{5,6},{6,5},{7,8},{8,7},{9,10},{10... | collective-permute-start | bytes 30728 | tf_op jit(solution)/shard_map/ppermute | solution.py:22
  109.3 4.9 %collective-permute-start.18 = (bf16[16,320]{1,0:T(8,128)(2,1)S(1)}, bf16[16,320]{1,0:T(8,128)(2,1)S(1)}, u32[]{:S(2)}, u32[]{:S(2)}) collective-permute-start(bf16[16,320]{1,0:T(8,128)(2,1)S(1)} %shard_map.109.refs_1_), channel_id=1, source_target_pairs={{0,511},{1,2},{2,1},{3,4},{4,3},{5,6},{6,5},{7,8},{8,7},{9,10},{10... | collective-permute-start | bytes 30728 | tf_op jit(solution)/shard_map/ppermute | solution.py:22
  116.2 2.5 %collective-permute-done.19.refs_2_ = bf16[16,320]{1,0:T(8,128)(2,1)S(1)} collective-permute-done((bf16[16,320]{1,0:T(8,128)(2,1)S(1)}, bf16[16,320]{1,0:T(8,128)(2,1)S(1)}, u32[]{:S(2)}, u32[]{:S(2)}) %collective-permute-start.19) | collective-permute-done | bytes 10272 | tf_op jit(solution)/shard_map/ppermute | solution.py:21
  120.9 6.5 %collective-permute-start.20 = (bf16[16,320]{1,0:T(8,128)(2,1)S(1)}, bf16[16,320]{1,0:T(8,128)(2,1)S(1)}, u32[]{:S(2)}, u32[]{:S(2)}) collective-permute-start(bf16[16,320]{1,0:T(8,128)(2,1)S(1)} %get-tuple-element.39.refs_1_), channel_id=1, source_target_pairs={{0,511},{1,2},{2,1},{3,4},{4,3},{5,6},{6,5},{7,8},{8,7},{9,10},{10... | collective-permute-start | bytes 30728 | tf_op jit(solution)/shard_map/ppermute | solution.py:22
  129.4 2.5 %collective-permute-done.21.refs_2_ = bf16[16,320]{1,0:T(8,128)(2,1)S(1)} collective-permute-done((bf16[16,320]{1,0:T(8,128)(2,1)S(1)}, bf16[16,320]{1,0:T(8,128)(2,1)S(1)}, u32[]{:S(2)}, u32[]{:S(2)}) %collective-permute-start.21) | collective-permute-done | bytes 10272 | tf_op jit(solution)/shard_map/ppermute | solution.py:21
  133.3 6.7 %all_to_all.11.refs_0_ = f32[4,8,384]{2,1,0:T(8,128)S(1)} all-to-all(f32[4,8,384]{2,1,0:T(8,128)S(1)} %shard_map.111), channel_id=1, replica_groups=mesh['fine'=128,'tele'=4] {'tele'}, dimensions={0} | all-to-all | bytes 98304 | tf_op jit(solution)/shard_map/all_to_all | solution.py:340
  142.7 10.7 %collective-permute-start.23 = (bf16[8,320]{1,0:T(8,128)(2,1)S(1)}, bf16[8,320]{1,0:T(8,128)(2,1)S(1)}, u32[]{:S(2)}, u32[]{:S(2)}) collective-permute-start(bf16[8,320]{1,0:T(8,128)(2,1)S(1)} %get-tuple-element.41.refs_1_), channel_id=1, source_target_pairs={{0,4},{4,0},{8,12},{12,8},{16,20},{20,16},{24,28},{28,24},{32,36},... | collective-permute-start | bytes 15368 | tf_op jit(solution)/shard_map/ppermute | solution.py:21
  158.0 6.5 %collective-permute-start.25 = (bf16[8,320]{1,0:T(8,128)(2,1)S(1)}, bf16[8,320]{1,0:T(8,128)(2,1)S(1)}, u32[]{:S(2)}, u32[]{:S(2)}) collective-permute-start(bf16[8,320]{1,0:T(8,128)(2,1)S(1)} %shard_map.113.refs_1_), channel_id=1, source_target_pairs={{0,4},{4,0},{8,12},{12,8},{16,20},{20,16},{24,28},{28,24},{32,36},... | collective-permute-start | bytes 15368 | tf_op jit(solution)/shard_map/ppermute | solution.py:21
  165.3 2.6 %shard_map.114 = f32[16,320]{1,0:T(8,128)} custom-call(bf16[8,320]{1,0:T(8,128)(2,1)S(1)} %collective-permute-done.24.refs_0_, bf16[8,320]{1,0:T(8,128)(2,1)S(1)} %shard_map.113.refs_1_, bf16[8,320]{1,0:T(8,128)(2,1)S(1)} %collective-permute-done.25.refs_2_, s32[8,64]{1,0:T(8,128)S(1)} %get-tuple-element.42.refs_3_, ...), custom_call_target="tpu_custom_call" | custom-call | flops 4294967296 | bytes 2964544 | tf_op jit(solution)/shard_map/pallas_call | solution.py:233
  (53 shorter events, 45.4 us)
Async XLA Ops:
  3.9 7.7 %collective-permute-start = (bf16[16,320]{1,0:T(8,128)(2,1)S(1)}, bf16[16,320]{1,0:T(8,128)(2,1)S(1)}, u32[]{:S(2)}, u32[]{:S(2)}) collective-permute-start(bf16[16,320]{1,0:T(8,128)(2,1)S(1)} %get-tuple-element.25.refs_1_), channel_id=1, source_target_pairs={{0,511},{1,2},{2,1},{3,4},{4,3},{5,6},{6,5},{7,8},{8,7},{9,10},{10... | collective-permute-start | bytes 30728 | tf_op jit(solution)/shard_map/ppermute | solution.py:22
  9.6 4.4 %collective-permute-start.1 = (bf16[16,320]{1,0:T(8,128)(2,1)S(1)}, bf16[16,320]{1,0:T(8,128)(2,1)S(1)}, u32[]{:S(2)}, u32[]{:S(2)}) collective-permute-start(bf16[16,320]{1,0:T(8,128)(2,1)S(1)} %get-tuple-element.25.refs_1_), channel_id=1, source_target_pairs={{0,1},{1,0},{2,3},{3,2},{4,5},{5,4},{6,7},{7,6},{8,9},{9,8},{10,11... | collective-permute-start | bytes 30728 | tf_op jit(solution)/shard_map/ppermute | solution.py:21
  16.4 13.7 %collective-permute-start.2 = (bf16[16,320]{1,0:T(8,128)(2,1)S(1)}, bf16[16,320]{1,0:T(8,128)(2,1)S(1)}, u32[]{:S(2)}, u32[]{:S(2)}) collective-permute-start(bf16[16,320]{1,0:T(8,128)(2,1)S(1)} %shard_map.101.refs_1_), channel_id=1, source_target_pairs={{0,511},{1,2},{2,1},{3,4},{4,3},{5,6},{6,5},{7,8},{8,7},{9,10},{10... | collective-permute-start | bytes 30728 | tf_op jit(solution)/shard_map/ppermute | solution.py:22
  19.5 10.5 %collective-permute-start.3 = (bf16[16,320]{1,0:T(8,128)(2,1)S(1)}, bf16[16,320]{1,0:T(8,128)(2,1)S(1)}, u32[]{:S(2)}, u32[]{:S(2)}) collective-permute-start(bf16[16,320]{1,0:T(8,128)(2,1)S(1)} %shard_map.101.refs_1_), channel_id=1, source_target_pairs={{0,1},{1,0},{2,3},{3,2},{4,5},{5,4},{6,7},{7,6},{8,9},{9,8},{10,11... | collective-permute-start | bytes 30728 | tf_op jit(solution)/shard_map/ppermute | solution.py:21
  21.6 29.1 %collective-permute-start.6 = (bf16[2,320,320]{2,1,0:T(8,128)(2,1)S(1)}, bf16[2,320,320]{2,1,0:T(8,128)(2,1)S(1)}, u32[]{:S(2)}, u32[]{:S(2)}) collective-permute-start(bf16[2,320,320]{2,1,0:T(8,128)(2,1)S(1)} %copy-done), channel_id=1, source_target_pairs={{0,1},{1,0},{2,3},{3,2},{4,5},{5,4},{6,7},{7,6},{8,9},{9,8},{10,11... | collective-permute-start | bytes 1228808 | tf_op jit(solution)/shard_map/ppermute | solution.py:264
  24.9 25.9 %collective-permute-start.7 = (bf16[2,320,320]{2,1,0:T(8,128)(2,1)S(1)}, bf16[2,320,320]{2,1,0:T(8,128)(2,1)S(1)}, u32[]{:S(2)}, u32[]{:S(2)}) collective-permute-start(bf16[2,320,320]{2,1,0:T(8,128)(2,1)S(1)} %copy-done), channel_id=1, source_target_pairs={{0,3},{1,2},{2,1},{3,0},{4,7},{5,6},{6,5},{7,4},{8,11},{9,10},{10,... | collective-permute-start | bytes 1228808 | tf_op jit(solution)/shard_map/ppermute | solution.py:264
  32.4 23.7 %collective-permute-start.4 = (bf16[16,320]{1,0:T(8,128)(2,1)S(1)}, bf16[16,320]{1,0:T(8,128)(2,1)S(1)}, u32[]{:S(2)}, u32[]{:S(2)}) collective-permute-start(bf16[16,320]{1,0:T(8,128)(2,1)S(1)} %get-tuple-element.29.refs_1_.refs_2_), channel_id=1, source_target_pairs={{0,511},{1,2},{2,1},{3,4},{4,3},{5,6},{6,5},{7,8},{8,7},{9,10},{10... | collective-permute-start | bytes 30728 | tf_op jit(solution)/shard_map/ppermute | solution.py:22
  48.8 7.3 %collective-permute-start.5 = (bf16[16,320]{1,0:T(8,128)(2,1)S(1)}, bf16[16,320]{1,0:T(8,128)(2,1)S(1)}, u32[]{:S(2)}, u32[]{:S(2)}) collective-permute-start(bf16[16,320]{1,0:T(8,128)(2,1)S(1)} %get-tuple-element.29.refs_1_.refs_2_), channel_id=1, source_target_pairs={{0,1},{1,0},{2,3},{3,2},{4,5},{5,4},{6,7},{7,6},{8,9},{9,8},{10,11... | collective-permute-start | bytes 30728 | tf_op jit(solution)/shard_map/ppermute | solution.py:21
  50.8 14.9 %collective-permute-start.8 = (bf16[1,320,320]{2,1,0:T(8,128)(2,1)S(1)}, bf16[1,320,320]{2,1,0:T(8,128)(2,1)S(1)}, u32[]{:S(2)}, u32[]{:S(2)}) collective-permute-start(bf16[1,320,320]{2,1,0:T(8,128)(2,1)S(1)} %get-tuple-element.33), channel_id=1, source_target_pairs={{0,1},{1,0},{2,3},{3,2},{4,5},{5,4},{6,7},{7,6},{8,9},{9,8},{10,11... | collective-permute-start | bytes 614408 | tf_op jit(solution)/shard_map/ppermute | solution.py:264
  54.1 11.5 %collective-permute-start.9 = (bf16[1,320,320]{2,1,0:T(8,128)(2,1)S(1)}, bf16[1,320,320]{2,1,0:T(8,128)(2,1)S(1)}, u32[]{:S(2)}, u32[]{:S(2)}) collective-permute-start(bf16[1,320,320]{2,1,0:T(8,128)(2,1)S(1)} %get-tuple-element.34), channel_id=1, source_target_pairs={{0,3},{1,2},{2,1},{3,0},{4,7},{5,6},{6,5},{7,4},{8,11},{9,10},{10,... | collective-permute-start | bytes 614408 | tf_op jit(solution)/shard_map/ppermute | solution.py:264
  66.3 7.1 %collective-permute-start.10 = (bf16[8,320]{1,0:T(8,128)(2,1)S(1)}, bf16[8,320]{1,0:T(8,128)(2,1)S(1)}, u32[]{:S(2)}, u32[]{:S(2)}) collective-permute-start(bf16[8,320]{1,0:T(8,128)(2,1)S(1)} %get-tuple-element.35.refs_1_), channel_id=1, source_target_pairs={{0,508},{4,8},{8,4},{12,16},{16,12},{20,24},{24,20},{28,32},{32,28... | collective-permute-start | bytes 15368 | tf_op jit(solution)/shard_map/ppermute | solution.py:22
  68.2 6.0 %collective-permute-start.11 = (bf16[8,320]{1,0:T(8,128)(2,1)S(1)}, bf16[8,320]{1,0:T(8,128)(2,1)S(1)}, u32[]{:S(2)}, u32[]{:S(2)}) collective-permute-start(bf16[8,320]{1,0:T(8,128)(2,1)S(1)} %get-tuple-element.35.refs_1_), channel_id=1, source_target_pairs={{0,4},{4,0},{8,12},{12,8},{16,20},{20,16},{24,28},{28,24},{32,36},... | collective-permute-start | bytes 15368 | tf_op jit(solution)/shard_map/ppermute | solution.py:21
  76.0 9.1 %collective-permute-start.12 = (bf16[8,320]{1,0:T(8,128)(2,1)S(1)}, bf16[8,320]{1,0:T(8,128)(2,1)S(1)}, u32[]{:S(2)}, u32[]{:S(2)}) collective-permute-start(bf16[8,320]{1,0:T(8,128)(2,1)S(1)} %shard_map.106.refs_1_), channel_id=1, source_target_pairs={{0,508},{4,8},{8,4},{12,16},{16,12},{20,24},{24,20},{28,32},{32,28... | collective-permute-start | bytes 15368 | tf_op jit(solution)/shard_map/ppermute | solution.py:22
  77.9 8.0 %collective-permute-start.13 = (bf16[8,320]{1,0:T(8,128)(2,1)S(1)}, bf16[8,320]{1,0:T(8,128)(2,1)S(1)}, u32[]{:S(2)}, u32[]{:S(2)}) collective-permute-start(bf16[8,320]{1,0:T(8,128)(2,1)S(1)} %shard_map.106.refs_1_), channel_id=1, source_target_pairs={{0,4},{4,0},{8,12},{12,8},{16,20},{20,16},{24,28},{28,24},{32,36},... | collective-permute-start | bytes 15368 | tf_op jit(solution)/shard_map/ppermute | solution.py:21
  87.8 6.5 %collective-permute-start.14 = (bf16[16,320]{1,0:T(8,128)(2,1)S(1)}, bf16[16,320]{1,0:T(8,128)(2,1)S(1)}, u32[]{:S(2)}, u32[]{:S(2)}) collective-permute-start(bf16[16,320]{1,0:T(8,128)(2,1)S(1)} %shard_map.107.refs_1_), channel_id=1, source_target_pairs={{0,511},{1,2},{2,1},{3,4},{4,3},{5,6},{6,5},{7,8},{8,7},{9,10},{10... | collective-permute-start | bytes 30728 | tf_op jit(solution)/shard_map/ppermute | solution.py:22
  92.4 4.7 %collective-permute-start.15 = (bf16[16,320]{1,0:T(8,128)(2,1)S(1)}, bf16[16,320]{1,0:T(8,128)(2,1)S(1)}, u32[]{:S(2)}, u32[]{:S(2)}) collective-permute-start(bf16[16,320]{1,0:T(8,128)(2,1)S(1)} %shard_map.107.refs_1_), channel_id=1, source_target_pairs={{0,1},{1,0},{2,3},{3,2},{4,5},{5,4},{6,7},{7,6},{8,9},{9,8},{10,11... | collective-permute-start | bytes 30728 | tf_op jit(solution)/shard_map/ppermute | solution.py:21
  99.4 6.3 %collective-permute-start.16 = (bf16[16,320]{1,0:T(8,128)(2,1)S(1)}, bf16[16,320]{1,0:T(8,128)(2,1)S(1)}, u32[]{:S(2)}, u32[]{:S(2)}) collective-permute-start(bf16[16,320]{1,0:T(8,128)(2,1)S(1)} %shard_map.108.refs_1_), channel_id=1, source_target_pairs={{0,511},{1,2},{2,1},{3,4},{4,3},{5,6},{6,5},{7,8},{8,7},{9,10},{10... | collective-permute-start | bytes 30728 | tf_op jit(solution)/shard_map/ppermute | solution.py:22
  102.6 4.4 %collective-permute-start.17 = (bf16[16,320]{1,0:T(8,128)(2,1)S(1)}, bf16[16,320]{1,0:T(8,128)(2,1)S(1)}, u32[]{:S(2)}, u32[]{:S(2)}) collective-permute-start(bf16[16,320]{1,0:T(8,128)(2,1)S(1)} %shard_map.108.refs_1_), channel_id=1, source_target_pairs={{0,1},{1,0},{2,3},{3,2},{4,5},{5,4},{6,7},{7,6},{8,9},{9,8},{10,11... | collective-permute-start | bytes 30728 | tf_op jit(solution)/shard_map/ppermute | solution.py:21
  109.3 6.9 %collective-permute-start.18 = (bf16[16,320]{1,0:T(8,128)(2,1)S(1)}, bf16[16,320]{1,0:T(8,128)(2,1)S(1)}, u32[]{:S(2)}, u32[]{:S(2)}) collective-permute-start(bf16[16,320]{1,0:T(8,128)(2,1)S(1)} %shard_map.109.refs_1_), channel_id=1, source_target_pairs={{0,511},{1,2},{2,1},{3,4},{4,3},{5,6},{6,5},{7,8},{8,7},{9,10},{10... | collective-permute-start | bytes 30728 | tf_op jit(solution)/shard_map/ppermute | solution.py:22
  120.9 8.5 %collective-permute-start.20 = (bf16[16,320]{1,0:T(8,128)(2,1)S(1)}, bf16[16,320]{1,0:T(8,128)(2,1)S(1)}, u32[]{:S(2)}, u32[]{:S(2)}) collective-permute-start(bf16[16,320]{1,0:T(8,128)(2,1)S(1)} %get-tuple-element.39.refs_1_), channel_id=1, source_target_pairs={{0,511},{1,2},{2,1},{3,4},{4,3},{5,6},{6,5},{7,8},{8,7},{9,10},{10... | collective-permute-start | bytes 30728 | tf_op jit(solution)/shard_map/ppermute | solution.py:22
  140.7 12.7 %collective-permute-start.22 = (bf16[8,320]{1,0:T(8,128)(2,1)S(1)}, bf16[8,320]{1,0:T(8,128)(2,1)S(1)}, u32[]{:S(2)}, u32[]{:S(2)}) collective-permute-start(bf16[8,320]{1,0:T(8,128)(2,1)S(1)} %get-tuple-element.41.refs_1_), channel_id=1, source_target_pairs={{0,508},{4,8},{8,4},{12,16},{16,12},{20,24},{24,20},{28,32},{32,28... | collective-permute-start | bytes 15368 | tf_op jit(solution)/shard_map/ppermute | solution.py:22
  142.7 11.5 %collective-permute-start.23 = (bf16[8,320]{1,0:T(8,128)(2,1)S(1)}, bf16[8,320]{1,0:T(8,128)(2,1)S(1)}, u32[]{:S(2)}, u32[]{:S(2)}) collective-permute-start(bf16[8,320]{1,0:T(8,128)(2,1)S(1)} %get-tuple-element.41.refs_1_), channel_id=1, source_target_pairs={{0,4},{4,0},{8,12},{12,8},{16,20},{20,16},{24,28},{28,24},{32,36},... | collective-permute-start | bytes 15368 | tf_op jit(solution)/shard_map/ppermute | solution.py:21
  156.0 8.5 %collective-permute-start.24 = (bf16[8,320]{1,0:T(8,128)(2,1)S(1)}, bf16[8,320]{1,0:T(8,128)(2,1)S(1)}, u32[]{:S(2)}, u32[]{:S(2)}) collective-permute-start(bf16[8,320]{1,0:T(8,128)(2,1)S(1)} %shard_map.113.refs_1_), channel_id=1, source_target_pairs={{0,508},{4,8},{8,4},{12,16},{16,12},{20,24},{24,20},{28,32},{32,28... | collective-permute-start | bytes 15368 | tf_op jit(solution)/shard_map/ppermute | solution.py:22
  158.0 7.3 %collective-permute-start.25 = (bf16[8,320]{1,0:T(8,128)(2,1)S(1)}, bf16[8,320]{1,0:T(8,128)(2,1)S(1)}, u32[]{:S(2)}, u32[]{:S(2)}) collective-permute-start(bf16[8,320]{1,0:T(8,128)(2,1)S(1)} %shard_map.113.refs_1_), channel_id=1, source_target_pairs={{0,4},{4,0},{8,12},{12,8},{16,20},{20,16},{24,28},{28,24},{32,36},... | collective-permute-start | bytes 15368 | tf_op jit(solution)/shard_map/ppermute | solution.py:21
  (6 other events, 68.3 us)

commit v8 on v5

--- a/solution.py
+++ b/solution.py
@@ -47,11 +47,10 @@
     )
 
 
-def coupling(states, index, operators, lift):
+def coupling(states, index, operators, pick, lift):
     count = states[0].shape[0]
     pool = jnp.concatenate([state.astype(jnp.float32) for state in states], axis=0).astype(jnp.bfloat16)
-    traces = lax.dot_general(pool, lift, (((1,), (1,)), ((), ())), preferred_element_type=jnp.float32)
-    traces = traces.astype(jnp.bfloat16)
+    traces = jnp.dot(pool, pick, preferred_element_type=jnp.float32).astype(jnp.bfloat16)
     column = lax.broadcasted_iota(jnp.int32, (count, pool.shape[0]), 1)
     face_rows, kinds = [], []
     for k in range(6):
@@ -73,24 +72,23 @@
     return lifted[:count] + lifted[count:]
 
 
-def apply_inverse(blocks, vector):
+def apply_inverse(blocks, vector, turned=False):
+    contracted = (((1,), (0 if turned else 1,)), ((), ()))
     row = lax.broadcasted_iota(jnp.int32, vector.shape, 0)
     result = jnp.zeros(vector.shape, jnp.float32)
     first = 0
     for block in blocks:
         for e in range(block.shape[0]):
-            product = lax.dot_general(
-                vector, block[e], (((1,), (1,)), ((), ())), preferred_element_type=jnp.float32
-            )
+            product = lax.dot_general(vector, block[e], contracted, preferred_element_type=jnp.float32)
             result = jnp.where(row == first + e, product, result)
         first += block.shape[0]
     return result
 
 
-def pool_rows(links, count, position, turn=0):
+def pool_rows(links, count, position):
     shift = count.bit_length() - 1
-    owner, within = links >> shift, (links & (count - 1)) ^ turn
-    place = jnp.where(owner == position, 1, jnp.where(owner == (position ^ 1), 2, 0))
+    owner, within = links >> shift, links & (count - 1)
+    place = jnp.where(owner == position, 1, jnp.where(owner == (position ^ 1), 0, 2))
     return jnp.where(links >= 0, place * count + within, -1)
 
 
@@ -133,16 +131,15 @@
 
     own = coarse_links_ref.shape[0]
     count = own * tele_size
+    rows = pool_rows(coarse_links_ref[...], count, column).astype(jnp.float32)
     kinds = coarse_faces_ref[...].astype(jnp.float32)
     lists_ref[...] = jnp.zeros(lists_ref.shape, jnp.float32)
     row = lax.broadcasted_iota(jnp.int32, (count, kinds.shape[1]), 0)
-    for t in range(tele_size):
-        rows = pool_rows(coarse_links_ref[...], count, column, own * t).astype(jnp.float32)
-        for part, values in enumerate((rows, kinds)):
-            placed = jnp.zeros(row.shape, jnp.float32)
-            for c in range(own):
-                placed = jnp.where(row == ((own * tele + c) ^ (own * t)), values[c : c + 1], placed)
-            lists_ref[t, :, part * 6 : part * 6 + 6] = placed
+    for part, values in enumerate((rows, kinds)):
+        placed = jnp.zeros(row.shape, jnp.float32)
+        for c in range(own):
+            placed = jnp.where(row == own * tele + c, values[c : c + 1], placed)
+        lists_ref[:, part * 6 : part * 6 + 6] = placed
 
     types, size, _ = operators_in_ref.shape
     unit = lax.broadcasted_iota(jnp.int32, (LANES, size), 0) == lax.broadcasted_iota(jnp.int32, (LANES, size), 1)
@@ -155,22 +152,31 @@
         operators_ref[q * LANES : (q + 1) * LANES, :size] = turned.astype(jnp.bfloat16)
 
 
+def turn_kernel(in_ref, out_ref):
+    size = in_ref.shape[1]
+    unit = lax.broadcasted_iota(jnp.int32, (size, size), 0) == lax.broadcasted_iota(jnp.int32, (size, size), 1)
+    unit = jnp.where(unit, 1.0, 0.0).astype(jnp.bfloat16)
+    for e in range(in_ref.shape[0]):
+        turned = lax.dot_general(unit, in_ref[e], (((1,), (1,)), ((), ())), preferred_element_type=jnp.float32)
+        out_ref[e] = turned.astype(jnp.bfloat16)
+
+
 def take_kernel(before_ref, after_ref, low_ref, high_ref):
     low_ref[...] = before_ref[0:1]
     high_ref[...] = after_ref[1:2]
 
 
-def sweep(refs, blocks):
-    prev_ref, own_ref, next_ref, index_ref, operators_ref, lift_ref, right_ref = refs
+def sweep(refs, blocks, turned=False):
+    prev_ref, own_ref, next_ref, index_ref, operators_ref, pick_ref, lift_ref, right_ref = refs
     states = [prev_ref[...], own_ref[...], next_ref[...]]
-    coupled = coupling(states, index_ref[...], operators_ref[...], lift_ref[...])
+    coupled = coupling(states, index_ref[...], operators_ref[...], pick_ref[...], lift_ref[...])
     lowered = (right_ref[...] - coupled).astype(jnp.bfloat16)
-    return apply_inverse(blocks, lowered), lowered
-
-
-def sweep_kernel(*refs, blocks):
-    result, lowered = sweep(refs[:7], refs[7 : 7 + blocks])
-    outs = refs[7 + blocks :]
+    return apply_inverse(blocks, lowered, turned), lowered
+
+
+def sweep_kernel(*refs, blocks, turned=False):
+    result, lowered = sweep(refs[:8], refs[8 : 8 + blocks], turned)
+    outs = refs[8 + blocks :]
     outs[0][...] = result.astype(jnp.bfloat16)
     if len(outs) > 1:
         outs[1][...] = result
@@ -178,10 +184,10 @@
 
 
 def restrict_kernel(
-    prev_ref, own_ref, next_ref, index_ref, operators_ref, lift_ref, lowered_ref, target_ref, lists_ref, out_ref
+    prev_ref, own_ref, next_ref, index_ref, operators_ref, pick_ref, lift_ref, lowered_ref, target_ref, lists_ref, out_ref
 ):
     states = [prev_ref[...], own_ref[...], next_ref[...]]
-    coupled = coupling(states, index_ref[...], operators_ref[...], lift_ref[...])
+    coupled = coupling(states, index_ref[...], operators_ref[...], pick_ref[...], lift_ref[...])
     residual = lowered_ref[...].astype(jnp.float32) - coupled
     tele_size, rows, dofs = out_ref.shape[0], out_ref.shape[1], residual.shape[1]
     shape = (tele_size * rows, residual.shape[0])
@@ -189,9 +195,11 @@
     element = (row & (rows - 1)) ^ ((row >> (rows.bit_length() - 1)) * (rows // tele_size))
     member = jnp.where((target_ref[...] & (rows - 1)) == element, 1.0, 0.0).astype(jnp.bfloat16)
     partial = exact_dot(member, residual)
+    own = rows // tele_size
     for t in range(tele_size):
         out_ref[t, :, :dofs] = partial[t * rows : (t + 1) * rows]
-        out_ref[t, :, dofs:] = lists_ref[t]
+        for s in range(tele_size):
+            out_ref[t, s * own : (s + 1) * own, dofs:] = lists_ref[(s ^ t) * own : ((s ^ t) + 1) * own]
 
 
 def coarse_first_kernel(*refs, blocks):
@@ -202,13 +210,16 @@
     dofs = restricted_ref.shape[1]
     restricted = total[:, :dofs]
     restricted_ref[...] = restricted
-    index_ref[...] = total[:, dofs:].astype(jnp.int32)
+    lists = total[:, dofs:].astype(jnp.int32)
+    turn = lax.axis_index("tele") * (total.shape[0] // parts_ref.shape[0])
+    turned = (lax.broadcasted_iota(jnp.int32, lists.shape, 1) < 6) & (lists >= 0)
+    index_ref[...] = jnp.where(turned, lists ^ turn, lists)
     state_ref[...] = apply_inverse(inverses, restricted.astype(jnp.bfloat16)).astype(jnp.bfloat16)
 
 
 def correct_kernel(*refs, blocks):
-    coarse, _ = sweep(refs[:7], refs[7 : 7 + blocks])
-    target_ref, solution_ref, out_ref = refs[7 + blocks :]
+    coarse, _ = sweep(refs[:8], refs[8 : 8 + blocks])
+    target_ref, solution_ref, out_ref = refs[8 + blocks :]
     rows, fine = coarse.shape[0], solution_ref.shape[0]
     turn = lax.axis_index("tele") * (rows // lax.axis_size("tele"))
     member = ((target_ref[...] & (rows - 1)) ^ turn) == lax.broadcasted_iota(jnp.int32, (rows, fine), 0)
@@ -238,7 +249,7 @@
         out_specs=[vmem] * len(shapes),
         scratch_shapes=scratch,
         compiler_params=pltpu.CompilerParams(vmem_limit_bytes=20 << 20),
-        cost_estimate=pl.CostEstimate(flops=1 << 28, bytes_accessed=moved, transcendentals=0),
+        cost_estimate=pl.CostEstimate(flops=1 << 32, bytes_accessed=moved, transcendentals=0),
     )(*operands)
     return result[0] if single else result
 
@@ -264,7 +275,8 @@
     def across(block, bits):
         return lax.ppermute(block, "tele", [(i, i ^ bits) for i in range(tele_size)])
 
-    lift = jnp.asarray(face_table(), bf16)
+    table = face_table()
+    pick, lift = jnp.asarray(table.T.copy(), bf16), jnp.asarray(table, bf16)
     target = agglomerate[None, :]
     operands = (
         right_side,
@@ -280,7 +292,7 @@
         [
             ((fine_rows, dofs), bf16),
             ((fine_rows, 12), i32),
-            ((tele_size, coarse_rows, spare), f32),
+            ((coarse_rows, spare), f32),
             ((types * LANES, LANES), bf16),
             (fine_inverse.shape, bf16),
         ],
@@ -290,38 +302,45 @@
         scratch=[pltpu.VMEM(o.shape, o.dtype) for o in operands[:-1]]
         + [pltpu.SemaphoreType.DMA((len(operands),)), pltpu.SemaphoreType.DMA((4,))],
     )
-    shared = (operators, lift)
-    own, state = lax.optimization_barrier((coarse_inverse, state))
-    near, other = across(own, 1), across(own, tele_size - 1)
+    shared = (operators, pick, lift)
 
     def halo(block, axis):
         inner, outer = swapped(block, axis)
-        return outer, block, inner
+        return inner, block, outer
 
     both = ("fine", "tele")
     for cycle in range(CYCLES):
         for sweep in range(SWEEPS):
             if cycle == 0 and sweep == 0:
                 continue
+            inner, own, outer = halo(state, both)
+            if cycle == 0 and sweep == 1:
+                sent, inner = lax.optimization_barrier((coarse_inverse, inner))
+                near, other = across(sent, 1), across(sent, tele_size - 1)
+            if cycle == 0 and sweep == 2:
+                near, other, outer = lax.optimization_barrier((near, other, outer))
+                far_low, far_high = run(take_kernel, [((1,) + near.shape[1:], bf16)] * 2, other, near)
+                far_low, far_high = across(far_low, 1), across(far_high, tele_size - 1)
+                blocks = (coarse_inverse, near, far_low, far_high, other)
+            turned = (cycle, sweep) != (0, 1)
+            if cycle == 0 and sweep == 2:
+                inverse = run(turn_kernel, (inverse.shape, bf16), inverse, held=(0,), keep=(state,), pinned=(0,))
             outs = [((fine_rows, dofs), bf16)]
             if sweep == SWEEPS - 1:
                 outs += [((fine_rows, dofs), f32), ((fine_rows, dofs), bf16)]
             result = run(
-                functools.partial(sweep_kernel, blocks=1),
+                functools.partial(sweep_kernel, blocks=1, turned=turned),
                 outs,
-                *halo(state, both),
+                inner,
+                own,
+                outer,
                 fine_index,
                 *shared,
                 right_side,
                 inverse,
-                held=(5, 7),
+                held=(5, 6, 8),
             )
             state = result[0]
-            if cycle == 0 and sweep == 1:
-                near, other, state = lax.optimization_barrier((near, other, state))
-                far_low, far_high = run(take_kernel, [((1,) + near.shape[1:], bf16)] * 2, other, near)
-                far_low, far_high = across(far_low, 1), across(far_high, tele_size - 1)
-                blocks = (coarse_inverse, near, far_low, far_high, other)
         solution, lowered = result[1], result[2]
         parts = run(
             restrict_kernel,
@@ -332,7 +351,7 @@
             lowered,
             target,
             lists,
-            held=(5,),
+            held=(5, 6),
         )
         parts = lax.all_to_all(parts, "tele", 0, 0, tiled=True)
         restricted, coarse, coarse_index = run(
@@ -351,7 +370,7 @@
                 *shared,
                 restricted,
                 *blocks,
-                held=(5, *range(7, 7 + len(blocks))),
+                held=(5, 6, *range(8, 8 + len(blocks))),
             )[0]
         last = cycle == CYCLES - 1
         state = run(
@@ -364,7 +383,7 @@
             *blocks,
             target,
             solution,
-            held=(5, *range(7, 7 + len(blocks))),
+            held=(5, 6, *range(8, 8 + len(blocks))),
         )
     return state
 

time: 171 us -> 162 us (0.947)
  waiting for transfers between devices: 21.8 us -> 13.4 us
  starting transfers between devices: 111 us -> 108 us
    ppermute x11, waiting for transfers between devices: 5.98 us -> 1.23 us  [swapped(): lax.ppermute(block, axis, [(i, (i - 1 if i % 2 == 0 else i + 1) % count)...]
    ppermute x11, waiting for transfers between devices: 15.8 us -> 12.2 us  [swapped(): inner = lax.ppermute(block, axis, [(i, i ^ 1) for i in range(count)])]
    pallas_call x15 -> x16, Pallas kernels: 23.8 us -> 23.4 us  [run(): pl.pallas_call(body, out_shape=[pltpu.VMEM(s, d) if i in pinned else jax....]
  transfers between devices with their start and end apart: 26 -> 26, of which waited for: 14 -> 10; matrix products, arithmetic and copies ran while one was open for 0% -> 0% of each run, Pallas kernels for 3% -> 3%
where the time goes in v8:
time: 162 us; the launch traced here: 161 us
  starting transfers between devices  108 us (67%)
  Pallas kernels  23.4 us (14%)
  blocking collectives  14.9 us (9%)
  waiting for transfers between devices  13.4 us (8%)
    ppermute x11, starting transfers between devices, swapped(): lax.ppermute(block, axis, [(i, (i - 1 if i % 2 == 0 else i + 1) % count)...  48.9 us
    ppermute x11, starting transfers between devices, swapped(): inner = lax.ppermute(block, axis, [(i, i ^ 1) for i in range(count)])  48.1 us
    pallas_call x16, Pallas kernels, run(): pl.pallas_call(body, out_shape=[pltpu.VMEM(s, d) if i in pinned else jax....  23.4 us
    all_to_all x2, blocking collectives, shards(): parts = lax.all_to_all(parts, 'tele', 0, 0, tiled=True)  14.9 us
    ppermute x11, waiting for transfers between devices, swapped(): inner = lax.ppermute(block, axis, [(i, i ^ 1) for i in range(count)])  12.2 us
    ppermute x4, starting transfers between devices, across(): lax.ppermute(block, 'tele', [(i, i ^ bits) for i in range(tele_size)])  11.4 us
  transfers between devices with their start and end apart: 26, of which 10 were waited for; matrix products, arithmetic and copies ran while one was open for 0% of the time, Pallas kernels for 3%

profile of v8, /device:TPU:1, one launch (start us, length us, event | category | flops | bytes accessed | tf_op | source)
XLA Modules:
  0.0 160.7 jit_solution(10962411406487640100)
XLA Ops:
  0.0 3.4 %shard_map.109 = (bf16[16,320]{1,0:T(8,128)(2,1)S(1)}, s32[16,12]{1,0:T(8,128)S(1)}, f32[8,64]{1,0:T(8,128)S(1)}, bf16[3072,128]{1,0:T(8,128)(2,1)S(1)}, bf16[16,320,320]{2,1,0:T(8,128)(2,1)S(1)}) custom-call(f32[16,320]{1,0:T(8,128)} %refs_7_.9, s32[6,16]{1,0:T(8,128)} %bitcast.7, s32[6,16]{1,0:T(8,128)} %bitcast.8, s32[2,6]{1,0:T(2,128)} %refs_3_.1, ...), custom_call_target="tpu_custom_call" | custom-call | flops 4294967296 | bytes 3605344 | tf_op jit(solution)/shard_map/pallas_call | solution.py:245
  3.5 3.9 %collective-permute-start = (bf16[16,320]{1,0:T(8,128)(2,1)S(1)}, bf16[16,320]{1,0:T(8,128)(2,1)S(1)}, u32[]{:S(2)}, u32[]{:S(2)}) collective-permute-start(bf16[16,320]{1,0:T(8,128)(2,1)S(1)} %get-tuple-element.29.refs_1_), channel_id=1, source_target_pairs={{0,1},{1,0},{2,3},{3,2},{4,5},{5,4},{6,7},{7,6},{8,9},{9,8},{10,11... | collective-permute-start | bytes 30728 | tf_op jit(solution)/shard_map/ppermute | solution.py:21
  7.4 4.6 %collective-permute-start.1 = (bf16[16,320]{1,0:T(8,128)(2,1)S(1)}, bf16[16,320]{1,0:T(8,128)(2,1)S(1)}, u32[]{:S(2)}, u32[]{:S(2)}) collective-permute-start(bf16[16,320]{1,0:T(8,128)(2,1)S(1)} %get-tuple-element.29.refs_1_), channel_id=1, source_target_pairs={{0,511},{1,2},{2,1},{3,4},{4,3},{5,6},{6,5},{7,8},{8,7},{9,10},{10... | collective-permute-start | bytes 30728 | tf_op jit(solution)/shard_map/ppermute | solution.py:22
  12.0 4.1 %collective-permute-start.4 = (bf16[2,320,320]{2,1,0:T(8,128)(2,1)S(1)}, bf16[2,320,320]{2,1,0:T(8,128)(2,1)S(1)}, u32[]{:S(2)}, u32[]{:S(2)}) collective-permute-start(bf16[2,320,320]{2,1,0:T(8,128)(2,1)S(1)} %copy-done), channel_id=1, source_target_pairs={{0,3},{1,2},{2,1},{3,0},{4,7},{5,6},{6,5},{7,4},{8,11},{9,10},{10,... | collective-permute-start | bytes 1228808 | tf_op jit(solution)/shard_map/ppermute | solution.py:276
  20.1 13.5 %collective-permute-start.5 = (bf16[16,320]{1,0:T(8,128)(2,1)S(1)}, bf16[16,320]{1,0:T(8,128)(2,1)S(1)}, u32[]{:S(2)}, u32[]{:S(2)}) collective-permute-start(bf16[16,320]{1,0:T(8,128)(2,1)S(1)} %shard_map.110.refs_1_), channel_id=1, source_target_pairs={{0,511},{1,2},{2,1},{3,4},{4,3},{5,6},{6,5},{7,8},{8,7},{9,10},{10... | collective-permute-start | bytes 30728 | tf_op jit(solution)/shard_map/ppermute | solution.py:22
  35.5 2.7 %shard_map.111.refs_8_ = bf16[16,320,320]{2,1,0:T(8,128)(2,1)S(1)} custom-call(bf16[16,320,320]{2,1,0:T(8,128)(2,1)S(1)} %get-tuple-element.33.refs_8_.refs_0_, bf16[16,320]{1,0:T(8,128)(2,1)S(1)} %shard_map.110.refs_1_), custom_call_target="tpu_custom_call" | custom-call | flops 4294967296 | bytes 3276800 | tf_op jit(solution)/shard_map/pallas_call | solution.py:245
  39.7 4.0 %collective-permute-start.7 = (bf16[16,320]{1,0:T(8,128)(2,1)S(1)}, bf16[16,320]{1,0:T(8,128)(2,1)S(1)}, u32[]{:S(2)}, u32[]{:S(2)}) collective-permute-start(bf16[16,320]{1,0:T(8,128)(2,1)S(1)} %get-tuple-element.36.refs_1_), channel_id=1, source_target_pairs={{0,511},{1,2},{2,1},{3,4},{4,3},{5,6},{6,5},{7,8},{8,7},{9,10},{10... | collective-permute-start | bytes 30728 | tf_op jit(solution)/shard_map/ppermute | solution.py:22
  45.7 3.4 %collective-permute-start.8 = (bf16[1,320,320]{2,1,0:T(8,128)(2,1)S(1)}, bf16[1,320,320]{2,1,0:T(8,128)(2,1)S(1)}, u32[]{:S(2)}, u32[]{:S(2)}) collective-permute-start(bf16[1,320,320]{2,1,0:T(8,128)(2,1)S(1)} %get-tuple-element.41), channel_id=1, source_target_pairs={{0,1},{1,0},{2,3},{3,2},{4,5},{5,4},{6,7},{7,6},{8,9},{9,8},{10,11... | collective-permute-start | bytes 614408 | tf_op jit(solution)/shard_map/ppermute | solution.py:276
  52.1 8.2 %all_to_all.10.refs_0_ = f32[4,8,384]{2,1,0:T(8,128)S(1)} all-to-all(f32[4,8,384]{2,1,0:T(8,128)S(1)} %shard_map.113), channel_id=1, replica_groups=mesh['fine'=128,'tele'=4] {'tele'}, dimensions={0} | all-to-all | bytes 98304 | tf_op jit(solution)/shard_map/all_to_all | solution.py:356
  62.9 8.7 %collective-permute-start.10 = (bf16[8,320]{1,0:T(8,128)(2,1)S(1)}, bf16[8,320]{1,0:T(8,128)(2,1)S(1)}, u32[]{:S(2)}, u32[]{:S(2)}) collective-permute-start(bf16[8,320]{1,0:T(8,128)(2,1)S(1)} %get-tuple-element.43.refs_1_), channel_id=1, source_target_pairs={{0,4},{4,0},{8,12},{12,8},{16,20},{20,16},{24,28},{28,24},{32,36},... | collective-permute-start | bytes 15368 | tf_op jit(solution)/shard_map/ppermute | solution.py:21
  75.7 6.5 %collective-permute-start.12 = (bf16[8,320]{1,0:T(8,128)(2,1)S(1)}, bf16[8,320]{1,0:T(8,128)(2,1)S(1)}, u32[]{:S(2)}, u32[]{:S(2)}) collective-permute-start(bf16[8,320]{1,0:T(8,128)(2,1)S(1)} %shard_map.116.refs_1_), channel_id=1, source_target_pairs={{0,4},{4,0},{8,12},{12,8},{16,20},{20,16},{24,28},{28,24},{32,36},... | collective-permute-start | bytes 15368 | tf_op jit(solution)/shard_map/ppermute | solution.py:21
  84.5 4.6 %collective-permute-start.15 = (bf16[16,320]{1,0:T(8,128)(2,1)S(1)}, bf16[16,320]{1,0:T(8,128)(2,1)S(1)}, u32[]{:S(2)}, u32[]{:S(2)}) collective-permute-start(bf16[16,320]{1,0:T(8,128)(2,1)S(1)} %shard_map.117.refs_1_), channel_id=1, source_target_pairs={{0,511},{1,2},{2,1},{3,4},{4,3},{5,6},{6,5},{7,8},{8,7},{9,10},{10... | collective-permute-start | bytes 30728 | tf_op jit(solution)/shard_map/ppermute | solution.py:22
  91.0 2.8 %collective-permute-done.14.refs_0_ = bf16[16,320]{1,0:T(8,128)(2,1)S(1)} collective-permute-done((bf16[16,320]{1,0:T(8,128)(2,1)S(1)}, bf16[16,320]{1,0:T(8,128)(2,1)S(1)}, u32[]{:S(2)}, u32[]{:S(2)}) %collective-permute-start.14) | collective-permute-done | bytes 10272 | tf_op jit(solution)/shard_map/ppermute | solution.py:21
  95.2 3.1 %collective-permute-start.17 = (bf16[16,320]{1,0:T(8,128)(2,1)S(1)}, bf16[16,320]{1,0:T(8,128)(2,1)S(1)}, u32[]{:S(2)}, u32[]{:S(2)}) collective-permute-start(bf16[16,320]{1,0:T(8,128)(2,1)S(1)} %shard_map.118.refs_1_), channel_id=1, source_target_pairs={{0,511},{1,2},{2,1},{3,4},{4,3},{5,6},{6,5},{7,8},{8,7},{9,10},{10... | collective-permute-start | bytes 30728 | tf_op jit(solution)/shard_map/ppermute | solution.py:22
  104.2 4.9 %collective-permute-start.19 = (bf16[16,320]{1,0:T(8,128)(2,1)S(1)}, bf16[16,320]{1,0:T(8,128)(2,1)S(1)}, u32[]{:S(2)}, u32[]{:S(2)}) collective-permute-start(bf16[16,320]{1,0:T(8,128)(2,1)S(1)} %shard_map.119.refs_1_), channel_id=1, source_target_pairs={{0,511},{1,2},{2,1},{3,4},{4,3},{5,6},{6,5},{7,8},{8,7},{9,10},{10... | collective-permute-start | bytes 30728 | tf_op jit(solution)/shard_map/ppermute | solution.py:22
  109.1 2.1 %collective-permute-start.18 = (bf16[16,320]{1,0:T(8,128)(2,1)S(1)}, bf16[16,320]{1,0:T(8,128)(2,1)S(1)}, u32[]{:S(2)}, u32[]{:S(2)}) collective-permute-start(bf16[16,320]{1,0:T(8,128)(2,1)S(1)} %shard_map.119.refs_1_), channel_id=1, source_target_pairs={{0,1},{1,0},{2,3},{3,2},{4,5},{5,4},{6,7},{7,6},{8,9},{9,8},{10,11... | collective-permute-start | bytes 30728 | tf_op jit(solution)/shard_map/ppermute | solution.py:21
  111.2 2.3 %collective-permute-done.18.refs_0_ = bf16[16,320]{1,0:T(8,128)(2,1)S(1)} collective-permute-done((bf16[16,320]{1,0:T(8,128)(2,1)S(1)}, bf16[16,320]{1,0:T(8,128)(2,1)S(1)}, u32[]{:S(2)}, u32[]{:S(2)}) %collective-permute-start.18) | collective-permute-done | bytes 10272 | tf_op jit(solution)/shard_map/ppermute | solution.py:21
  115.0 6.5 %collective-permute-start.21 = (bf16[16,320]{1,0:T(8,128)(2,1)S(1)}, bf16[16,320]{1,0:T(8,128)(2,1)S(1)}, u32[]{:S(2)}, u32[]{:S(2)}) collective-permute-start(bf16[16,320]{1,0:T(8,128)(2,1)S(1)} %get-tuple-element.47.refs_1_), channel_id=1, source_target_pairs={{0,511},{1,2},{2,1},{3,4},{4,3},{5,6},{6,5},{7,8},{8,7},{9,10},{10... | collective-permute-start | bytes 30728 | tf_op jit(solution)/shard_map/ppermute | solution.py:22
  123.4 2.5 %collective-permute-done.20.refs_0_ = bf16[16,320]{1,0:T(8,128)(2,1)S(1)} collective-permute-done((bf16[16,320]{1,0:T(8,128)(2,1)S(1)}, bf16[16,320]{1,0:T(8,128)(2,1)S(1)}, u32[]{:S(2)}, u32[]{:S(2)}) %collective-permute-start.20) | collective-permute-done | bytes 10272 | tf_op jit(solution)/shard_map/ppermute | solution.py:21
  126.8 6.7 %all_to_all.11.refs_0_ = f32[4,8,384]{2,1,0:T(8,128)S(1)} all-to-all(f32[4,8,384]{2,1,0:T(8,128)S(1)} %shard_map.121), channel_id=1, replica_groups=mesh['fine'=128,'tele'=4] {'tele'}, dimensions={0} | all-to-all | bytes 98304 | tf_op jit(solution)/shard_map/all_to_all | solution.py:356
  134.2 2.0 %collective-permute-start.23 = (bf16[8,320]{1,0:T(8,128)(2,1)S(1)}, bf16[8,320]{1,0:T(8,128)(2,1)S(1)}, u32[]{:S(2)}, u32[]{:S(2)}) collective-permute-start(bf16[8,320]{1,0:T(8,128)(2,1)S(1)} %get-tuple-element.49.refs_1_), channel_id=1, source_target_pairs={{0,508},{4,8},{8,4},{12,16},{16,12},{20,24},{24,20},{28,32},{32,28... | collective-permute-start | bytes 15368 | tf_op jit(solution)/shard_map/ppermute | solution.py:22
  136.2 11.0 %collective-permute-start.22 = (bf16[8,320]{1,0:T(8,128)(2,1)S(1)}, bf16[8,320]{1,0:T(8,128)(2,1)S(1)}, u32[]{:S(2)}, u32[]{:S(2)}) collective-permute-start(bf16[8,320]{1,0:T(8,128)(2,1)S(1)} %get-tuple-element.49.refs_1_), channel_id=1, source_target_pairs={{0,4},{4,0},{8,12},{12,8},{16,20},{20,16},{24,28},{28,24},{32,36},... | collective-permute-start | bytes 15368 | tf_op jit(solution)/shard_map/ppermute | solution.py:21
  151.4 6.3 %collective-permute-start.24 = (bf16[8,320]{1,0:T(8,128)(2,1)S(1)}, bf16[8,320]{1,0:T(8,128)(2,1)S(1)}, u32[]{:S(2)}, u32[]{:S(2)}) collective-permute-start(bf16[8,320]{1,0:T(8,128)(2,1)S(1)} %shard_map.123.refs_1_), channel_id=1, source_target_pairs={{0,4},{4,0},{8,12},{12,8},{16,20},{20,16},{24,28},{28,24},{32,36},... | collective-permute-start | bytes 15368 | tf_op jit(solution)/shard_map/ppermute | solution.py:21
  158.5 2.1 %shard_map.124 = f32[16,320]{1,0:T(8,128)} custom-call(bf16[8,320]{1,0:T(8,128)(2,1)S(1)} %collective-permute-done.24.refs_0_, bf16[8,320]{1,0:T(8,128)(2,1)S(1)} %shard_map.123.refs_1_, bf16[8,320]{1,0:T(8,128)(2,1)S(1)} %collective-permute-done.25.refs_2_, s32[8,64]{1,0:T(8,128)S(1)} %get-tuple-element.50.refs_3_, ...), custom_call_target="tpu_custom_call" | custom-call | flops 4294967296 | bytes 3456064 | tf_op jit(solution)/shard_map/pallas_call | solution.py:245
  (56 shorter events, 40.2 us)
Async XLA Ops:
  3.5 8.5 %collective-permute-start = (bf16[16,320]{1,0:T(8,128)(2,1)S(1)}, bf16[16,320]{1,0:T(8,128)(2,1)S(1)}, u32[]{:S(2)}, u32[]{:S(2)}) collective-permute-start(bf16[16,320]{1,0:T(8,128)(2,1)S(1)} %get-tuple-element.29.refs_1_), channel_id=1, source_target_pairs={{0,1},{1,0},{2,3},{3,2},{4,5},{5,4},{6,7},{7,6},{8,9},{9,8},{10,11... | collective-permute-start | bytes 30728 | tf_op jit(solution)/shard_map/ppermute | solution.py:21
  7.4 10.7 %collective-permute-start.1 = (bf16[16,320]{1,0:T(8,128)(2,1)S(1)}, bf16[16,320]{1,0:T(8,128)(2,1)S(1)}, u32[]{:S(2)}, u32[]{:S(2)}) collective-permute-start(bf16[16,320]{1,0:T(8,128)(2,1)S(1)} %get-tuple-element.29.refs_1_), channel_id=1, source_target_pairs={{0,511},{1,2},{2,1},{3,4},{4,3},{5,6},{6,5},{7,8},{8,7},{9,10},{10... | collective-permute-start | bytes 30728 | tf_op jit(solution)/shard_map/ppermute | solution.py:22
  12.0 26.2 %collective-permute-start.4 = (bf16[2,320,320]{2,1,0:T(8,128)(2,1)S(1)}, bf16[2,320,320]{2,1,0:T(8,128)(2,1)S(1)}, u32[]{:S(2)}, u32[]{:S(2)}) collective-permute-start(bf16[2,320,320]{2,1,0:T(8,128)(2,1)S(1)} %copy-done), channel_id=1, source_target_pairs={{0,3},{1,2},{2,1},{3,0},{4,7},{5,6},{6,5},{7,4},{8,11},{9,10},{10,... | collective-permute-start | bytes 1228808 | tf_op jit(solution)/shard_map/ppermute | solution.py:276
  16.1 22.1 %collective-permute-start.3 = (bf16[2,320,320]{2,1,0:T(8,128)(2,1)S(1)}, bf16[2,320,320]{2,1,0:T(8,128)(2,1)S(1)}, u32[]{:S(2)}, u32[]{:S(2)}) collective-permute-start(bf16[2,320,320]{2,1,0:T(8,128)(2,1)S(1)} %copy-done), channel_id=1, source_target_pairs={{0,1},{1,0},{2,3},{3,2},{4,5},{5,4},{6,7},{7,6},{8,9},{9,8},{10,11... | collective-permute-start | bytes 1228808 | tf_op jit(solution)/shard_map/ppermute | solution.py:276
  20.1 18.1 %collective-permute-start.5 = (bf16[16,320]{1,0:T(8,128)(2,1)S(1)}, bf16[16,320]{1,0:T(8,128)(2,1)S(1)}, u32[]{:S(2)}, u32[]{:S(2)}) collective-permute-start(bf16[16,320]{1,0:T(8,128)(2,1)S(1)} %shard_map.110.refs_1_), channel_id=1, source_target_pairs={{0,511},{1,2},{2,1},{3,4},{4,3},{5,6},{6,5},{7,8},{8,7},{9,10},{10... | collective-permute-start | bytes 30728 | tf_op jit(solution)/shard_map/ppermute | solution.py:22
  33.6 4.7 %collective-permute-start.2 = (bf16[16,320]{1,0:T(8,128)(2,1)S(1)}, bf16[16,320]{1,0:T(8,128)(2,1)S(1)}, u32[]{:S(2)}, u32[]{:S(2)}) collective-permute-start(bf16[16,320]{1,0:T(8,128)(2,1)S(1)} %shard_map.110.refs_1_), channel_id=1, source_target_pairs={{0,1},{1,0},{2,3},{3,2},{4,5},{5,4},{6,7},{7,6},{8,9},{9,8},{10,11... | collective-permute-start | bytes 30728 | tf_op jit(solution)/shard_map/ppermute | solution.py:21
  39.7 11.3 %collective-permute-start.7 = (bf16[16,320]{1,0:T(8,128)(2,1)S(1)}, bf16[16,320]{1,0:T(8,128)(2,1)S(1)}, u32[]{:S(2)}, u32[]{:S(2)}) collective-permute-start(bf16[16,320]{1,0:T(8,128)(2,1)S(1)} %get-tuple-element.36.refs_1_), channel_id=1, source_target_pairs={{0,511},{1,2},{2,1},{3,4},{4,3},{5,6},{6,5},{7,8},{8,7},{9,10},{10... | collective-permute-start | bytes 30728 | tf_op jit(solution)/shard_map/ppermute | solution.py:22
  43.8 7.3 %collective-permute-start.6 = (bf16[16,320]{1,0:T(8,128)(2,1)S(1)}, bf16[16,320]{1,0:T(8,128)(2,1)S(1)}, u32[]{:S(2)}, u32[]{:S(2)}) collective-permute-start(bf16[16,320]{1,0:T(8,128)(2,1)S(1)} %get-tuple-element.36.refs_1_), channel_id=1, source_target_pairs={{0,1},{1,0},{2,3},{3,2},{4,5},{5,4},{6,7},{7,6},{8,9},{9,8},{10,11... | collective-permute-start | bytes 30728 | tf_op jit(solution)/shard_map/ppermute | solution.py:21
  45.7 14.5 %collective-permute-start.8 = (bf16[1,320,320]{2,1,0:T(8,128)(2,1)S(1)}, bf16[1,320,320]{2,1,0:T(8,128)(2,1)S(1)}, u32[]{:S(2)}, u32[]{:S(2)}) collective-permute-start(bf16[1,320,320]{2,1,0:T(8,128)(2,1)S(1)} %get-tuple-element.41), channel_id=1, source_target_pairs={{0,1},{1,0},{2,3},{3,2},{4,5},{5,4},{6,7},{7,6},{8,9},{9,8},{10,11... | collective-permute-start | bytes 614408 | tf_op jit(solution)/shard_map/ppermute | solution.py:276
  49.1 11.2 %collective-permute-start.9 = (bf16[1,320,320]{2,1,0:T(8,128)(2,1)S(1)}, bf16[1,320,320]{2,1,0:T(8,128)(2,1)S(1)}, u32[]{:S(2)}, u32[]{:S(2)}) collective-permute-start(bf16[1,320,320]{2,1,0:T(8,128)(2,1)S(1)} %get-tuple-element.42), channel_id=1, source_target_pairs={{0,3},{1,2},{2,1},{3,0},{4,7},{5,6},{6,5},{7,4},{8,11},{9,10},{10,... | collective-permute-start | bytes 614408 | tf_op jit(solution)/shard_map/ppermute | solution.py:276
  60.9 10.6 %collective-permute-start.11 = (bf16[8,320]{1,0:T(8,128)(2,1)S(1)}, bf16[8,320]{1,0:T(8,128)(2,1)S(1)}, u32[]{:S(2)}, u32[]{:S(2)}) collective-permute-start(bf16[8,320]{1,0:T(8,128)(2,1)S(1)} %get-tuple-element.43.refs_1_), channel_id=1, source_target_pairs={{0,508},{4,8},{8,4},{12,16},{16,12},{20,24},{24,20},{28,32},{32,28... | collective-permute-start | bytes 15368 | tf_op jit(solution)/shard_map/ppermute | solution.py:22
  62.9 9.5 %collective-permute-start.10 = (bf16[8,320]{1,0:T(8,128)(2,1)S(1)}, bf16[8,320]{1,0:T(8,128)(2,1)S(1)}, u32[]{:S(2)}, u32[]{:S(2)}) collective-permute-start(bf16[8,320]{1,0:T(8,128)(2,1)S(1)} %get-tuple-element.43.refs_1_), channel_id=1, source_target_pairs={{0,4},{4,0},{8,12},{12,8},{16,20},{20,16},{24,28},{28,24},{32,36},... | collective-permute-start | bytes 15368 | tf_op jit(solution)/shard_map/ppermute | solution.py:21
  73.7 8.4 %collective-permute-start.13 = (bf16[8,320]{1,0:T(8,128)(2,1)S(1)}, bf16[8,320]{1,0:T(8,128)(2,1)S(1)}, u32[]{:S(2)}, u32[]{:S(2)}) collective-permute-start(bf16[8,320]{1,0:T(8,128)(2,1)S(1)} %shard_map.116.refs_1_), channel_id=1, source_target_pairs={{0,508},{4,8},{8,4},{12,16},{16,12},{20,24},{24,20},{28,32},{32,28... | collective-permute-start | bytes 15368 | tf_op jit(solution)/shard_map/ppermute | solution.py:22
  75.7 7.3 %collective-permute-start.12 = (bf16[8,320]{1,0:T(8,128)(2,1)S(1)}, bf16[8,320]{1,0:T(8,128)(2,1)S(1)}, u32[]{:S(2)}, u32[]{:S(2)}) collective-permute-start(bf16[8,320]{1,0:T(8,128)(2,1)S(1)} %shard_map.116.refs_1_), channel_id=1, source_target_pairs={{0,4},{4,0},{8,12},{12,8},{16,20},{20,16},{24,28},{28,24},{32,36},... | collective-permute-start | bytes 15368 | tf_op jit(solution)/shard_map/ppermute | solution.py:21
  84.5 6.5 %collective-permute-start.15 = (bf16[16,320]{1,0:T(8,128)(2,1)S(1)}, bf16[16,320]{1,0:T(8,128)(2,1)S(1)}, u32[]{:S(2)}, u32[]{:S(2)}) collective-permute-start(bf16[16,320]{1,0:T(8,128)(2,1)S(1)} %shard_map.117.refs_1_), channel_id=1, source_target_pairs={{0,511},{1,2},{2,1},{3,4},{4,3},{5,6},{6,5},{7,8},{8,7},{9,10},{10... | collective-permute-start | bytes 30728 | tf_op jit(solution)/shard_map/ppermute | solution.py:22
  89.0 4.7 %collective-permute-start.14 = (bf16[16,320]{1,0:T(8,128)(2,1)S(1)}, bf16[16,320]{1,0:T(8,128)(2,1)S(1)}, u32[]{:S(2)}, u32[]{:S(2)}) collective-permute-start(bf16[16,320]{1,0:T(8,128)(2,1)S(1)} %shard_map.117.refs_1_), channel_id=1, source_target_pairs={{0,1},{1,0},{2,3},{3,2},{4,5},{5,4},{6,7},{7,6},{8,9},{9,8},{10,11... | collective-permute-start | bytes 30728 | tf_op jit(solution)/shard_map/ppermute | solution.py:21
  95.2 6.3 %collective-permute-start.17 = (bf16[16,320]{1,0:T(8,128)(2,1)S(1)}, bf16[16,320]{1,0:T(8,128)(2,1)S(1)}, u32[]{:S(2)}, u32[]{:S(2)}) collective-permute-start(bf16[16,320]{1,0:T(8,128)(2,1)S(1)} %shard_map.118.refs_1_), channel_id=1, source_target_pairs={{0,511},{1,2},{2,1},{3,4},{4,3},{5,6},{6,5},{7,8},{8,7},{9,10},{10... | collective-permute-start | bytes 30728 | tf_op jit(solution)/shard_map/ppermute | solution.py:22
  98.3 4.4 %collective-permute-start.16 = (bf16[16,320]{1,0:T(8,128)(2,1)S(1)}, bf16[16,320]{1,0:T(8,128)(2,1)S(1)}, u32[]{:S(2)}, u32[]{:S(2)}) collective-permute-start(bf16[16,320]{1,0:T(8,128)(2,1)S(1)} %shard_map.118.refs_1_), channel_id=1, source_target_pairs={{0,1},{1,0},{2,3},{3,2},{4,5},{5,4},{6,7},{7,6},{8,9},{9,8},{10,11... | collective-permute-start | bytes 30728 | tf_op jit(solution)/shard_map/ppermute | solution.py:21
  104.2 7.0 %collective-permute-start.19 = (bf16[16,320]{1,0:T(8,128)(2,1)S(1)}, bf16[16,320]{1,0:T(8,128)(2,1)S(1)}, u32[]{:S(2)}, u32[]{:S(2)}) collective-permute-start(bf16[16,320]{1,0:T(8,128)(2,1)S(1)} %shard_map.119.refs_1_), channel_id=1, source_target_pairs={{0,511},{1,2},{2,1},{3,4},{4,3},{5,6},{6,5},{7,8},{8,7},{9,10},{10... | collective-permute-start | bytes 30728 | tf_op jit(solution)/shard_map/ppermute | solution.py:22
  115.0 8.4 %collective-permute-start.21 = (bf16[16,320]{1,0:T(8,128)(2,1)S(1)}, bf16[16,320]{1,0:T(8,128)(2,1)S(1)}, u32[]{:S(2)}, u32[]{:S(2)}) collective-permute-start(bf16[16,320]{1,0:T(8,128)(2,1)S(1)} %get-tuple-element.47.refs_1_), channel_id=1, source_target_pairs={{0,511},{1,2},{2,1},{3,4},{4,3},{5,6},{6,5},{7,8},{8,7},{9,10},{10... | collective-permute-start | bytes 30728 | tf_op jit(solution)/shard_map/ppermute | solution.py:22
  134.2 13.0 %collective-permute-start.23 = (bf16[8,320]{1,0:T(8,128)(2,1)S(1)}, bf16[8,320]{1,0:T(8,128)(2,1)S(1)}, u32[]{:S(2)}, u32[]{:S(2)}) collective-permute-start(bf16[8,320]{1,0:T(8,128)(2,1)S(1)} %get-tuple-element.49.refs_1_), channel_id=1, source_target_pairs={{0,508},{4,8},{8,4},{12,16},{16,12},{20,24},{24,20},{28,32},{32,28... | collective-permute-start | bytes 15368 | tf_op jit(solution)/shard_map/ppermute | solution.py:22
  136.2 11.8 %collective-permute-start.22 = (bf16[8,320]{1,0:T(8,128)(2,1)S(1)}, bf16[8,320]{1,0:T(8,128)(2,1)S(1)}, u32[]{:S(2)}, u32[]{:S(2)}) collective-permute-start(bf16[8,320]{1,0:T(8,128)(2,1)S(1)} %get-tuple-element.49.refs_1_), channel_id=1, source_target_pairs={{0,4},{4,0},{8,12},{12,8},{16,20},{20,16},{24,28},{28,24},{32,36},... | collective-permute-start | bytes 15368 | tf_op jit(solution)/shard_map/ppermute | solution.py:21
  149.4 8.3 %collective-permute-start.25 = (bf16[8,320]{1,0:T(8,128)(2,1)S(1)}, bf16[8,320]{1,0:T(8,128)(2,1)S(1)}, u32[]{:S(2)}, u32[]{:S(2)}) collective-permute-start(bf16[8,320]{1,0:T(8,128)(2,1)S(1)} %shard_map.123.refs_1_), channel_id=1, source_target_pairs={{0,508},{4,8},{8,4},{12,16},{16,12},{20,24},{24,20},{28,32},{32,28... | collective-permute-start | bytes 15368 | tf_op jit(solution)/shard_map/ppermute | solution.py:22
  151.4 7.1 %collective-permute-start.24 = (bf16[8,320]{1,0:T(8,128)(2,1)S(1)}, bf16[8,320]{1,0:T(8,128)(2,1)S(1)}, u32[]{:S(2)}, u32[]{:S(2)}) collective-permute-start(bf16[8,320]{1,0:T(8,128)(2,1)S(1)} %shard_map.123.refs_1_), channel_id=1, source_target_pairs={{0,4},{4,0},{8,12},{12,8},{16,20},{20,16},{24,28},{28,24},{32,36},... | collective-permute-start | bytes 15368 | tf_op jit(solution)/shard_map/ppermute | solution.py:21
  (7 other events, 86.5 us)

commit v9 on v8

--- a/solution.py
+++ b/solution.py
@@ -152,13 +152,15 @@
         operators_ref[q * LANES : (q + 1) * LANES, :size] = turned.astype(jnp.bfloat16)
 
 
-def turn_kernel(in_ref, out_ref):
-    size = in_ref.shape[1]
+def turn_kernel(*refs):
+    out_ref = refs[-1]
+    size = out_ref.shape[1]
     unit = lax.broadcasted_iota(jnp.int32, (size, size), 0) == lax.broadcasted_iota(jnp.int32, (size, size), 1)
     unit = jnp.where(unit, 1.0, 0.0).astype(jnp.bfloat16)
-    for e in range(in_ref.shape[0]):
-        turned = lax.dot_general(unit, in_ref[e], (((1,), (1,)), ((), ())), preferred_element_type=jnp.float32)
-        out_ref[e] = turned.astype(jnp.bfloat16)
+    blocks = [(ref, e) for ref in refs[:-1] for e in range(ref.shape[0])]
+    for place, (ref, e) in enumerate(blocks):
+        turned = lax.dot_general(unit, ref[e], (((1,), (1,)), ((), ())), preferred_element_type=jnp.float32)
+        out_ref[place] = turned.astype(jnp.bfloat16)
 
 
 def take_kernel(before_ref, after_ref, low_ref, high_ref):
@@ -202,7 +204,7 @@
             out_ref[t, s * own : (s + 1) * own, dofs:] = lists_ref[(s ^ t) * own : ((s ^ t) + 1) * own]
 
 
-def coarse_first_kernel(*refs, blocks):
+def coarse_first_kernel(*refs, blocks, turned):
     parts_ref, inverses, (restricted_ref, state_ref, index_ref) = refs[0], refs[1 : 1 + blocks], refs[1 + blocks :]
     total = parts_ref[0]
     for t in range(1, parts_ref.shape[0]):
@@ -212,13 +214,13 @@
     restricted_ref[...] = restricted
     lists = total[:, dofs:].astype(jnp.int32)
     turn = lax.axis_index("tele") * (total.shape[0] // parts_ref.shape[0])
-    turned = (lax.broadcasted_iota(jnp.int32, lists.shape, 1) < 6) & (lists >= 0)
-    index_ref[...] = jnp.where(turned, lists ^ turn, lists)
-    state_ref[...] = apply_inverse(inverses, restricted.astype(jnp.bfloat16)).astype(jnp.bfloat16)
+    moved = (lax.broadcasted_iota(jnp.int32, lists.shape, 1) < 6) & (lists >= 0)
+    index_ref[...] = jnp.where(moved, lists ^ turn, lists)
+    state_ref[...] = apply_inverse(inverses, restricted.astype(jnp.bfloat16), turned).astype(jnp.bfloat16)
 
 
 def correct_kernel(*refs, blocks):
-    coarse, _ = sweep(refs[:8], refs[8 : 8 + blocks])
+    coarse, _ = sweep(refs[:8], refs[8 : 8 + blocks], True)
     target_ref, solution_ref, out_ref = refs[8 + blocks :]
     rows, fine = coarse.shape[0], solution_ref.shape[0]
     turn = lax.axis_index("tele") * (rows // lax.axis_size("tele"))
@@ -355,15 +357,19 @@
         )
         parts = lax.all_to_all(parts, "tele", 0, 0, tiled=True)
         restricted, coarse, coarse_index = run(
-            functools.partial(coarse_first_kernel, blocks=len(blocks)),
+            functools.partial(coarse_first_kernel, blocks=len(blocks), turned=cycle > 0),
             [((coarse_rows, dofs), f32), ((coarse_rows, dofs), bf16), ((coarse_rows, spare), i32)],
             parts,
             *blocks,
             held=range(1, 1 + len(blocks)),
         )
+        if cycle == 0:
+            turned_shape = ((coarse_rows, dofs, dofs), bf16)
+            held = range(len(blocks))
+            blocks = (run(turn_kernel, turned_shape, *blocks, held=held, keep=(coarse,), pinned=(0,)),)
         for sweep in range(SWEEPS - 2):
             coarse = run(
-                functools.partial(sweep_kernel, blocks=len(blocks)),
+                functools.partial(sweep_kernel, blocks=len(blocks), turned=True),
                 [((coarse_rows, dofs), bf16)],
                 *halo(coarse, "fine"),
                 coarse_index,

time: 162 us -> 160 us (0.988)
    pallas_call x16 -> x17, Pallas kernels: 23.4 us -> 23.4 us  [run(): pl.pallas_call(body, out_shape=[pltpu.VMEM(s, d) if i in pinned else jax....]
  transfers between devices with their start and end apart: 26 -> 26, of which waited for: 10 -> 9; matrix products, arithmetic and copies ran while one was open for 0% -> 0% of each run, Pallas kernels for 3% -> 4%
where the time goes in v9:
time: 160 us; the launch traced here: 159 us
  starting transfers between devices  108 us (68%)
  Pallas kernels  23.4 us (15%)
  blocking collectives  14.9 us (9%)
  waiting for transfers between devices  12.6 us (8%)
    ppermute x11, starting transfers between devices, swapped(): lax.ppermute(block, axis, [(i, (i - 1 if i % 2 == 0 else i + 1) % count)...  48.8 us
    ppermute x11, starting transfers between devices, swapped(): inner = lax.ppermute(block, axis, [(i, i ^ 1) for i in range(count)])  47.5 us
    pallas_call x17, Pallas kernels, run(): pl.pallas_call(body, out_shape=[pltpu.VMEM(s, d) if i in pinned else jax....  23.4 us
    all_to_all x2, blocking collectives, shards(): parts = lax.all_to_all(parts, 'tele', 0, 0, tiled=True)  14.9 us
    ppermute x11, waiting for transfers between devices, swapped(): inner = lax.ppermute(block, axis, [(i, i ^ 1) for i in range(count)])  11.8 us
    ppermute x4, starting transfers between devices, across(): lax.ppermute(block, 'tele', [(i, i ^ bits) for i in range(tele_size)])  11.4 us
  transfers between devices with their start and end apart: 26, of which 9 were waited for; matrix products, arithmetic and copies ran while one was open for 0% of the time, Pallas kernels for 4%

profile of v9, /device:TPU:1, one launch (start us, length us, event | category | flops | bytes accessed | tf_op | source)
XLA Modules:
  0.0 159.2 jit_solution(12575446638939597187)
XLA Ops:
  0.0 3.4 %shard_map.109 = (bf16[16,320]{1,0:T(8,128)(2,1)S(1)}, s32[16,12]{1,0:T(8,128)S(1)}, f32[8,64]{1,0:T(8,128)S(1)}, bf16[3072,128]{1,0:T(8,128)(2,1)S(1)}, bf16[16,320,320]{2,1,0:T(8,128)(2,1)S(1)}) custom-call(f32[16,320]{1,0:T(8,128)} %refs_7_.9, s32[6,16]{1,0:T(8,128)} %bitcast.7, s32[6,16]{1,0:T(8,128)} %bitcast.8, s32[2,6]{1,0:T(2,128)} %refs_3_.1, ...), custom_call_target="tpu_custom_call" | custom-call | flops 4294967296 | bytes 3605344 | tf_op jit(solution)/shard_map/pallas_call | solution.py:247
  3.5 3.9 %collective-permute-start = (bf16[16,320]{1,0:T(8,128)(2,1)S(1)}, bf16[16,320]{1,0:T(8,128)(2,1)S(1)}, u32[]{:S(2)}, u32[]{:S(2)}) collective-permute-start(bf16[16,320]{1,0:T(8,128)(2,1)S(1)} %get-tuple-element.29.refs_1_), channel_id=1, source_target_pairs={{0,1},{1,0},{2,3},{3,2},{4,5},{5,4},{6,7},{7,6},{8,9},{9,8},{10,11... | collective-permute-start | bytes 30728 | tf_op jit(solution)/shard_map/ppermute | solution.py:21
  7.4 4.6 %collective-permute-start.1 = (bf16[16,320]{1,0:T(8,128)(2,1)S(1)}, bf16[16,320]{1,0:T(8,128)(2,1)S(1)}, u32[]{:S(2)}, u32[]{:S(2)}) collective-permute-start(bf16[16,320]{1,0:T(8,128)(2,1)S(1)} %get-tuple-element.29.refs_1_), channel_id=1, source_target_pairs={{0,511},{1,2},{2,1},{3,4},{4,3},{5,6},{6,5},{7,8},{8,7},{9,10},{10... | collective-permute-start | bytes 30728 | tf_op jit(solution)/shard_map/ppermute | solution.py:22
  12.0 4.1 %collective-permute-start.4 = (bf16[2,320,320]{2,1,0:T(8,128)(2,1)S(1)}, bf16[2,320,320]{2,1,0:T(8,128)(2,1)S(1)}, u32[]{:S(2)}, u32[]{:S(2)}) collective-permute-start(bf16[2,320,320]{2,1,0:T(8,128)(2,1)S(1)} %copy-done), channel_id=1, source_target_pairs={{0,3},{1,2},{2,1},{3,0},{4,7},{5,6},{6,5},{7,4},{8,11},{9,10},{10,... | collective-permute-start | bytes 1228808 | tf_op jit(solution)/shard_map/ppermute | solution.py:278
  20.1 13.5 %collective-permute-start.5 = (bf16[16,320]{1,0:T(8,128)(2,1)S(1)}, bf16[16,320]{1,0:T(8,128)(2,1)S(1)}, u32[]{:S(2)}, u32[]{:S(2)}) collective-permute-start(bf16[16,320]{1,0:T(8,128)(2,1)S(1)} %shard_map.110.refs_1_), channel_id=1, source_target_pairs={{0,511},{1,2},{2,1},{3,4},{4,3},{5,6},{6,5},{7,8},{8,7},{9,10},{10... | collective-permute-start | bytes 30728 | tf_op jit(solution)/shard_map/ppermute | solution.py:22
  35.5 2.7 %shard_map.111.refs_8_ = bf16[16,320,320]{2,1,0:T(8,128)(2,1)S(1)} custom-call(bf16[16,320,320]{2,1,0:T(8,128)(2,1)S(1)} %get-tuple-element.33.refs_8_.refs_0_, bf16[16,320]{1,0:T(8,128)(2,1)S(1)} %shard_map.110.refs_1_), custom_call_target="tpu_custom_call" | custom-call | flops 4294967296 | bytes 3276800 | tf_op jit(solution)/shard_map/pallas_call | solution.py:247
  39.7 4.0 %collective-permute-start.7 = (bf16[16,320]{1,0:T(8,128)(2,1)S(1)}, bf16[16,320]{1,0:T(8,128)(2,1)S(1)}, u32[]{:S(2)}, u32[]{:S(2)}) collective-permute-start(bf16[16,320]{1,0:T(8,128)(2,1)S(1)} %get-tuple-element.36.refs_1_), channel_id=1, source_target_pairs={{0,511},{1,2},{2,1},{3,4},{4,3},{5,6},{6,5},{7,8},{8,7},{9,10},{10... | collective-permute-start | bytes 30728 | tf_op jit(solution)/shard_map/ppermute | solution.py:22
  45.7 3.4 %collective-permute-start.8 = (bf16[1,320,320]{2,1,0:T(8,128)(2,1)S(1)}, bf16[1,320,320]{2,1,0:T(8,128)(2,1)S(1)}, u32[]{:S(2)}, u32[]{:S(2)}) collective-permute-start(bf16[1,320,320]{2,1,0:T(8,128)(2,1)S(1)} %get-tuple-element.41), channel_id=1, source_target_pairs={{0,1},{1,0},{2,3},{3,2},{4,5},{5,4},{6,7},{7,6},{8,9},{9,8},{10,11... | collective-permute-start | bytes 614408 | tf_op jit(solution)/shard_map/ppermute | solution.py:278
  49.1 2.0 %collective-permute-start.9 = (bf16[1,320,320]{2,1,0:T(8,128)(2,1)S(1)}, bf16[1,320,320]{2,1,0:T(8,128)(2,1)S(1)}, u32[]{:S(2)}, u32[]{:S(2)}) collective-permute-start(bf16[1,320,320]{2,1,0:T(8,128)(2,1)S(1)} %get-tuple-element.42), channel_id=1, source_target_pairs={{0,3},{1,2},{2,1},{3,0},{4,7},{5,6},{6,5},{7,4},{8,11},{9,10},{10,... | collective-permute-start | bytes 614408 | tf_op jit(solution)/shard_map/ppermute | solution.py:278
  52.1 8.2 %all_to_all.10.refs_0_ = f32[4,8,384]{2,1,0:T(8,128)S(1)} all-to-all(f32[4,8,384]{2,1,0:T(8,128)S(1)} %shard_map.113), channel_id=1, replica_groups=mesh['fine'=128,'tele'=4] {'tele'}, dimensions={0} | all-to-all | bytes 98304 | tf_op jit(solution)/shard_map/all_to_all | solution.py:358
  62.9 8.7 %collective-permute-start.10 = (bf16[8,320]{1,0:T(8,128)(2,1)S(1)}, bf16[8,320]{1,0:T(8,128)(2,1)S(1)}, u32[]{:S(2)}, u32[]{:S(2)}) collective-permute-start(bf16[8,320]{1,0:T(8,128)(2,1)S(1)} %get-tuple-element.43.refs_5_.refs_1_), channel_id=1, source_target_pairs={{0,4},{4,0},{8,12},{12,8},{16,20},{20,16},{24,28},{28,24},{32,36},... | collective-permute-start | bytes 15368 | tf_op jit(solution)/shard_map/ppermute | solution.py:21
  76.0 6.1 %collective-permute-start.12 = (bf16[8,320]{1,0:T(8,128)(2,1)S(1)}, bf16[8,320]{1,0:T(8,128)(2,1)S(1)}, u32[]{:S(2)}, u32[]{:S(2)}) collective-permute-start(bf16[8,320]{1,0:T(8,128)(2,1)S(1)} %shard_map.117.refs_1_), channel_id=1, source_target_pairs={{0,4},{4,0},{8,12},{12,8},{16,20},{20,16},{24,28},{28,24},{32,36},... | collective-permute-start | bytes 15368 | tf_op jit(solution)/shard_map/ppermute | solution.py:21
  84.2 4.3 %collective-permute-start.15 = (bf16[16,320]{1,0:T(8,128)(2,1)S(1)}, bf16[16,320]{1,0:T(8,128)(2,1)S(1)}, u32[]{:S(2)}, u32[]{:S(2)}) collective-permute-start(bf16[16,320]{1,0:T(8,128)(2,1)S(1)} %shard_map.118.refs_1_), channel_id=1, source_target_pairs={{0,511},{1,2},{2,1},{3,4},{4,3},{5,6},{6,5},{7,8},{8,7},{9,10},{10... | collective-permute-start | bytes 30728 | tf_op jit(solution)/shard_map/ppermute | solution.py:22
  90.4 2.8 %collective-permute-done.14.refs_0_ = bf16[16,320]{1,0:T(8,128)(2,1)S(1)} collective-permute-done((bf16[16,320]{1,0:T(8,128)(2,1)S(1)}, bf16[16,320]{1,0:T(8,128)(2,1)S(1)}, u32[]{:S(2)}, u32[]{:S(2)}) %collective-permute-start.14) | collective-permute-done | bytes 10272 | tf_op jit(solution)/shard_map/ppermute | solution.py:21
  94.6 3.4 %collective-permute-start.17 = (bf16[16,320]{1,0:T(8,128)(2,1)S(1)}, bf16[16,320]{1,0:T(8,128)(2,1)S(1)}, u32[]{:S(2)}, u32[]{:S(2)}) collective-permute-start(bf16[16,320]{1,0:T(8,128)(2,1)S(1)} %shard_map.119.refs_1_), channel_id=1, source_target_pairs={{0,511},{1,2},{2,1},{3,4},{4,3},{5,6},{6,5},{7,8},{8,7},{9,10},{10... | collective-permute-start | bytes 30728 | tf_op jit(solution)/shard_map/ppermute | solution.py:22
  98.1 2.1 %collective-permute-start.16 = (bf16[16,320]{1,0:T(8,128)(2,1)S(1)}, bf16[16,320]{1,0:T(8,128)(2,1)S(1)}, u32[]{:S(2)}, u32[]{:S(2)}) collective-permute-start(bf16[16,320]{1,0:T(8,128)(2,1)S(1)} %shard_map.119.refs_1_), channel_id=1, source_target_pairs={{0,1},{1,0},{2,3},{3,2},{4,5},{5,4},{6,7},{7,6},{8,9},{9,8},{10,11... | collective-permute-start | bytes 30728 | tf_op jit(solution)/shard_map/ppermute | solution.py:21
  103.9 4.6 %collective-permute-start.19 = (bf16[16,320]{1,0:T(8,128)(2,1)S(1)}, bf16[16,320]{1,0:T(8,128)(2,1)S(1)}, u32[]{:S(2)}, u32[]{:S(2)}) collective-permute-start(bf16[16,320]{1,0:T(8,128)(2,1)S(1)} %shard_map.120.refs_1_), channel_id=1, source_target_pairs={{0,511},{1,2},{2,1},{3,4},{4,3},{5,6},{6,5},{7,8},{8,7},{9,10},{10... | collective-permute-start | bytes 30728 | tf_op jit(solution)/shard_map/ppermute | solution.py:22
  110.5 2.5 %collective-permute-done.18.refs_0_ = bf16[16,320]{1,0:T(8,128)(2,1)S(1)} collective-permute-done((bf16[16,320]{1,0:T(8,128)(2,1)S(1)}, bf16[16,320]{1,0:T(8,128)(2,1)S(1)}, u32[]{:S(2)}, u32[]{:S(2)}) %collective-permute-start.18) | collective-permute-done | bytes 10272 | tf_op jit(solution)/shard_map/ppermute | solution.py:21
  114.4 6.4 %collective-permute-start.21 = (bf16[16,320]{1,0:T(8,128)(2,1)S(1)}, bf16[16,320]{1,0:T(8,128)(2,1)S(1)}, u32[]{:S(2)}, u32[]{:S(2)}) collective-permute-start(bf16[16,320]{1,0:T(8,128)(2,1)S(1)} %get-tuple-element.47.refs_1_), channel_id=1, source_target_pairs={{0,511},{1,2},{2,1},{3,4},{4,3},{5,6},{6,5},{7,8},{8,7},{9,10},{10... | collective-permute-start | bytes 30728 | tf_op jit(solution)/shard_map/ppermute | solution.py:22
  122.8 2.5 %collective-permute-done.20.refs_0_ = bf16[16,320]{1,0:T(8,128)(2,1)S(1)} collective-permute-done((bf16[16,320]{1,0:T(8,128)(2,1)S(1)}, bf16[16,320]{1,0:T(8,128)(2,1)S(1)}, u32[]{:S(2)}, u32[]{:S(2)}) %collective-permute-start.20) | collective-permute-done | bytes 10272 | tf_op jit(solution)/shard_map/ppermute | solution.py:21
  126.3 6.7 %all_to_all.11.refs_0_ = f32[4,8,384]{2,1,0:T(8,128)S(1)} all-to-all(f32[4,8,384]{2,1,0:T(8,128)S(1)} %shard_map.122), channel_id=1, replica_groups=mesh['fine'=128,'tele'=4] {'tele'}, dimensions={0} | all-to-all | bytes 98304 | tf_op jit(solution)/shard_map/all_to_all | solution.py:358
  133.4 2.2 %collective-permute-start.23 = (bf16[8,320]{1,0:T(8,128)(2,1)S(1)}, bf16[8,320]{1,0:T(8,128)(2,1)S(1)}, u32[]{:S(2)}, u32[]{:S(2)}) collective-permute-start(bf16[8,320]{1,0:T(8,128)(2,1)S(1)} %get-tuple-element.49.refs_1_), channel_id=1, source_target_pairs={{0,508},{4,8},{8,4},{12,16},{16,12},{20,24},{24,20},{28,32},{32,28... | collective-permute-start | bytes 15368 | tf_op jit(solution)/shard_map/ppermute | solution.py:22
  135.6 10.8 %collective-permute-start.22 = (bf16[8,320]{1,0:T(8,128)(2,1)S(1)}, bf16[8,320]{1,0:T(8,128)(2,1)S(1)}, u32[]{:S(2)}, u32[]{:S(2)}) collective-permute-start(bf16[8,320]{1,0:T(8,128)(2,1)S(1)} %get-tuple-element.49.refs_1_), channel_id=1, source_target_pairs={{0,4},{4,0},{8,12},{12,8},{16,20},{20,16},{24,28},{28,24},{32,36},... | collective-permute-start | bytes 15368 | tf_op jit(solution)/shard_map/ppermute | solution.py:21
  150.2 6.3 %collective-permute-start.24 = (bf16[8,320]{1,0:T(8,128)(2,1)S(1)}, bf16[8,320]{1,0:T(8,128)(2,1)S(1)}, u32[]{:S(2)}, u32[]{:S(2)}) collective-permute-start(bf16[8,320]{1,0:T(8,128)(2,1)S(1)} %shard_map.124.refs_1_), channel_id=1, source_target_pairs={{0,4},{4,0},{8,12},{12,8},{16,20},{20,16},{24,28},{28,24},{32,36},... | collective-permute-start | bytes 15368 | tf_op jit(solution)/shard_map/ppermute | solution.py:21
  (57 shorter events, 39.5 us)
Async XLA Ops:
  3.5 8.5 %collective-permute-start = (bf16[16,320]{1,0:T(8,128)(2,1)S(1)}, bf16[16,320]{1,0:T(8,128)(2,1)S(1)}, u32[]{:S(2)}, u32[]{:S(2)}) collective-permute-start(bf16[16,320]{1,0:T(8,128)(2,1)S(1)} %get-tuple-element.29.refs_1_), channel_id=1, source_target_pairs={{0,1},{1,0},{2,3},{3,2},{4,5},{5,4},{6,7},{7,6},{8,9},{9,8},{10,11... | collective-permute-start | bytes 30728 | tf_op jit(solution)/shard_map/ppermute | solution.py:21
  7.4 10.7 %collective-permute-start.1 = (bf16[16,320]{1,0:T(8,128)(2,1)S(1)}, bf16[16,320]{1,0:T(8,128)(2,1)S(1)}, u32[]{:S(2)}, u32[]{:S(2)}) collective-permute-start(bf16[16,320]{1,0:T(8,128)(2,1)S(1)} %get-tuple-element.29.refs_1_), channel_id=1, source_target_pairs={{0,511},{1,2},{2,1},{3,4},{4,3},{5,6},{6,5},{7,8},{8,7},{9,10},{10... | collective-permute-start | bytes 30728 | tf_op jit(solution)/shard_map/ppermute | solution.py:22
  12.0 26.2 %collective-permute-start.4 = (bf16[2,320,320]{2,1,0:T(8,128)(2,1)S(1)}, bf16[2,320,320]{2,1,0:T(8,128)(2,1)S(1)}, u32[]{:S(2)}, u32[]{:S(2)}) collective-permute-start(bf16[2,320,320]{2,1,0:T(8,128)(2,1)S(1)} %copy-done), channel_id=1, source_target_pairs={{0,3},{1,2},{2,1},{3,0},{4,7},{5,6},{6,5},{7,4},{8,11},{9,10},{10,... | collective-permute-start | bytes 1228808 | tf_op jit(solution)/shard_map/ppermute | solution.py:278
  16.1 22.1 %collective-permute-start.3 = (bf16[2,320,320]{2,1,0:T(8,128)(2,1)S(1)}, bf16[2,320,320]{2,1,0:T(8,128)(2,1)S(1)}, u32[]{:S(2)}, u32[]{:S(2)}) collective-permute-start(bf16[2,320,320]{2,1,0:T(8,128)(2,1)S(1)} %copy-done), channel_id=1, source_target_pairs={{0,1},{1,0},{2,3},{3,2},{4,5},{5,4},{6,7},{7,6},{8,9},{9,8},{10,11... | collective-permute-start | bytes 1228808 | tf_op jit(solution)/shard_map/ppermute | solution.py:278
  20.1 18.1 %collective-permute-start.5 = (bf16[16,320]{1,0:T(8,128)(2,1)S(1)}, bf16[16,320]{1,0:T(8,128)(2,1)S(1)}, u32[]{:S(2)}, u32[]{:S(2)}) collective-permute-start(bf16[16,320]{1,0:T(8,128)(2,1)S(1)} %shard_map.110.refs_1_), channel_id=1, source_target_pairs={{0,511},{1,2},{2,1},{3,4},{4,3},{5,6},{6,5},{7,8},{8,7},{9,10},{10... | collective-permute-start | bytes 30728 | tf_op jit(solution)/shard_map/ppermute | solution.py:22
  33.6 4.7 %collective-permute-start.2 = (bf16[16,320]{1,0:T(8,128)(2,1)S(1)}, bf16[16,320]{1,0:T(8,128)(2,1)S(1)}, u32[]{:S(2)}, u32[]{:S(2)}) collective-permute-start(bf16[16,320]{1,0:T(8,128)(2,1)S(1)} %shard_map.110.refs_1_), channel_id=1, source_target_pairs={{0,1},{1,0},{2,3},{3,2},{4,5},{5,4},{6,7},{7,6},{8,9},{9,8},{10,11... | collective-permute-start | bytes 30728 | tf_op jit(solution)/shard_map/ppermute | solution.py:21
  39.7 11.3 %collective-permute-start.7 = (bf16[16,320]{1,0:T(8,128)(2,1)S(1)}, bf16[16,320]{1,0:T(8,128)(2,1)S(1)}, u32[]{:S(2)}, u32[]{:S(2)}) collective-permute-start(bf16[16,320]{1,0:T(8,128)(2,1)S(1)} %get-tuple-element.36.refs_1_), channel_id=1, source_target_pairs={{0,511},{1,2},{2,1},{3,4},{4,3},{5,6},{6,5},{7,8},{8,7},{9,10},{10... | collective-permute-start | bytes 30728 | tf_op jit(solution)/shard_map/ppermute | solution.py:22
  43.8 7.3 %collective-permute-start.6 = (bf16[16,320]{1,0:T(8,128)(2,1)S(1)}, bf16[16,320]{1,0:T(8,128)(2,1)S(1)}, u32[]{:S(2)}, u32[]{:S(2)}) collective-permute-start(bf16[16,320]{1,0:T(8,128)(2,1)S(1)} %get-tuple-element.36.refs_1_), channel_id=1, source_target_pairs={{0,1},{1,0},{2,3},{3,2},{4,5},{5,4},{6,7},{7,6},{8,9},{9,8},{10,11... | collective-permute-start | bytes 30728 | tf_op jit(solution)/shard_map/ppermute | solution.py:21
  45.7 14.5 %collective-permute-start.8 = (bf16[1,320,320]{2,1,0:T(8,128)(2,1)S(1)}, bf16[1,320,320]{2,1,0:T(8,128)(2,1)S(1)}, u32[]{:S(2)}, u32[]{:S(2)}) collective-permute-start(bf16[1,320,320]{2,1,0:T(8,128)(2,1)S(1)} %get-tuple-element.41), channel_id=1, source_target_pairs={{0,1},{1,0},{2,3},{3,2},{4,5},{5,4},{6,7},{7,6},{8,9},{9,8},{10,11... | collective-permute-start | bytes 614408 | tf_op jit(solution)/shard_map/ppermute | solution.py:278
  49.1 11.2 %collective-permute-start.9 = (bf16[1,320,320]{2,1,0:T(8,128)(2,1)S(1)}, bf16[1,320,320]{2,1,0:T(8,128)(2,1)S(1)}, u32[]{:S(2)}, u32[]{:S(2)}) collective-permute-start(bf16[1,320,320]{2,1,0:T(8,128)(2,1)S(1)} %get-tuple-element.42), channel_id=1, source_target_pairs={{0,3},{1,2},{2,1},{3,0},{4,7},{5,6},{6,5},{7,4},{8,11},{9,10},{10,... | collective-permute-start | bytes 614408 | tf_op jit(solution)/shard_map/ppermute | solution.py:278
  60.9 12.0 %collective-permute-start.11 = (bf16[8,320]{1,0:T(8,128)(2,1)S(1)}, bf16[8,320]{1,0:T(8,128)(2,1)S(1)}, u32[]{:S(2)}, u32[]{:S(2)}) collective-permute-start(bf16[8,320]{1,0:T(8,128)(2,1)S(1)} %get-tuple-element.43.refs_5_.refs_1_), channel_id=1, source_target_pairs={{0,508},{4,8},{8,4},{12,16},{16,12},{20,24},{24,20},{28,32},{32,28... | collective-permute-start | bytes 15368 | tf_op jit(solution)/shard_map/ppermute | solution.py:22
  62.9 10.1 %collective-permute-start.10 = (bf16[8,320]{1,0:T(8,128)(2,1)S(1)}, bf16[8,320]{1,0:T(8,128)(2,1)S(1)}, u32[]{:S(2)}, u32[]{:S(2)}) collective-permute-start(bf16[8,320]{1,0:T(8,128)(2,1)S(1)} %get-tuple-element.43.refs_5_.refs_1_), channel_id=1, source_target_pairs={{0,4},{4,0},{8,12},{12,8},{16,20},{20,16},{24,28},{28,24},{32,36},... | collective-permute-start | bytes 15368 | tf_op jit(solution)/shard_map/ppermute | solution.py:21
  74.1 8.1 %collective-permute-start.13 = (bf16[8,320]{1,0:T(8,128)(2,1)S(1)}, bf16[8,320]{1,0:T(8,128)(2,1)S(1)}, u32[]{:S(2)}, u32[]{:S(2)}) collective-permute-start(bf16[8,320]{1,0:T(8,128)(2,1)S(1)} %shard_map.117.refs_1_), channel_id=1, source_target_pairs={{0,508},{4,8},{8,4},{12,16},{16,12},{20,24},{24,20},{28,32},{32,28... | collective-permute-start | bytes 15368 | tf_op jit(solution)/shard_map/ppermute | solution.py:22
  76.0 6.9 %collective-permute-start.12 = (bf16[8,320]{1,0:T(8,128)(2,1)S(1)}, bf16[8,320]{1,0:T(8,128)(2,1)S(1)}, u32[]{:S(2)}, u32[]{:S(2)}) collective-permute-start(bf16[8,320]{1,0:T(8,128)(2,1)S(1)} %shard_map.117.refs_1_), channel_id=1, source_target_pairs={{0,4},{4,0},{8,12},{12,8},{16,20},{20,16},{24,28},{28,24},{32,36},... | collective-permute-start | bytes 15368 | tf_op jit(solution)/shard_map/ppermute | solution.py:21
  84.2 6.3 %collective-permute-start.15 = (bf16[16,320]{1,0:T(8,128)(2,1)S(1)}, bf16[16,320]{1,0:T(8,128)(2,1)S(1)}, u32[]{:S(2)}, u32[]{:S(2)}) collective-permute-start(bf16[16,320]{1,0:T(8,128)(2,1)S(1)} %shard_map.118.refs_1_), channel_id=1, source_target_pairs={{0,511},{1,2},{2,1},{3,4},{4,3},{5,6},{6,5},{7,8},{8,7},{9,10},{10... | collective-permute-start | bytes 30728 | tf_op jit(solution)/shard_map/ppermute | solution.py:22
  88.5 4.7 %collective-permute-start.14 = (bf16[16,320]{1,0:T(8,128)(2,1)S(1)}, bf16[16,320]{1,0:T(8,128)(2,1)S(1)}, u32[]{:S(2)}, u32[]{:S(2)}) collective-permute-start(bf16[16,320]{1,0:T(8,128)(2,1)S(1)} %shard_map.118.refs_1_), channel_id=1, source_target_pairs={{0,1},{1,0},{2,3},{3,2},{4,5},{5,4},{6,7},{7,6},{8,9},{9,8},{10,11... | collective-permute-start | bytes 30728 | tf_op jit(solution)/shard_map/ppermute | solution.py:21
  94.6 6.3 %collective-permute-start.17 = (bf16[16,320]{1,0:T(8,128)(2,1)S(1)}, bf16[16,320]{1,0:T(8,128)(2,1)S(1)}, u32[]{:S(2)}, u32[]{:S(2)}) collective-permute-start(bf16[16,320]{1,0:T(8,128)(2,1)S(1)} %shard_map.119.refs_1_), channel_id=1, source_target_pairs={{0,511},{1,2},{2,1},{3,4},{4,3},{5,6},{6,5},{7,8},{8,7},{9,10},{10... | collective-permute-start | bytes 30728 | tf_op jit(solution)/shard_map/ppermute | solution.py:22
  98.1 4.4 %collective-permute-start.16 = (bf16[16,320]{1,0:T(8,128)(2,1)S(1)}, bf16[16,320]{1,0:T(8,128)(2,1)S(1)}, u32[]{:S(2)}, u32[]{:S(2)}) collective-permute-start(bf16[16,320]{1,0:T(8,128)(2,1)S(1)} %shard_map.119.refs_1_), channel_id=1, source_target_pairs={{0,1},{1,0},{2,3},{3,2},{4,5},{5,4},{6,7},{7,6},{8,9},{9,8},{10,11... | collective-permute-start | bytes 30728 | tf_op jit(solution)/shard_map/ppermute | solution.py:21
  103.9 6.5 %collective-permute-start.19 = (bf16[16,320]{1,0:T(8,128)(2,1)S(1)}, bf16[16,320]{1,0:T(8,128)(2,1)S(1)}, u32[]{:S(2)}, u32[]{:S(2)}) collective-permute-start(bf16[16,320]{1,0:T(8,128)(2,1)S(1)} %shard_map.120.refs_1_), channel_id=1, source_target_pairs={{0,511},{1,2},{2,1},{3,4},{4,3},{5,6},{6,5},{7,8},{8,7},{9,10},{10... | collective-permute-start | bytes 30728 | tf_op jit(solution)/shard_map/ppermute | solution.py:22
  114.4 8.4 %collective-permute-start.21 = (bf16[16,320]{1,0:T(8,128)(2,1)S(1)}, bf16[16,320]{1,0:T(8,128)(2,1)S(1)}, u32[]{:S(2)}, u32[]{:S(2)}) collective-permute-start(bf16[16,320]{1,0:T(8,128)(2,1)S(1)} %get-tuple-element.47.refs_1_), channel_id=1, source_target_pairs={{0,511},{1,2},{2,1},{3,4},{4,3},{5,6},{6,5},{7,8},{8,7},{9,10},{10... | collective-permute-start | bytes 30728 | tf_op jit(solution)/shard_map/ppermute | solution.py:22
  133.4 13.0 %collective-permute-start.23 = (bf16[8,320]{1,0:T(8,128)(2,1)S(1)}, bf16[8,320]{1,0:T(8,128)(2,1)S(1)}, u32[]{:S(2)}, u32[]{:S(2)}) collective-permute-start(bf16[8,320]{1,0:T(8,128)(2,1)S(1)} %get-tuple-element.49.refs_1_), channel_id=1, source_target_pairs={{0,508},{4,8},{8,4},{12,16},{16,12},{20,24},{24,20},{28,32},{32,28... | collective-permute-start | bytes 15368 | tf_op jit(solution)/shard_map/ppermute | solution.py:22
  135.6 11.6 %collective-permute-start.22 = (bf16[8,320]{1,0:T(8,128)(2,1)S(1)}, bf16[8,320]{1,0:T(8,128)(2,1)S(1)}, u32[]{:S(2)}, u32[]{:S(2)}) collective-permute-start(bf16[8,320]{1,0:T(8,128)(2,1)S(1)} %get-tuple-element.49.refs_1_), channel_id=1, source_target_pairs={{0,4},{4,0},{8,12},{12,8},{16,20},{20,16},{24,28},{28,24},{32,36},... | collective-permute-start | bytes 15368 | tf_op jit(solution)/shard_map/ppermute | solution.py:21
  148.3 8.3 %collective-permute-start.25 = (bf16[8,320]{1,0:T(8,128)(2,1)S(1)}, bf16[8,320]{1,0:T(8,128)(2,1)S(1)}, u32[]{:S(2)}, u32[]{:S(2)}) collective-permute-start(bf16[8,320]{1,0:T(8,128)(2,1)S(1)} %shard_map.124.refs_1_), channel_id=1, source_target_pairs={{0,508},{4,8},{8,4},{12,16},{16,12},{20,24},{24,20},{28,32},{32,28... | collective-permute-start | bytes 15368 | tf_op jit(solution)/shard_map/ppermute | solution.py:22
  150.2 7.1 %collective-permute-start.24 = (bf16[8,320]{1,0:T(8,128)(2,1)S(1)}, bf16[8,320]{1,0:T(8,128)(2,1)S(1)}, u32[]{:S(2)}, u32[]{:S(2)}) collective-permute-start(bf16[8,320]{1,0:T(8,128)(2,1)S(1)} %shard_map.124.refs_1_), channel_id=1, source_target_pairs={{0,4},{4,0},{8,12},{12,8},{16,20},{20,16},{24,28},{28,24},{32,36},... | collective-permute-start | bytes 15368 | tf_op jit(solution)/shard_map/ppermute | solution.py:21
  (7 other events, 86.5 us)

commit v10 on v9

--- a/solution.py
+++ b/solution.py
@@ -16,10 +16,11 @@
 OPPOSITE = (1, 0, 3, 2, 5, 4)
 
 
-def swapped(block, axis):
+def swapped(block, axis, wide=None):
     count = lax.axis_size(axis)
     inner = lax.ppermute(block, axis, [(i, i ^ 1) for i in range(count)])
-    outer = lax.ppermute(block, axis, [(i, (i - 1 if i % 2 == 0 else i + 1) % count) for i in range(count)])
+    wide = block if wide is None else wide
+    outer = lax.ppermute(wide, axis, [(i, (i - 1 if i % 2 == 0 else i + 1) % count) for i in range(count)])
     return inner, outer
 
 
@@ -93,8 +94,8 @@
 
 
 def first_kernel(*refs, count):
-    sources, (state_ref, index_ref, lists_ref, operators_ref, inverse_ref) = refs[:count], refs[count : count + 5]
-    targets, (sems, block_sems) = refs[count + 5 : -2], refs[-2:]
+    sources, (state_ref, index_ref, lists_ref, operators_ref, inverse_ref, wide_ref) = refs[:count], refs[count : count + 6]
+    targets, (sems, block_sems) = refs[count + 6 : -2], refs[-2:]
     right_ref, links_ref, faces_ref, coarse_links_ref, coarse_faces_ref, operators_in_ref = targets
     whole = [pltpu.make_async_copy(sources[i], targets[i], sems.at[i]) for i in range(count - 1)]
     step = inverse_ref.shape[0] // block_sems.shape[0]
@@ -121,6 +122,8 @@
         )
         result = jnp.where(row == e, product, result)
     state_ref[...] = result.astype(jnp.bfloat16)
+    wide_ref[...] = jnp.zeros(wide_ref.shape, jnp.bfloat16)
+    wide_ref[: result.shape[0]] = result.astype(jnp.bfloat16)
     for copy in whole[1:]:
         copy.wait()
 
@@ -170,7 +173,7 @@
 
 def sweep(refs, blocks, turned=False):
     prev_ref, own_ref, next_ref, index_ref, operators_ref, pick_ref, lift_ref, right_ref = refs
-    states = [prev_ref[...], own_ref[...], next_ref[...]]
+    states = [prev_ref[...], own_ref[...], next_ref[: own_ref.shape[0]]]
     coupled = coupling(states, index_ref[...], operators_ref[...], pick_ref[...], lift_ref[...])
     lowered = (right_ref[...] - coupled).astype(jnp.bfloat16)
     return apply_inverse(blocks, lowered, turned), lowered
@@ -289,7 +292,7 @@
         face_operators,
         fine_inverse,
     )
-    state, fine_index, lists, operators, inverse = run(
+    state, fine_index, lists, operators, inverse, wide = run(
         functools.partial(first_kernel, count=len(operands)),
         [
             ((fine_rows, dofs), bf16),
@@ -297,6 +300,7 @@
             ((coarse_rows, spare), f32),
             ((types * LANES, LANES), bf16),
             (fine_inverse.shape, bf16),
+            ((2 * fine_rows, dofs), bf16),
         ],
         *operands,
         hbm=range(len(operands)),
@@ -306,8 +310,8 @@
     )
     shared = (operators, pick, lift)
 
-    def halo(block, axis):
-        inner, outer = swapped(block, axis)
+    def halo(block, axis, wide=None):
+        inner, outer = swapped(block, axis, wide)
         return inner, block, outer
 
     both = ("fine", "tele")
@@ -315,7 +319,7 @@
         for sweep in range(SWEEPS):
             if cycle == 0 and sweep == 0:
                 continue
-            inner, own, outer = halo(state, both)
+            inner, own, outer = halo(state, both, wide if (cycle, sweep) == (0, 1) else None)
             if cycle == 0 and sweep == 1:
                 sent, inner = lax.optimization_barrier((coarse_inverse, inner))
                 near, other = across(sent, 1), across(sent, tele_size - 1)

time: 160 us -> 162 us (1.012)
  waiting for transfers between devices: 12.6 us -> 15.2 us
    ppermute x11, starting transfers between devices: 48.8 us -> 52.3 us  [swapped(): lax.ppermute(wide, axis, [(i, (i - 1 if i % 2 == 0 else i + 1) % count) f...]
    ppermute x11, starting transfers between devices: 47.5 us -> 44.1 us  [swapped(): inner = lax.ppermute(block, axis, [(i, i ^ 1) for i in range(count)])]
    ppermute x11, waiting for transfers between devices: 11.8 us -> 14.4 us  [swapped(): inner = lax.ppermute(block, axis, [(i, i ^ 1) for i in range(count)])]
  transfers between devices with their start and end apart: 26 -> 26, of which waited for: 9 -> 10; matrix products, arithmetic and copies ran while one was open for 0% -> 0% of each run, Pallas kernels for 4% -> 4%
where the time goes in v10:
time: 162 us; the launch traced here: 161 us
  starting transfers between devices  107 us (66%)
  Pallas kernels  23.4 us (14%)
  waiting for transfers between devices  15.2 us (9%)
  blocking collectives  14.9 us (9%)
    ppermute x11, starting transfers between devices, swapped(): lax.ppermute(wide, axis, [(i, (i - 1 if i % 2 == 0 else i + 1) % count) f...  52.3 us
    ppermute x11, starting transfers between devices, swapped(): inner = lax.ppermute(block, axis, [(i, i ^ 1) for i in range(count)])  44.1 us
    pallas_call x17, Pallas kernels, run(): pl.pallas_call(body, out_shape=[pltpu.VMEM(s, d) if i in pinned else jax....  23.4 us
    all_to_all x2, blocking collectives, shards(): parts = lax.all_to_all(parts, 'tele', 0, 0, tiled=True)  14.9 us
    ppermute x11, waiting for transfers between devices, swapped(): inner = lax.ppermute(block, axis, [(i, i ^ 1) for i in range(count)])  14.4 us
    ppermute x4, starting transfers between devices, across(): lax.ppermute(block, 'tele', [(i, i ^ bits) for i in range(tele_size)])  10.7 us
  transfers between devices with their start and end apart: 26, of which 10 were waited for; matrix products, arithmetic and copies ran while one was open for 0% of the time, Pallas kernels for 4%

profile of v10, /device:TPU:1, one launch (start us, length us, event | category | flops | bytes accessed | tf_op | source)
XLA Modules:
  0.0 161.1 jit_solution(14519999174056788834)
XLA Ops:
  0.0 3.5 %shard_map.109 = (bf16[16,320]{1,0:T(8,128)(2,1)S(1)}, s32[16,12]{1,0:T(8,128)S(1)}, f32[8,64]{1,0:T(8,128)S(1)}, bf16[3072,128]{1,0:T(8,128)(2,1)S(1)}, bf16[16...) custom-call(f32[16,320]{1,0:T(8,128)} %refs_7_.9, s32[6,16]{1,0:T(8,128)} %bitcast.7, s32[6,16]{1,0:T(8,128)} %bitcast.8, ...), custom_call_target="tpu_custom_call" | custom-call | flops 4294967296 | bytes 3605344 | tf_op jit(solution)/shard_map/pallas_call | solution.py:250
  3.5 5.8 %collective-permute-start.1 = (bf16[32,320]{1,0:T(8,128)(2,1)S(1)}, bf16[32,320]{1,0:T(8,128)(2,1)S(1)}, u32[]{:S(2)}, u32[]{:S(2)}) collective-permute-start(bf16[32,320]{1,0:T(8,128)(2,1)S(1)} %get-tuple-element.32), channel_id=1, source_target_pairs={{0,511},{1,2},{2,1},{3,4},{4,3},{5,6},{6,5},{7,8},{8,7},{9,10},{10... | collective-permute-start | bytes 61448 | tf_op jit(solution)/shard_map/ppermute | solution.py:23
  11.2 2.5 %collective-permute-done.refs_0_ = bf16[16,320]{1,0:T(8,128)(2,1)S(1)} collective-permute-done((bf16[16,320]{1,0:T(8,128)(2,1)S(1)}, bf16[16,320]{1,0:T(8,128)(2,1)S(1)}, u32[]{:S(2)}, u32[]{:S(2)}) %collective-permute-start) | collective-permute-done | bytes 10272 | tf_op jit(solution)/shard_map/ppermute | solution.py:21
  13.7 3.5 %collective-permute-start.4 = (bf16[2,320,320]{2,1,0:T(8,128)(2,1)S(1)}, bf16[2,320,320]{2,1,0:T(8,128)(2,1)S(1)}, u32[]{:S(2)}, u32[]{:S(2)}) collective-permute-start(bf16[2,320,320]{2,1,0:T(8,128)(2,1)S(1)} %copy-done), channel_id=1, source_target_pairs={{0,3},{1,2},{2,1},{3,0},{4,7},{5,6},{6,5},{7,4},{8,11},{9,10},{10,... | collective-permute-start | bytes 1228808 | tf_op jit(solution)/shard_map/ppermute | solution.py:281
  21.1 15.8 %collective-permute-start.5 = (bf16[16,320]{1,0:T(8,128)(2,1)S(1)}, bf16[16,320]{1,0:T(8,128)(2,1)S(1)}, u32[]{:S(2)}, u32[]{:S(2)}) collective-permute-start(bf16[16,320]{1,0:T(8,128)(2,1)S(1)} %shard_map.110.refs_1_), channel_id=1, source_target_pairs={{0,511},{1,2},{2,1},{3,4},{4,3},{5,6},{6,5},{7,8},{8,7},{9,10},{10... | collective-permute-start | bytes 30728 | tf_op jit(solution)/shard_map/ppermute | solution.py:23
  38.8 2.7 %shard_map.111.refs_8_ = bf16[16,320,320]{2,1,0:T(8,128)(2,1)S(1)} custom-call(bf16[16,320,320]{2,1,0:T(8,128)(2,1)S(1)} %get-tuple-element.35.refs_8_.refs_0_, bf16[16,320]{1,0:T(8,128)(2,1)S(1)} %shard_map.110.refs_1_), custom_call_target="tpu_custom_call" | custom-call | flops 4294967296 | bytes 3276800 | tf_op jit(solution)/shard_map/pallas_call | solution.py:250
  43.1 4.0 %collective-permute-start.7 = (bf16[16,320]{1,0:T(8,128)(2,1)S(1)}, bf16[16,320]{1,0:T(8,128)(2,1)S(1)}, u32[]{:S(2)}, u32[]{:S(2)}) collective-permute-start(bf16[16,320]{1,0:T(8,128)(2,1)S(1)} %get-tuple-element.38.refs_1_), channel_id=1, source_target_pairs={{0,511},{1,2},{2,1},{3,4},{4,3},{5,6},{6,5},{7,8},{8,7},{9,10},{10... | collective-permute-start | bytes 30728 | tf_op jit(solution)/shard_map/ppermute | solution.py:23
  49.1 3.4 %collective-permute-start.8 = (bf16[1,320,320]{2,1,0:T(8,128)(2,1)S(1)}, bf16[1,320,320]{2,1,0:T(8,128)(2,1)S(1)}, u32[]{:S(2)}, u32[]{:S(2)}) collective-permute-start(bf16[1,320,320]{2,1,0:T(8,128)(2,1)S(1)} %get-tuple-element.43), channel_id=1, source_target_pairs={{0,1},{1,0},{2,3},{3,2},{4,5},{5,4},{6,7},{7,6},{8,9},{9,8},{10,11... | collective-permute-start | bytes 614408 | tf_op jit(solution)/shard_map/ppermute | solution.py:281
  52.4 2.0 %collective-permute-start.9 = (bf16[1,320,320]{2,1,0:T(8,128)(2,1)S(1)}, bf16[1,320,320]{2,1,0:T(8,128)(2,1)S(1)}, u32[]{:S(2)}, u32[]{:S(2)}) collective-permute-start(bf16[1,320,320]{2,1,0:T(8,128)(2,1)S(1)} %get-tuple-element.44), channel_id=1, source_target_pairs={{0,3},{1,2},{2,1},{3,0},{4,7},{5,6},{6,5},{7,4},{8,11},{9,10},{10,... | collective-permute-start | bytes 614408 | tf_op jit(solution)/shard_map/ppermute | solution.py:281
  55.4 8.2 %all_to_all.10.refs_0_ = f32[4,8,384]{2,1,0:T(8,128)S(1)} all-to-all(f32[4,8,384]{2,1,0:T(8,128)S(1)} %shard_map.113), channel_id=1, replica_groups=mesh['fine'=128,'tele'=4] {'tele'}, dimensions={0} | all-to-all | bytes 98304 | tf_op jit(solution)/shard_map/all_to_all | solution.py:362
  66.2 7.6 %collective-permute-start.10 = (bf16[8,320]{1,0:T(8,128)(2,1)S(1)}, bf16[8,320]{1,0:T(8,128)(2,1)S(1)}, u32[]{:S(2)}, u32[]{:S(2)}) collective-permute-start(bf16[8,320]{1,0:T(8,128)(2,1)S(1)} %get-tuple-element.45.refs_5_.refs_1_), channel_id=1, source_target_pairs={{0,4},{4,0},{8,12},{12,8},{16,20},{20,16},{24,28},{28,24},{32,36},... | collective-permute-start | bytes 15368 | tf_op jit(solution)/shard_map/ppermute | solution.py:21
  78.3 5.7 %collective-permute-start.12 = (bf16[8,320]{1,0:T(8,128)(2,1)S(1)}, bf16[8,320]{1,0:T(8,128)(2,1)S(1)}, u32[]{:S(2)}, u32[]{:S(2)}) collective-permute-start(bf16[8,320]{1,0:T(8,128)(2,1)S(1)} %shard_map.117.refs_1_), channel_id=1, source_target_pairs={{0,4},{4,0},{8,12},{12,8},{16,20},{20,16},{24,28},{28,24},{32,36},... | collective-permute-start | bytes 15368 | tf_op jit(solution)/shard_map/ppermute | solution.py:21
  86.0 4.3 %collective-permute-start.15 = (bf16[16,320]{1,0:T(8,128)(2,1)S(1)}, bf16[16,320]{1,0:T(8,128)(2,1)S(1)}, u32[]{:S(2)}, u32[]{:S(2)}) collective-permute-start(bf16[16,320]{1,0:T(8,128)(2,1)S(1)} %shard_map.118.refs_1_), channel_id=1, source_target_pairs={{0,511},{1,2},{2,1},{3,4},{4,3},{5,6},{6,5},{7,8},{8,7},{9,10},{10... | collective-permute-start | bytes 30728 | tf_op jit(solution)/shard_map/ppermute | solution.py:23
  92.3 2.8 %collective-permute-done.14.refs_0_ = bf16[16,320]{1,0:T(8,128)(2,1)S(1)} collective-permute-done((bf16[16,320]{1,0:T(8,128)(2,1)S(1)}, bf16[16,320]{1,0:T(8,128)(2,1)S(1)}, u32[]{:S(2)}, u32[]{:S(2)}) %collective-permute-start.14) | collective-permute-done | bytes 10272 | tf_op jit(solution)/shard_map/ppermute | solution.py:21
  96.5 3.4 %collective-permute-start.17 = (bf16[16,320]{1,0:T(8,128)(2,1)S(1)}, bf16[16,320]{1,0:T(8,128)(2,1)S(1)}, u32[]{:S(2)}, u32[]{:S(2)}) collective-permute-start(bf16[16,320]{1,0:T(8,128)(2,1)S(1)} %shard_map.119.refs_1_), channel_id=1, source_target_pairs={{0,511},{1,2},{2,1},{3,4},{4,3},{5,6},{6,5},{7,8},{8,7},{9,10},{10... | collective-permute-start | bytes 30728 | tf_op jit(solution)/shard_map/ppermute | solution.py:23
  99.9 2.1 %collective-permute-start.16 = (bf16[16,320]{1,0:T(8,128)(2,1)S(1)}, bf16[16,320]{1,0:T(8,128)(2,1)S(1)}, u32[]{:S(2)}, u32[]{:S(2)}) collective-permute-start(bf16[16,320]{1,0:T(8,128)(2,1)S(1)} %shard_map.119.refs_1_), channel_id=1, source_target_pairs={{0,1},{1,0},{2,3},{3,2},{4,5},{5,4},{6,7},{7,6},{8,9},{9,8},{10,11... | collective-permute-start | bytes 30728 | tf_op jit(solution)/shard_map/ppermute | solution.py:21
  105.8 4.6 %collective-permute-start.19 = (bf16[16,320]{1,0:T(8,128)(2,1)S(1)}, bf16[16,320]{1,0:T(8,128)(2,1)S(1)}, u32[]{:S(2)}, u32[]{:S(2)}) collective-permute-start(bf16[16,320]{1,0:T(8,128)(2,1)S(1)} %shard_map.120.refs_1_), channel_id=1, source_target_pairs={{0,511},{1,2},{2,1},{3,4},{4,3},{5,6},{6,5},{7,8},{8,7},{9,10},{10... | collective-permute-start | bytes 30728 | tf_op jit(solution)/shard_map/ppermute | solution.py:23
  112.4 2.5 %collective-permute-done.18.refs_0_ = bf16[16,320]{1,0:T(8,128)(2,1)S(1)} collective-permute-done((bf16[16,320]{1,0:T(8,128)(2,1)S(1)}, bf16[16,320]{1,0:T(8,128)(2,1)S(1)}, u32[]{:S(2)}, u32[]{:S(2)}) %collective-permute-start.18) | collective-permute-done | bytes 10272 | tf_op jit(solution)/shard_map/ppermute | solution.py:21
  116.3 6.4 %collective-permute-start.21 = (bf16[16,320]{1,0:T(8,128)(2,1)S(1)}, bf16[16,320]{1,0:T(8,128)(2,1)S(1)}, u32[]{:S(2)}, u32[]{:S(2)}) collective-permute-start(bf16[16,320]{1,0:T(8,128)(2,1)S(1)} %get-tuple-element.49.refs_1_), channel_id=1, source_target_pairs={{0,511},{1,2},{2,1},{3,4},{4,3},{5,6},{6,5},{7,8},{8,7},{9,10},{10... | collective-permute-start | bytes 30728 | tf_op jit(solution)/shard_map/ppermute | solution.py:23
  124.7 2.5 %collective-permute-done.20.refs_0_ = bf16[16,320]{1,0:T(8,128)(2,1)S(1)} collective-permute-done((bf16[16,320]{1,0:T(8,128)(2,1)S(1)}, bf16[16,320]{1,0:T(8,128)(2,1)S(1)}, u32[]{:S(2)}, u32[]{:S(2)}) %collective-permute-start.20) | collective-permute-done | bytes 10272 | tf_op jit(solution)/shard_map/ppermute | solution.py:21
  128.2 6.7 %all_to_all.11.refs_0_ = f32[4,8,384]{2,1,0:T(8,128)S(1)} all-to-all(f32[4,8,384]{2,1,0:T(8,128)S(1)} %shard_map.122), channel_id=1, replica_groups=mesh['fine'=128,'tele'=4] {'tele'}, dimensions={0} | all-to-all | bytes 98304 | tf_op jit(solution)/shard_map/all_to_all | solution.py:362
  135.3 2.2 %collective-permute-start.23 = (bf16[8,320]{1,0:T(8,128)(2,1)S(1)}, bf16[8,320]{1,0:T(8,128)(2,1)S(1)}, u32[]{:S(2)}, u32[]{:S(2)}) collective-permute-start(bf16[8,320]{1,0:T(8,128)(2,1)S(1)} %get-tuple-element.51.refs_1_), channel_id=1, source_target_pairs={{0,508},{4,8},{8,4},{12,16},{16,12},{20,24},{24,20},{28,32},{32,28... | collective-permute-start | bytes 15368 | tf_op jit(solution)/shard_map/ppermute | solution.py:23
  137.5 10.8 %collective-permute-start.22 = (bf16[8,320]{1,0:T(8,128)(2,1)S(1)}, bf16[8,320]{1,0:T(8,128)(2,1)S(1)}, u32[]{:S(2)}, u32[]{:S(2)}) collective-permute-start(bf16[8,320]{1,0:T(8,128)(2,1)S(1)} %get-tuple-element.51.refs_1_), channel_id=1, source_target_pairs={{0,4},{4,0},{8,12},{12,8},{16,20},{20,16},{24,28},{28,24},{32,36},... | collective-permute-start | bytes 15368 | tf_op jit(solution)/shard_map/ppermute | solution.py:21
  152.1 6.3 %collective-permute-start.24 = (bf16[8,320]{1,0:T(8,128)(2,1)S(1)}, bf16[8,320]{1,0:T(8,128)(2,1)S(1)}, u32[]{:S(2)}, u32[]{:S(2)}) collective-permute-start(bf16[8,320]{1,0:T(8,128)(2,1)S(1)} %shard_map.124.refs_1_), channel_id=1, source_target_pairs={{0,4},{4,0},{8,12},{12,8},{16,20},{20,16},{24,28},{28,24},{32,36},... | collective-permute-start | bytes 15368 | tf_op jit(solution)/shard_map/ppermute | solution.py:21
  (57 shorter events, 41.4 us)
Async XLA Ops:
  3.5 15.6 %collective-permute-start.1 = (bf16[32,320]{1,0:T(8,128)(2,1)S(1)}, bf16[32,320]{1,0:T(8,128)(2,1)S(1)}, u32[]{:S(2)}, u32[]{:S(2)}) collective-permute-start(bf16[32,320]{1,0:T(8,128)(2,1)S(1)} %get-tuple-element.32), channel_id=1, source_target_pairs={{0,511},{1,2},{2,1},{3,4},{4,3},{5,6},{6,5},{7,8},{8,7},{9,10},{10... | collective-permute-start | bytes 61448 | tf_op jit(solution)/shard_map/ppermute | solution.py:23
  13.7 27.8 %collective-permute-start.4 = (bf16[2,320,320]{2,1,0:T(8,128)(2,1)S(1)}, bf16[2,320,320]{2,1,0:T(8,128)(2,1)S(1)}, u32[]{:S(2)}, u32[]{:S(2)}) collective-permute-start(bf16[2,320,320]{2,1,0:T(8,128)(2,1)S(1)} %copy-done), channel_id=1, source_target_pairs={{0,3},{1,2},{2,1},{3,0},{4,7},{5,6},{6,5},{7,4},{8,11},{9,10},{10,... | collective-permute-start | bytes 1228808 | tf_op jit(solution)/shard_map/ppermute | solution.py:281
  17.2 24.3 %collective-permute-start.3 = (bf16[2,320,320]{2,1,0:T(8,128)(2,1)S(1)}, bf16[2,320,320]{2,1,0:T(8,128)(2,1)S(1)}, u32[]{:S(2)}, u32[]{:S(2)}) collective-permute-start(bf16[2,320,320]{2,1,0:T(8,128)(2,1)S(1)} %copy-done), channel_id=1, source_target_pairs={{0,1},{1,0},{2,3},{3,2},{4,5},{5,4},{6,7},{7,6},{8,9},{9,8},{10,11... | collective-permute-start | bytes 1228808 | tf_op jit(solution)/shard_map/ppermute | solution.py:281
  21.1 20.4 %collective-permute-start.5 = (bf16[16,320]{1,0:T(8,128)(2,1)S(1)}, bf16[16,320]{1,0:T(8,128)(2,1)S(1)}, u32[]{:S(2)}, u32[]{:S(2)}) collective-permute-start(bf16[16,320]{1,0:T(8,128)(2,1)S(1)} %shard_map.110.refs_1_), channel_id=1, source_target_pairs={{0,511},{1,2},{2,1},{3,4},{4,3},{5,6},{6,5},{7,8},{8,7},{9,10},{10... | collective-permute-start | bytes 30728 | tf_op jit(solution)/shard_map/ppermute | solution.py:23
  36.9 4.7 %collective-permute-start.2 = (bf16[16,320]{1,0:T(8,128)(2,1)S(1)}, bf16[16,320]{1,0:T(8,128)(2,1)S(1)}, u32[]{:S(2)}, u32[]{:S(2)}) collective-permute-start(bf16[16,320]{1,0:T(8,128)(2,1)S(1)} %shard_map.110.refs_1_), channel_id=1, source_target_pairs={{0,1},{1,0},{2,3},{3,2},{4,5},{5,4},{6,7},{7,6},{8,9},{9,8},{10,11... | collective-permute-start | bytes 30728 | tf_op jit(solution)/shard_map/ppermute | solution.py:21
  43.1 11.3 %collective-permute-start.7 = (bf16[16,320]{1,0:T(8,128)(2,1)S(1)}, bf16[16,320]{1,0:T(8,128)(2,1)S(1)}, u32[]{:S(2)}, u32[]{:S(2)}) collective-permute-start(bf16[16,320]{1,0:T(8,128)(2,1)S(1)} %get-tuple-element.38.refs_1_), channel_id=1, source_target_pairs={{0,511},{1,2},{2,1},{3,4},{4,3},{5,6},{6,5},{7,8},{8,7},{9,10},{10... | collective-permute-start | bytes 30728 | tf_op jit(solution)/shard_map/ppermute | solution.py:23
  47.1 7.3 %collective-permute-start.6 = (bf16[16,320]{1,0:T(8,128)(2,1)S(1)}, bf16[16,320]{1,0:T(8,128)(2,1)S(1)}, u32[]{:S(2)}, u32[]{:S(2)}) collective-permute-start(bf16[16,320]{1,0:T(8,128)(2,1)S(1)} %get-tuple-element.38.refs_1_), channel_id=1, source_target_pairs={{0,1},{1,0},{2,3},{3,2},{4,5},{5,4},{6,7},{7,6},{8,9},{9,8},{10,11... | collective-permute-start | bytes 30728 | tf_op jit(solution)/shard_map/ppermute | solution.py:21
  49.1 14.5 %collective-permute-start.8 = (bf16[1,320,320]{2,1,0:T(8,128)(2,1)S(1)}, bf16[1,320,320]{2,1,0:T(8,128)(2,1)S(1)}, u32[]{:S(2)}, u32[]{:S(2)}) collective-permute-start(bf16[1,320,320]{2,1,0:T(8,128)(2,1)S(1)} %get-tuple-element.43), channel_id=1, source_target_pairs={{0,1},{1,0},{2,3},{3,2},{4,5},{5,4},{6,7},{7,6},{8,9},{9,8},{10,11... | collective-permute-start | bytes 614408 | tf_op jit(solution)/shard_map/ppermute | solution.py:281
  52.4 11.2 %collective-permute-start.9 = (bf16[1,320,320]{2,1,0:T(8,128)(2,1)S(1)}, bf16[1,320,320]{2,1,0:T(8,128)(2,1)S(1)}, u32[]{:S(2)}, u32[]{:S(2)}) collective-permute-start(bf16[1,320,320]{2,1,0:T(8,128)(2,1)S(1)} %get-tuple-element.44), channel_id=1, source_target_pairs={{0,3},{1,2},{2,1},{3,0},{4,7},{5,6},{6,5},{7,4},{8,11},{9,10},{10,... | collective-permute-start | bytes 614408 | tf_op jit(solution)/shard_map/ppermute | solution.py:281
  64.2 11.0 %collective-permute-start.11 = (bf16[8,320]{1,0:T(8,128)(2,1)S(1)}, bf16[8,320]{1,0:T(8,128)(2,1)S(1)}, u32[]{:S(2)}, u32[]{:S(2)}) collective-permute-start(bf16[8,320]{1,0:T(8,128)(2,1)S(1)} %get-tuple-element.45.refs_5_.refs_1_), channel_id=1, source_target_pairs={{0,508},{4,8},{8,4},{12,16},{16,12},{20,24},{24,20},{28,32},{32,28... | collective-permute-start | bytes 15368 | tf_op jit(solution)/shard_map/ppermute | solution.py:23
  66.2 9.1 %collective-permute-start.10 = (bf16[8,320]{1,0:T(8,128)(2,1)S(1)}, bf16[8,320]{1,0:T(8,128)(2,1)S(1)}, u32[]{:S(2)}, u32[]{:S(2)}) collective-permute-start(bf16[8,320]{1,0:T(8,128)(2,1)S(1)} %get-tuple-element.45.refs_5_.refs_1_), channel_id=1, source_target_pairs={{0,4},{4,0},{8,12},{12,8},{16,20},{20,16},{24,28},{28,24},{32,36},... | collective-permute-start | bytes 15368 | tf_op jit(solution)/shard_map/ppermute | solution.py:21
  76.3 7.7 %collective-permute-start.13 = (bf16[8,320]{1,0:T(8,128)(2,1)S(1)}, bf16[8,320]{1,0:T(8,128)(2,1)S(1)}, u32[]{:S(2)}, u32[]{:S(2)}) collective-permute-start(bf16[8,320]{1,0:T(8,128)(2,1)S(1)} %shard_map.117.refs_1_), channel_id=1, source_target_pairs={{0,508},{4,8},{8,4},{12,16},{16,12},{20,24},{24,20},{28,32},{32,28... | collective-permute-start | bytes 15368 | tf_op jit(solution)/shard_map/ppermute | solution.py:23
  78.3 6.6 %collective-permute-start.12 = (bf16[8,320]{1,0:T(8,128)(2,1)S(1)}, bf16[8,320]{1,0:T(8,128)(2,1)S(1)}, u32[]{:S(2)}, u32[]{:S(2)}) collective-permute-start(bf16[8,320]{1,0:T(8,128)(2,1)S(1)} %shard_map.117.refs_1_), channel_id=1, source_target_pairs={{0,4},{4,0},{8,12},{12,8},{16,20},{20,16},{24,28},{28,24},{32,36},... | collective-permute-start | bytes 15368 | tf_op jit(solution)/shard_map/ppermute | solution.py:21
  86.0 6.3 %collective-permute-start.15 = (bf16[16,320]{1,0:T(8,128)(2,1)S(1)}, bf16[16,320]{1,0:T(8,128)(2,1)S(1)}, u32[]{:S(2)}, u32[]{:S(2)}) collective-permute-start(bf16[16,320]{1,0:T(8,128)(2,1)S(1)} %shard_map.118.refs_1_), channel_id=1, source_target_pairs={{0,511},{1,2},{2,1},{3,4},{4,3},{5,6},{6,5},{7,8},{8,7},{9,10},{10... | collective-permute-start | bytes 30728 | tf_op jit(solution)/shard_map/ppermute | solution.py:23
  90.3 4.7 %collective-permute-start.14 = (bf16[16,320]{1,0:T(8,128)(2,1)S(1)}, bf16[16,320]{1,0:T(8,128)(2,1)S(1)}, u32[]{:S(2)}, u32[]{:S(2)}) collective-permute-start(bf16[16,320]{1,0:T(8,128)(2,1)S(1)} %shard_map.118.refs_1_), channel_id=1, source_target_pairs={{0,1},{1,0},{2,3},{3,2},{4,5},{5,4},{6,7},{7,6},{8,9},{9,8},{10,11... | collective-permute-start | bytes 30728 | tf_op jit(solution)/shard_map/ppermute | solution.py:21
  96.5 6.3 %collective-permute-start.17 = (bf16[16,320]{1,0:T(8,128)(2,1)S(1)}, bf16[16,320]{1,0:T(8,128)(2,1)S(1)}, u32[]{:S(2)}, u32[]{:S(2)}) collective-permute-start(bf16[16,320]{1,0:T(8,128)(2,1)S(1)} %shard_map.119.refs_1_), channel_id=1, source_target_pairs={{0,511},{1,2},{2,1},{3,4},{4,3},{5,6},{6,5},{7,8},{8,7},{9,10},{10... | collective-permute-start | bytes 30728 | tf_op jit(solution)/shard_map/ppermute | solution.py:23
  99.9 4.4 %collective-permute-start.16 = (bf16[16,320]{1,0:T(8,128)(2,1)S(1)}, bf16[16,320]{1,0:T(8,128)(2,1)S(1)}, u32[]{:S(2)}, u32[]{:S(2)}) collective-permute-start(bf16[16,320]{1,0:T(8,128)(2,1)S(1)} %shard_map.119.refs_1_), channel_id=1, source_target_pairs={{0,1},{1,0},{2,3},{3,2},{4,5},{5,4},{6,7},{7,6},{8,9},{9,8},{10,11... | collective-permute-start | bytes 30728 | tf_op jit(solution)/shard_map/ppermute | solution.py:21
  105.8 6.6 %collective-permute-start.19 = (bf16[16,320]{1,0:T(8,128)(2,1)S(1)}, bf16[16,320]{1,0:T(8,128)(2,1)S(1)}, u32[]{:S(2)}, u32[]{:S(2)}) collective-permute-start(bf16[16,320]{1,0:T(8,128)(2,1)S(1)} %shard_map.120.refs_1_), channel_id=1, source_target_pairs={{0,511},{1,2},{2,1},{3,4},{4,3},{5,6},{6,5},{7,8},{8,7},{9,10},{10... | collective-permute-start | bytes 30728 | tf_op jit(solution)/shard_map/ppermute | solution.py:23
  116.3 8.4 %collective-permute-start.21 = (bf16[16,320]{1,0:T(8,128)(2,1)S(1)}, bf16[16,320]{1,0:T(8,128)(2,1)S(1)}, u32[]{:S(2)}, u32[]{:S(2)}) collective-permute-start(bf16[16,320]{1,0:T(8,128)(2,1)S(1)} %get-tuple-element.49.refs_1_), channel_id=1, source_target_pairs={{0,511},{1,2},{2,1},{3,4},{4,3},{5,6},{6,5},{7,8},{8,7},{9,10},{10... | collective-permute-start | bytes 30728 | tf_op jit(solution)/shard_map/ppermute | solution.py:23
  122.8 4.4 %collective-permute-start.20 = (bf16[16,320]{1,0:T(8,128)(2,1)S(1)}, bf16[16,320]{1,0:T(8,128)(2,1)S(1)}, u32[]{:S(2)}, u32[]{:S(2)}) collective-permute-start(bf16[16,320]{1,0:T(8,128)(2,1)S(1)} %get-tuple-element.49.refs_1_), channel_id=1, source_target_pairs={{0,1},{1,0},{2,3},{3,2},{4,5},{5,4},{6,7},{7,6},{8,9},{9,8},{10,11... | collective-permute-start | bytes 30728 | tf_op jit(solution)/shard_map/ppermute | solution.py:21
  135.3 13.0 %collective-permute-start.23 = (bf16[8,320]{1,0:T(8,128)(2,1)S(1)}, bf16[8,320]{1,0:T(8,128)(2,1)S(1)}, u32[]{:S(2)}, u32[]{:S(2)}) collective-permute-start(bf16[8,320]{1,0:T(8,128)(2,1)S(1)} %get-tuple-element.51.refs_1_), channel_id=1, source_target_pairs={{0,508},{4,8},{8,4},{12,16},{16,12},{20,24},{24,20},{28,32},{32,28... | collective-permute-start | bytes 15368 | tf_op jit(solution)/shard_map/ppermute | solution.py:23
  137.5 11.6 %collective-permute-start.22 = (bf16[8,320]{1,0:T(8,128)(2,1)S(1)}, bf16[8,320]{1,0:T(8,128)(2,1)S(1)}, u32[]{:S(2)}, u32[]{:S(2)}) collective-permute-start(bf16[8,320]{1,0:T(8,128)(2,1)S(1)} %get-tuple-element.51.refs_1_), channel_id=1, source_target_pairs={{0,4},{4,0},{8,12},{12,8},{16,20},{20,16},{24,28},{28,24},{32,36},... | collective-permute-start | bytes 15368 | tf_op jit(solution)/shard_map/ppermute | solution.py:21
  150.2 8.3 %collective-permute-start.25 = (bf16[8,320]{1,0:T(8,128)(2,1)S(1)}, bf16[8,320]{1,0:T(8,128)(2,1)S(1)}, u32[]{:S(2)}, u32[]{:S(2)}) collective-permute-start(bf16[8,320]{1,0:T(8,128)(2,1)S(1)} %shard_map.124.refs_1_), channel_id=1, source_target_pairs={{0,508},{4,8},{8,4},{12,16},{16,12},{20,24},{24,20},{28,32},{32,28... | collective-permute-start | bytes 15368 | tf_op jit(solution)/shard_map/ppermute | solution.py:23
  152.1 7.1 %collective-permute-start.24 = (bf16[8,320]{1,0:T(8,128)(2,1)S(1)}, bf16[8,320]{1,0:T(8,128)(2,1)S(1)}, u32[]{:S(2)}, u32[]{:S(2)}) collective-permute-start(bf16[8,320]{1,0:T(8,128)(2,1)S(1)} %shard_map.124.refs_1_), channel_id=1, source_target_pairs={{0,4},{4,0},{8,12},{12,8},{16,20},{20,16},{24,28},{28,24},{32,36},... | collective-permute-start | bytes 15368 | tf_op jit(solution)/shard_map/ppermute | solution.py:21
  (7 other events, 91.4 us)

commit v11 on v9

--- a/solution.py
+++ b/solution.py
@@ -161,11 +161,6 @@
     for place, (ref, e) in enumerate(blocks):
         turned = lax.dot_general(unit, ref[e], (((1,), (1,)), ((), ())), preferred_element_type=jnp.float32)
         out_ref[place] = turned.astype(jnp.bfloat16)
-
-
-def take_kernel(before_ref, after_ref, low_ref, high_ref):
-    low_ref[...] = before_ref[0:1]
-    high_ref[...] = after_ref[1:2]
 
 
 def sweep(refs, blocks, turned=False):
@@ -321,12 +316,9 @@
                 near, other = across(sent, 1), across(sent, tele_size - 1)
             if cycle == 0 and sweep == 2:
                 near, other, outer = lax.optimization_barrier((near, other, outer))
-                far_low, far_high = run(take_kernel, [((1,) + near.shape[1:], bf16)] * 2, other, near)
-                far_low, far_high = across(far_low, 1), across(far_high, tele_size - 1)
-                blocks = (coarse_inverse, near, far_low, far_high, other)
-            turned = (cycle, sweep) != (0, 1)
-            if cycle == 0 and sweep == 2:
-                inverse = run(turn_kernel, (inverse.shape, bf16), inverse, held=(0,), keep=(state,), pinned=(0,))
+                far = across(other, 1)
+                blocks = (coarse_inverse, near, far, other)
+            turned = cycle > 0
             outs = [((fine_rows, dofs), bf16)]
             if sweep == SWEEPS - 1:
                 outs += [((fine_rows, dofs), f32), ((fine_rows, dofs), bf16)]
@@ -343,6 +335,8 @@
                 held=(5, 6, 8),
             )
             state = result[0]
+            if cycle == 0 and sweep == SWEEPS - 1:
+                inverse = run(turn_kernel, (inverse.shape, bf16), inverse, held=(0,), keep=(state,), pinned=(0,))
         solution, lowered = result[1], result[2]
         parts = run(
             restrict_kernel,
@@ -354,6 +348,7 @@
             target,
             lists,
             held=(5, 6),
+            keep=(far,) if cycle == 0 else (),
         )
         parts = lax.all_to_all(parts, "tele", 0, 0, tiled=True)
         restricted, coarse, coarse_index = run(

time: 160 us -> 158 us (0.988)
    ppermute x11, starting transfers between devices: 48.8 us -> 53.4 us  [swapped(): lax.ppermute(block, axis, [(i, (i - 1 if i % 2 == 0 else i + 1) % count)...]
    ppermute x11, starting transfers between devices: 47.5 us -> 44.6 us  [swapped(): inner = lax.ppermute(block, axis, [(i, i ^ 1) for i in range(count)])]
    ppermute x4 -> x3, starting transfers between devices: 11.4 us -> 9.4 us  [across(): lax.ppermute(block, 'tele', [(i, i ^ bits) for i in range(tele_size)])]
    pallas_call x17 -> x16, Pallas kernels: 23.4 us -> 23.8 us  [run(): pl.pallas_call(body, out_shape=[pltpu.VMEM(s, d) if i in pinned else jax....]
  transfers between devices with their start and end apart: 26 -> 25, of which waited for: 9 -> 9; matrix products, arithmetic and copies ran while one was open for 0% -> 0% of each run, Pallas kernels for 4% -> 5%
where the time goes in v11:
time: 158 us
  starting transfers between devices  107 us (68%)
  Pallas kernels  23.8 us (15%)
  blocking collectives  13.5 us (9%)
  waiting for transfers between devices  12.4 us (8%)
    ppermute x11, starting transfers between devices, swapped(): lax.ppermute(block, axis, [(i, (i - 1 if i % 2 == 0 else i + 1) % count)...  53.4 us
    ppermute x11, starting transfers between devices, swapped(): inner = lax.ppermute(block, axis, [(i, i ^ 1) for i in range(count)])  44.6 us
    pallas_call x16, Pallas kernels, run(): pl.pallas_call(body, out_shape=[pltpu.VMEM(s, d) if i in pinned else jax....  23.8 us
    all_to_all x2, blocking collectives, shards(): parts = lax.all_to_all(parts, 'tele', 0, 0, tiled=True)  13.5 us
    ppermute x11, waiting for transfers between devices, swapped(): inner = lax.ppermute(block, axis, [(i, i ^ 1) for i in range(count)])  12.1 us
    ppermute x3, starting transfers between devices, across(): lax.ppermute(block, 'tele', [(i, i ^ bits) for i in range(tele_size)])  9.4 us
  transfers between devices with their start and end apart: 25, of which 9 were waited for; matrix products, arithmetic and copies ran while one was open for 0% of the time, Pallas kernels for 5%

profile of v11, /device:TPU:1, one launch (start us, length us, event | category | flops | bytes accessed | tf_op | source)
XLA Modules:
  0.0 157.6 jit_solution(1676993317279886190)
XLA Ops:
  0.0 3.4 %shard_map.109 = (bf16[16,320]{1,0:T(8,128)(2,1)S(1)}, s32[16,12]{1,0:T(8,128)S(1)}, f32[8,64]{1,0:T(8,128)S(1)}, bf16[3072,128]{1,0:T(8,128)(2,1)S(1)}, bf16[16,320,320]{2,1,0:T(8,128)(2,1)S(1)}) custom-call(f32[16,320]{1,0:T(8,128)} %refs_7_.9, s32[6,16]{1,0:T(8,128)} %bitcast.7, s32[6,16]{1,0:T(8,128)} %bitcast.8, s32[2,6]{1,0:T(2,128)} %refs_3_.1, ...), custom_call_target="tpu_custom_call" | custom-call | flops 4294967296 | bytes 3605344 | tf_op jit(solution)/shard_map/pallas_call | solution.py:242
  3.5 3.9 %collective-permute-start = (bf16[16,320]{1,0:T(8,128)(2,1)S(1)}, bf16[16,320]{1,0:T(8,128)(2,1)S(1)}, u32[]{:S(2)}, u32[]{:S(2)}) collective-permute-start(bf16[16,320]{1,0:T(8,128)(2,1)S(1)} %get-tuple-element.27.refs_1_), channel_id=1, source_target_pairs={{0,1},{1,0},{2,3},{3,2},{4,5},{5,4},{6,7},{7,6},{8,9},{9,8},{10,11... | collective-permute-start | bytes 30728 | tf_op jit(solution)/shard_map/ppermute | solution.py:21
  7.4 4.6 %collective-permute-start.1 = (bf16[16,320]{1,0:T(8,128)(2,1)S(1)}, bf16[16,320]{1,0:T(8,128)(2,1)S(1)}, u32[]{:S(2)}, u32[]{:S(2)}) collective-permute-start(bf16[16,320]{1,0:T(8,128)(2,1)S(1)} %get-tuple-element.27.refs_1_), channel_id=1, source_target_pairs={{0,511},{1,2},{2,1},{3,4},{4,3},{5,6},{6,5},{7,8},{8,7},{9,10},{10... | collective-permute-start | bytes 30728 | tf_op jit(solution)/shard_map/ppermute | solution.py:22
  12.0 4.1 %collective-permute-start.4 = (bf16[2,320,320]{2,1,0:T(8,128)(2,1)S(1)}, bf16[2,320,320]{2,1,0:T(8,128)(2,1)S(1)}, u32[]{:S(2)}, u32[]{:S(2)}) collective-permute-start(bf16[2,320,320]{2,1,0:T(8,128)(2,1)S(1)} %copy-done), channel_id=1, source_target_pairs={{0,3},{1,2},{2,1},{3,0},{4,7},{5,6},{6,5},{7,4},{8,11},{9,10},{10,... | collective-permute-start | bytes 1228808 | tf_op jit(solution)/shard_map/ppermute | solution.py:273
  20.1 13.6 %collective-permute-start.5 = (bf16[16,320]{1,0:T(8,128)(2,1)S(1)}, bf16[16,320]{1,0:T(8,128)(2,1)S(1)}, u32[]{:S(2)}, u32[]{:S(2)}) collective-permute-start(bf16[16,320]{1,0:T(8,128)(2,1)S(1)} %shard_map.110.refs_1_), channel_id=1, source_target_pairs={{0,511},{1,2},{2,1},{3,4},{4,3},{5,6},{6,5},{7,8},{8,7},{9,10},{10... | collective-permute-start | bytes 30728 | tf_op jit(solution)/shard_map/ppermute | solution.py:22
  35.7 3.4 %collective-permute-start.8 = (bf16[2,320,320]{2,1,0:T(8,128)(2,1)S(1)}, bf16[2,320,320]{2,1,0:T(8,128)(2,1)S(1)}, u32[]{:S(2)}, u32[]{:S(2)}) collective-permute-start(bf16[2,320,320]{2,1,0:T(8,128)(2,1)S(1)} %collective-permute-done.4.refs_4_.refs_3_), channel_id=1, source_target_pairs={{0,1},{1,0},{2,3},{3,2},{4,5},{5,4},{6,7},{7,6},{8,9},{9,8},{10,11... | collective-permute-start | bytes 1228808 | tf_op jit(solution)/shard_map/ppermute | solution.py:273
  41.0 8.0 %collective-permute-start.7 = (bf16[16,320]{1,0:T(8,128)(2,1)S(1)}, bf16[16,320]{1,0:T(8,128)(2,1)S(1)}, u32[]{:S(2)}, u32[]{:S(2)}) collective-permute-start(bf16[16,320]{1,0:T(8,128)(2,1)S(1)} %get-tuple-element.34.refs_1_), channel_id=1, source_target_pairs={{0,511},{1,2},{2,1},{3,4},{4,3},{5,6},{6,5},{7,8},{8,7},{9,10},{10... | collective-permute-start | bytes 30728 | tf_op jit(solution)/shard_map/ppermute | solution.py:22
  51.0 2.5 %collective-permute-done.6.refs_0_ = bf16[16,320]{1,0:T(8,128)(2,1)S(1)} collective-permute-done((bf16[16,320]{1,0:T(8,128)(2,1)S(1)}, bf16[16,320]{1,0:T(8,128)(2,1)S(1)}, u32[]{:S(2)}, u32[]{:S(2)}) %collective-permute-start.6) | collective-permute-done | bytes 10272 | tf_op jit(solution)/shard_map/ppermute | solution.py:21
  54.5 6.7 %all_to_all.10.refs_0_ = f32[4,8,384]{2,1,0:T(8,128)S(1)} all-to-all(f32[4,8,384]{2,1,0:T(8,128)S(1)} %shard_map.112), channel_id=1, replica_groups=mesh['fine'=128,'tele'=4] {'tele'}, dimensions={0} | all-to-all | bytes 98304 | tf_op jit(solution)/shard_map/all_to_all | solution.py:353
  63.8 6.6 %collective-permute-start.9 = (bf16[8,320]{1,0:T(8,128)(2,1)S(1)}, bf16[8,320]{1,0:T(8,128)(2,1)S(1)}, u32[]{:S(2)}, u32[]{:S(2)}) collective-permute-start(bf16[8,320]{1,0:T(8,128)(2,1)S(1)} %get-tuple-element.39.refs_4_.refs_1_), channel_id=1, source_target_pairs={{0,4},{4,0},{8,12},{12,8},{16,20},{20,16},{24,28},{28,24},{32,36},... | collective-permute-start | bytes 15368 | tf_op jit(solution)/shard_map/ppermute | solution.py:21
  74.9 5.4 %collective-permute-start.11 = (bf16[8,320]{1,0:T(8,128)(2,1)S(1)}, bf16[8,320]{1,0:T(8,128)(2,1)S(1)}, u32[]{:S(2)}, u32[]{:S(2)}) collective-permute-start(bf16[8,320]{1,0:T(8,128)(2,1)S(1)} %shard_map.115.refs_1_), channel_id=1, source_target_pairs={{0,4},{4,0},{8,12},{12,8},{16,20},{20,16},{24,28},{28,24},{32,36},... | collective-permute-start | bytes 15368 | tf_op jit(solution)/shard_map/ppermute | solution.py:21
  82.3 4.3 %collective-permute-start.14 = (bf16[16,320]{1,0:T(8,128)(2,1)S(1)}, bf16[16,320]{1,0:T(8,128)(2,1)S(1)}, u32[]{:S(2)}, u32[]{:S(2)}) collective-permute-start(bf16[16,320]{1,0:T(8,128)(2,1)S(1)} %shard_map.116.refs_1_), channel_id=1, source_target_pairs={{0,511},{1,2},{2,1},{3,4},{4,3},{5,6},{6,5},{7,8},{8,7},{9,10},{10... | collective-permute-start | bytes 30728 | tf_op jit(solution)/shard_map/ppermute | solution.py:22
  88.6 2.7 %shard_map.117.refs_8_ = bf16[16,320,320]{2,1,0:T(8,128)(2,1)S(1)} custom-call(bf16[16,320,320]{2,1,0:T(8,128)(2,1)S(1)} %get-tuple-element.31.refs_8_.refs_0_, bf16[16,320]{1,0:T(8,128)(2,1)S(1)} %get-tuple-element.34.refs_1_), custom_call_target="tpu_custom_call" | custom-call | flops 4294967296 | bytes 3276800 | tf_op jit(solution)/shard_map/pallas_call | solution.py:242
  92.8 3.9 %collective-permute-start.16 = (bf16[16,320]{1,0:T(8,128)(2,1)S(1)}, bf16[16,320]{1,0:T(8,128)(2,1)S(1)}, u32[]{:S(2)}, u32[]{:S(2)}) collective-permute-start(bf16[16,320]{1,0:T(8,128)(2,1)S(1)} %shard_map.118.refs_1_), channel_id=1, source_target_pairs={{0,511},{1,2},{2,1},{3,4},{4,3},{5,6},{6,5},{7,8},{8,7},{9,10},{10... | collective-permute-start | bytes 30728 | tf_op jit(solution)/shard_map/ppermute | solution.py:22
  96.7 2.1 %collective-permute-start.15 = (bf16[16,320]{1,0:T(8,128)(2,1)S(1)}, bf16[16,320]{1,0:T(8,128)(2,1)S(1)}, u32[]{:S(2)}, u32[]{:S(2)}) collective-permute-start(bf16[16,320]{1,0:T(8,128)(2,1)S(1)} %shard_map.118.refs_1_), channel_id=1, source_target_pairs={{0,1},{1,0},{2,3},{3,2},{4,5},{5,4},{6,7},{7,6},{8,9},{9,8},{10,11... | collective-permute-start | bytes 30728 | tf_op jit(solution)/shard_map/ppermute | solution.py:21
  99.1 2.1 %collective-permute-done.15.refs_0_ = bf16[16,320]{1,0:T(8,128)(2,1)S(1)} collective-permute-done((bf16[16,320]{1,0:T(8,128)(2,1)S(1)}, bf16[16,320]{1,0:T(8,128)(2,1)S(1)}, u32[]{:S(2)}, u32[]{:S(2)}) %collective-permute-start.15) | collective-permute-done | bytes 10272 | tf_op jit(solution)/shard_map/ppermute | solution.py:21
  102.6 5.2 %collective-permute-start.18 = (bf16[16,320]{1,0:T(8,128)(2,1)S(1)}, bf16[16,320]{1,0:T(8,128)(2,1)S(1)}, u32[]{:S(2)}, u32[]{:S(2)}) collective-permute-start(bf16[16,320]{1,0:T(8,128)(2,1)S(1)} %shard_map.119.refs_1_), channel_id=1, source_target_pairs={{0,511},{1,2},{2,1},{3,4},{4,3},{5,6},{6,5},{7,8},{8,7},{9,10},{10... | collective-permute-start | bytes 30728 | tf_op jit(solution)/shard_map/ppermute | solution.py:22
  109.7 2.5 %collective-permute-done.17.refs_0_ = bf16[16,320]{1,0:T(8,128)(2,1)S(1)} collective-permute-done((bf16[16,320]{1,0:T(8,128)(2,1)S(1)}, bf16[16,320]{1,0:T(8,128)(2,1)S(1)}, u32[]{:S(2)}, u32[]{:S(2)}) %collective-permute-start.17) | collective-permute-done | bytes 10272 | tf_op jit(solution)/shard_map/ppermute | solution.py:21
  113.7 5.6 %collective-permute-start.20 = (bf16[16,320]{1,0:T(8,128)(2,1)S(1)}, bf16[16,320]{1,0:T(8,128)(2,1)S(1)}, u32[]{:S(2)}, u32[]{:S(2)}) collective-permute-start(bf16[16,320]{1,0:T(8,128)(2,1)S(1)} %get-tuple-element.43.refs_1_), channel_id=1, source_target_pairs={{0,511},{1,2},{2,1},{3,4},{4,3},{5,6},{6,5},{7,8},{8,7},{9,10},{10... | collective-permute-start | bytes 30728 | tf_op jit(solution)/shard_map/ppermute | solution.py:22
  121.2 2.5 %collective-permute-done.19.refs_0_ = bf16[16,320]{1,0:T(8,128)(2,1)S(1)} collective-permute-done((bf16[16,320]{1,0:T(8,128)(2,1)S(1)}, bf16[16,320]{1,0:T(8,128)(2,1)S(1)}, u32[]{:S(2)}, u32[]{:S(2)}) %collective-permute-start.19) | collective-permute-done | bytes 10272 | tf_op jit(solution)/shard_map/ppermute | solution.py:21
  124.7 6.7 %all_to_all.11.refs_0_ = f32[4,8,384]{2,1,0:T(8,128)S(1)} all-to-all(f32[4,8,384]{2,1,0:T(8,128)S(1)} %shard_map.121), channel_id=1, replica_groups=mesh['fine'=128,'tele'=4] {'tele'}, dimensions={0} | all-to-all | bytes 98304 | tf_op jit(solution)/shard_map/all_to_all | solution.py:353
  131.8 2.4 %collective-permute-start.22 = (bf16[8,320]{1,0:T(8,128)(2,1)S(1)}, bf16[8,320]{1,0:T(8,128)(2,1)S(1)}, u32[]{:S(2)}, u32[]{:S(2)}) collective-permute-start(bf16[8,320]{1,0:T(8,128)(2,1)S(1)} %get-tuple-element.45.refs_1_), channel_id=1, source_target_pairs={{0,508},{4,8},{8,4},{12,16},{16,12},{20,24},{24,20},{28,32},{32,28... | collective-permute-start | bytes 15368 | tf_op jit(solution)/shard_map/ppermute | solution.py:22
  134.2 10.6 %collective-permute-start.21 = (bf16[8,320]{1,0:T(8,128)(2,1)S(1)}, bf16[8,320]{1,0:T(8,128)(2,1)S(1)}, u32[]{:S(2)}, u32[]{:S(2)}) collective-permute-start(bf16[8,320]{1,0:T(8,128)(2,1)S(1)} %get-tuple-element.45.refs_1_), channel_id=1, source_target_pairs={{0,4},{4,0},{8,12},{12,8},{16,20},{20,16},{24,28},{28,24},{32,36},... | collective-permute-start | bytes 15368 | tf_op jit(solution)/shard_map/ppermute | solution.py:21
  148.6 6.3 %collective-permute-start.23 = (bf16[8,320]{1,0:T(8,128)(2,1)S(1)}, bf16[8,320]{1,0:T(8,128)(2,1)S(1)}, u32[]{:S(2)}, u32[]{:S(2)}) collective-permute-start(bf16[8,320]{1,0:T(8,128)(2,1)S(1)} %shard_map.123.refs_1_), channel_id=1, source_target_pairs={{0,4},{4,0},{8,12},{12,8},{16,20},{20,16},{24,28},{28,24},{32,36},... | collective-permute-start | bytes 15368 | tf_op jit(solution)/shard_map/ppermute | solution.py:21
  (54 shorter events, 37.8 us)
Async XLA Ops:
  3.5 8.5 %collective-permute-start = (bf16[16,320]{1,0:T(8,128)(2,1)S(1)}, bf16[16,320]{1,0:T(8,128)(2,1)S(1)}, u32[]{:S(2)}, u32[]{:S(2)}) collective-permute-start(bf16[16,320]{1,0:T(8,128)(2,1)S(1)} %get-tuple-element.27.refs_1_), channel_id=1, source_target_pairs={{0,1},{1,0},{2,3},{3,2},{4,5},{5,4},{6,7},{7,6},{8,9},{9,8},{10,11... | collective-permute-start | bytes 30728 | tf_op jit(solution)/shard_map/ppermute | solution.py:21
  7.4 10.7 %collective-permute-start.1 = (bf16[16,320]{1,0:T(8,128)(2,1)S(1)}, bf16[16,320]{1,0:T(8,128)(2,1)S(1)}, u32[]{:S(2)}, u32[]{:S(2)}) collective-permute-start(bf16[16,320]{1,0:T(8,128)(2,1)S(1)} %get-tuple-element.27.refs_1_), channel_id=1, source_target_pairs={{0,511},{1,2},{2,1},{3,4},{4,3},{5,6},{6,5},{7,8},{8,7},{9,10},{10... | collective-permute-start | bytes 30728 | tf_op jit(solution)/shard_map/ppermute | solution.py:22
  12.0 23.6 %collective-permute-start.4 = (bf16[2,320,320]{2,1,0:T(8,128)(2,1)S(1)}, bf16[2,320,320]{2,1,0:T(8,128)(2,1)S(1)}, u32[]{:S(2)}, u32[]{:S(2)}) collective-permute-start(bf16[2,320,320]{2,1,0:T(8,128)(2,1)S(1)} %copy-done), channel_id=1, source_target_pairs={{0,3},{1,2},{2,1},{3,0},{4,7},{5,6},{6,5},{7,4},{8,11},{9,10},{10,... | collective-permute-start | bytes 1228808 | tf_op jit(solution)/shard_map/ppermute | solution.py:273
  16.1 19.5 %collective-permute-start.3 = (bf16[2,320,320]{2,1,0:T(8,128)(2,1)S(1)}, bf16[2,320,320]{2,1,0:T(8,128)(2,1)S(1)}, u32[]{:S(2)}, u32[]{:S(2)}) collective-permute-start(bf16[2,320,320]{2,1,0:T(8,128)(2,1)S(1)} %copy-done), channel_id=1, source_target_pairs={{0,1},{1,0},{2,3},{3,2},{4,5},{5,4},{6,7},{7,6},{8,9},{9,8},{10,11... | collective-permute-start | bytes 1228808 | tf_op jit(solution)/shard_map/ppermute | solution.py:273
  20.1 15.6 %collective-permute-start.5 = (bf16[16,320]{1,0:T(8,128)(2,1)S(1)}, bf16[16,320]{1,0:T(8,128)(2,1)S(1)}, u32[]{:S(2)}, u32[]{:S(2)}) collective-permute-start(bf16[16,320]{1,0:T(8,128)(2,1)S(1)} %shard_map.110.refs_1_), channel_id=1, source_target_pairs={{0,511},{1,2},{2,1},{3,4},{4,3},{5,6},{6,5},{7,8},{8,7},{9,10},{10... | collective-permute-start | bytes 30728 | tf_op jit(solution)/shard_map/ppermute | solution.py:22
  33.7 5.3 %collective-permute-start.2 = (bf16[16,320]{1,0:T(8,128)(2,1)S(1)}, bf16[16,320]{1,0:T(8,128)(2,1)S(1)}, u32[]{:S(2)}, u32[]{:S(2)}) collective-permute-start(bf16[16,320]{1,0:T(8,128)(2,1)S(1)} %shard_map.110.refs_1_), channel_id=1, source_target_pairs={{0,1},{1,0},{2,3},{3,2},{4,5},{5,4},{6,7},{7,6},{8,9},{9,8},{10,11... | collective-permute-start | bytes 30728 | tf_op jit(solution)/shard_map/ppermute | solution.py:21
  35.7 17.9 %collective-permute-start.8 = (bf16[2,320,320]{2,1,0:T(8,128)(2,1)S(1)}, bf16[2,320,320]{2,1,0:T(8,128)(2,1)S(1)}, u32[]{:S(2)}, u32[]{:S(2)}) collective-permute-start(bf16[2,320,320]{2,1,0:T(8,128)(2,1)S(1)} %collective-permute-done.4.refs_4_.refs_3_), channel_id=1, source_target_pairs={{0,1},{1,0},{2,3},{3,2},{4,5},{5,4},{6,7},{7,6},{8,9},{9,8},{10,11... | collective-permute-start | bytes 1228808 | tf_op jit(solution)/shard_map/ppermute | solution.py:273
  41.0 10.0 %collective-permute-start.7 = (bf16[16,320]{1,0:T(8,128)(2,1)S(1)}, bf16[16,320]{1,0:T(8,128)(2,1)S(1)}, u32[]{:S(2)}, u32[]{:S(2)}) collective-permute-start(bf16[16,320]{1,0:T(8,128)(2,1)S(1)} %get-tuple-element.34.refs_1_), channel_id=1, source_target_pairs={{0,511},{1,2},{2,1},{3,4},{4,3},{5,6},{6,5},{7,8},{8,7},{9,10},{10... | collective-permute-start | bytes 30728 | tf_op jit(solution)/shard_map/ppermute | solution.py:22
  49.0 4.5 %collective-permute-start.6 = (bf16[16,320]{1,0:T(8,128)(2,1)S(1)}, bf16[16,320]{1,0:T(8,128)(2,1)S(1)}, u32[]{:S(2)}, u32[]{:S(2)}) collective-permute-start(bf16[16,320]{1,0:T(8,128)(2,1)S(1)} %get-tuple-element.34.refs_1_), channel_id=1, source_target_pairs={{0,1},{1,0},{2,3},{3,2},{4,5},{5,4},{6,7},{7,6},{8,9},{9,8},{10,11... | collective-permute-start | bytes 30728 | tf_op jit(solution)/shard_map/ppermute | solution.py:21
  61.9 10.0 %collective-permute-start.10 = (bf16[8,320]{1,0:T(8,128)(2,1)S(1)}, bf16[8,320]{1,0:T(8,128)(2,1)S(1)}, u32[]{:S(2)}, u32[]{:S(2)}) collective-permute-start(bf16[8,320]{1,0:T(8,128)(2,1)S(1)} %get-tuple-element.39.refs_4_.refs_1_), channel_id=1, source_target_pairs={{0,508},{4,8},{8,4},{12,16},{16,12},{20,24},{24,20},{28,32},{32,28... | collective-permute-start | bytes 15368 | tf_op jit(solution)/shard_map/ppermute | solution.py:22
  63.8 8.1 %collective-permute-start.9 = (bf16[8,320]{1,0:T(8,128)(2,1)S(1)}, bf16[8,320]{1,0:T(8,128)(2,1)S(1)}, u32[]{:S(2)}, u32[]{:S(2)}) collective-permute-start(bf16[8,320]{1,0:T(8,128)(2,1)S(1)} %get-tuple-element.39.refs_4_.refs_1_), channel_id=1, source_target_pairs={{0,4},{4,0},{8,12},{12,8},{16,20},{20,16},{24,28},{28,24},{32,36},... | collective-permute-start | bytes 15368 | tf_op jit(solution)/shard_map/ppermute | solution.py:21
  73.0 7.3 %collective-permute-start.12 = (bf16[8,320]{1,0:T(8,128)(2,1)S(1)}, bf16[8,320]{1,0:T(8,128)(2,1)S(1)}, u32[]{:S(2)}, u32[]{:S(2)}) collective-permute-start(bf16[8,320]{1,0:T(8,128)(2,1)S(1)} %shard_map.115.refs_1_), channel_id=1, source_target_pairs={{0,508},{4,8},{8,4},{12,16},{16,12},{20,24},{24,20},{28,32},{32,28... | collective-permute-start | bytes 15368 | tf_op jit(solution)/shard_map/ppermute | solution.py:22
  74.9 6.2 %collective-permute-start.11 = (bf16[8,320]{1,0:T(8,128)(2,1)S(1)}, bf16[8,320]{1,0:T(8,128)(2,1)S(1)}, u32[]{:S(2)}, u32[]{:S(2)}) collective-permute-start(bf16[8,320]{1,0:T(8,128)(2,1)S(1)} %shard_map.115.refs_1_), channel_id=1, source_target_pairs={{0,4},{4,0},{8,12},{12,8},{16,20},{20,16},{24,28},{28,24},{32,36},... | collective-permute-start | bytes 15368 | tf_op jit(solution)/shard_map/ppermute | solution.py:21
  82.3 8.9 %collective-permute-start.14 = (bf16[16,320]{1,0:T(8,128)(2,1)S(1)}, bf16[16,320]{1,0:T(8,128)(2,1)S(1)}, u32[]{:S(2)}, u32[]{:S(2)}) collective-permute-start(bf16[16,320]{1,0:T(8,128)(2,1)S(1)} %shard_map.116.refs_1_), channel_id=1, source_target_pairs={{0,511},{1,2},{2,1},{3,4},{4,3},{5,6},{6,5},{7,8},{8,7},{9,10},{10... | collective-permute-start | bytes 30728 | tf_op jit(solution)/shard_map/ppermute | solution.py:22
  86.6 4.7 %collective-permute-start.13 = (bf16[16,320]{1,0:T(8,128)(2,1)S(1)}, bf16[16,320]{1,0:T(8,128)(2,1)S(1)}, u32[]{:S(2)}, u32[]{:S(2)}) collective-permute-start(bf16[16,320]{1,0:T(8,128)(2,1)S(1)} %shard_map.116.refs_1_), channel_id=1, source_target_pairs={{0,1},{1,0},{2,3},{3,2},{4,5},{5,4},{6,7},{7,6},{8,9},{9,8},{10,11... | collective-permute-start | bytes 30728 | tf_op jit(solution)/shard_map/ppermute | solution.py:21
  92.8 6.3 %collective-permute-start.16 = (bf16[16,320]{1,0:T(8,128)(2,1)S(1)}, bf16[16,320]{1,0:T(8,128)(2,1)S(1)}, u32[]{:S(2)}, u32[]{:S(2)}) collective-permute-start(bf16[16,320]{1,0:T(8,128)(2,1)S(1)} %shard_map.118.refs_1_), channel_id=1, source_target_pairs={{0,511},{1,2},{2,1},{3,4},{4,3},{5,6},{6,5},{7,8},{8,7},{9,10},{10... | collective-permute-start | bytes 30728 | tf_op jit(solution)/shard_map/ppermute | solution.py:22
  96.7 4.4 %collective-permute-start.15 = (bf16[16,320]{1,0:T(8,128)(2,1)S(1)}, bf16[16,320]{1,0:T(8,128)(2,1)S(1)}, u32[]{:S(2)}, u32[]{:S(2)}) collective-permute-start(bf16[16,320]{1,0:T(8,128)(2,1)S(1)} %shard_map.118.refs_1_), channel_id=1, source_target_pairs={{0,1},{1,0},{2,3},{3,2},{4,5},{5,4},{6,7},{7,6},{8,9},{9,8},{10,11... | collective-permute-start | bytes 30728 | tf_op jit(solution)/shard_map/ppermute | solution.py:21
  102.6 7.2 %collective-permute-start.18 = (bf16[16,320]{1,0:T(8,128)(2,1)S(1)}, bf16[16,320]{1,0:T(8,128)(2,1)S(1)}, u32[]{:S(2)}, u32[]{:S(2)}) collective-permute-start(bf16[16,320]{1,0:T(8,128)(2,1)S(1)} %shard_map.119.refs_1_), channel_id=1, source_target_pairs={{0,511},{1,2},{2,1},{3,4},{4,3},{5,6},{6,5},{7,8},{8,7},{9,10},{10... | collective-permute-start | bytes 30728 | tf_op jit(solution)/shard_map/ppermute | solution.py:22
  107.8 4.4 %collective-permute-start.17 = (bf16[16,320]{1,0:T(8,128)(2,1)S(1)}, bf16[16,320]{1,0:T(8,128)(2,1)S(1)}, u32[]{:S(2)}, u32[]{:S(2)}) collective-permute-start(bf16[16,320]{1,0:T(8,128)(2,1)S(1)} %shard_map.119.refs_1_), channel_id=1, source_target_pairs={{0,1},{1,0},{2,3},{3,2},{4,5},{5,4},{6,7},{7,6},{8,9},{9,8},{10,11... | collective-permute-start | bytes 30728 | tf_op jit(solution)/shard_map/ppermute | solution.py:21
  113.7 7.5 %collective-permute-start.20 = (bf16[16,320]{1,0:T(8,128)(2,1)S(1)}, bf16[16,320]{1,0:T(8,128)(2,1)S(1)}, u32[]{:S(2)}, u32[]{:S(2)}) collective-permute-start(bf16[16,320]{1,0:T(8,128)(2,1)S(1)} %get-tuple-element.43.refs_1_), channel_id=1, source_target_pairs={{0,511},{1,2},{2,1},{3,4},{4,3},{5,6},{6,5},{7,8},{8,7},{9,10},{10... | collective-permute-start | bytes 30728 | tf_op jit(solution)/shard_map/ppermute | solution.py:22
  131.8 13.0 %collective-permute-start.22 = (bf16[8,320]{1,0:T(8,128)(2,1)S(1)}, bf16[8,320]{1,0:T(8,128)(2,1)S(1)}, u32[]{:S(2)}, u32[]{:S(2)}) collective-permute-start(bf16[8,320]{1,0:T(8,128)(2,1)S(1)} %get-tuple-element.45.refs_1_), channel_id=1, source_target_pairs={{0,508},{4,8},{8,4},{12,16},{16,12},{20,24},{24,20},{28,32},{32,28... | collective-permute-start | bytes 15368 | tf_op jit(solution)/shard_map/ppermute | solution.py:22
  134.2 11.4 %collective-permute-start.21 = (bf16[8,320]{1,0:T(8,128)(2,1)S(1)}, bf16[8,320]{1,0:T(8,128)(2,1)S(1)}, u32[]{:S(2)}, u32[]{:S(2)}) collective-permute-start(bf16[8,320]{1,0:T(8,128)(2,1)S(1)} %get-tuple-element.45.refs_1_), channel_id=1, source_target_pairs={{0,4},{4,0},{8,12},{12,8},{16,20},{20,16},{24,28},{28,24},{32,36},... | collective-permute-start | bytes 15368 | tf_op jit(solution)/shard_map/ppermute | solution.py:21
  146.7 8.3 %collective-permute-start.24 = (bf16[8,320]{1,0:T(8,128)(2,1)S(1)}, bf16[8,320]{1,0:T(8,128)(2,1)S(1)}, u32[]{:S(2)}, u32[]{:S(2)}) collective-permute-start(bf16[8,320]{1,0:T(8,128)(2,1)S(1)} %shard_map.123.refs_1_), channel_id=1, source_target_pairs={{0,508},{4,8},{8,4},{12,16},{16,12},{20,24},{24,20},{28,32},{32,28... | collective-permute-start | bytes 15368 | tf_op jit(solution)/shard_map/ppermute | solution.py:22
  148.6 7.1 %collective-permute-start.23 = (bf16[8,320]{1,0:T(8,128)(2,1)S(1)}, bf16[8,320]{1,0:T(8,128)(2,1)S(1)}, u32[]{:S(2)}, u32[]{:S(2)}) collective-permute-start(bf16[8,320]{1,0:T(8,128)(2,1)S(1)} %shard_map.123.refs_1_), channel_id=1, source_target_pairs={{0,4},{4,0},{8,12},{12,8},{16,20},{20,16},{24,28},{28,24},{32,36},... | collective-permute-start | bytes 15368 | tf_op jit(solution)/shard_map/ppermute | solution.py:21
  (6 other events, 104.2 us)

commit v12 on v11

--- a/solution.py
+++ b/solution.py
@@ -315,7 +315,6 @@
                 sent, inner = lax.optimization_barrier((coarse_inverse, inner))
                 near, other = across(sent, 1), across(sent, tele_size - 1)
             if cycle == 0 and sweep == 2:
-                near, other, outer = lax.optimization_barrier((near, other, outer))
                 far = across(other, 1)
                 blocks = (coarse_inverse, near, far, other)
             turned = cycle > 0

time: 158 us -> 160 us (1.013)
  blocking collectives: 13.5 us -> 6.75 us
  starting transfers between devices: 107 us -> 113 us
  waiting for transfers between devices: 12.4 us -> 14.4 us
    all_to_all x2 -> x1, blocking collectives: 13.5 us -> 6.75 us  [shards(): parts = lax.all_to_all(parts, 'tele', 0, 0, tiled=True)]
    ppermute x11, starting transfers between devices: 44.6 us -> 49.8 us  [swapped(): inner = lax.ppermute(block, axis, [(i, i ^ 1) for i in range(count)])]
    ppermute x11, starting transfers between devices: 53.4 us -> 48.8 us  [swapped(): lax.ppermute(block, axis, [(i, (i - 1 if i % 2 == 0 else i + 1) % count)...]
    all_to_all x0 -> x1, starting transfers between devices: none -> 3.27 us  [shards(): parts = lax.all_to_all(parts, 'tele', 0, 0, tiled=True)]
    ppermute x3, waiting for transfers between devices: 0.01 us -> 2.43 us  [across(): lax.ppermute(block, 'tele', [(i, i ^ bits) for i in range(tele_size)])]
    ppermute x11, waiting for transfers between devices: 12.1 us -> 9.71 us  [swapped(): inner = lax.ppermute(block, axis, [(i, i ^ 1) for i in range(count)])]
    all_to_all x0 -> x1, waiting for transfers between devices: none -> 2.25 us  [shards(): parts = lax.all_to_all(parts, 'tele', 0, 0, tiled=True)]
  transfers between devices with their start and end apart: 25 -> 26, of which waited for: 9 -> 8; matrix products, arithmetic and copies ran while one was open for 0% -> 0% of each run, Pallas kernels for 5% -> 6%
where the time goes in v12:
time: 160 us; the launch traced here: 159 us
  starting transfers between devices  113 us (71%)
  Pallas kernels  24.4 us (15%)
  waiting for transfers between devices  14.4 us (9%)
  blocking collectives  6.75 us (4%)
    ppermute x11, starting transfers between devices, swapped(): inner = lax.ppermute(block, axis, [(i, i ^ 1) for i in range(count)])  49.8 us
    ppermute x11, starting transfers between devices, swapped(): lax.ppermute(block, axis, [(i, (i - 1 if i % 2 == 0 else i + 1) % count)...  48.8 us
    pallas_call x16, Pallas kernels, run(): pl.pallas_call(body, out_shape=[pltpu.VMEM(s, d) if i in pinned else jax....  24.4 us
    ppermute x3, starting transfers between devices, across(): lax.ppermute(block, 'tele', [(i, i ^ bits) for i in range(tele_size)])  10.8 us
    ppermute x11, waiting for transfers between devices, swapped(): inner = lax.ppermute(block, axis, [(i, i ^ 1) for i in range(count)])  9.71 us
    all_to_all x1, blocking collectives, shards(): parts = lax.all_to_all(parts, 'tele', 0, 0, tiled=True)  6.75 us
    all_to_all x1, starting transfers between devices, shards(): parts = lax.all_to_all(parts, 'tele', 0, 0, tiled=True)  3.27 us
  transfers between devices with their start and end apart: 26, of which 8 were waited for; matrix products, arithmetic and copies ran while one was open for 0% of the time, Pallas kernels for 6%

profile of v12, /device:TPU:1, one launch (start us, length us, event | category | flops | bytes accessed | tf_op | source)
XLA Modules:
  0.0 159.0 jit_solution(12283375327213077211)
XLA Ops:
  0.0 3.4 %shard_map.109 = (bf16[16,320]{1,0:T(8,128)(2,1)S(1)}, s32[16,12]{1,0:T(8,128)S(1)}, f32[8,64]{1,0:T(8,128)S(1)}, bf16[3072,128]{1,0:T(8,128)(2,1)S(1)}, bf16[16,320,320]{2,1,0:T(8,128)(2,1)S(1)}) custom-call(f32[16,320]{1,0:T(8,128)} %refs_7_.9, s32[6,16]{1,0:T(8,128)} %bitcast.7, s32[6,16]{1,0:T(8,128)} %bitcast.8, s32[2,6]{1,0:T(2,128)} %refs_3_.1, ...), custom_call_target="tpu_custom_call" | custom-call | flops 4294967296 | bytes 3605344 | tf_op jit(solution)/shard_map/pallas_call | solution.py:242
  3.5 3.9 %collective-permute-start = (bf16[16,320]{1,0:T(8,128)(2,1)S(1)}, bf16[16,320]{1,0:T(8,128)(2,1)S(1)}, u32[]{:S(2)}, u32[]{:S(2)}) collective-permute-start(bf16[16,320]{1,0:T(8,128)(2,1)S(1)} %get-tuple-element.24.refs_1_), channel_id=1, source_target_pairs={{0,1},{1,0},{2,3},{3,2},{4,5},{5,4},{6,7},{7,6},{8,9},{9,8},{10,11... | collective-permute-start | bytes 30728 | tf_op jit(solution)/shard_map/ppermute | solution.py:21
  7.4 4.6 %collective-permute-start.1 = (bf16[16,320]{1,0:T(8,128)(2,1)S(1)}, bf16[16,320]{1,0:T(8,128)(2,1)S(1)}, u32[]{:S(2)}, u32[]{:S(2)}) collective-permute-start(bf16[16,320]{1,0:T(8,128)(2,1)S(1)} %get-tuple-element.24.refs_1_), channel_id=1, source_target_pairs={{0,511},{1,2},{2,1},{3,4},{4,3},{5,6},{6,5},{7,8},{8,7},{9,10},{10... | collective-permute-start | bytes 30728 | tf_op jit(solution)/shard_map/ppermute | solution.py:22
  12.0 4.1 %collective-permute-start.6 = (bf16[2,320,320]{2,1,0:T(8,128)(2,1)S(1)}, bf16[2,320,320]{2,1,0:T(8,128)(2,1)S(1)}, u32[]{:S(2)}, u32[]{:S(2)}) collective-permute-start(bf16[2,320,320]{2,1,0:T(8,128)(2,1)S(1)} %copy-done), channel_id=1, source_target_pairs={{0,3},{1,2},{2,1},{3,0},{4,7},{5,6},{6,5},{7,4},{8,11},{9,10},{10,... | collective-permute-start | bytes 1228808 | tf_op jit(solution)/shard_map/ppermute | solution.py:273
  18.2 13.6 %collective-permute-start.3 = (bf16[16,320]{1,0:T(8,128)(2,1)S(1)}, bf16[16,320]{1,0:T(8,128)(2,1)S(1)}, u32[]{:S(2)}, u32[]{:S(2)}) collective-permute-start(bf16[16,320]{1,0:T(8,128)(2,1)S(1)} %shard_map.110.refs_1_), channel_id=1, source_target_pairs={{0,511},{1,2},{2,1},{3,4},{4,3},{5,6},{6,5},{7,8},{8,7},{9,10},{10... | collective-permute-start | bytes 30728 | tf_op jit(solution)/shard_map/ppermute | solution.py:22
  33.7 3.4 %collective-permute-start.7 = (bf16[2,320,320]{2,1,0:T(8,128)(2,1)S(1)}, bf16[2,320,320]{2,1,0:T(8,128)(2,1)S(1)}, u32[]{:S(2)}, u32[]{:S(2)}) collective-permute-start(bf16[2,320,320]{2,1,0:T(8,128)(2,1)S(1)} %collective-permute-done.6.refs_4_.refs_3_), channel_id=1, source_target_pairs={{0,1},{1,0},{2,3},{3,2},{4,5},{5,4},{6,7},{7,6},{8,9},{9,8},{10,11... | collective-permute-start | bytes 1228808 | tf_op jit(solution)/shard_map/ppermute | solution.py:273
  39.1 2.5 %collective-permute-start.5 = (bf16[16,320]{1,0:T(8,128)(2,1)S(1)}, bf16[16,320]{1,0:T(8,128)(2,1)S(1)}, u32[]{:S(2)}, u32[]{:S(2)}) collective-permute-start(bf16[16,320]{1,0:T(8,128)(2,1)S(1)} %get-tuple-element.29.refs_1_), channel_id=1, source_target_pairs={{0,511},{1,2},{2,1},{3,4},{4,3},{5,6},{6,5},{7,8},{8,7},{9,10},{10... | collective-permute-start | bytes 30728 | tf_op jit(solution)/shard_map/ppermute | solution.py:22
  43.5 3.4 %collective-permute-start.8 = (bf16[2,320,320]{2,1,0:T(8,128)(2,1)S(1)}, bf16[2,320,320]{2,1,0:T(8,128)(2,1)S(1)}, u32[]{:S(2)}, u32[]{:S(2)}) collective-permute-start(bf16[2,320,320]{2,1,0:T(8,128)(2,1)S(1)} %copy-done), channel_id=1, source_target_pairs={{0,1},{1,0},{2,3},{3,2},{4,5},{5,4},{6,7},{7,6},{8,9},{9,8},{10,11... | collective-permute-start | bytes 1228808 | tf_op jit(solution)/shard_map/ppermute | solution.py:273
  48.5 3.3 %all-to-all-start = ((f32[4,8,384]{2,1,0:T(8,128)}), f32[4,8,384]{2,1,0:T(8,128)S(1)}, u32[]{:S(2)}, u32[]{:S(2)}) async-start(f32[4,8,384]{2,1,0:T(8,128)} %shard_map.112), calls=%async_computation | async-start | bytes 98304 | tf_op jit(solution)/shard_map/all_to_all | solution.py:352
  51.8 2.4 %collective-permute-done.8.refs_2_.refs_1_ = bf16[2,320,320]{2,1,0:T(8,128)(2,1)S(1)} collective-permute-done((bf16[2,320,320]{2,1,0:T(8,128)(2,1)S(1)}, bf16[2,320,320]{2,1,0:T(8,128)(2,1)S(1)}, u32[]{:S(2)}, u32[]{:S(2)}) %collective-permute-start.8) | collective-permute-done | bytes 409632 | tf_op jit(solution)/shard_map/ppermute | solution.py:273
  57.1 3.3 %collective-permute-start.10 = (bf16[8,320]{1,0:T(8,128)(2,1)S(1)}, bf16[8,320]{1,0:T(8,128)(2,1)S(1)}, u32[]{:S(2)}, u32[]{:S(2)}) collective-permute-start(bf16[8,320]{1,0:T(8,128)(2,1)S(1)} %get-tuple-element.33.refs_4_.refs_1_), channel_id=1, source_target_pairs={{0,508},{4,8},{8,4},{12,16},{16,12},{20,24},{24,20},{28,32},{32,28... | collective-permute-start | bytes 15368 | tf_op jit(solution)/shard_map/ppermute | solution.py:22
  60.5 12.8 %collective-permute-start.9 = (bf16[8,320]{1,0:T(8,128)(2,1)S(1)}, bf16[8,320]{1,0:T(8,128)(2,1)S(1)}, u32[]{:S(2)}, u32[]{:S(2)}) collective-permute-start(bf16[8,320]{1,0:T(8,128)(2,1)S(1)} %get-tuple-element.33.refs_4_.refs_1_), channel_id=1, source_target_pairs={{0,4},{4,0},{8,12},{12,8},{16,20},{20,16},{24,28},{28,24},{32,36},... | collective-permute-start | bytes 15368 | tf_op jit(solution)/shard_map/ppermute | solution.py:21
  77.7 4.9 %collective-permute-start.11 = (bf16[8,320]{1,0:T(8,128)(2,1)S(1)}, bf16[8,320]{1,0:T(8,128)(2,1)S(1)}, u32[]{:S(2)}, u32[]{:S(2)}) collective-permute-start(bf16[8,320]{1,0:T(8,128)(2,1)S(1)} %shard_map.115.refs_1_), channel_id=1, source_target_pairs={{0,4},{4,0},{8,12},{12,8},{16,20},{20,16},{24,28},{28,24},{32,36},... | collective-permute-start | bytes 15368 | tf_op jit(solution)/shard_map/ppermute | solution.py:21
  84.6 2.9 %collective-permute-start.14 = (bf16[16,320]{1,0:T(8,128)(2,1)S(1)}, bf16[16,320]{1,0:T(8,128)(2,1)S(1)}, u32[]{:S(2)}, u32[]{:S(2)}) collective-permute-start(bf16[16,320]{1,0:T(8,128)(2,1)S(1)} %shard_map.116.refs_1_), channel_id=1, source_target_pairs={{0,511},{1,2},{2,1},{3,4},{4,3},{5,6},{6,5},{7,8},{8,7},{9,10},{10... | collective-permute-start | bytes 30728 | tf_op jit(solution)/shard_map/ppermute | solution.py:22
  89.5 2.7 %shard_map.117.refs_8_ = bf16[16,320,320]{2,1,0:T(8,128)(2,1)S(1)} custom-call(bf16[16,320,320]{2,1,0:T(8,128)(2,1)S(1)} %copy-done.6, bf16[16,320]{1,0:T(8,128)(2,1)S(1)} %get-tuple-element.29.refs_1_), custom_call_target="tpu_custom_call" | custom-call | flops 4294967296 | bytes 3276800 | tf_op jit(solution)/shard_map/pallas_call | solution.py:242
  93.6 4.9 %collective-permute-start.16 = (bf16[16,320]{1,0:T(8,128)(2,1)S(1)}, bf16[16,320]{1,0:T(8,128)(2,1)S(1)}, u32[]{:S(2)}, u32[]{:S(2)}) collective-permute-start(bf16[16,320]{1,0:T(8,128)(2,1)S(1)} %shard_map.118.refs_1_), channel_id=1, source_target_pairs={{0,511},{1,2},{2,1},{3,4},{4,3},{5,6},{6,5},{7,8},{8,7},{9,10},{10... | collective-permute-start | bytes 30728 | tf_op jit(solution)/shard_map/ppermute | solution.py:22
  104.4 5.2 %collective-permute-start.18 = (bf16[16,320]{1,0:T(8,128)(2,1)S(1)}, bf16[16,320]{1,0:T(8,128)(2,1)S(1)}, u32[]{:S(2)}, u32[]{:S(2)}) collective-permute-start(bf16[16,320]{1,0:T(8,128)(2,1)S(1)} %shard_map.119.refs_1_), channel_id=1, source_target_pairs={{0,511},{1,2},{2,1},{3,4},{4,3},{5,6},{6,5},{7,8},{8,7},{9,10},{10... | collective-permute-start | bytes 30728 | tf_op jit(solution)/shard_map/ppermute | solution.py:22
  111.5 2.5 %collective-permute-done.17.refs_0_ = bf16[16,320]{1,0:T(8,128)(2,1)S(1)} collective-permute-done((bf16[16,320]{1,0:T(8,128)(2,1)S(1)}, bf16[16,320]{1,0:T(8,128)(2,1)S(1)}, u32[]{:S(2)}, u32[]{:S(2)}) %collective-permute-start.17) | collective-permute-done | bytes 10272 | tf_op jit(solution)/shard_map/ppermute | solution.py:21
  115.5 5.2 %collective-permute-start.20 = (bf16[16,320]{1,0:T(8,128)(2,1)S(1)}, bf16[16,320]{1,0:T(8,128)(2,1)S(1)}, u32[]{:S(2)}, u32[]{:S(2)}) collective-permute-start(bf16[16,320]{1,0:T(8,128)(2,1)S(1)} %get-tuple-element.37.refs_1_), channel_id=1, source_target_pairs={{0,511},{1,2},{2,1},{3,4},{4,3},{5,6},{6,5},{7,8},{8,7},{9,10},{10... | collective-permute-start | bytes 30728 | tf_op jit(solution)/shard_map/ppermute | solution.py:22
  122.6 2.5 %collective-permute-done.19.refs_0_ = bf16[16,320]{1,0:T(8,128)(2,1)S(1)} collective-permute-done((bf16[16,320]{1,0:T(8,128)(2,1)S(1)}, bf16[16,320]{1,0:T(8,128)(2,1)S(1)}, u32[]{:S(2)}, u32[]{:S(2)}) %collective-permute-start.19) | collective-permute-done | bytes 10272 | tf_op jit(solution)/shard_map/ppermute | solution.py:21
  126.1 6.7 %all_to_all.10.refs_0_ = f32[4,8,384]{2,1,0:T(8,128)S(1)} all-to-all(f32[4,8,384]{2,1,0:T(8,128)S(1)} %shard_map.121), channel_id=1, replica_groups=mesh['fine'=128,'tele'=4] {'tele'}, dimensions={0} | all-to-all | bytes 98304 | tf_op jit(solution)/shard_map/all_to_all | solution.py:352
  133.2 2.8 %collective-permute-start.22 = (bf16[8,320]{1,0:T(8,128)(2,1)S(1)}, bf16[8,320]{1,0:T(8,128)(2,1)S(1)}, u32[]{:S(2)}, u32[]{:S(2)}) collective-permute-start(bf16[8,320]{1,0:T(8,128)(2,1)S(1)} %get-tuple-element.39.refs_1_), channel_id=1, source_target_pairs={{0,508},{4,8},{8,4},{12,16},{16,12},{20,24},{24,20},{28,32},{32,28... | collective-permute-start | bytes 15368 | tf_op jit(solution)/shard_map/ppermute | solution.py:22
  136.0 10.2 %collective-permute-start.21 = (bf16[8,320]{1,0:T(8,128)(2,1)S(1)}, bf16[8,320]{1,0:T(8,128)(2,1)S(1)}, u32[]{:S(2)}, u32[]{:S(2)}) collective-permute-start(bf16[8,320]{1,0:T(8,128)(2,1)S(1)} %get-tuple-element.39.refs_1_), channel_id=1, source_target_pairs={{0,4},{4,0},{8,12},{12,8},{16,20},{20,16},{24,28},{28,24},{32,36},... | collective-permute-start | bytes 15368 | tf_op jit(solution)/shard_map/ppermute | solution.py:21
  150.0 6.3 %collective-permute-start.23 = (bf16[8,320]{1,0:T(8,128)(2,1)S(1)}, bf16[8,320]{1,0:T(8,128)(2,1)S(1)}, u32[]{:S(2)}, u32[]{:S(2)}) collective-permute-start(bf16[8,320]{1,0:T(8,128)(2,1)S(1)} %shard_map.123.refs_1_), channel_id=1, source_target_pairs={{0,4},{4,0},{8,12},{12,8},{16,20},{20,16},{24,28},{28,24},{32,36},... | collective-permute-start | bytes 15368 | tf_op jit(solution)/shard_map/ppermute | solution.py:21
  (63 shorter events, 40.9 us)
Async XLA Ops:
  3.5 8.5 %collective-permute-start = (bf16[16,320]{1,0:T(8,128)(2,1)S(1)}, bf16[16,320]{1,0:T(8,128)(2,1)S(1)}, u32[]{:S(2)}, u32[]{:S(2)}) collective-permute-start(bf16[16,320]{1,0:T(8,128)(2,1)S(1)} %get-tuple-element.24.refs_1_), channel_id=1, source_target_pairs={{0,1},{1,0},{2,3},{3,2},{4,5},{5,4},{6,7},{7,6},{8,9},{9,8},{10,11... | collective-permute-start | bytes 30728 | tf_op jit(solution)/shard_map/ppermute | solution.py:21
  7.4 8.7 %collective-permute-start.1 = (bf16[16,320]{1,0:T(8,128)(2,1)S(1)}, bf16[16,320]{1,0:T(8,128)(2,1)S(1)}, u32[]{:S(2)}, u32[]{:S(2)}) collective-permute-start(bf16[16,320]{1,0:T(8,128)(2,1)S(1)} %get-tuple-element.24.refs_1_), channel_id=1, source_target_pairs={{0,511},{1,2},{2,1},{3,4},{4,3},{5,6},{6,5},{7,8},{8,7},{9,10},{10... | collective-permute-start | bytes 30728 | tf_op jit(solution)/shard_map/ppermute | solution.py:22
  12.0 21.7 %collective-permute-start.6 = (bf16[2,320,320]{2,1,0:T(8,128)(2,1)S(1)}, bf16[2,320,320]{2,1,0:T(8,128)(2,1)S(1)}, u32[]{:S(2)}, u32[]{:S(2)}) collective-permute-start(bf16[2,320,320]{2,1,0:T(8,128)(2,1)S(1)} %copy-done), channel_id=1, source_target_pairs={{0,3},{1,2},{2,1},{3,0},{4,7},{5,6},{6,5},{7,4},{8,11},{9,10},{10,... | collective-permute-start | bytes 1228808 | tf_op jit(solution)/shard_map/ppermute | solution.py:273
  18.2 18.9 %collective-permute-start.3 = (bf16[16,320]{1,0:T(8,128)(2,1)S(1)}, bf16[16,320]{1,0:T(8,128)(2,1)S(1)}, u32[]{:S(2)}, u32[]{:S(2)}) collective-permute-start(bf16[16,320]{1,0:T(8,128)(2,1)S(1)} %shard_map.110.refs_1_), channel_id=1, source_target_pairs={{0,511},{1,2},{2,1},{3,4},{4,3},{5,6},{6,5},{7,8},{8,7},{9,10},{10... | collective-permute-start | bytes 30728 | tf_op jit(solution)/shard_map/ppermute | solution.py:22
  31.8 5.3 %collective-permute-start.2 = (bf16[16,320]{1,0:T(8,128)(2,1)S(1)}, bf16[16,320]{1,0:T(8,128)(2,1)S(1)}, u32[]{:S(2)}, u32[]{:S(2)}) collective-permute-start(bf16[16,320]{1,0:T(8,128)(2,1)S(1)} %shard_map.110.refs_1_), channel_id=1, source_target_pairs={{0,1},{1,0},{2,3},{3,2},{4,5},{5,4},{6,7},{7,6},{8,9},{9,8},{10,11... | collective-permute-start | bytes 30728 | tf_op jit(solution)/shard_map/ppermute | solution.py:21
  33.7 13.2 %collective-permute-start.7 = (bf16[2,320,320]{2,1,0:T(8,128)(2,1)S(1)}, bf16[2,320,320]{2,1,0:T(8,128)(2,1)S(1)}, u32[]{:S(2)}, u32[]{:S(2)}) collective-permute-start(bf16[2,320,320]{2,1,0:T(8,128)(2,1)S(1)} %collective-permute-done.6.refs_4_.refs_3_), channel_id=1, source_target_pairs={{0,1},{1,0},{2,3},{3,2},{4,5},{5,4},{6,7},{7,6},{8,9},{9,8},{10,11... | collective-permute-start | bytes 1228808 | tf_op jit(solution)/shard_map/ppermute | solution.py:273
  39.1 7.8 %collective-permute-start.5 = (bf16[16,320]{1,0:T(8,128)(2,1)S(1)}, bf16[16,320]{1,0:T(8,128)(2,1)S(1)}, u32[]{:S(2)}, u32[]{:S(2)}) collective-permute-start(bf16[16,320]{1,0:T(8,128)(2,1)S(1)} %get-tuple-element.29.refs_1_), channel_id=1, source_target_pairs={{0,511},{1,2},{2,1},{3,4},{4,3},{5,6},{6,5},{7,8},{8,7},{9,10},{10... | collective-permute-start | bytes 30728 | tf_op jit(solution)/shard_map/ppermute | solution.py:22
  41.6 5.3 %collective-permute-start.4 = (bf16[16,320]{1,0:T(8,128)(2,1)S(1)}, bf16[16,320]{1,0:T(8,128)(2,1)S(1)}, u32[]{:S(2)}, u32[]{:S(2)}) collective-permute-start(bf16[16,320]{1,0:T(8,128)(2,1)S(1)} %get-tuple-element.29.refs_1_), channel_id=1, source_target_pairs={{0,1},{1,0},{2,3},{3,2},{4,5},{5,4},{6,7},{7,6},{8,9},{9,8},{10,11... | collective-permute-start | bytes 30728 | tf_op jit(solution)/shard_map/ppermute | solution.py:21
  43.5 10.7 %collective-permute-start.8 = (bf16[2,320,320]{2,1,0:T(8,128)(2,1)S(1)}, bf16[2,320,320]{2,1,0:T(8,128)(2,1)S(1)}, u32[]{:S(2)}, u32[]{:S(2)}) collective-permute-start(bf16[2,320,320]{2,1,0:T(8,128)(2,1)S(1)} %copy-done), channel_id=1, source_target_pairs={{0,1},{1,0},{2,3},{3,2},{4,5},{5,4},{6,7},{7,6},{8,9},{9,8},{10,11... | collective-permute-start | bytes 1228808 | tf_op jit(solution)/shard_map/ppermute | solution.py:273
  48.5 8.0 %all-to-all-start = ((f32[4,8,384]{2,1,0:T(8,128)}), f32[4,8,384]{2,1,0:T(8,128)S(1)}, u32[]{:S(2)}, u32[]{:S(2)}) async-start(f32[4,8,384]{2,1,0:T(8,128)} %shard_map.112), calls=%async_computation | async-start | bytes 98304 | tf_op jit(solution)/shard_map/all_to_all | solution.py:352
  57.1 17.5 %collective-permute-start.10 = (bf16[8,320]{1,0:T(8,128)(2,1)S(1)}, bf16[8,320]{1,0:T(8,128)(2,1)S(1)}, u32[]{:S(2)}, u32[]{:S(2)}) collective-permute-start(bf16[8,320]{1,0:T(8,128)(2,1)S(1)} %get-tuple-element.33.refs_4_.refs_1_), channel_id=1, source_target_pairs={{0,508},{4,8},{8,4},{12,16},{16,12},{20,24},{24,20},{28,32},{32,28... | collective-permute-start | bytes 15368 | tf_op jit(solution)/shard_map/ppermute | solution.py:22
  60.5 14.2 %collective-permute-start.9 = (bf16[8,320]{1,0:T(8,128)(2,1)S(1)}, bf16[8,320]{1,0:T(8,128)(2,1)S(1)}, u32[]{:S(2)}, u32[]{:S(2)}) collective-permute-start(bf16[8,320]{1,0:T(8,128)(2,1)S(1)} %get-tuple-element.33.refs_4_.refs_1_), channel_id=1, source_target_pairs={{0,4},{4,0},{8,12},{12,8},{16,20},{20,16},{24,28},{28,24},{32,36},... | collective-permute-start | bytes 15368 | tf_op jit(solution)/shard_map/ppermute | solution.py:21
  75.8 6.8 %collective-permute-start.12 = (bf16[8,320]{1,0:T(8,128)(2,1)S(1)}, bf16[8,320]{1,0:T(8,128)(2,1)S(1)}, u32[]{:S(2)}, u32[]{:S(2)}) collective-permute-start(bf16[8,320]{1,0:T(8,128)(2,1)S(1)} %shard_map.115.refs_1_), channel_id=1, source_target_pairs={{0,508},{4,8},{8,4},{12,16},{16,12},{20,24},{24,20},{28,32},{32,28... | collective-permute-start | bytes 15368 | tf_op jit(solution)/shard_map/ppermute | solution.py:22
  77.7 5.7 %collective-permute-start.11 = (bf16[8,320]{1,0:T(8,128)(2,1)S(1)}, bf16[8,320]{1,0:T(8,128)(2,1)S(1)}, u32[]{:S(2)}, u32[]{:S(2)}) collective-permute-start(bf16[8,320]{1,0:T(8,128)(2,1)S(1)} %shard_map.115.refs_1_), channel_id=1, source_target_pairs={{0,4},{4,0},{8,12},{12,8},{16,20},{20,16},{24,28},{28,24},{32,36},... | collective-permute-start | bytes 15368 | tf_op jit(solution)/shard_map/ppermute | solution.py:21
  84.6 7.5 %collective-permute-start.14 = (bf16[16,320]{1,0:T(8,128)(2,1)S(1)}, bf16[16,320]{1,0:T(8,128)(2,1)S(1)}, u32[]{:S(2)}, u32[]{:S(2)}) collective-permute-start(bf16[16,320]{1,0:T(8,128)(2,1)S(1)} %shard_map.116.refs_1_), channel_id=1, source_target_pairs={{0,511},{1,2},{2,1},{3,4},{4,3},{5,6},{6,5},{7,8},{8,7},{9,10},{10... | collective-permute-start | bytes 30728 | tf_op jit(solution)/shard_map/ppermute | solution.py:22
  87.5 4.6 %collective-permute-start.13 = (bf16[16,320]{1,0:T(8,128)(2,1)S(1)}, bf16[16,320]{1,0:T(8,128)(2,1)S(1)}, u32[]{:S(2)}, u32[]{:S(2)}) collective-permute-start(bf16[16,320]{1,0:T(8,128)(2,1)S(1)} %shard_map.116.refs_1_), channel_id=1, source_target_pairs={{0,1},{1,0},{2,3},{3,2},{4,5},{5,4},{6,7},{7,6},{8,9},{9,8},{10,11... | collective-permute-start | bytes 30728 | tf_op jit(solution)/shard_map/ppermute | solution.py:21
  93.6 7.0 %collective-permute-start.16 = (bf16[16,320]{1,0:T(8,128)(2,1)S(1)}, bf16[16,320]{1,0:T(8,128)(2,1)S(1)}, u32[]{:S(2)}, u32[]{:S(2)}) collective-permute-start(bf16[16,320]{1,0:T(8,128)(2,1)S(1)} %shard_map.118.refs_1_), channel_id=1, source_target_pairs={{0,511},{1,2},{2,1},{3,4},{4,3},{5,6},{6,5},{7,8},{8,7},{9,10},{10... | collective-permute-start | bytes 30728 | tf_op jit(solution)/shard_map/ppermute | solution.py:22
  98.5 4.4 %collective-permute-start.15 = (bf16[16,320]{1,0:T(8,128)(2,1)S(1)}, bf16[16,320]{1,0:T(8,128)(2,1)S(1)}, u32[]{:S(2)}, u32[]{:S(2)}) collective-permute-start(bf16[16,320]{1,0:T(8,128)(2,1)S(1)} %shard_map.118.refs_1_), channel_id=1, source_target_pairs={{0,1},{1,0},{2,3},{3,2},{4,5},{5,4},{6,7},{7,6},{8,9},{9,8},{10,11... | collective-permute-start | bytes 30728 | tf_op jit(solution)/shard_map/ppermute | solution.py:21
  104.4 7.1 %collective-permute-start.18 = (bf16[16,320]{1,0:T(8,128)(2,1)S(1)}, bf16[16,320]{1,0:T(8,128)(2,1)S(1)}, u32[]{:S(2)}, u32[]{:S(2)}) collective-permute-start(bf16[16,320]{1,0:T(8,128)(2,1)S(1)} %shard_map.119.refs_1_), channel_id=1, source_target_pairs={{0,511},{1,2},{2,1},{3,4},{4,3},{5,6},{6,5},{7,8},{8,7},{9,10},{10... | collective-permute-start | bytes 30728 | tf_op jit(solution)/shard_map/ppermute | solution.py:22
  115.5 7.1 %collective-permute-start.20 = (bf16[16,320]{1,0:T(8,128)(2,1)S(1)}, bf16[16,320]{1,0:T(8,128)(2,1)S(1)}, u32[]{:S(2)}, u32[]{:S(2)}) collective-permute-start(bf16[16,320]{1,0:T(8,128)(2,1)S(1)} %get-tuple-element.37.refs_1_), channel_id=1, source_target_pairs={{0,511},{1,2},{2,1},{3,4},{4,3},{5,6},{6,5},{7,8},{8,7},{9,10},{10... | collective-permute-start | bytes 30728 | tf_op jit(solution)/shard_map/ppermute | solution.py:22
  133.2 13.0 %collective-permute-start.22 = (bf16[8,320]{1,0:T(8,128)(2,1)S(1)}, bf16[8,320]{1,0:T(8,128)(2,1)S(1)}, u32[]{:S(2)}, u32[]{:S(2)}) collective-permute-start(bf16[8,320]{1,0:T(8,128)(2,1)S(1)} %get-tuple-element.39.refs_1_), channel_id=1, source_target_pairs={{0,508},{4,8},{8,4},{12,16},{16,12},{20,24},{24,20},{28,32},{32,28... | collective-permute-start | bytes 15368 | tf_op jit(solution)/shard_map/ppermute | solution.py:22
  136.0 11.0 %collective-permute-start.21 = (bf16[8,320]{1,0:T(8,128)(2,1)S(1)}, bf16[8,320]{1,0:T(8,128)(2,1)S(1)}, u32[]{:S(2)}, u32[]{:S(2)}) collective-permute-start(bf16[8,320]{1,0:T(8,128)(2,1)S(1)} %get-tuple-element.39.refs_1_), channel_id=1, source_target_pairs={{0,4},{4,0},{8,12},{12,8},{16,20},{20,16},{24,28},{28,24},{32,36},... | collective-permute-start | bytes 15368 | tf_op jit(solution)/shard_map/ppermute | solution.py:21
  148.1 8.3 %collective-permute-start.24 = (bf16[8,320]{1,0:T(8,128)(2,1)S(1)}, bf16[8,320]{1,0:T(8,128)(2,1)S(1)}, u32[]{:S(2)}, u32[]{:S(2)}) collective-permute-start(bf16[8,320]{1,0:T(8,128)(2,1)S(1)} %shard_map.123.refs_1_), channel_id=1, source_target_pairs={{0,508},{4,8},{8,4},{12,16},{16,12},{20,24},{24,20},{28,32},{32,28... | collective-permute-start | bytes 15368 | tf_op jit(solution)/shard_map/ppermute | solution.py:22
  150.0 7.1 %collective-permute-start.23 = (bf16[8,320]{1,0:T(8,128)(2,1)S(1)}, bf16[8,320]{1,0:T(8,128)(2,1)S(1)}, u32[]{:S(2)}, u32[]{:S(2)}) collective-permute-start(bf16[8,320]{1,0:T(8,128)(2,1)S(1)} %shard_map.123.refs_1_), channel_id=1, source_target_pairs={{0,4},{4,0},{8,12},{12,8},{16,20},{20,16},{24,28},{28,24},{32,36},... | collective-permute-start | bytes 15368 | tf_op jit(solution)/shard_map/ppermute | solution.py:21
  (11 other events, 198.9 us)

commit v13 on v11

--- a/solution.py
+++ b/solution.py
@@ -104,16 +104,49 @@
         )
         for i in range(block_sems.shape[0])
     ]
-    for copy in [whole[0], *blocks, *whole[1:]]:
+    for copy in [whole[0], *blocks[:2], *whole[1:], *blocks[2:]]:
         copy.start()
 
     tele, column = lax.axis_index("tele"), lax.axis_index("fine")
     tele_size = lax.axis_size("tele")
+    def set_up():
+        for copy in whole[1:]:
+            copy.wait()
+
+        fine_rows = right_ref.shape[0]
+        rows = pool_rows(links_ref[...], fine_rows, column * tele_size + tele)
+        index = jnp.concatenate([rows.astype(jnp.float32), faces_ref[...].astype(jnp.float32)], axis=0)
+        index_ref[...] = index.T.astype(jnp.int32)
+
+        own = coarse_links_ref.shape[0]
+        count = own * tele_size
+        rows = pool_rows(coarse_links_ref[...], count, column).astype(jnp.float32)
+        kinds = coarse_faces_ref[...].astype(jnp.float32)
+        lists_ref[...] = jnp.zeros(lists_ref.shape, jnp.float32)
+        row = lax.broadcasted_iota(jnp.int32, (count, kinds.shape[1]), 0)
+        for part, values in enumerate((rows, kinds)):
+            placed = jnp.zeros(row.shape, jnp.float32)
+            for c in range(own):
+                placed = jnp.where(row == own * tele + c, values[c : c + 1], placed)
+            lists_ref[:, part * 6 : part * 6 + 6] = placed
+
+        types, size, _ = operators_in_ref.shape
+        unit = lax.broadcasted_iota(jnp.int32, (LANES, size), 0) == lax.broadcasted_iota(jnp.int32, (LANES, size), 1)
+        unit = jnp.where(unit, 1.0, 0.0).astype(jnp.bfloat16)
+        operators_ref[...] = jnp.zeros(operators_ref.shape, jnp.bfloat16)
+        for q in range(types):
+            turned = lax.dot_general(
+                unit, operators_in_ref[q], (((1,), (1,)), ((), ())), preferred_element_type=jnp.float32
+            )
+            operators_ref[q * LANES : (q + 1) * LANES, :size] = turned.astype(jnp.bfloat16)
+
     whole[0].wait()
     lowered = right_ref[...].astype(jnp.bfloat16)
     row = lax.broadcasted_iota(jnp.int32, lowered.shape, 0)
     result = jnp.zeros(lowered.shape, jnp.float32)
     for e in range(inverse_ref.shape[0]):
+        if e == 2 * step:
+            set_up()
         if e % step == 0:
             blocks[e // step].wait()
         product = lax.dot_general(
@@ -121,35 +154,6 @@
         )
         result = jnp.where(row == e, product, result)
     state_ref[...] = result.astype(jnp.bfloat16)
-    for copy in whole[1:]:
-        copy.wait()
-
-    fine_rows = right_ref.shape[0]
-    rows = pool_rows(links_ref[...], fine_rows, column * tele_size + tele)
-    index = jnp.concatenate([rows.astype(jnp.float32), faces_ref[...].astype(jnp.float32)], axis=0)
-    index_ref[...] = index.T.astype(jnp.int32)
-
-    own = coarse_links_ref.shape[0]
-    count = own * tele_size
-    rows = pool_rows(coarse_links_ref[...], count, column).astype(jnp.float32)
-    kinds = coarse_faces_ref[...].astype(jnp.float32)
-    lists_ref[...] = jnp.zeros(lists_ref.shape, jnp.float32)
-    row = lax.broadcasted_iota(jnp.int32, (count, kinds.shape[1]), 0)
-    for part, values in enumerate((rows, kinds)):
-        placed = jnp.zeros(row.shape, jnp.float32)
-        for c in range(own):
-            placed = jnp.where(row == own * tele + c, values[c : c + 1], placed)
-        lists_ref[:, part * 6 : part * 6 + 6] = placed
-
-    types, size, _ = operators_in_ref.shape
-    unit = lax.broadcasted_iota(jnp.int32, (LANES, size), 0) == lax.broadcasted_iota(jnp.int32, (LANES, size), 1)
-    unit = jnp.where(unit, 1.0, 0.0).astype(jnp.bfloat16)
-    operators_ref[...] = jnp.zeros(operators_ref.shape, jnp.bfloat16)
-    for q in range(types):
-        turned = lax.dot_general(
-            unit, operators_in_ref[q], (((1,), (1,)), ((), ())), preferred_element_type=jnp.float32
-        )
-        operators_ref[q * LANES : (q + 1) * LANES, :size] = turned.astype(jnp.bfloat16)
 
 
 def turn_kernel(*refs):

time: 158 us -> 159 us (level)
  no operation moved by 1% of the time
where the time goes in v13:
time: 159 us; the launch traced here: 158 us
  starting transfers between devices  107 us (67%)
  Pallas kernels  23.8 us (15%)
  blocking collectives  13.5 us (8%)
  waiting for transfers between devices  12.4 us (8%)
    ppermute x11, starting transfers between devices, swapped(): lax.ppermute(block, axis, [(i, (i - 1 if i % 2 == 0 else i + 1) % count)...  53.3 us
    ppermute x11, starting transfers between devices, swapped(): inner = lax.ppermute(block, axis, [(i, i ^ 1) for i in range(count)])  44.6 us
    pallas_call x16, Pallas kernels, run(): pl.pallas_call(body, out_shape=[pltpu.VMEM(s, d) if i in pinned else jax....  23.8 us
    all_to_all x2, blocking collectives, shards(): parts = lax.all_to_all(parts, 'tele', 0, 0, tiled=True)  13.5 us
    ppermute x11, waiting for transfers between devices, swapped(): inner = lax.ppermute(block, axis, [(i, i ^ 1) for i in range(count)])  12.1 us
    ppermute x3, starting transfers between devices, across(): lax.ppermute(block, 'tele', [(i, i ^ bits) for i in range(tele_size)])  9.41 us
  transfers between devices with their start and end apart: 25, of which 9 were waited for; matrix products, arithmetic and copies ran while one was open for 0% of the time, Pallas kernels for 5%

profile of v13, /device:TPU:1, one launch (start us, length us, event | category | flops | bytes accessed | tf_op | source)
XLA Modules:
  0.0 157.7 jit_solution(12937637403837723028)
XLA Ops:
  0.0 3.4 %shard_map.109 = (bf16[16,320]{1,0:T(8,128)(2,1)S(1)}, s32[16,12]{1,0:T(8,128)S(1)}, f32[8,64]{1,0:T(8,128)S(1)}, bf16[3072,128]{1,0:T(8,128)(2,1)S(1)}, bf16[16,320,320]{2,1,0:T(8,128)(2,1)S(1)}) custom-call(f32[16,320]{1,0:T(8,128)} %refs_7_.9, s32[6,16]{1,0:T(8,128)} %bitcast.7, s32[6,16]{1,0:T(8,128)} %bitcast.8, s32[2,6]{1,0:T(2,128)} %refs_3_.1, ...), custom_call_target="tpu_custom_call" | custom-call | flops 4294967296 | bytes 3605344 | tf_op jit(solution)/shard_map/pallas_call | solution.py:246
  3.5 3.9 %collective-permute-start = (bf16[16,320]{1,0:T(8,128)(2,1)S(1)}, bf16[16,320]{1,0:T(8,128)(2,1)S(1)}, u32[]{:S(2)}, u32[]{:S(2)}) collective-permute-start(bf16[16,320]{1,0:T(8,128)(2,1)S(1)} %get-tuple-element.27.refs_1_), channel_id=1, source_target_pairs={{0,1},{1,0},{2,3},{3,2},{4,5},{5,4},{6,7},{7,6},{8,9},{9,8},{10,11... | collective-permute-start | bytes 30728 | tf_op jit(solution)/shard_map/ppermute | solution.py:21
  7.4 4.6 %collective-permute-start.1 = (bf16[16,320]{1,0:T(8,128)(2,1)S(1)}, bf16[16,320]{1,0:T(8,128)(2,1)S(1)}, u32[]{:S(2)}, u32[]{:S(2)}) collective-permute-start(bf16[16,320]{1,0:T(8,128)(2,1)S(1)} %get-tuple-element.27.refs_1_), channel_id=1, source_target_pairs={{0,511},{1,2},{2,1},{3,4},{4,3},{5,6},{6,5},{7,8},{8,7},{9,10},{10... | collective-permute-start | bytes 30728 | tf_op jit(solution)/shard_map/ppermute | solution.py:22
  12.0 4.1 %collective-permute-start.4 = (bf16[2,320,320]{2,1,0:T(8,128)(2,1)S(1)}, bf16[2,320,320]{2,1,0:T(8,128)(2,1)S(1)}, u32[]{:S(2)}, u32[]{:S(2)}) collective-permute-start(bf16[2,320,320]{2,1,0:T(8,128)(2,1)S(1)} %copy-done), channel_id=1, source_target_pairs={{0,3},{1,2},{2,1},{3,0},{4,7},{5,6},{6,5},{7,4},{8,11},{9,10},{10,... | collective-permute-start | bytes 1228808 | tf_op jit(solution)/shard_map/ppermute | solution.py:277
  20.1 13.6 %collective-permute-start.5 = (bf16[16,320]{1,0:T(8,128)(2,1)S(1)}, bf16[16,320]{1,0:T(8,128)(2,1)S(1)}, u32[]{:S(2)}, u32[]{:S(2)}) collective-permute-start(bf16[16,320]{1,0:T(8,128)(2,1)S(1)} %shard_map.110.refs_1_), channel_id=1, source_target_pairs={{0,511},{1,2},{2,1},{3,4},{4,3},{5,6},{6,5},{7,8},{8,7},{9,10},{10... | collective-permute-start | bytes 30728 | tf_op jit(solution)/shard_map/ppermute | solution.py:22
  35.7 3.4 %collective-permute-start.8 = (bf16[2,320,320]{2,1,0:T(8,128)(2,1)S(1)}, bf16[2,320,320]{2,1,0:T(8,128)(2,1)S(1)}, u32[]{:S(2)}, u32[]{:S(2)}) collective-permute-start(bf16[2,320,320]{2,1,0:T(8,128)(2,1)S(1)} %collective-permute-done.4.refs_4_.refs_3_), channel_id=1, source_target_pairs={{0,1},{1,0},{2,3},{3,2},{4,5},{5,4},{6,7},{7,6},{8,9},{9,8},{10,11... | collective-permute-start | bytes 1228808 | tf_op jit(solution)/shard_map/ppermute | solution.py:277
  41.0 8.0 %collective-permute-start.7 = (bf16[16,320]{1,0:T(8,128)(2,1)S(1)}, bf16[16,320]{1,0:T(8,128)(2,1)S(1)}, u32[]{:S(2)}, u32[]{:S(2)}) collective-permute-start(bf16[16,320]{1,0:T(8,128)(2,1)S(1)} %get-tuple-element.34.refs_1_), channel_id=1, source_target_pairs={{0,511},{1,2},{2,1},{3,4},{4,3},{5,6},{6,5},{7,8},{8,7},{9,10},{10... | collective-permute-start | bytes 30728 | tf_op jit(solution)/shard_map/ppermute | solution.py:22
  51.0 2.5 %collective-permute-done.6.refs_0_ = bf16[16,320]{1,0:T(8,128)(2,1)S(1)} collective-permute-done((bf16[16,320]{1,0:T(8,128)(2,1)S(1)}, bf16[16,320]{1,0:T(8,128)(2,1)S(1)}, u32[]{:S(2)}, u32[]{:S(2)}) %collective-permute-start.6) | collective-permute-done | bytes 10272 | tf_op jit(solution)/shard_map/ppermute | solution.py:21
  54.5 6.7 %all_to_all.10.refs_0_ = f32[4,8,384]{2,1,0:T(8,128)S(1)} all-to-all(f32[4,8,384]{2,1,0:T(8,128)S(1)} %shard_map.112), channel_id=1, replica_groups=mesh['fine'=128,'tele'=4] {'tele'}, dimensions={0} | all-to-all | bytes 98304 | tf_op jit(solution)/shard_map/all_to_all | solution.py:357
  63.8 6.6 %collective-permute-start.9 = (bf16[8,320]{1,0:T(8,128)(2,1)S(1)}, bf16[8,320]{1,0:T(8,128)(2,1)S(1)}, u32[]{:S(2)}, u32[]{:S(2)}) collective-permute-start(bf16[8,320]{1,0:T(8,128)(2,1)S(1)} %get-tuple-element.39.refs_4_.refs_1_), channel_id=1, source_target_pairs={{0,4},{4,0},{8,12},{12,8},{16,20},{20,16},{24,28},{28,24},{32,36},... | collective-permute-start | bytes 15368 | tf_op jit(solution)/shard_map/ppermute | solution.py:21
  74.9 5.4 %collective-permute-start.11 = (bf16[8,320]{1,0:T(8,128)(2,1)S(1)}, bf16[8,320]{1,0:T(8,128)(2,1)S(1)}, u32[]{:S(2)}, u32[]{:S(2)}) collective-permute-start(bf16[8,320]{1,0:T(8,128)(2,1)S(1)} %shard_map.115.refs_1_), channel_id=1, source_target_pairs={{0,4},{4,0},{8,12},{12,8},{16,20},{20,16},{24,28},{28,24},{32,36},... | collective-permute-start | bytes 15368 | tf_op jit(solution)/shard_map/ppermute | solution.py:21
  82.4 4.3 %collective-permute-start.14 = (bf16[16,320]{1,0:T(8,128)(2,1)S(1)}, bf16[16,320]{1,0:T(8,128)(2,1)S(1)}, u32[]{:S(2)}, u32[]{:S(2)}) collective-permute-start(bf16[16,320]{1,0:T(8,128)(2,1)S(1)} %shard_map.116.refs_1_), channel_id=1, source_target_pairs={{0,511},{1,2},{2,1},{3,4},{4,3},{5,6},{6,5},{7,8},{8,7},{9,10},{10... | collective-permute-start | bytes 30728 | tf_op jit(solution)/shard_map/ppermute | solution.py:22
  88.6 2.7 %shard_map.117.refs_8_ = bf16[16,320,320]{2,1,0:T(8,128)(2,1)S(1)} custom-call(bf16[16,320,320]{2,1,0:T(8,128)(2,1)S(1)} %get-tuple-element.31.refs_8_.refs_0_, bf16[16,320]{1,0:T(8,128)(2,1)S(1)} %get-tuple-element.34.refs_1_), custom_call_target="tpu_custom_call" | custom-call | flops 4294967296 | bytes 3276800 | tf_op jit(solution)/shard_map/pallas_call | solution.py:246
  92.8 3.9 %collective-permute-start.16 = (bf16[16,320]{1,0:T(8,128)(2,1)S(1)}, bf16[16,320]{1,0:T(8,128)(2,1)S(1)}, u32[]{:S(2)}, u32[]{:S(2)}) collective-permute-start(bf16[16,320]{1,0:T(8,128)(2,1)S(1)} %shard_map.118.refs_1_), channel_id=1, source_target_pairs={{0,511},{1,2},{2,1},{3,4},{4,3},{5,6},{6,5},{7,8},{8,7},{9,10},{10... | collective-permute-start | bytes 30728 | tf_op jit(solution)/shard_map/ppermute | solution.py:22
  96.7 2.1 %collective-permute-start.15 = (bf16[16,320]{1,0:T(8,128)(2,1)S(1)}, bf16[16,320]{1,0:T(8,128)(2,1)S(1)}, u32[]{:S(2)}, u32[]{:S(2)}) collective-permute-start(bf16[16,320]{1,0:T(8,128)(2,1)S(1)} %shard_map.118.refs_1_), channel_id=1, source_target_pairs={{0,1},{1,0},{2,3},{3,2},{4,5},{5,4},{6,7},{7,6},{8,9},{9,8},{10,11... | collective-permute-start | bytes 30728 | tf_op jit(solution)/shard_map/ppermute | solution.py:21
  99.1 2.1 %collective-permute-done.15.refs_0_ = bf16[16,320]{1,0:T(8,128)(2,1)S(1)} collective-permute-done((bf16[16,320]{1,0:T(8,128)(2,1)S(1)}, bf16[16,320]{1,0:T(8,128)(2,1)S(1)}, u32[]{:S(2)}, u32[]{:S(2)}) %collective-permute-start.15) | collective-permute-done | bytes 10272 | tf_op jit(solution)/shard_map/ppermute | solution.py:21
  102.6 5.2 %collective-permute-start.18 = (bf16[16,320]{1,0:T(8,128)(2,1)S(1)}, bf16[16,320]{1,0:T(8,128)(2,1)S(1)}, u32[]{:S(2)}, u32[]{:S(2)}) collective-permute-start(bf16[16,320]{1,0:T(8,128)(2,1)S(1)} %shard_map.119.refs_1_), channel_id=1, source_target_pairs={{0,511},{1,2},{2,1},{3,4},{4,3},{5,6},{6,5},{7,8},{8,7},{9,10},{10... | collective-permute-start | bytes 30728 | tf_op jit(solution)/shard_map/ppermute | solution.py:22
  109.7 2.5 %collective-permute-done.17.refs_0_ = bf16[16,320]{1,0:T(8,128)(2,1)S(1)} collective-permute-done((bf16[16,320]{1,0:T(8,128)(2,1)S(1)}, bf16[16,320]{1,0:T(8,128)(2,1)S(1)}, u32[]{:S(2)}, u32[]{:S(2)}) %collective-permute-start.17) | collective-permute-done | bytes 10272 | tf_op jit(solution)/shard_map/ppermute | solution.py:21
  113.7 5.6 %collective-permute-start.20 = (bf16[16,320]{1,0:T(8,128)(2,1)S(1)}, bf16[16,320]{1,0:T(8,128)(2,1)S(1)}, u32[]{:S(2)}, u32[]{:S(2)}) collective-permute-start(bf16[16,320]{1,0:T(8,128)(2,1)S(1)} %get-tuple-element.43.refs_1_), channel_id=1, source_target_pairs={{0,511},{1,2},{2,1},{3,4},{4,3},{5,6},{6,5},{7,8},{8,7},{9,10},{10... | collective-permute-start | bytes 30728 | tf_op jit(solution)/shard_map/ppermute | solution.py:22
  121.2 2.5 %collective-permute-done.19.refs_0_ = bf16[16,320]{1,0:T(8,128)(2,1)S(1)} collective-permute-done((bf16[16,320]{1,0:T(8,128)(2,1)S(1)}, bf16[16,320]{1,0:T(8,128)(2,1)S(1)}, u32[]{:S(2)}, u32[]{:S(2)}) %collective-permute-start.19) | collective-permute-done | bytes 10272 | tf_op jit(solution)/shard_map/ppermute | solution.py:21
  124.7 6.7 %all_to_all.11.refs_0_ = f32[4,8,384]{2,1,0:T(8,128)S(1)} all-to-all(f32[4,8,384]{2,1,0:T(8,128)S(1)} %shard_map.121), channel_id=1, replica_groups=mesh['fine'=128,'tele'=4] {'tele'}, dimensions={0} | all-to-all | bytes 98304 | tf_op jit(solution)/shard_map/all_to_all | solution.py:357
  131.8 2.4 %collective-permute-start.22 = (bf16[8,320]{1,0:T(8,128)(2,1)S(1)}, bf16[8,320]{1,0:T(8,128)(2,1)S(1)}, u32[]{:S(2)}, u32[]{:S(2)}) collective-permute-start(bf16[8,320]{1,0:T(8,128)(2,1)S(1)} %get-tuple-element.45.refs_1_), channel_id=1, source_target_pairs={{0,508},{4,8},{8,4},{12,16},{16,12},{20,24},{24,20},{28,32},{32,28... | collective-permute-start | bytes 15368 | tf_op jit(solution)/shard_map/ppermute | solution.py:22
  134.2 10.6 %collective-permute-start.21 = (bf16[8,320]{1,0:T(8,128)(2,1)S(1)}, bf16[8,320]{1,0:T(8,128)(2,1)S(1)}, u32[]{:S(2)}, u32[]{:S(2)}) collective-permute-start(bf16[8,320]{1,0:T(8,128)(2,1)S(1)} %get-tuple-element.45.refs_1_), channel_id=1, source_target_pairs={{0,4},{4,0},{8,12},{12,8},{16,20},{20,16},{24,28},{28,24},{32,36},... | collective-permute-start | bytes 15368 | tf_op jit(solution)/shard_map/ppermute | solution.py:21
  148.7 6.3 %collective-permute-start.23 = (bf16[8,320]{1,0:T(8,128)(2,1)S(1)}, bf16[8,320]{1,0:T(8,128)(2,1)S(1)}, u32[]{:S(2)}, u32[]{:S(2)}) collective-permute-start(bf16[8,320]{1,0:T(8,128)(2,1)S(1)} %shard_map.123.refs_1_), channel_id=1, source_target_pairs={{0,4},{4,0},{8,12},{12,8},{16,20},{20,16},{24,28},{28,24},{32,36},... | collective-permute-start | bytes 15368 | tf_op jit(solution)/shard_map/ppermute | solution.py:21
  (54 shorter events, 37.8 us)
Async XLA Ops:
  3.5 8.5 %collective-permute-start = (bf16[16,320]{1,0:T(8,128)(2,1)S(1)}, bf16[16,320]{1,0:T(8,128)(2,1)S(1)}, u32[]{:S(2)}, u32[]{:S(2)}) collective-permute-start(bf16[16,320]{1,0:T(8,128)(2,1)S(1)} %get-tuple-element.27.refs_1_), channel_id=1, source_target_pairs={{0,1},{1,0},{2,3},{3,2},{4,5},{5,4},{6,7},{7,6},{8,9},{9,8},{10,11... | collective-permute-start | bytes 30728 | tf_op jit(solution)/shard_map/ppermute | solution.py:21
  7.4 10.7 %collective-permute-start.1 = (bf16[16,320]{1,0:T(8,128)(2,1)S(1)}, bf16[16,320]{1,0:T(8,128)(2,1)S(1)}, u32[]{:S(2)}, u32[]{:S(2)}) collective-permute-start(bf16[16,320]{1,0:T(8,128)(2,1)S(1)} %get-tuple-element.27.refs_1_), channel_id=1, source_target_pairs={{0,511},{1,2},{2,1},{3,4},{4,3},{5,6},{6,5},{7,8},{8,7},{9,10},{10... | collective-permute-start | bytes 30728 | tf_op jit(solution)/shard_map/ppermute | solution.py:22
  12.0 23.6 %collective-permute-start.4 = (bf16[2,320,320]{2,1,0:T(8,128)(2,1)S(1)}, bf16[2,320,320]{2,1,0:T(8,128)(2,1)S(1)}, u32[]{:S(2)}, u32[]{:S(2)}) collective-permute-start(bf16[2,320,320]{2,1,0:T(8,128)(2,1)S(1)} %copy-done), channel_id=1, source_target_pairs={{0,3},{1,2},{2,1},{3,0},{4,7},{5,6},{6,5},{7,4},{8,11},{9,10},{10,... | collective-permute-start | bytes 1228808 | tf_op jit(solution)/shard_map/ppermute | solution.py:277
  16.2 19.5 %collective-permute-start.3 = (bf16[2,320,320]{2,1,0:T(8,128)(2,1)S(1)}, bf16[2,320,320]{2,1,0:T(8,128)(2,1)S(1)}, u32[]{:S(2)}, u32[]{:S(2)}) collective-permute-start(bf16[2,320,320]{2,1,0:T(8,128)(2,1)S(1)} %copy-done), channel_id=1, source_target_pairs={{0,1},{1,0},{2,3},{3,2},{4,5},{5,4},{6,7},{7,6},{8,9},{9,8},{10,11... | collective-permute-start | bytes 1228808 | tf_op jit(solution)/shard_map/ppermute | solution.py:277
  20.1 15.5 %collective-permute-start.5 = (bf16[16,320]{1,0:T(8,128)(2,1)S(1)}, bf16[16,320]{1,0:T(8,128)(2,1)S(1)}, u32[]{:S(2)}, u32[]{:S(2)}) collective-permute-start(bf16[16,320]{1,0:T(8,128)(2,1)S(1)} %shard_map.110.refs_1_), channel_id=1, source_target_pairs={{0,511},{1,2},{2,1},{3,4},{4,3},{5,6},{6,5},{7,8},{8,7},{9,10},{10... | collective-permute-start | bytes 30728 | tf_op jit(solution)/shard_map/ppermute | solution.py:22
  33.7 5.3 %collective-permute-start.2 = (bf16[16,320]{1,0:T(8,128)(2,1)S(1)}, bf16[16,320]{1,0:T(8,128)(2,1)S(1)}, u32[]{:S(2)}, u32[]{:S(2)}) collective-permute-start(bf16[16,320]{1,0:T(8,128)(2,1)S(1)} %shard_map.110.refs_1_), channel_id=1, source_target_pairs={{0,1},{1,0},{2,3},{3,2},{4,5},{5,4},{6,7},{7,6},{8,9},{9,8},{10,11... | collective-permute-start | bytes 30728 | tf_op jit(solution)/shard_map/ppermute | solution.py:21
  35.7 17.9 %collective-permute-start.8 = (bf16[2,320,320]{2,1,0:T(8,128)(2,1)S(1)}, bf16[2,320,320]{2,1,0:T(8,128)(2,1)S(1)}, u32[]{:S(2)}, u32[]{:S(2)}) collective-permute-start(bf16[2,320,320]{2,1,0:T(8,128)(2,1)S(1)} %collective-permute-done.4.refs_4_.refs_3_), channel_id=1, source_target_pairs={{0,1},{1,0},{2,3},{3,2},{4,5},{5,4},{6,7},{7,6},{8,9},{9,8},{10,11... | collective-permute-start | bytes 1228808 | tf_op jit(solution)/shard_map/ppermute | solution.py:277
  41.0 10.0 %collective-permute-start.7 = (bf16[16,320]{1,0:T(8,128)(2,1)S(1)}, bf16[16,320]{1,0:T(8,128)(2,1)S(1)}, u32[]{:S(2)}, u32[]{:S(2)}) collective-permute-start(bf16[16,320]{1,0:T(8,128)(2,1)S(1)} %get-tuple-element.34.refs_1_), channel_id=1, source_target_pairs={{0,511},{1,2},{2,1},{3,4},{4,3},{5,6},{6,5},{7,8},{8,7},{9,10},{10... | collective-permute-start | bytes 30728 | tf_op jit(solution)/shard_map/ppermute | solution.py:22
  49.0 4.5 %collective-permute-start.6 = (bf16[16,320]{1,0:T(8,128)(2,1)S(1)}, bf16[16,320]{1,0:T(8,128)(2,1)S(1)}, u32[]{:S(2)}, u32[]{:S(2)}) collective-permute-start(bf16[16,320]{1,0:T(8,128)(2,1)S(1)} %get-tuple-element.34.refs_1_), channel_id=1, source_target_pairs={{0,1},{1,0},{2,3},{3,2},{4,5},{5,4},{6,7},{7,6},{8,9},{9,8},{10,11... | collective-permute-start | bytes 30728 | tf_op jit(solution)/shard_map/ppermute | solution.py:21
  61.9 10.0 %collective-permute-start.10 = (bf16[8,320]{1,0:T(8,128)(2,1)S(1)}, bf16[8,320]{1,0:T(8,128)(2,1)S(1)}, u32[]{:S(2)}, u32[]{:S(2)}) collective-permute-start(bf16[8,320]{1,0:T(8,128)(2,1)S(1)} %get-tuple-element.39.refs_4_.refs_1_), channel_id=1, source_target_pairs={{0,508},{4,8},{8,4},{12,16},{16,12},{20,24},{24,20},{28,32},{32,28... | collective-permute-start | bytes 15368 | tf_op jit(solution)/shard_map/ppermute | solution.py:22
  63.8 8.0 %collective-permute-start.9 = (bf16[8,320]{1,0:T(8,128)(2,1)S(1)}, bf16[8,320]{1,0:T(8,128)(2,1)S(1)}, u32[]{:S(2)}, u32[]{:S(2)}) collective-permute-start(bf16[8,320]{1,0:T(8,128)(2,1)S(1)} %get-tuple-element.39.refs_4_.refs_1_), channel_id=1, source_target_pairs={{0,4},{4,0},{8,12},{12,8},{16,20},{20,16},{24,28},{28,24},{32,36},... | collective-permute-start | bytes 15368 | tf_op jit(solution)/shard_map/ppermute | solution.py:21
  73.0 7.4 %collective-permute-start.12 = (bf16[8,320]{1,0:T(8,128)(2,1)S(1)}, bf16[8,320]{1,0:T(8,128)(2,1)S(1)}, u32[]{:S(2)}, u32[]{:S(2)}) collective-permute-start(bf16[8,320]{1,0:T(8,128)(2,1)S(1)} %shard_map.115.refs_1_), channel_id=1, source_target_pairs={{0,508},{4,8},{8,4},{12,16},{16,12},{20,24},{24,20},{28,32},{32,28... | collective-permute-start | bytes 15368 | tf_op jit(solution)/shard_map/ppermute | solution.py:22
  74.9 6.3 %collective-permute-start.11 = (bf16[8,320]{1,0:T(8,128)(2,1)S(1)}, bf16[8,320]{1,0:T(8,128)(2,1)S(1)}, u32[]{:S(2)}, u32[]{:S(2)}) collective-permute-start(bf16[8,320]{1,0:T(8,128)(2,1)S(1)} %shard_map.115.refs_1_), channel_id=1, source_target_pairs={{0,4},{4,0},{8,12},{12,8},{16,20},{20,16},{24,28},{28,24},{32,36},... | collective-permute-start | bytes 15368 | tf_op jit(solution)/shard_map/ppermute | solution.py:21
  82.4 8.9 %collective-permute-start.14 = (bf16[16,320]{1,0:T(8,128)(2,1)S(1)}, bf16[16,320]{1,0:T(8,128)(2,1)S(1)}, u32[]{:S(2)}, u32[]{:S(2)}) collective-permute-start(bf16[16,320]{1,0:T(8,128)(2,1)S(1)} %shard_map.116.refs_1_), channel_id=1, source_target_pairs={{0,511},{1,2},{2,1},{3,4},{4,3},{5,6},{6,5},{7,8},{8,7},{9,10},{10... | collective-permute-start | bytes 30728 | tf_op jit(solution)/shard_map/ppermute | solution.py:22
  86.7 4.7 %collective-permute-start.13 = (bf16[16,320]{1,0:T(8,128)(2,1)S(1)}, bf16[16,320]{1,0:T(8,128)(2,1)S(1)}, u32[]{:S(2)}, u32[]{:S(2)}) collective-permute-start(bf16[16,320]{1,0:T(8,128)(2,1)S(1)} %shard_map.116.refs_1_), channel_id=1, source_target_pairs={{0,1},{1,0},{2,3},{3,2},{4,5},{5,4},{6,7},{7,6},{8,9},{9,8},{10,11... | collective-permute-start | bytes 30728 | tf_op jit(solution)/shard_map/ppermute | solution.py:21
  92.8 6.3 %collective-permute-start.16 = (bf16[16,320]{1,0:T(8,128)(2,1)S(1)}, bf16[16,320]{1,0:T(8,128)(2,1)S(1)}, u32[]{:S(2)}, u32[]{:S(2)}) collective-permute-start(bf16[16,320]{1,0:T(8,128)(2,1)S(1)} %shard_map.118.refs_1_), channel_id=1, source_target_pairs={{0,511},{1,2},{2,1},{3,4},{4,3},{5,6},{6,5},{7,8},{8,7},{9,10},{10... | collective-permute-start | bytes 30728 | tf_op jit(solution)/shard_map/ppermute | solution.py:22
  96.7 4.4 %collective-permute-start.15 = (bf16[16,320]{1,0:T(8,128)(2,1)S(1)}, bf16[16,320]{1,0:T(8,128)(2,1)S(1)}, u32[]{:S(2)}, u32[]{:S(2)}) collective-permute-start(bf16[16,320]{1,0:T(8,128)(2,1)S(1)} %shard_map.118.refs_1_), channel_id=1, source_target_pairs={{0,1},{1,0},{2,3},{3,2},{4,5},{5,4},{6,7},{7,6},{8,9},{9,8},{10,11... | collective-permute-start | bytes 30728 | tf_op jit(solution)/shard_map/ppermute | solution.py:21
  102.6 7.1 %collective-permute-start.18 = (bf16[16,320]{1,0:T(8,128)(2,1)S(1)}, bf16[16,320]{1,0:T(8,128)(2,1)S(1)}, u32[]{:S(2)}, u32[]{:S(2)}) collective-permute-start(bf16[16,320]{1,0:T(8,128)(2,1)S(1)} %shard_map.119.refs_1_), channel_id=1, source_target_pairs={{0,511},{1,2},{2,1},{3,4},{4,3},{5,6},{6,5},{7,8},{8,7},{9,10},{10... | collective-permute-start | bytes 30728 | tf_op jit(solution)/shard_map/ppermute | solution.py:22
  107.8 4.4 %collective-permute-start.17 = (bf16[16,320]{1,0:T(8,128)(2,1)S(1)}, bf16[16,320]{1,0:T(8,128)(2,1)S(1)}, u32[]{:S(2)}, u32[]{:S(2)}) collective-permute-start(bf16[16,320]{1,0:T(8,128)(2,1)S(1)} %shard_map.119.refs_1_), channel_id=1, source_target_pairs={{0,1},{1,0},{2,3},{3,2},{4,5},{5,4},{6,7},{7,6},{8,9},{9,8},{10,11... | collective-permute-start | bytes 30728 | tf_op jit(solution)/shard_map/ppermute | solution.py:21
  113.7 7.5 %collective-permute-start.20 = (bf16[16,320]{1,0:T(8,128)(2,1)S(1)}, bf16[16,320]{1,0:T(8,128)(2,1)S(1)}, u32[]{:S(2)}, u32[]{:S(2)}) collective-permute-start(bf16[16,320]{1,0:T(8,128)(2,1)S(1)} %get-tuple-element.43.refs_1_), channel_id=1, source_target_pairs={{0,511},{1,2},{2,1},{3,4},{4,3},{5,6},{6,5},{7,8},{8,7},{9,10},{10... | collective-permute-start | bytes 30728 | tf_op jit(solution)/shard_map/ppermute | solution.py:22
  131.8 13.0 %collective-permute-start.22 = (bf16[8,320]{1,0:T(8,128)(2,1)S(1)}, bf16[8,320]{1,0:T(8,128)(2,1)S(1)}, u32[]{:S(2)}, u32[]{:S(2)}) collective-permute-start(bf16[8,320]{1,0:T(8,128)(2,1)S(1)} %get-tuple-element.45.refs_1_), channel_id=1, source_target_pairs={{0,508},{4,8},{8,4},{12,16},{16,12},{20,24},{24,20},{28,32},{32,28... | collective-permute-start | bytes 15368 | tf_op jit(solution)/shard_map/ppermute | solution.py:22
  134.2 11.4 %collective-permute-start.21 = (bf16[8,320]{1,0:T(8,128)(2,1)S(1)}, bf16[8,320]{1,0:T(8,128)(2,1)S(1)}, u32[]{:S(2)}, u32[]{:S(2)}) collective-permute-start(bf16[8,320]{1,0:T(8,128)(2,1)S(1)} %get-tuple-element.45.refs_1_), channel_id=1, source_target_pairs={{0,4},{4,0},{8,12},{12,8},{16,20},{20,16},{24,28},{28,24},{32,36},... | collective-permute-start | bytes 15368 | tf_op jit(solution)/shard_map/ppermute | solution.py:21
  146.7 8.3 %collective-permute-start.24 = (bf16[8,320]{1,0:T(8,128)(2,1)S(1)}, bf16[8,320]{1,0:T(8,128)(2,1)S(1)}, u32[]{:S(2)}, u32[]{:S(2)}) collective-permute-start(bf16[8,320]{1,0:T(8,128)(2,1)S(1)} %shard_map.123.refs_1_), channel_id=1, source_target_pairs={{0,508},{4,8},{8,4},{12,16},{16,12},{20,24},{24,20},{28,32},{32,28... | collective-permute-start | bytes 15368 | tf_op jit(solution)/shard_map/ppermute | solution.py:22
  148.7 7.1 %collective-permute-start.23 = (bf16[8,320]{1,0:T(8,128)(2,1)S(1)}, bf16[8,320]{1,0:T(8,128)(2,1)S(1)}, u32[]{:S(2)}, u32[]{:S(2)}) collective-permute-start(bf16[8,320]{1,0:T(8,128)(2,1)S(1)} %shard_map.123.refs_1_), channel_id=1, source_target_pairs={{0,4},{4,0},{8,12},{12,8},{16,20},{20,16},{24,28},{28,24},{32,36},... | collective-permute-start | bytes 15368 | tf_op jit(solution)/shard_map/ppermute | solution.py:21
  (6 other events, 104.2 us)
